TPU v7x, 256 devices: a whole 4x4x8 slice. The times are simulated.
256 devices in a mesh: row: 32 (over z, y_lo, core), pair: 8 (over x, y_hi).
Axes of the slice: x: 4, y: 4 (y_hi: 2, y_lo: 2; y = y_hi * 2 + y_lo), z: 8, core: 2. Of those that a mesh axis runs over, the one named last changes fastest.
Arguments:
- panel: float32 [16384, 2048], P('row', 'pair'), may hold values from -200 to 200, as said below
Outputs:
- rotated: float32 [16384, 2048], P('row', 'pair')
Inputs may be any that keep to these rules, and one draw needn't show every extreme that they name: `panel`: real entries.
All inputs are finite; a program needn't handle non-finite values.
Results may differ from a plain program's by a relative error of at most 0.00016.
Values sent between devices are 32-bit elements; how exact they have to be, the bound alone decides.
No kernel may reach another device: no remote copies, remote signals or barrier semaphores. Data moves between devices by JAX's collectives and lax.ppermute only.
A program may use at most 64 MiB of HBM per device.

v0:
```python
import jax
import jax.numpy as jnp
from jax import lax
from jax.experimental import pallas as pl
from jax.experimental.pallas import tpu as pltpu
from jax.sharding import PartitionSpec as P


STEPS = 3

BF16 = jnp.bfloat16
F32 = jnp.float32
HIGH = lax.Precision.HIGHEST

QUAD = 4
PAD = 8


def split(x):
    hi = x.astype(BF16)
    return hi, (x - hi.astype(F32)).astype(BF16)


def left3(x):
    return jnp.concatenate(split(x), 1)


def right3(x):
    hi, lo = split(x)
    top = jnp.concatenate([hi, lo], 1)
    low = jnp.concatenate([hi, jnp.zeros_like(hi)], 1)
    return jnp.concatenate([top, low], 0)


def times3(left, right):
    out = jnp.dot(left, right, preferred_element_type=F32)
    n = out.shape[1] // 2
    return out[:, :n] + out[:, n:]


def times(a, b):
    return jnp.dot(a, b, precision=HIGH, preferred_element_type=F32)


def rotation(cross, diag_a, diag_b):
    n = cross.shape[0]
    scale_a = lax.rsqrt(diag_a + 1e-06)
    scale_b = lax.rsqrt(diag_b + 1e-06)
    d = 0.25 * (cross * jnp.transpose(jnp.broadcast_to(scale_a, (n, n))) * scale_b)
    dt = jnp.transpose(d)
    shape = (n, n)
    eye = jnp.where(
        lax.broadcasted_iota(jnp.int32, shape, 0) == lax.broadcasted_iota(jnp.int32, shape, 1),
        1.0,
        0.0,
    ).astype(F32)
    base = eye + times(d, dt)
    top = 1.0 + 1.001 * (0.25 * n) ** 2
    start = 2.0 / (1.0 + top)
    gap = (top - 1.0) / (top + 1.0)
    y = start * base
    x = None
    while gap > 1e-3:
        z = 2.0 * eye - y
        stretch = 2.0 / (2.0 - gap * gap)
        right = right3(z)
        if x is None:
            y = stretch * times3(left3(y), right)
            x = (stretch * start) * z
        else:
            both = stretch * times3(jnp.concatenate([left3(x), left3(y)], 0), right)
            x, y = both[:n], both[n:]
        gap = gap * gap / (2.0 - gap * gap)
    for _ in range(2):
        x = times(x, 2.0 * eye - times(base, x))
    md = times(x, d)
    mixed = 2.0 * md
    return 2.0 * x - eye, mixed, -jnp.transpose(mixed), eye - 2.0 * times(dt, md)


def message(diag_a, diag_b, cross, core, cross_ref, mine_ref, other_ref):
    n = cross.shape[0]
    half = n // 2
    step = half + PAD
    cross_ref[:half] = cross[:half]
    cross_ref[step : step + half] = cross[half:]
    cross_ref[half:step] = jnp.broadcast_to(diag_a, (PAD, n))
    cross_ref[step + half :] = jnp.broadcast_to(diag_b, (PAD, n))
    mine_ref[...] = cross_ref[pl.ds(pl.multiple_of(core * step, 8), step), :]
    other_ref[...] = cross_ref[pl.ds(pl.multiple_of((1 - core) * step, 8), step), :]


def both_blocks(refs):
    if len(refs) == 1:
        n = refs[0].shape[1] // 2
        return refs[0][:, :n], refs[0][:, n:]
    return refs[0][...], refs[1][...]


def gram_kernel(core_ref, *refs):
    *blocks, mine_ref, other_ref, cross_ref = refs
    a, b = both_blocks(blocks)
    n = a.shape[1]
    a_hi, a_lo = split(jnp.transpose(a))
    b_hi, b_lo = split(b)
    wide = jnp.dot(a_hi, jnp.concatenate([b_hi, b_lo], 1), preferred_element_type=F32)
    cross = wide[:, :n] + wide[:, n:] + jnp.dot(a_lo, b_hi, preferred_element_type=F32)
    message(
        jnp.sum(a * a, 0, keepdims=True),
        jnp.sum(b * b, 0, keepdims=True),
        cross,
        core_ref[0],
        cross_ref,
        mine_ref,
        other_ref,
    )


def cayley_blocks(core_ref, mine_ref, other_ref):
    half = mine_ref.shape[0] - PAD
    first = core_ref[0] == 0
    mine = mine_ref[...]
    other = other_ref[...]
    low = jnp.where(first, mine, other)
    high = jnp.where(first, other, mine)
    cross = jnp.concatenate([low[:half], high[:half]], 0)
    return rotation(cross, low[half : half + 1], high[half : half + 1])


def rows_times(rows, top, low):
    x_hi, x_lo = rows
    n = top.shape[1]
    c_hi, c_lo = split(jnp.concatenate([top, low], 0))
    wide = jnp.dot(x_hi, jnp.concatenate([c_hi, c_lo], 1), preferred_element_type=F32)
    return wide[:, :n] + wide[:, n:] + jnp.dot(x_lo, c_hi, preferred_element_type=F32)


def first_kernel(core_ref, mine_ref, other_ref, *refs):
    *blocks, a_out = refs
    c11, _, c21, _ = cayley_blocks(core_ref, mine_ref, other_ref)
    rows = split(jnp.concatenate(both_blocks(blocks), 1))
    a_out[...] = rows_times(rows, c11, c21)


def both_kernel(core_ref, mine_ref, other_ref, *refs):
    *blocks, a_out, b_out = refs
    c11, c12, c21, c22 = cayley_blocks(core_ref, mine_ref, other_ref)
    rows = split(jnp.concatenate(both_blocks(blocks), 1))
    b_out[...] = rows_times(rows, c12, c22)
    a_out[...] = rows_times(rows, c11, c21)


def last_kernel(core_ref, mine_ref, other_ref, *refs):
    own_ref, *blocks, out_ref, b_ref, sems = refs
    n = own_ref.shape[1]
    own_copy = pltpu.make_async_copy(own_ref, out_ref.at[:, :n], sems.at[0])
    own_copy.start()
    _, c12, _, c22 = cayley_blocks(core_ref, mine_ref, other_ref)
    rows = split(jnp.concatenate(both_blocks(blocks), 1))
    b_ref[...] = rows_times(rows, c12, c22)
    b_copy = pltpu.make_async_copy(b_ref, out_ref.at[:, n:], sems.at[1])
    b_copy.start()
    own_copy.wait()
    b_copy.wait()


def in_specs(count):
    return [pl.BlockSpec(memory_space=pltpu.SMEM)] + [
        pl.BlockSpec(memory_space=pltpu.VMEM)
    ] * count


def near(x):
    return pltpu.with_memory_space_constraint(x, pltpu.VMEM)


def gram(core, blocks, n):
    half = pltpu.VMEM((n // 2 + PAD, n), F32)
    return pl.pallas_call(
        gram_kernel,
        out_shape=[half, half],
        in_specs=in_specs(len(blocks)),
        scratch_shapes=[pltpu.VMEM((n + 2 * PAD, n), F32)],
        name="gram",
    )(core, *map(near, blocks))


def turn_first(core, halves, blocks, n):
    return pl.pallas_call(
        first_kernel,
        out_shape=pltpu.VMEM((blocks[0].shape[0], n), F32),
        in_specs=in_specs(2 + len(blocks)),
        name="turn_first",
    )(core, *map(near, halves), *map(near, blocks))


def turn_both(core, halves, blocks, n):
    return pl.pallas_call(
        both_kernel,
        out_shape=[pltpu.VMEM((blocks[0].shape[0], n), F32)] * 2,
        in_specs=in_specs(2 + len(blocks)),
        name="turn_both",
    )(core, *map(near, halves), *map(near, blocks))


def turn_last(core, halves, own, blocks):
    rows, n = own.shape
    return pl.pallas_call(
        last_kernel,
        out_shape=jax.ShapeDtypeStruct((rows, 2 * n), F32),
        in_specs=in_specs(3 + len(blocks)),
        out_specs=pl.BlockSpec(memory_space=pl.ANY),
        scratch_shapes=[pltpu.VMEM((rows, n), F32), pltpu.SemaphoreType.DMA((2,))],
        name="turn_last",
    )(core, *map(near, halves), near(own), *map(near, blocks))


def from_row(x, source):
    devices = range(lax.axis_size("row"))
    line = len(devices) // QUAD
    route = []
    for i in devices:
        z, y_lo, core = source(i // QUAD, i // 2 % 2, i % 2)
        route.append((z % line * QUAD + y_lo * 2 + core, i))
    return lax.ppermute(x, "row", route)


def side(z):
    return 1 if z % 2 else -1


def summed_halves(mine, other):
    x = mine + from_row(other, lambda z, y, c: (z, y, 1 - c))
    x = (
        (x + from_row(x, lambda z, y, c: (z ^ 1, y, c)))
        + from_row(x, lambda z, y, c: (z, 1 - y, c))
        + from_row(x, lambda z, y, c: (z ^ 1, 1 - y, c))
    )
    x = (
        (x + from_row(x, lambda z, y, c: (z + side(z), y, c)))
        + from_row(x, lambda z, y, c: (z - 2 * side(z), y, c))
        + from_row(x, lambda z, y, c: (z + 3 * side(z), y, c))
    )
    return x


def with_other(half):
    return [half, from_row(half, lambda z, y, c: (z, y, 1 - c))]


def shifted(block):
    devices = range(lax.axis_size("pair"))
    route = [((i - 1) % len(devices), i) for i in devices]
    return lax.ppermute(block, "pair", route)


def local(panel):
    n = panel.shape[1] // 2
    core = (lax.axis_index("row") & 1).astype(jnp.int32).reshape(1)
    own = [panel]
    before = [shifted(panel)]
    for step in range(STEPS):
        mine, other = gram(core, own, n)
        half = summed_halves(mine, other)
        hopped = shifted(half)
        a = turn_first(core, with_other(half), own, n)
        halves = with_other(hopped)
        if step + 1 == STEPS:
            return turn_last(core, halves, a, before)
        a_before, b = turn_both(core, halves, before, n)
        own = [a, b]
        before = [a_before, shifted(b)]


def solution(mesh):
    return jax.shard_map(
        local,
        mesh=mesh,
        in_specs=(P("row", "pair"),),
        out_specs=P("row", "pair"),
        check_vma=False,
    )
```

profile of v0, /device:TPU:1, one launch (start us, length us, event | category | flops | bytes accessed | tf_op | source)
XLA Modules:
  0.0 108.8 jit_solution(1371699137639911397)
XLA Ops:
  1.3 3.3 %collective-permute-start = (f32[72,128]{1,0:T(8,128)S(1)}, f32[72,128]{1,0:T(8,128)S(1)}, u32[]{:S(2)}, u32[]{:S(2)}) collective-permute-start(f32[72,128]{1,0:T(8,128)S(1)} %get-tuple-element.16), channel_id=1, source_target_pairs={{8,0},{0,8},{24,16},{16,24},{40,32},{32,40},{56,48},{48,56},{72,64... | collective-permute-start | bytes 110600 | tf_op jit(solution)/shard_map/ppermute | solution.py:225
  6.6 1.5 %collective-permute-start.1 = (f32[72,128]{1,0:T(8,128)S(1)}, f32[72,128]{1,0:T(8,128)S(1)}, u32[]{:S(2)}, u32[]{:S(2)}) collective-permute-start(f32[72,128]{1,0:T(8,128)S(1)} %add.63), channel_id=1, source_target_pairs={{32,0},{40,8},{48,16},{56,24},{0,32},{8,40},{16,48},{24,56},{96,64... | collective-permute-start | bytes 110600 | tf_op jit(solution)/shard_map/ppermute | solution.py:225
  8.1 1.4 %collective-permute-start.10 = (f32[512,256]{1,0:T(8,128)S(1)}, f32[512,256]{1,0:T(8,128)S(1)}, u32[]{:S(2)}, u32[]{:S(2)}) collective-permute-start(f32[512,256]{1,0:T(8,128)S(1)} %copy-done), channel_id=1, source_target_pairs={{7,0},{0,1},{1,2},{2,3},{3,4},{4,5},{5,6},{6,7},{15,8},{8,9},{9,10... | collective-permute-start | bytes 1572872 | tf_op jit(solution)/shard_map/ppermute | solution.py:254
  9.9 6.0 %collective-permute-start.6 = (f32[72,128]{1,0:T(8,128)S(1)}, f32[72,128]{1,0:T(8,128)S(1)}, u32[]{:S(2)}, u32[]{:S(2)}) collective-permute-start(f32[72,128]{1,0:T(8,128)S(1)} %add_add_fusion.5), channel_id=1, source_target_pairs={{160,0},{168,8},{176,16},{184,24},{128,32},{136,40},{144,48},{152,... | collective-permute-start | bytes 110600 | tf_op jit(solution)/shard_map/ppermute | solution.py:225
  16.2 2.9 %collective-permute-start.4 = (f32[72,128]{1,0:T(8,128)S(1)}, f32[72,128]{1,0:T(8,128)S(1)}, u32[]{:S(2)}, u32[]{:S(2)}) collective-permute-start(f32[72,128]{1,0:T(8,128)S(1)} %add_add_fusion.5), channel_id=1, source_target_pairs={{224,0},{232,8},{240,16},{248,24},{64,32},{72,40},{80,48},{88,56},... | collective-permute-start | bytes 110600 | tf_op jit(solution)/shard_map/ppermute | solution.py:225
  19.1 1.3 %collective-permute-done.5 = f32[72,128]{1,0:T(8,128)S(1)} collective-permute-done((f32[72,128]{1,0:T(8,128)S(1)}, f32[72,128]{1,0:T(8,128)S(1)}, u32[]{:S(2)}, u32[]{:S(2)}) %collective-permute-start.5) | collective-permute-done | bytes 36896 | tf_op jit(solution)/shard_map/ppermute | solution.py:225
  21.1 2.1 %collective-permute-start.8 = (f32[72,128]{1,0:T(8,128)S(1)}, f32[72,128]{1,0:T(8,128)S(1)}, u32[]{:S(2)}, u32[]{:S(2)}) collective-permute-start(f32[72,128]{1,0:T(8,128)S(1)} %add_add_fusion.4.mine_ref), channel_id=1, source_target_pairs={{7,0},{0,1},{1,2},{2,3},{3,4},{4,5},{5,6},{6,7},{15,8},{8,9},{9,10... | collective-permute-start | bytes 110600 | tf_op jit(solution)/shard_map/ppermute | solution.py:254
  23.2 3.5 %collective-permute-start.7 = (f32[72,128]{1,0:T(8,128)S(1)}, f32[72,128]{1,0:T(8,128)S(1)}, u32[]{:S(2)}, u32[]{:S(2)}) collective-permute-start(f32[72,128]{1,0:T(8,128)S(1)} %add_add_fusion.4.mine_ref), channel_id=1, source_target_pairs={{8,0},{0,8},{24,16},{16,24},{40,32},{32,40},{56,48},{48,56},{72,64... | collective-permute-start | bytes 110600 | tf_op jit(solution)/shard_map/ppermute | solution.py:225
  27.6 8.8 %collective-permute-start.9 = (f32[72,128]{1,0:T(8,128)S(1)}, f32[72,128]{1,0:T(8,128)S(1)}, u32[]{:S(2)}, u32[]{:S(2)}) collective-permute-start(f32[72,128]{1,0:T(8,128)S(1)} %collective-permute-done.8.mine_ref), channel_id=1, source_target_pairs={{8,0},{0,8},{24,16},{16,24},{40,32},{32,40},{56,48},{48,56},{72,64... | collective-permute-start | bytes 110600 | tf_op jit(solution)/shard_map/ppermute | solution.py:225
  36.5 3.3 %turn_first.3.refs_0_ = f32[512,128]{1,0:T(8,128)S(1)} custom-call(s32[1]{0:T(128)} %bitcast.core_ref, f32[72,128]{1,0:T(8,128)S(1)} %add_add_fusion.4.mine_ref, f32[72,128]{1,0:T(8,128)S(1)} %collective-permute-done.7.other_ref, f32[512,256]{1,0:T(8,128)S(1)} %copy-done), custom_call_target="tpu_custom_call" | custom-call | tf_op jit(solution)/shard_map/turn_first/pallas_call | solution.py:189
  39.7 3.5 %turn_both.2 = (f32[512,128]{1,0:T(8,128)S(1)}, f32[512,128]{1,0:T(8,128)S(1)}) custom-call(s32[1]{0:T(128)} %bitcast.core_ref, f32[72,128]{1,0:T(8,128)S(1)} %collective-permute-done.8.mine_ref, f32[72,128]{1,0:T(8,128)S(1)} %collective-permute-done.9.other_ref, f32[512,256]{1,0:T(8,128)S(1)} %collective-permute-done.10.refs_0_), custom_call_target="tpu_custom_call" | custom-call | tf_op jit(solution)/shard_map/turn_both/pallas_call | solution.py:198
  43.6 1.2 %collective-permute-done.11 = f32[72,128]{1,0:T(8,128)S(1)} collective-permute-done((f32[72,128]{1,0:T(8,128)S(1)}, f32[72,128]{1,0:T(8,128)S(1)}, u32[]{:S(2)}, u32[]{:S(2)}) %collective-permute-start.11) | collective-permute-done | bytes 36896 | tf_op jit(solution)/shard_map/ppermute | solution.py:225
  44.8 2.1 %collective-permute-start.14 = (f32[72,128]{1,0:T(8,128)S(1)}, f32[72,128]{1,0:T(8,128)S(1)}, u32[]{:S(2)}, u32[]{:S(2)}) collective-permute-start(f32[72,128]{1,0:T(8,128)S(1)} %add.70), channel_id=1, source_target_pairs={{48,0},{56,8},{32,16},{40,24},{16,32},{24,40},{0,48},{8,56},{112,6... | collective-permute-start | bytes 110600 | tf_op jit(solution)/shard_map/ppermute | solution.py:225
  49.9 3.6 %collective-permute-start.17 = (f32[72,128]{1,0:T(8,128)S(1)}, f32[72,128]{1,0:T(8,128)S(1)}, u32[]{:S(2)}, u32[]{:S(2)}) collective-permute-start(f32[72,128]{1,0:T(8,128)S(1)} %add_add_fusion.3), channel_id=1, source_target_pairs={{160,0},{168,8},{176,16},{184,24},{128,32},{136,40},{144,48},{152,... | collective-permute-start | bytes 110600 | tf_op jit(solution)/shard_map/ppermute | solution.py:225
  53.5 1.7 %collective-permute-start.16 = (f32[72,128]{1,0:T(8,128)S(1)}, f32[72,128]{1,0:T(8,128)S(1)}, u32[]{:S(2)}, u32[]{:S(2)}) collective-permute-start(f32[72,128]{1,0:T(8,128)S(1)} %add_add_fusion.3), channel_id=1, source_target_pairs={{64,0},{72,8},{80,16},{88,24},{224,32},{232,40},{240,48},{248,56},... | collective-permute-start | bytes 110600 | tf_op jit(solution)/shard_map/ppermute | solution.py:225
  56.2 1.7 %collective-permute-done.16 = f32[72,128]{1,0:T(8,128)S(1)} collective-permute-done((f32[72,128]{1,0:T(8,128)S(1)}, f32[72,128]{1,0:T(8,128)S(1)}, u32[]{:S(2)}, u32[]{:S(2)}) %collective-permute-start.16) | collective-permute-done | bytes 36896 | tf_op jit(solution)/shard_map/ppermute | solution.py:225
  57.9 1.4 %collective-permute-done.15 = f32[72,128]{1,0:T(8,128)S(1)} collective-permute-done((f32[72,128]{1,0:T(8,128)S(1)}, f32[72,128]{1,0:T(8,128)S(1)}, u32[]{:S(2)}, u32[]{:S(2)}) %collective-permute-start.15) | collective-permute-done | bytes 36896 | tf_op jit(solution)/shard_map/ppermute | solution.py:225
  59.4 2.7 %collective-permute-start.18 = (f32[72,128]{1,0:T(8,128)S(1)}, f32[72,128]{1,0:T(8,128)S(1)}, u32[]{:S(2)}, u32[]{:S(2)}) collective-permute-start(f32[72,128]{1,0:T(8,128)S(1)} %add_add_fusion.2.mine_ref), channel_id=1, source_target_pairs={{8,0},{0,8},{24,16},{16,24},{40,32},{32,40},{56,48},{48,56},{72,64... | collective-permute-start | bytes 110600 | tf_op jit(solution)/shard_map/ppermute | solution.py:225
  62.2 4.3 %collective-permute-done.19.mine_ref = f32[72,128]{1,0:T(8,128)S(1)} collective-permute-done((f32[72,128]{1,0:T(8,128)S(1)}, f32[72,128]{1,0:T(8,128)S(1)}, u32[]{:S(2)}, u32[]{:S(2)}) %collective-permute-start.19) | collective-permute-done | bytes 36896 | tf_op jit(solution)/shard_map/ppermute | solution.py:254
  66.5 3.1 %collective-permute-start.20 = (f32[72,128]{1,0:T(8,128)S(1)}, f32[72,128]{1,0:T(8,128)S(1)}, u32[]{:S(2)}, u32[]{:S(2)}) collective-permute-start(f32[72,128]{1,0:T(8,128)S(1)} %collective-permute-done.19.mine_ref), channel_id=1, source_target_pairs={{8,0},{0,8},{24,16},{16,24},{40,32},{32,40},{56,48},{48,56},{72,64... | collective-permute-start | bytes 110600 | tf_op jit(solution)/shard_map/ppermute | solution.py:225
  69.7 3.3 %turn_first.4.refs_0_ = f32[512,128]{1,0:T(8,128)S(1)} custom-call(s32[1]{0:T(128)} %bitcast.core_ref, f32[72,128]{1,0:T(8,128)S(1)} %add_add_fusion.2.mine_ref, f32[72,128]{1,0:T(8,128)S(1)} %collective-permute-done.18.other_ref, f32[512,128]{1,0:T(8,128)S(1)} %turn_first.3.refs_0_, f32[512,128]{1,0:T(8,128)S(1)} %get-tuple-element.17.refs_1_), custom_call_target="tpu_custom_call" | custom-call | tf_op jit(solution)/shard_map/turn_first/pallas_call | solution.py:189
  72.9 3.5 %turn_both.3 = (f32[512,128]{1,0:T(8,128)S(1)}, f32[512,128]{1,0:T(8,128)S(1)}) custom-call(s32[1]{0:T(128)} %bitcast.core_ref, f32[72,128]{1,0:T(8,128)S(1)} %collective-permute-done.19.mine_ref, f32[72,128]{1,0:T(8,128)S(1)} %collective-permute-done.20.other_ref, f32[512,128]{1,0:T(8,128)S(1)} %get-tuple-element.20.refs_0_, ...), custom_call_target="tpu_custom_call" | custom-call | tf_op jit(solution)/shard_map/turn_both/pallas_call | solution.py:198
  79.4 1.3 %collective-permute-start.23 = (f32[72,128]{1,0:T(8,128)S(1)}, f32[72,128]{1,0:T(8,128)S(1)}, u32[]{:S(2)}, u32[]{:S(2)}) collective-permute-start(f32[72,128]{1,0:T(8,128)S(1)} %add.77), channel_id=1, source_target_pairs={{32,0},{40,8},{48,16},{56,24},{0,32},{8,40},{16,48},{24,56},{96,64... | collective-permute-start | bytes 110600 | tf_op jit(solution)/shard_map/ppermute | solution.py:225
  82.7 2.3 %collective-permute-start.28 = (f32[72,128]{1,0:T(8,128)S(1)}, f32[72,128]{1,0:T(8,128)S(1)}, u32[]{:S(2)}, u32[]{:S(2)}) collective-permute-start(f32[72,128]{1,0:T(8,128)S(1)} %add_add_fusion.1), channel_id=1, source_target_pairs={{160,0},{168,8},{176,16},{184,24},{128,32},{136,40},{144,48},{152,... | collective-permute-start | bytes 110600 | tf_op jit(solution)/shard_map/ppermute | solution.py:225
  84.9 1.6 %collective-permute-start.27 = (f32[72,128]{1,0:T(8,128)S(1)}, f32[72,128]{1,0:T(8,128)S(1)}, u32[]{:S(2)}, u32[]{:S(2)}) collective-permute-start(f32[72,128]{1,0:T(8,128)S(1)} %add_add_fusion.1), channel_id=1, source_target_pairs={{64,0},{72,8},{80,16},{88,24},{224,32},{232,40},{240,48},{248,56},... | collective-permute-start | bytes 110600 | tf_op jit(solution)/shard_map/ppermute | solution.py:225
  86.5 1.7 %collective-permute-start.26 = (f32[72,128]{1,0:T(8,128)S(1)}, f32[72,128]{1,0:T(8,128)S(1)}, u32[]{:S(2)}, u32[]{:S(2)}) collective-permute-start(f32[72,128]{1,0:T(8,128)S(1)} %add_add_fusion.1), channel_id=1, source_target_pairs={{224,0},{232,8},{240,16},{248,24},{64,32},{72,40},{80,48},{88,56},... | collective-permute-start | bytes 110600 | tf_op jit(solution)/shard_map/ppermute | solution.py:225
  88.6 2.1 %collective-permute-done.26 = f32[72,128]{1,0:T(8,128)S(1)} collective-permute-done((f32[72,128]{1,0:T(8,128)S(1)}, f32[72,128]{1,0:T(8,128)S(1)}, u32[]{:S(2)}, u32[]{:S(2)}) %collective-permute-start.26) | collective-permute-done | bytes 36896 | tf_op jit(solution)/shard_map/ppermute | solution.py:225
  90.9 2.7 %collective-permute-start.31 = (f32[72,128]{1,0:T(8,128)S(1)}, f32[72,128]{1,0:T(8,128)S(1)}, u32[]{:S(2)}, u32[]{:S(2)}) collective-permute-start(f32[72,128]{1,0:T(8,128)S(1)} %add_add_fusion.mine_ref), channel_id=1, source_target_pairs={{8,0},{0,8},{24,16},{16,24},{40,32},{32,40},{56,48},{48,56},{72,64... | collective-permute-start | bytes 110600 | tf_op jit(solution)/shard_map/ppermute | solution.py:225
  93.5 5.0 %collective-permute-done.29.mine_ref = f32[72,128]{1,0:T(8,128)S(1)} collective-permute-done((f32[72,128]{1,0:T(8,128)S(1)}, f32[72,128]{1,0:T(8,128)S(1)}, u32[]{:S(2)}, u32[]{:S(2)}) %collective-permute-start.29) | collective-permute-done | bytes 36896 | tf_op jit(solution)/shard_map/ppermute | solution.py:254
  98.5 2.8 %collective-permute-start.30 = (f32[72,128]{1,0:T(8,128)S(1)}, f32[72,128]{1,0:T(8,128)S(1)}, u32[]{:S(2)}, u32[]{:S(2)}) collective-permute-start(f32[72,128]{1,0:T(8,128)S(1)} %collective-permute-done.29.mine_ref), channel_id=1, source_target_pairs={{8,0},{0,8},{24,16},{16,24},{40,32},{32,40},{56,48},{48,56},{72,64... | collective-permute-start | bytes 110600 | tf_op jit(solution)/shard_map/ppermute | solution.py:225
  101.3 3.3 %turn_first.5.refs_0_ = f32[512,128]{1,0:T(8,128)S(1)} custom-call(s32[1]{0:T(128)} %bitcast.core_ref, f32[72,128]{1,0:T(8,128)S(1)} %add_add_fusion.mine_ref, f32[72,128]{1,0:T(8,128)S(1)} %collective-permute-done.31.other_ref, f32[512,128]{1,0:T(8,128)S(1)} %turn_first.4.refs_0_, f32[512,128]{1,0:T(8,128)S(1)} %get-tuple-element.21.refs_1_), custom_call_target="tpu_custom_call" | custom-call | tf_op jit(solution)/shard_map/turn_first/pallas_call | solution.py:189
  104.6 4.1 %turn_last.1 = f32[512,256]{1,0:T(8,128)} custom-call(s32[1]{0:T(128)} %bitcast.core_ref, f32[72,128]{1,0:T(8,128)S(1)} %collective-permute-done.29.mine_ref, f32[72,128]{1,0:T(8,128)S(1)} %collective-permute-done.30.other_ref, f32[512,128]{1,0:T(8,128)S(1)} %turn_first.5.refs_0_, f32[512,128]{1,0:T(8,128)S(1)} %get-tuple-element.24.refs_1_, ...), custom_call_target="tpu_custom_call" | custom-call | tf_op jit(solution)/shard_map/turn_last/pallas_call | solution.py:208
  (54 shorter events, 15.6 us)
Async XLA Ops:
  1.3 4.2 %collective-permute-start = (f32[72,128]{1,0:T(8,128)S(1)}, f32[72,128]{1,0:T(8,128)S(1)}, u32[]{:S(2)}, u32[]{:S(2)}) collective-permute-start(f32[72,128]{1,0:T(8,128)S(1)} %get-tuple-element.16), channel_id=1, source_target_pairs={{8,0},{0,8},{24,16},{16,24},{40,32},{32,40},{56,48},{48,56},{72,64... | collective-permute-start | bytes 110600 | tf_op jit(solution)/shard_map/ppermute | solution.py:225
  5.5 4.0 %collective-permute-start.3 = (f32[72,128]{1,0:T(8,128)S(1)}, f32[72,128]{1,0:T(8,128)S(1)}, u32[]{:S(2)}, u32[]{:S(2)}) collective-permute-start(f32[72,128]{1,0:T(8,128)S(1)} %add.63), channel_id=1, source_target_pairs={{48,0},{56,8},{32,16},{40,24},{16,32},{24,40},{0,48},{8,56},{112,6... | collective-permute-start | bytes 110600 | tf_op jit(solution)/shard_map/ppermute | solution.py:225
  6.4 3.5 %collective-permute-start.2 = (f32[72,128]{1,0:T(8,128)S(1)}, f32[72,128]{1,0:T(8,128)S(1)}, u32[]{:S(2)}, u32[]{:S(2)}) collective-permute-start(f32[72,128]{1,0:T(8,128)S(1)} %add.63), channel_id=1, source_target_pairs={{16,0},{24,8},{0,16},{8,24},{48,32},{56,40},{32,48},{40,56},{80,64... | collective-permute-start | bytes 110600 | tf_op jit(solution)/shard_map/ppermute | solution.py:225
  6.6 3.3 %collective-permute-start.1 = (f32[72,128]{1,0:T(8,128)S(1)}, f32[72,128]{1,0:T(8,128)S(1)}, u32[]{:S(2)}, u32[]{:S(2)}) collective-permute-start(f32[72,128]{1,0:T(8,128)S(1)} %add.63), channel_id=1, source_target_pairs={{32,0},{40,8},{48,16},{56,24},{0,32},{8,40},{16,48},{24,56},{96,64... | collective-permute-start | bytes 110600 | tf_op jit(solution)/shard_map/ppermute | solution.py:225
  8.1 31.6 %collective-permute-start.10 = (f32[512,256]{1,0:T(8,128)S(1)}, f32[512,256]{1,0:T(8,128)S(1)}, u32[]{:S(2)}, u32[]{:S(2)}) collective-permute-start(f32[512,256]{1,0:T(8,128)S(1)} %copy-done), channel_id=1, source_target_pairs={{7,0},{0,1},{1,2},{2,3},{3,4},{4,5},{5,6},{6,7},{15,8},{8,9},{9,10... | collective-permute-start | bytes 1572872 | tf_op jit(solution)/shard_map/ppermute | solution.py:254
  9.9 9.2 %collective-permute-start.6 = (f32[72,128]{1,0:T(8,128)S(1)}, f32[72,128]{1,0:T(8,128)S(1)}, u32[]{:S(2)}, u32[]{:S(2)}) collective-permute-start(f32[72,128]{1,0:T(8,128)S(1)} %add_add_fusion.5), channel_id=1, source_target_pairs={{160,0},{168,8},{176,16},{184,24},{128,32},{136,40},{144,48},{152,... | collective-permute-start | bytes 110600 | tf_op jit(solution)/shard_map/ppermute | solution.py:225
  15.9 4.4 %collective-permute-start.5 = (f32[72,128]{1,0:T(8,128)S(1)}, f32[72,128]{1,0:T(8,128)S(1)}, u32[]{:S(2)}, u32[]{:S(2)}) collective-permute-start(f32[72,128]{1,0:T(8,128)S(1)} %add_add_fusion.5), channel_id=1, source_target_pairs={{64,0},{72,8},{80,16},{88,24},{224,32},{232,40},{240,48},{248,56},... | collective-permute-start | bytes 110600 | tf_op jit(solution)/shard_map/ppermute | solution.py:225
  16.2 4.9 %collective-permute-start.4 = (f32[72,128]{1,0:T(8,128)S(1)}, f32[72,128]{1,0:T(8,128)S(1)}, u32[]{:S(2)}, u32[]{:S(2)}) collective-permute-start(f32[72,128]{1,0:T(8,128)S(1)} %add_add_fusion.5), channel_id=1, source_target_pairs={{224,0},{232,8},{240,16},{248,24},{64,32},{72,40},{80,48},{88,56},... | collective-permute-start | bytes 110600 | tf_op jit(solution)/shard_map/ppermute | solution.py:225
  21.1 6.5 %collective-permute-start.8 = (f32[72,128]{1,0:T(8,128)S(1)}, f32[72,128]{1,0:T(8,128)S(1)}, u32[]{:S(2)}, u32[]{:S(2)}) collective-permute-start(f32[72,128]{1,0:T(8,128)S(1)} %add_add_fusion.4.mine_ref), channel_id=1, source_target_pairs={{7,0},{0,1},{1,2},{2,3},{3,4},{4,5},{5,6},{6,7},{15,8},{8,9},{9,10... | collective-permute-start | bytes 110600 | tf_op jit(solution)/shard_map/ppermute | solution.py:254
  23.2 13.3 %collective-permute-start.7 = (f32[72,128]{1,0:T(8,128)S(1)}, f32[72,128]{1,0:T(8,128)S(1)}, u32[]{:S(2)}, u32[]{:S(2)}) collective-permute-start(f32[72,128]{1,0:T(8,128)S(1)} %add_add_fusion.4.mine_ref), channel_id=1, source_target_pairs={{8,0},{0,8},{24,16},{16,24},{40,32},{32,40},{56,48},{48,56},{72,64... | collective-permute-start | bytes 110600 | tf_op jit(solution)/shard_map/ppermute | solution.py:225
  27.6 12.1 %collective-permute-start.9 = (f32[72,128]{1,0:T(8,128)S(1)}, f32[72,128]{1,0:T(8,128)S(1)}, u32[]{:S(2)}, u32[]{:S(2)}) collective-permute-start(f32[72,128]{1,0:T(8,128)S(1)} %collective-permute-done.8.mine_ref), channel_id=1, source_target_pairs={{8,0},{0,8},{24,16},{16,24},{40,32},{32,40},{56,48},{48,56},{72,64... | collective-permute-start | bytes 110600 | tf_op jit(solution)/shard_map/ppermute | solution.py:225
  43.5 1.3 %collective-permute-start.11 = (f32[72,128]{1,0:T(8,128)S(1)}, f32[72,128]{1,0:T(8,128)S(1)}, u32[]{:S(2)}, u32[]{:S(2)}) collective-permute-start(f32[72,128]{1,0:T(8,128)S(1)} %get-tuple-element.19), channel_id=1, source_target_pairs={{8,0},{0,8},{24,16},{16,24},{40,32},{32,40},{56,48},{48,56},{72,64... | collective-permute-start | bytes 110600 | tf_op jit(solution)/shard_map/ppermute | solution.py:225
  44.8 3.7 %collective-permute-start.14 = (f32[72,128]{1,0:T(8,128)S(1)}, f32[72,128]{1,0:T(8,128)S(1)}, u32[]{:S(2)}, u32[]{:S(2)}) collective-permute-start(f32[72,128]{1,0:T(8,128)S(1)} %add.70), channel_id=1, source_target_pairs={{48,0},{56,8},{32,16},{40,24},{16,32},{24,40},{0,48},{8,56},{112,6... | collective-permute-start | bytes 110600 | tf_op jit(solution)/shard_map/ppermute | solution.py:225
  46.9 2.8 %collective-permute-start.13 = (f32[72,128]{1,0:T(8,128)S(1)}, f32[72,128]{1,0:T(8,128)S(1)}, u32[]{:S(2)}, u32[]{:S(2)}) collective-permute-start(f32[72,128]{1,0:T(8,128)S(1)} %add.70), channel_id=1, source_target_pairs={{16,0},{24,8},{0,16},{8,24},{48,32},{56,40},{32,48},{40,56},{80,64... | collective-permute-start | bytes 110600 | tf_op jit(solution)/shard_map/ppermute | solution.py:225
  46.9 3.0 %collective-permute-start.12 = (f32[72,128]{1,0:T(8,128)S(1)}, f32[72,128]{1,0:T(8,128)S(1)}, u32[]{:S(2)}, u32[]{:S(2)}) collective-permute-start(f32[72,128]{1,0:T(8,128)S(1)} %add.70), channel_id=1, source_target_pairs={{32,0},{40,8},{48,16},{56,24},{0,32},{8,40},{16,48},{24,56},{96,64... | collective-permute-start | bytes 110600 | tf_op jit(solution)/shard_map/ppermute | solution.py:225
  49.9 6.3 %collective-permute-start.17 = (f32[72,128]{1,0:T(8,128)S(1)}, f32[72,128]{1,0:T(8,128)S(1)}, u32[]{:S(2)}, u32[]{:S(2)}) collective-permute-start(f32[72,128]{1,0:T(8,128)S(1)} %add_add_fusion.3), channel_id=1, source_target_pairs={{160,0},{168,8},{176,16},{184,24},{128,32},{136,40},{144,48},{152,... | collective-permute-start | bytes 110600 | tf_op jit(solution)/shard_map/ppermute | solution.py:225
  53.5 4.4 %collective-permute-start.16 = (f32[72,128]{1,0:T(8,128)S(1)}, f32[72,128]{1,0:T(8,128)S(1)}, u32[]{:S(2)}, u32[]{:S(2)}) collective-permute-start(f32[72,128]{1,0:T(8,128)S(1)} %add_add_fusion.3), channel_id=1, source_target_pairs={{64,0},{72,8},{80,16},{88,24},{224,32},{232,40},{240,48},{248,56},... | collective-permute-start | bytes 110600 | tf_op jit(solution)/shard_map/ppermute | solution.py:225
  55.2 4.1 %collective-permute-start.15 = (f32[72,128]{1,0:T(8,128)S(1)}, f32[72,128]{1,0:T(8,128)S(1)}, u32[]{:S(2)}, u32[]{:S(2)}) collective-permute-start(f32[72,128]{1,0:T(8,128)S(1)} %add_add_fusion.3), channel_id=1, source_target_pairs={{224,0},{232,8},{240,16},{248,24},{64,32},{72,40},{80,48},{88,56},... | collective-permute-start | bytes 110600 | tf_op jit(solution)/shard_map/ppermute | solution.py:225
  56.2 16.7 %collective-permute-start.21 = (f32[512,128]{1,0:T(8,128)S(1)}, f32[512,128]{1,0:T(8,128)S(1)}, u32[]{:S(2)}, u32[]{:S(2)}) collective-permute-start(f32[512,128]{1,0:T(8,128)S(1)} %get-tuple-element.17.refs_1_), channel_id=1, source_target_pairs={{7,0},{0,1},{1,2},{2,3},{3,4},{4,5},{5,6},{6,7},{15,8},{8,9},{9,10... | collective-permute-start | bytes 786440 | tf_op jit(solution)/shard_map/ppermute | solution.py:254
  59.4 7.2 %collective-permute-start.19 = (f32[72,128]{1,0:T(8,128)S(1)}, f32[72,128]{1,0:T(8,128)S(1)}, u32[]{:S(2)}, u32[]{:S(2)}) collective-permute-start(f32[72,128]{1,0:T(8,128)S(1)} %add_add_fusion.2.mine_ref), channel_id=1, source_target_pairs={{7,0},{0,1},{1,2},{2,3},{3,4},{4,5},{5,6},{6,7},{15,8},{8,9},{9,10... | collective-permute-start | bytes 110600 | tf_op jit(solution)/shard_map/ppermute | solution.py:254
  59.4 10.2 %collective-permute-start.18 = (f32[72,128]{1,0:T(8,128)S(1)}, f32[72,128]{1,0:T(8,128)S(1)}, u32[]{:S(2)}, u32[]{:S(2)}) collective-permute-start(f32[72,128]{1,0:T(8,128)S(1)} %add_add_fusion.2.mine_ref), channel_id=1, source_target_pairs={{8,0},{0,8},{24,16},{16,24},{40,32},{32,40},{56,48},{48,56},{72,64... | collective-permute-start | bytes 110600 | tf_op jit(solution)/shard_map/ppermute | solution.py:225
  66.5 6.4 %collective-permute-start.20 = (f32[72,128]{1,0:T(8,128)S(1)}, f32[72,128]{1,0:T(8,128)S(1)}, u32[]{:S(2)}, u32[]{:S(2)}) collective-permute-start(f32[72,128]{1,0:T(8,128)S(1)} %collective-permute-done.19.mine_ref), channel_id=1, source_target_pairs={{8,0},{0,8},{24,16},{16,24},{40,32},{32,40},{56,48},{48,56},{72,64... | collective-permute-start | bytes 110600 | tf_op jit(solution)/shard_map/ppermute | solution.py:225
  78.0 3.7 %collective-permute-start.25 = (f32[72,128]{1,0:T(8,128)S(1)}, f32[72,128]{1,0:T(8,128)S(1)}, u32[]{:S(2)}, u32[]{:S(2)}) collective-permute-start(f32[72,128]{1,0:T(8,128)S(1)} %add.77), channel_id=1, source_target_pairs={{48,0},{56,8},{32,16},{40,24},{16,32},{24,40},{0,48},{8,56},{112,6... | collective-permute-start | bytes 110600 | tf_op jit(solution)/shard_map/ppermute | solution.py:225
  79.2 3.4 %collective-permute-start.24 = (f32[72,128]{1,0:T(8,128)S(1)}, f32[72,128]{1,0:T(8,128)S(1)}, u32[]{:S(2)}, u32[]{:S(2)}) collective-permute-start(f32[72,128]{1,0:T(8,128)S(1)} %add.77), channel_id=1, source_target_pairs={{16,0},{24,8},{0,16},{8,24},{48,32},{56,40},{32,48},{40,56},{80,64... | collective-permute-start | bytes 110600 | tf_op jit(solution)/shard_map/ppermute | solution.py:225
  79.4 3.3 %collective-permute-start.23 = (f32[72,128]{1,0:T(8,128)S(1)}, f32[72,128]{1,0:T(8,128)S(1)}, u32[]{:S(2)}, u32[]{:S(2)}) collective-permute-start(f32[72,128]{1,0:T(8,128)S(1)} %add.77), channel_id=1, source_target_pairs={{32,0},{40,8},{48,16},{56,24},{0,32},{8,40},{16,48},{24,56},{96,64... | collective-permute-start | bytes 110600 | tf_op jit(solution)/shard_map/ppermute | solution.py:225
  82.7 5.9 %collective-permute-start.28 = (f32[72,128]{1,0:T(8,128)S(1)}, f32[72,128]{1,0:T(8,128)S(1)}, u32[]{:S(2)}, u32[]{:S(2)}) collective-permute-start(f32[72,128]{1,0:T(8,128)S(1)} %add_add_fusion.1), channel_id=1, source_target_pairs={{160,0},{168,8},{176,16},{184,24},{128,32},{136,40},{144,48},{152,... | collective-permute-start | bytes 110600 | tf_op jit(solution)/shard_map/ppermute | solution.py:225
  84.9 3.7 %collective-permute-start.27 = (f32[72,128]{1,0:T(8,128)S(1)}, f32[72,128]{1,0:T(8,128)S(1)}, u32[]{:S(2)}, u32[]{:S(2)}) collective-permute-start(f32[72,128]{1,0:T(8,128)S(1)} %add_add_fusion.1), channel_id=1, source_target_pairs={{64,0},{72,8},{80,16},{88,24},{224,32},{232,40},{240,48},{248,56},... | collective-permute-start | bytes 110600 | tf_op jit(solution)/shard_map/ppermute | solution.py:225
  86.5 4.2 %collective-permute-start.26 = (f32[72,128]{1,0:T(8,128)S(1)}, f32[72,128]{1,0:T(8,128)S(1)}, u32[]{:S(2)}, u32[]{:S(2)}) collective-permute-start(f32[72,128]{1,0:T(8,128)S(1)} %add_add_fusion.1), channel_id=1, source_target_pairs={{224,0},{232,8},{240,16},{248,24},{64,32},{72,40},{80,48},{88,56},... | collective-permute-start | bytes 110600 | tf_op jit(solution)/shard_map/ppermute | solution.py:225
  88.2 16.4 %collective-permute-start.32 = (f32[512,128]{1,0:T(8,128)S(1)}, f32[512,128]{1,0:T(8,128)S(1)}, u32[]{:S(2)}, u32[]{:S(2)}) collective-permute-start(f32[512,128]{1,0:T(8,128)S(1)} %get-tuple-element.21.refs_1_), channel_id=1, source_target_pairs={{7,0},{0,1},{1,2},{2,3},{3,4},{4,5},{5,6},{6,7},{15,8},{8,9},{9,10... | collective-permute-start | bytes 786440 | tf_op jit(solution)/shard_map/ppermute | solution.py:254
  90.8 7.7 %collective-permute-start.29 = (f32[72,128]{1,0:T(8,128)S(1)}, f32[72,128]{1,0:T(8,128)S(1)}, u32[]{:S(2)}, u32[]{:S(2)}) collective-permute-start(f32[72,128]{1,0:T(8,128)S(1)} %add_add_fusion.mine_ref), channel_id=1, source_target_pairs={{7,0},{0,1},{1,2},{2,3},{3,4},{4,5},{5,6},{6,7},{15,8},{8,9},{9,10... | collective-permute-start | bytes 110600 | tf_op jit(solution)/shard_map/ppermute | solution.py:254
  90.9 10.4 %collective-permute-start.31 = (f32[72,128]{1,0:T(8,128)S(1)}, f32[72,128]{1,0:T(8,128)S(1)}, u32[]{:S(2)}, u32[]{:S(2)}) collective-permute-start(f32[72,128]{1,0:T(8,128)S(1)} %add_add_fusion.mine_ref), channel_id=1, source_target_pairs={{8,0},{0,8},{24,16},{16,24},{40,32},{32,40},{56,48},{48,56},{72,64... | collective-permute-start | bytes 110600 | tf_op jit(solution)/shard_map/ppermute | solution.py:225
  98.5 6.1 %collective-permute-start.30 = (f32[72,128]{1,0:T(8,128)S(1)}, f32[72,128]{1,0:T(8,128)S(1)}, u32[]{:S(2)}, u32[]{:S(2)}) collective-permute-start(f32[72,128]{1,0:T(8,128)S(1)} %collective-permute-done.29.mine_ref), channel_id=1, source_target_pairs={{8,0},{0,8},{24,16},{16,24},{40,32},{32,40},{56,48},{48,56},{72,64... | collective-permute-start | bytes 110600 | tf_op jit(solution)/shard_map/ppermute | solution.py:225
  (2 other events, 2.3 us)
where the time goes:
time: 109 us
  starting transfers between devices  59.8 us (55%)
  waiting for transfers between devices  25.9 us (24%)
  Pallas kernels  21.7 us (20%)
    ppermute x27, starting transfers between devices, from_row(): return lax.ppermute(x, 'row', route)  56.2 us
    ppermute x27, waiting for transfers between devices, from_row(): return lax.ppermute(x, 'row', route)  15.7 us
    ppermute x6, waiting for transfers between devices, shifted(): return lax.ppermute(block, 'pair', route)  10.2 us
    pallas_call x3, Pallas kernels, turn_first(): pl.pallas_call(first_kernel, out_shape=pltpu.VMEM((blocks[0].shape[0], n)...  9.76 us
    pallas_call x2, Pallas kernels, turn_both(): pl.pallas_call(both_kernel, out_shape=[pltpu.VMEM((blocks[0].shape[0], n)...  6.97 us
    pallas_call x1, Pallas kernels, turn_last(): pl.pallas_call(last_kernel, out_shape=jax.ShapeDtypeStruct((rows, 2 * n),...  4.07 us
    ppermute x6, starting transfers between devices, shifted(): return lax.ppermute(block, 'pair', route)  3.62 us
  transfers between devices with their start and end apart: 33, of which 19 were waited for; matrix products, arithmetic and copies ran while one was open for 0% of the time, Pallas kernels for 9%

commit v1 on v0

--- a/solution.py
+++ b/solution.py
@@ -14,6 +14,7 @@
 
 QUAD = 4
 PAD = 8
+CHUNKS = 4
 
 
 def split(x):
@@ -60,7 +61,7 @@
     gap = (top - 1.0) / (top + 1.0)
     y = start * base
     x = None
-    while gap > 1e-3:
+    while gap > 0.05:
         z = 2.0 * eye - y
         stretch = 2.0 / (2.0 - gap * gap)
         right = right3(z)
@@ -71,11 +72,14 @@
             both = stretch * times3(jnp.concatenate([left3(x), left3(y)], 0), right)
             x, y = both[:n], both[n:]
         gap = gap * gap / (2.0 - gap * gap)
-    for _ in range(2):
-        x = times(x, 2.0 * eye - times(base, x))
+    left = eye - times3(left3(x), right3(base))
+    x = x + times3(left3(left), right3(x))
+    left = eye - times(x, base)
+    x = x + times3(left3(left), right3(x))
     md = times(x, d)
     mixed = 2.0 * md
-    return 2.0 * x - eye, mixed, -jnp.transpose(mixed), eye - 2.0 * times(dt, md)
+    corner = eye - 2.0 * times3(left3(dt), right3(md))
+    return 2.0 * x - eye, mixed, -jnp.transpose(mixed), corner
 
 
 def message(diag_a, diag_b, cross, core, cross_ref, mine_ref, other_ref):
@@ -152,16 +156,20 @@
 
 def last_kernel(core_ref, mine_ref, other_ref, *refs):
     own_ref, *blocks, out_ref, b_ref, sems = refs
-    n = own_ref.shape[1]
-    own_copy = pltpu.make_async_copy(own_ref, out_ref.at[:, :n], sems.at[0])
-    own_copy.start()
+    rows, n = own_ref.shape
+    copies = [pltpu.make_async_copy(own_ref, out_ref.at[:, :n], sems.at[CHUNKS])]
+    copies[0].start()
     _, c12, _, c22 = cayley_blocks(core_ref, mine_ref, other_ref)
-    rows = split(jnp.concatenate(both_blocks(blocks), 1))
-    b_ref[...] = rows_times(rows, c12, c22)
-    b_copy = pltpu.make_async_copy(b_ref, out_ref.at[:, n:], sems.at[1])
-    b_copy.start()
-    own_copy.wait()
-    b_copy.wait()
+    both = jnp.concatenate(both_blocks(blocks), 1)
+    size = rows // CHUNKS
+    for i in range(CHUNKS):
+        part = slice(i * size, (i + 1) * size)
+        b_ref[part] = rows_times(split(both[part]), c12, c22)
+        copy = pltpu.make_async_copy(b_ref.at[part], out_ref.at[part, n:], sems.at[i])
+        copy.start()
+        copies.append(copy)
+    for copy in copies:
+        copy.wait()
 
 
 def in_specs(count):
@@ -210,7 +218,7 @@
         out_shape=jax.ShapeDtypeStruct((rows, 2 * n), F32),
         in_specs=in_specs(3 + len(blocks)),
         out_specs=pl.BlockSpec(memory_space=pl.ANY),
-        scratch_shapes=[pltpu.VMEM((rows, n), F32), pltpu.SemaphoreType.DMA((2,))],
+        scratch_shapes=[pltpu.VMEM((rows, n), F32), pltpu.SemaphoreType.DMA((CHUNKS + 1,))],
         name="turn_last",
     )(core, *map(near, halves), near(own), *map(near, blocks))
 
@@ -229,18 +237,23 @@
     return 1 if z % 2 else -1
 
 
-def summed_halves(mine, other):
+def summed_halves(mine, other, y_last):
     x = mine + from_row(other, lambda z, y, c: (z, y, 1 - c))
-    x = (
-        (x + from_row(x, lambda z, y, c: (z ^ 1, y, c)))
-        + from_row(x, lambda z, y, c: (z, 1 - y, c))
-        + from_row(x, lambda z, y, c: (z ^ 1, 1 - y, c))
-    )
+    if y_last:
+        x = x + from_row(x, lambda z, y, c: (z ^ 1, y, c))
+    else:
+        x = (
+            (x + from_row(x, lambda z, y, c: (z ^ 1, y, c)))
+            + from_row(x, lambda z, y, c: (z, 1 - y, c))
+            + from_row(x, lambda z, y, c: (z ^ 1, 1 - y, c))
+        )
     x = (
         (x + from_row(x, lambda z, y, c: (z + side(z), y, c)))
         + from_row(x, lambda z, y, c: (z - 2 * side(z), y, c))
         + from_row(x, lambda z, y, c: (z + 3 * side(z), y, c))
     )
+    if y_last:
+        x = x + from_row(x, lambda z, y, c: (z, 1 - y, c))
     return x
 
 
@@ -258,10 +271,11 @@
     n = panel.shape[1] // 2
     core = (lax.axis_index("row") & 1).astype(jnp.int32).reshape(1)
     own = [panel]
-    before = [shifted(panel)]
     for step in range(STEPS):
+        if step == 0:
+            before = [shifted(panel)]
         mine, other = gram(core, own, n)
-        half = summed_halves(mine, other)
+        half = summed_halves(mine, other, y_last=step == 0)
         hopped = shifted(half)
         a = turn_first(core, with_other(half), own, n)
         halves = with_other(hopped)

time: 109 us -> 105 us (0.963)
  starting transfers between devices: 59.8 us -> 56.4 us
  Pallas kernels: 21.7 us -> 18.5 us
  waiting for transfers between devices: 25.9 us -> 28.6 us
    ppermute x27 -> x26, starting transfers between devices: 56.2 us -> 50.8 us  [from_row(): return lax.ppermute(x, 'row', route)]
    ppermute x27 -> x26, waiting for transfers between devices: 15.7 us -> 18.9 us  [from_row(): return lax.ppermute(x, 'row', route)]
    ppermute x6, starting transfers between devices: 3.62 us -> 5.59 us  [shifted(): return lax.ppermute(block, 'pair', route)]
    pallas_call x3, Pallas kernels: 9.76 us -> 8.22 us  [turn_first(): pl.pallas_call(first_kernel, out_shape=pltpu.VMEM((blocks[0].shape[0], n)...]
  transfers between devices with their start and end apart: 33 -> 32, of which waited for: 19 -> 20; matrix products, arithmetic and copies ran while one was open for 0% -> 0% of each run, Pallas kernels for 9% -> 8%
where the time goes in v1:
time: 105 us
  starting transfers between devices  56.4 us (54%)
  waiting for transfers between devices  28.6 us (27%)
  Pallas kernels  18.5 us (18%)
  local copies, waits for them, and re-layouts  1.08 us (1%)
    ppermute x26, starting transfers between devices, from_row(): return lax.ppermute(x, 'row', route)  50.8 us
    ppermute x26, waiting for transfers between devices, from_row(): return lax.ppermute(x, 'row', route)  18.9 us
    ppermute x6, waiting for transfers between devices, shifted(): return lax.ppermute(block, 'pair', route)  9.79 us
    pallas_call x3, Pallas kernels, turn_first(): pl.pallas_call(first_kernel, out_shape=pltpu.VMEM((blocks[0].shape[0], n)...  8.22 us
    pallas_call x2, Pallas kernels, turn_both(): pl.pallas_call(both_kernel, out_shape=[pltpu.VMEM((blocks[0].shape[0], n)...  5.92 us
    ppermute x6, starting transfers between devices, shifted(): return lax.ppermute(block, 'pair', route)  5.59 us
    pallas_call x1, Pallas kernels, turn_last(): pl.pallas_call(last_kernel, out_shape=jax.ShapeDtypeStruct((rows, 2 * n),...  3.51 us
  transfers between devices with their start and end apart: 32, of which 20 were waited for; matrix products, arithmetic and copies ran while one was open for 0% of the time, Pallas kernels for 8%

profile of v1, /device:TPU:1, one launch (start us, length us, event | category | flops | bytes accessed | tf_op | source)
XLA Modules:
  0.0 105.0 jit_solution(1831372828588250011)
XLA Ops:
  0.0 3.7 %collective-permute-start.9 = (f32[512,256]{1,0:T(8,128)}, f32[512,256]{1,0:T(8,128)S(1)}, u32[]{:S(2)}, u32[]{:S(2)}) collective-permute-start(f32[512,256]{1,0:T(8,128)} %refs_0_.3), channel_id=1, source_target_pairs={{7,0},{0,1},{1,2},{2,3},{3,4},{4,5},{5,6},{6,7},{15,8},{8,9},{9,10... | collective-permute-start | bytes 1572872 | tf_op jit(solution)/shard_map/ppermute | solution.py:267
  7.0 1.6 %collective-permute-start.1 = (f32[72,128]{1,0:T(8,128)S(1)}, f32[72,128]{1,0:T(8,128)S(1)}, u32[]{:S(2)}, u32[]{:S(2)}) collective-permute-start(f32[72,128]{1,0:T(8,128)S(1)} %add.60), channel_id=1, source_target_pairs={{32,0},{40,8},{48,16},{56,24},{0,32},{8,40},{16,48},{24,56},{96,64... | collective-permute-start | bytes 110600 | tf_op jit(solution)/shard_map/ppermute | solution.py:233
  8.7 1.6 %collective-permute-done.1 = f32[72,128]{1,0:T(8,128)S(1)} collective-permute-done((f32[72,128]{1,0:T(8,128)S(1)}, f32[72,128]{1,0:T(8,128)S(1)}, u32[]{:S(2)}, u32[]{:S(2)}) %collective-permute-start.1) | collective-permute-done | bytes 36896 | tf_op jit(solution)/shard_map/ppermute | solution.py:233
  10.3 6.3 %collective-permute-start.4 = (f32[72,128]{1,0:T(8,128)S(1)}, f32[72,128]{1,0:T(8,128)S(1)}, u32[]{:S(2)}, u32[]{:S(2)}) collective-permute-start(f32[72,128]{1,0:T(8,128)S(1)} %add.61), channel_id=1, source_target_pairs={{160,0},{168,8},{176,16},{184,24},{128,32},{136,40},{144,48},{152,... | collective-permute-start | bytes 110600 | tf_op jit(solution)/shard_map/ppermute | solution.py:233
  16.9 2.8 %collective-permute-start.2 = (f32[72,128]{1,0:T(8,128)S(1)}, f32[72,128]{1,0:T(8,128)S(1)}, u32[]{:S(2)}, u32[]{:S(2)}) collective-permute-start(f32[72,128]{1,0:T(8,128)S(1)} %add.61), channel_id=1, source_target_pairs={{224,0},{232,8},{240,16},{248,24},{64,32},{72,40},{80,48},{88,56},... | collective-permute-start | bytes 110600 | tf_op jit(solution)/shard_map/ppermute | solution.py:233
  22.0 2.4 %collective-permute-done.5 = f32[72,128]{1,0:T(8,128)S(1)} collective-permute-done((f32[72,128]{1,0:T(8,128)S(1)}, f32[72,128]{1,0:T(8,128)S(1)}, u32[]{:S(2)}, u32[]{:S(2)}) %collective-permute-start.5) | collective-permute-done | bytes 36896 | tf_op jit(solution)/shard_map/ppermute | solution.py:233
  24.4 1.4 %collective-permute-start.7 = (f32[72,128]{1,0:T(8,128)S(1)}, f32[72,128]{1,0:T(8,128)S(1)}, u32[]{:S(2)}, u32[]{:S(2)}) collective-permute-start(f32[72,128]{1,0:T(8,128)S(1)} %add.65.mine_ref), channel_id=1, source_target_pairs={{7,0},{0,1},{1,2},{2,3},{3,4},{4,5},{5,6},{6,7},{15,8},{8,9},{9,10... | collective-permute-start | bytes 110600 | tf_op jit(solution)/shard_map/ppermute | solution.py:267
  25.8 3.8 %collective-permute-start.6 = (f32[72,128]{1,0:T(8,128)S(1)}, f32[72,128]{1,0:T(8,128)S(1)}, u32[]{:S(2)}, u32[]{:S(2)}) collective-permute-start(f32[72,128]{1,0:T(8,128)S(1)} %add.65.mine_ref), channel_id=1, source_target_pairs={{8,0},{0,8},{24,16},{16,24},{40,32},{32,40},{56,48},{48,56},{72,64... | collective-permute-start | bytes 110600 | tf_op jit(solution)/shard_map/ppermute | solution.py:233
  29.6 1.2 %collective-permute-done.7.mine_ref = f32[72,128]{1,0:T(8,128)S(1)} collective-permute-done((f32[72,128]{1,0:T(8,128)S(1)}, f32[72,128]{1,0:T(8,128)S(1)}, u32[]{:S(2)}, u32[]{:S(2)}) %collective-permute-start.7) | collective-permute-done | bytes 36896 | tf_op jit(solution)/shard_map/ppermute | solution.py:267
  30.8 4.9 %collective-permute-start.8 = (f32[72,128]{1,0:T(8,128)S(1)}, f32[72,128]{1,0:T(8,128)S(1)}, u32[]{:S(2)}, u32[]{:S(2)}) collective-permute-start(f32[72,128]{1,0:T(8,128)S(1)} %collective-permute-done.7.mine_ref), channel_id=1, source_target_pairs={{8,0},{0,8},{24,16},{16,24},{40,32},{32,40},{56,48},{48,56},{72,64... | collective-permute-start | bytes 110600 | tf_op jit(solution)/shard_map/ppermute | solution.py:233
  35.7 2.7 %turn_first.3.refs_0_ = f32[512,128]{1,0:T(8,128)S(1)} custom-call(s32[1]{0:T(128)} %bitcast.core_ref, f32[72,128]{1,0:T(8,128)S(1)} %add.65.mine_ref, f32[72,128]{1,0:T(8,128)S(1)} %collective-permute-done.6.other_ref, f32[512,256]{1,0:T(8,128)S(1)} %copy-done.1), custom_call_target="tpu_custom_call" | custom-call | tf_op jit(solution)/shard_map/turn_first/pallas_call | solution.py:197
  38.5 3.0 %turn_both.2 = (f32[512,128]{1,0:T(8,128)S(1)}, f32[512,128]{1,0:T(8,128)S(1)}) custom-call(s32[1]{0:T(128)} %bitcast.core_ref, f32[72,128]{1,0:T(8,128)S(1)} %collective-permute-done.7.mine_ref, f32[72,128]{1,0:T(8,128)S(1)} %collective-permute-done.8.other_ref, f32[512,256]{1,0:T(8,128)S(1)} %collective-permute-done.9.refs_0_), custom_call_target="tpu_custom_call" | custom-call | tf_op jit(solution)/shard_map/turn_both/pallas_call | solution.py:206
  41.9 1.2 %collective-permute-done.10 = f32[72,128]{1,0:T(8,128)S(1)} collective-permute-done((f32[72,128]{1,0:T(8,128)S(1)}, f32[72,128]{1,0:T(8,128)S(1)}, u32[]{:S(2)}, u32[]{:S(2)}) %collective-permute-start.10) | collective-permute-done | bytes 36896 | tf_op jit(solution)/shard_map/ppermute | solution.py:233
  46.8 1.2 %collective-permute-done.12 = f32[72,128]{1,0:T(8,128)S(1)} collective-permute-done((f32[72,128]{1,0:T(8,128)S(1)}, f32[72,128]{1,0:T(8,128)S(1)}, u32[]{:S(2)}, u32[]{:S(2)}) %collective-permute-start.12) | collective-permute-done | bytes 36896 | tf_op jit(solution)/shard_map/ppermute | solution.py:233
  48.2 3.5 %collective-permute-start.16 = (f32[72,128]{1,0:T(8,128)S(1)}, f32[72,128]{1,0:T(8,128)S(1)}, u32[]{:S(2)}, u32[]{:S(2)}) collective-permute-start(f32[72,128]{1,0:T(8,128)S(1)} %add_add_fusion.3), channel_id=1, source_target_pairs={{160,0},{168,8},{176,16},{184,24},{128,32},{136,40},{144,48},{152,... | collective-permute-start | bytes 110600 | tf_op jit(solution)/shard_map/ppermute | solution.py:233
  52.5 1.9 %collective-permute-start.14 = (f32[72,128]{1,0:T(8,128)S(1)}, f32[72,128]{1,0:T(8,128)S(1)}, u32[]{:S(2)}, u32[]{:S(2)}) collective-permute-start(f32[72,128]{1,0:T(8,128)S(1)} %add_add_fusion.3), channel_id=1, source_target_pairs={{224,0},{232,8},{240,16},{248,24},{64,32},{72,40},{80,48},{88,56},... | collective-permute-start | bytes 110600 | tf_op jit(solution)/shard_map/ppermute | solution.py:233
  54.4 1.3 %collective-permute-done.15 = f32[72,128]{1,0:T(8,128)S(1)} collective-permute-done((f32[72,128]{1,0:T(8,128)S(1)}, f32[72,128]{1,0:T(8,128)S(1)}, u32[]{:S(2)}, u32[]{:S(2)}) %collective-permute-start.15) | collective-permute-done | bytes 36896 | tf_op jit(solution)/shard_map/ppermute | solution.py:233
  55.6 1.4 %collective-permute-done.14 = f32[72,128]{1,0:T(8,128)S(1)} collective-permute-done((f32[72,128]{1,0:T(8,128)S(1)}, f32[72,128]{1,0:T(8,128)S(1)}, u32[]{:S(2)}, u32[]{:S(2)}) %collective-permute-start.14) | collective-permute-done | bytes 36896 | tf_op jit(solution)/shard_map/ppermute | solution.py:233
  57.2 2.8 %collective-permute-start.17 = (f32[72,128]{1,0:T(8,128)S(1)}, f32[72,128]{1,0:T(8,128)S(1)}, u32[]{:S(2)}, u32[]{:S(2)}) collective-permute-start(f32[72,128]{1,0:T(8,128)S(1)} %add_add_fusion.2.mine_ref), channel_id=1, source_target_pairs={{8,0},{0,8},{24,16},{16,24},{40,32},{32,40},{56,48},{48,56},{72,64... | collective-permute-start | bytes 110600 | tf_op jit(solution)/shard_map/ppermute | solution.py:233
  60.0 4.5 %collective-permute-done.18.mine_ref = f32[72,128]{1,0:T(8,128)S(1)} collective-permute-done((f32[72,128]{1,0:T(8,128)S(1)}, f32[72,128]{1,0:T(8,128)S(1)}, u32[]{:S(2)}, u32[]{:S(2)}) %collective-permute-start.18) | collective-permute-done | bytes 36896 | tf_op jit(solution)/shard_map/ppermute | solution.py:267
  64.5 3.0 %collective-permute-start.19 = (f32[72,128]{1,0:T(8,128)S(1)}, f32[72,128]{1,0:T(8,128)S(1)}, u32[]{:S(2)}, u32[]{:S(2)}) collective-permute-start(f32[72,128]{1,0:T(8,128)S(1)} %collective-permute-done.18.mine_ref), channel_id=1, source_target_pairs={{8,0},{0,8},{24,16},{16,24},{40,32},{32,40},{56,48},{48,56},{72,64... | collective-permute-start | bytes 110600 | tf_op jit(solution)/shard_map/ppermute | solution.py:233
  67.5 2.7 %turn_first.4.refs_0_ = f32[512,128]{1,0:T(8,128)S(1)} custom-call(s32[1]{0:T(128)} %bitcast.core_ref, f32[72,128]{1,0:T(8,128)S(1)} %add_add_fusion.2.mine_ref, f32[72,128]{1,0:T(8,128)S(1)} %collective-permute-done.17.other_ref, f32[512,128]{1,0:T(8,128)S(1)} %turn_first.3.refs_0_, f32[512,128]{1,0:T(8,128)S(1)} %get-tuple-element.17.refs_1_), custom_call_target="tpu_custom_call" | custom-call | tf_op jit(solution)/shard_map/turn_first/pallas_call | solution.py:197
  70.3 3.0 %turn_both.3 = (f32[512,128]{1,0:T(8,128)S(1)}, f32[512,128]{1,0:T(8,128)S(1)}) custom-call(s32[1]{0:T(128)} %bitcast.core_ref, f32[72,128]{1,0:T(8,128)S(1)} %collective-permute-done.18.mine_ref, f32[72,128]{1,0:T(8,128)S(1)} %collective-permute-done.19.other_ref, f32[512,128]{1,0:T(8,128)S(1)} %get-tuple-element.20.refs_0_, ...), custom_call_target="tpu_custom_call" | custom-call | tf_op jit(solution)/shard_map/turn_both/pallas_call | solution.py:206
  76.2 1.3 %collective-permute-start.22 = (f32[72,128]{1,0:T(8,128)S(1)}, f32[72,128]{1,0:T(8,128)S(1)}, u32[]{:S(2)}, u32[]{:S(2)}) collective-permute-start(f32[72,128]{1,0:T(8,128)S(1)} %add.73), channel_id=1, source_target_pairs={{32,0},{40,8},{48,16},{56,24},{0,32},{8,40},{16,48},{24,56},{96,64... | collective-permute-start | bytes 110600 | tf_op jit(solution)/shard_map/ppermute | solution.py:233
  79.3 2.9 %collective-permute-start.27 = (f32[72,128]{1,0:T(8,128)S(1)}, f32[72,128]{1,0:T(8,128)S(1)}, u32[]{:S(2)}, u32[]{:S(2)}) collective-permute-start(f32[72,128]{1,0:T(8,128)S(1)} %add_add_fusion.1), channel_id=1, source_target_pairs={{160,0},{168,8},{176,16},{184,24},{128,32},{136,40},{144,48},{152,... | collective-permute-start | bytes 110600 | tf_op jit(solution)/shard_map/ppermute | solution.py:233
  83.4 1.4 %collective-permute-start.25 = (f32[72,128]{1,0:T(8,128)S(1)}, f32[72,128]{1,0:T(8,128)S(1)}, u32[]{:S(2)}, u32[]{:S(2)}) collective-permute-start(f32[72,128]{1,0:T(8,128)S(1)} %add_add_fusion.1), channel_id=1, source_target_pairs={{224,0},{232,8},{240,16},{248,24},{64,32},{72,40},{80,48},{88,56},... | collective-permute-start | bytes 110600 | tf_op jit(solution)/shard_map/ppermute | solution.py:233
  85.2 1.4 %collective-permute-done.26 = f32[72,128]{1,0:T(8,128)S(1)} collective-permute-done((f32[72,128]{1,0:T(8,128)S(1)}, f32[72,128]{1,0:T(8,128)S(1)}, u32[]{:S(2)}, u32[]{:S(2)}) %collective-permute-start.26) | collective-permute-done | bytes 36896 | tf_op jit(solution)/shard_map/ppermute | solution.py:233
  88.0 3.1 %collective-permute-start.30 = (f32[72,128]{1,0:T(8,128)S(1)}, f32[72,128]{1,0:T(8,128)S(1)}, u32[]{:S(2)}, u32[]{:S(2)}) collective-permute-start(f32[72,128]{1,0:T(8,128)S(1)} %add_add_fusion.mine_ref), channel_id=1, source_target_pairs={{8,0},{0,8},{24,16},{16,24},{40,32},{32,40},{56,48},{48,56},{72,64... | collective-permute-start | bytes 110600 | tf_op jit(solution)/shard_map/ppermute | solution.py:233
  91.1 4.0 %collective-permute-done.28.mine_ref = f32[72,128]{1,0:T(8,128)S(1)} collective-permute-done((f32[72,128]{1,0:T(8,128)S(1)}, f32[72,128]{1,0:T(8,128)S(1)}, u32[]{:S(2)}, u32[]{:S(2)}) %collective-permute-start.28) | collective-permute-done | bytes 36896 | tf_op jit(solution)/shard_map/ppermute | solution.py:267
  95.1 3.4 %collective-permute-start.29 = (f32[72,128]{1,0:T(8,128)S(1)}, f32[72,128]{1,0:T(8,128)S(1)}, u32[]{:S(2)}, u32[]{:S(2)}) collective-permute-start(f32[72,128]{1,0:T(8,128)S(1)} %collective-permute-done.28.mine_ref), channel_id=1, source_target_pairs={{8,0},{0,8},{24,16},{16,24},{40,32},{32,40},{56,48},{48,56},{72,64... | collective-permute-start | bytes 110600 | tf_op jit(solution)/shard_map/ppermute | solution.py:233
  98.6 2.7 %turn_first.5.refs_0_ = f32[512,128]{1,0:T(8,128)S(1)} custom-call(s32[1]{0:T(128)} %bitcast.core_ref, f32[72,128]{1,0:T(8,128)S(1)} %add_add_fusion.mine_ref, f32[72,128]{1,0:T(8,128)S(1)} %collective-permute-done.30.other_ref, f32[512,128]{1,0:T(8,128)S(1)} %turn_first.4.refs_0_, f32[512,128]{1,0:T(8,128)S(1)} %get-tuple-element.21.refs_1_), custom_call_target="tpu_custom_call" | custom-call | tf_op jit(solution)/shard_map/turn_first/pallas_call | solution.py:197
  101.4 3.5 %turn_last.1 = f32[512,256]{1,0:T(8,128)} custom-call(s32[1]{0:T(128)} %bitcast.core_ref, f32[72,128]{1,0:T(8,128)S(1)} %collective-permute-done.28.mine_ref, f32[72,128]{1,0:T(8,128)S(1)} %collective-permute-done.29.other_ref, f32[512,128]{1,0:T(8,128)S(1)} %turn_first.5.refs_0_, f32[512,128]{1,0:T(8,128)S(1)} %get-tuple-element.24.refs_1_, ...), custom_call_target="tpu_custom_call" | custom-call | tf_op jit(solution)/shard_map/turn_last/pallas_call | solution.py:216
  (55 shorter events, 18.7 us)
Async XLA Ops:
  0.0 38.5 %collective-permute-start.9 = (f32[512,256]{1,0:T(8,128)}, f32[512,256]{1,0:T(8,128)S(1)}, u32[]{:S(2)}, u32[]{:S(2)}) collective-permute-start(f32[512,256]{1,0:T(8,128)} %refs_0_.3), channel_id=1, source_target_pairs={{7,0},{0,1},{1,2},{2,3},{3,4},{4,5},{5,6},{6,7},{15,8},{8,9},{9,10... | collective-permute-start | bytes 1572872 | tf_op jit(solution)/shard_map/ppermute | solution.py:267
  5.1 1.9 %collective-permute-start = (f32[72,128]{1,0:T(8,128)S(1)}, f32[72,128]{1,0:T(8,128)S(1)}, u32[]{:S(2)}, u32[]{:S(2)}) collective-permute-start(f32[72,128]{1,0:T(8,128)S(1)} %get-tuple-element.16), channel_id=1, source_target_pairs={{8,0},{0,8},{24,16},{16,24},{40,32},{32,40},{56,48},{48,56},{72,64... | collective-permute-start | bytes 110600 | tf_op jit(solution)/shard_map/ppermute | solution.py:233
  7.0 3.3 %collective-permute-start.1 = (f32[72,128]{1,0:T(8,128)S(1)}, f32[72,128]{1,0:T(8,128)S(1)}, u32[]{:S(2)}, u32[]{:S(2)}) collective-permute-start(f32[72,128]{1,0:T(8,128)S(1)} %add.60), channel_id=1, source_target_pairs={{32,0},{40,8},{48,16},{56,24},{0,32},{8,40},{16,48},{24,56},{96,64... | collective-permute-start | bytes 110600 | tf_op jit(solution)/shard_map/ppermute | solution.py:233
  10.3 9.4 %collective-permute-start.4 = (f32[72,128]{1,0:T(8,128)S(1)}, f32[72,128]{1,0:T(8,128)S(1)}, u32[]{:S(2)}, u32[]{:S(2)}) collective-permute-start(f32[72,128]{1,0:T(8,128)S(1)} %add.61), channel_id=1, source_target_pairs={{160,0},{168,8},{176,16},{184,24},{128,32},{136,40},{144,48},{152,... | collective-permute-start | bytes 110600 | tf_op jit(solution)/shard_map/ppermute | solution.py:233
  16.6 3.8 %collective-permute-start.3 = (f32[72,128]{1,0:T(8,128)S(1)}, f32[72,128]{1,0:T(8,128)S(1)}, u32[]{:S(2)}, u32[]{:S(2)}) collective-permute-start(f32[72,128]{1,0:T(8,128)S(1)} %add.61), channel_id=1, source_target_pairs={{64,0},{72,8},{80,16},{88,24},{224,32},{232,40},{240,48},{248,56},... | collective-permute-start | bytes 110600 | tf_op jit(solution)/shard_map/ppermute | solution.py:233
  16.9 4.6 %collective-permute-start.2 = (f32[72,128]{1,0:T(8,128)S(1)}, f32[72,128]{1,0:T(8,128)S(1)}, u32[]{:S(2)}, u32[]{:S(2)}) collective-permute-start(f32[72,128]{1,0:T(8,128)S(1)} %add.61), channel_id=1, source_target_pairs={{224,0},{232,8},{240,16},{248,24},{64,32},{72,40},{80,48},{88,56},... | collective-permute-start | bytes 110600 | tf_op jit(solution)/shard_map/ppermute | solution.py:233
  21.5 2.9 %collective-permute-start.5 = (f32[72,128]{1,0:T(8,128)S(1)}, f32[72,128]{1,0:T(8,128)S(1)}, u32[]{:S(2)}, u32[]{:S(2)}) collective-permute-start(f32[72,128]{1,0:T(8,128)S(1)} %add_add_fusion.4), channel_id=1, source_target_pairs={{16,0},{24,8},{0,16},{8,24},{48,32},{56,40},{32,48},{40,56},{80,64... | collective-permute-start | bytes 110600 | tf_op jit(solution)/shard_map/ppermute | solution.py:233
  24.4 6.4 %collective-permute-start.7 = (f32[72,128]{1,0:T(8,128)S(1)}, f32[72,128]{1,0:T(8,128)S(1)}, u32[]{:S(2)}, u32[]{:S(2)}) collective-permute-start(f32[72,128]{1,0:T(8,128)S(1)} %add.65.mine_ref), channel_id=1, source_target_pairs={{7,0},{0,1},{1,2},{2,3},{3,4},{4,5},{5,6},{6,7},{15,8},{8,9},{9,10... | collective-permute-start | bytes 110600 | tf_op jit(solution)/shard_map/ppermute | solution.py:267
  25.8 9.9 %collective-permute-start.6 = (f32[72,128]{1,0:T(8,128)S(1)}, f32[72,128]{1,0:T(8,128)S(1)}, u32[]{:S(2)}, u32[]{:S(2)}) collective-permute-start(f32[72,128]{1,0:T(8,128)S(1)} %add.65.mine_ref), channel_id=1, source_target_pairs={{8,0},{0,8},{24,16},{16,24},{40,32},{32,40},{56,48},{48,56},{72,64... | collective-permute-start | bytes 110600 | tf_op jit(solution)/shard_map/ppermute | solution.py:233
  30.8 7.7 %collective-permute-start.8 = (f32[72,128]{1,0:T(8,128)S(1)}, f32[72,128]{1,0:T(8,128)S(1)}, u32[]{:S(2)}, u32[]{:S(2)}) collective-permute-start(f32[72,128]{1,0:T(8,128)S(1)} %collective-permute-done.7.mine_ref), channel_id=1, source_target_pairs={{8,0},{0,8},{24,16},{16,24},{40,32},{32,40},{56,48},{48,56},{72,64... | collective-permute-start | bytes 110600 | tf_op jit(solution)/shard_map/ppermute | solution.py:233
  41.8 1.3 %collective-permute-start.10 = (f32[72,128]{1,0:T(8,128)S(1)}, f32[72,128]{1,0:T(8,128)S(1)}, u32[]{:S(2)}, u32[]{:S(2)}) collective-permute-start(f32[72,128]{1,0:T(8,128)S(1)} %get-tuple-element.19), channel_id=1, source_target_pairs={{8,0},{0,8},{24,16},{16,24},{40,32},{32,40},{56,48},{48,56},{72,64... | collective-permute-start | bytes 110600 | tf_op jit(solution)/shard_map/ppermute | solution.py:233
  43.1 3.7 %collective-permute-start.13 = (f32[72,128]{1,0:T(8,128)S(1)}, f32[72,128]{1,0:T(8,128)S(1)}, u32[]{:S(2)}, u32[]{:S(2)}) collective-permute-start(f32[72,128]{1,0:T(8,128)S(1)} %add.66), channel_id=1, source_target_pairs={{48,0},{56,8},{32,16},{40,24},{16,32},{24,40},{0,48},{8,56},{112,6... | collective-permute-start | bytes 110600 | tf_op jit(solution)/shard_map/ppermute | solution.py:233
  44.0 4.1 %collective-permute-start.12 = (f32[72,128]{1,0:T(8,128)S(1)}, f32[72,128]{1,0:T(8,128)S(1)}, u32[]{:S(2)}, u32[]{:S(2)}) collective-permute-start(f32[72,128]{1,0:T(8,128)S(1)} %add.66), channel_id=1, source_target_pairs={{16,0},{24,8},{0,16},{8,24},{48,32},{56,40},{32,48},{40,56},{80,64... | collective-permute-start | bytes 110600 | tf_op jit(solution)/shard_map/ppermute | solution.py:233
  45.0 3.1 %collective-permute-start.11 = (f32[72,128]{1,0:T(8,128)S(1)}, f32[72,128]{1,0:T(8,128)S(1)}, u32[]{:S(2)}, u32[]{:S(2)}) collective-permute-start(f32[72,128]{1,0:T(8,128)S(1)} %add.66), channel_id=1, source_target_pairs={{32,0},{40,8},{48,16},{56,24},{0,32},{8,40},{16,48},{24,56},{96,64... | collective-permute-start | bytes 110600 | tf_op jit(solution)/shard_map/ppermute | solution.py:233
  48.2 6.2 %collective-permute-start.16 = (f32[72,128]{1,0:T(8,128)S(1)}, f32[72,128]{1,0:T(8,128)S(1)}, u32[]{:S(2)}, u32[]{:S(2)}) collective-permute-start(f32[72,128]{1,0:T(8,128)S(1)} %add_add_fusion.3), channel_id=1, source_target_pairs={{160,0},{168,8},{176,16},{184,24},{128,32},{136,40},{144,48},{152,... | collective-permute-start | bytes 110600 | tf_op jit(solution)/shard_map/ppermute | solution.py:233
  51.7 4.0 %collective-permute-start.15 = (f32[72,128]{1,0:T(8,128)S(1)}, f32[72,128]{1,0:T(8,128)S(1)}, u32[]{:S(2)}, u32[]{:S(2)}) collective-permute-start(f32[72,128]{1,0:T(8,128)S(1)} %add_add_fusion.3), channel_id=1, source_target_pairs={{64,0},{72,8},{80,16},{88,24},{224,32},{232,40},{240,48},{248,56},... | collective-permute-start | bytes 110600 | tf_op jit(solution)/shard_map/ppermute | solution.py:233
  52.5 4.6 %collective-permute-start.14 = (f32[72,128]{1,0:T(8,128)S(1)}, f32[72,128]{1,0:T(8,128)S(1)}, u32[]{:S(2)}, u32[]{:S(2)}) collective-permute-start(f32[72,128]{1,0:T(8,128)S(1)} %add_add_fusion.3), channel_id=1, source_target_pairs={{224,0},{232,8},{240,16},{248,24},{64,32},{72,40},{80,48},{88,56},... | collective-permute-start | bytes 110600 | tf_op jit(solution)/shard_map/ppermute | solution.py:233
  54.4 15.9 %collective-permute-start.20 = (f32[512,128]{1,0:T(8,128)S(1)}, f32[512,128]{1,0:T(8,128)S(1)}, u32[]{:S(2)}, u32[]{:S(2)}) collective-permute-start(f32[512,128]{1,0:T(8,128)S(1)} %get-tuple-element.17.refs_1_), channel_id=1, source_target_pairs={{7,0},{0,1},{1,2},{2,3},{3,4},{4,5},{5,6},{6,7},{15,8},{8,9},{9,10... | collective-permute-start | bytes 786440 | tf_op jit(solution)/shard_map/ppermute | solution.py:267
  57.0 7.5 %collective-permute-start.18 = (f32[72,128]{1,0:T(8,128)S(1)}, f32[72,128]{1,0:T(8,128)S(1)}, u32[]{:S(2)}, u32[]{:S(2)}) collective-permute-start(f32[72,128]{1,0:T(8,128)S(1)} %add_add_fusion.2.mine_ref), channel_id=1, source_target_pairs={{7,0},{0,1},{1,2},{2,3},{3,4},{4,5},{5,6},{6,7},{15,8},{8,9},{9,10... | collective-permute-start | bytes 110600 | tf_op jit(solution)/shard_map/ppermute | solution.py:267
  57.2 10.3 %collective-permute-start.17 = (f32[72,128]{1,0:T(8,128)S(1)}, f32[72,128]{1,0:T(8,128)S(1)}, u32[]{:S(2)}, u32[]{:S(2)}) collective-permute-start(f32[72,128]{1,0:T(8,128)S(1)} %add_add_fusion.2.mine_ref), channel_id=1, source_target_pairs={{8,0},{0,8},{24,16},{16,24},{40,32},{32,40},{56,48},{48,56},{72,64... | collective-permute-start | bytes 110600 | tf_op jit(solution)/shard_map/ppermute | solution.py:233
  64.5 5.7 %collective-permute-start.19 = (f32[72,128]{1,0:T(8,128)S(1)}, f32[72,128]{1,0:T(8,128)S(1)}, u32[]{:S(2)}, u32[]{:S(2)}) collective-permute-start(f32[72,128]{1,0:T(8,128)S(1)} %collective-permute-done.18.mine_ref), channel_id=1, source_target_pairs={{8,0},{0,8},{24,16},{16,24},{40,32},{32,40},{56,48},{48,56},{72,64... | collective-permute-start | bytes 110600 | tf_op jit(solution)/shard_map/ppermute | solution.py:233
  73.5 1.3 %collective-permute-start.21 = (f32[72,128]{1,0:T(8,128)S(1)}, f32[72,128]{1,0:T(8,128)S(1)}, u32[]{:S(2)}, u32[]{:S(2)}) collective-permute-start(f32[72,128]{1,0:T(8,128)S(1)} %get-tuple-element.23), channel_id=1, source_target_pairs={{8,0},{0,8},{24,16},{16,24},{40,32},{32,40},{56,48},{48,56},{72,64... | collective-permute-start | bytes 110600 | tf_op jit(solution)/shard_map/ppermute | solution.py:233
  74.8 3.7 %collective-permute-start.24 = (f32[72,128]{1,0:T(8,128)S(1)}, f32[72,128]{1,0:T(8,128)S(1)}, u32[]{:S(2)}, u32[]{:S(2)}) collective-permute-start(f32[72,128]{1,0:T(8,128)S(1)} %add.73), channel_id=1, source_target_pairs={{48,0},{56,8},{32,16},{40,24},{16,32},{24,40},{0,48},{8,56},{112,6... | collective-permute-start | bytes 110600 | tf_op jit(solution)/shard_map/ppermute | solution.py:233
  75.1 3.4 %collective-permute-start.23 = (f32[72,128]{1,0:T(8,128)S(1)}, f32[72,128]{1,0:T(8,128)S(1)}, u32[]{:S(2)}, u32[]{:S(2)}) collective-permute-start(f32[72,128]{1,0:T(8,128)S(1)} %add.73), channel_id=1, source_target_pairs={{16,0},{24,8},{0,16},{8,24},{48,32},{56,40},{32,48},{40,56},{80,64... | collective-permute-start | bytes 110600 | tf_op jit(solution)/shard_map/ppermute | solution.py:233
  76.2 3.1 %collective-permute-start.22 = (f32[72,128]{1,0:T(8,128)S(1)}, f32[72,128]{1,0:T(8,128)S(1)}, u32[]{:S(2)}, u32[]{:S(2)}) collective-permute-start(f32[72,128]{1,0:T(8,128)S(1)} %add.73), channel_id=1, source_target_pairs={{32,0},{40,8},{48,16},{56,24},{0,32},{8,40},{16,48},{24,56},{96,64... | collective-permute-start | bytes 110600 | tf_op jit(solution)/shard_map/ppermute | solution.py:233
  79.3 6.0 %collective-permute-start.27 = (f32[72,128]{1,0:T(8,128)S(1)}, f32[72,128]{1,0:T(8,128)S(1)}, u32[]{:S(2)}, u32[]{:S(2)}) collective-permute-start(f32[72,128]{1,0:T(8,128)S(1)} %add_add_fusion.1), channel_id=1, source_target_pairs={{160,0},{168,8},{176,16},{184,24},{128,32},{136,40},{144,48},{152,... | collective-permute-start | bytes 110600 | tf_op jit(solution)/shard_map/ppermute | solution.py:233
  82.2 4.4 %collective-permute-start.26 = (f32[72,128]{1,0:T(8,128)S(1)}, f32[72,128]{1,0:T(8,128)S(1)}, u32[]{:S(2)}, u32[]{:S(2)}) collective-permute-start(f32[72,128]{1,0:T(8,128)S(1)} %add_add_fusion.1), channel_id=1, source_target_pairs={{64,0},{72,8},{80,16},{88,24},{224,32},{232,40},{240,48},{248,56},... | collective-permute-start | bytes 110600 | tf_op jit(solution)/shard_map/ppermute | solution.py:233
  83.4 4.3 %collective-permute-start.25 = (f32[72,128]{1,0:T(8,128)S(1)}, f32[72,128]{1,0:T(8,128)S(1)}, u32[]{:S(2)}, u32[]{:S(2)}) collective-permute-start(f32[72,128]{1,0:T(8,128)S(1)} %add_add_fusion.1), channel_id=1, source_target_pairs={{224,0},{232,8},{240,16},{248,24},{64,32},{72,40},{80,48},{88,56},... | collective-permute-start | bytes 110600 | tf_op jit(solution)/shard_map/ppermute | solution.py:233
  84.8 16.5 %collective-permute-start.31 = (f32[512,128]{1,0:T(8,128)S(1)}, f32[512,128]{1,0:T(8,128)S(1)}, u32[]{:S(2)}, u32[]{:S(2)}) collective-permute-start(f32[512,128]{1,0:T(8,128)S(1)} %get-tuple-element.21.refs_1_), channel_id=1, source_target_pairs={{7,0},{0,1},{1,2},{2,3},{3,4},{4,5},{5,6},{6,7},{15,8},{8,9},{9,10... | collective-permute-start | bytes 786440 | tf_op jit(solution)/shard_map/ppermute | solution.py:267
  87.7 7.4 %collective-permute-start.28 = (f32[72,128]{1,0:T(8,128)S(1)}, f32[72,128]{1,0:T(8,128)S(1)}, u32[]{:S(2)}, u32[]{:S(2)}) collective-permute-start(f32[72,128]{1,0:T(8,128)S(1)} %add_add_fusion.mine_ref), channel_id=1, source_target_pairs={{7,0},{0,1},{1,2},{2,3},{3,4},{4,5},{5,6},{6,7},{15,8},{8,9},{9,10... | collective-permute-start | bytes 110600 | tf_op jit(solution)/shard_map/ppermute | solution.py:267
  88.0 10.5 %collective-permute-start.30 = (f32[72,128]{1,0:T(8,128)S(1)}, f32[72,128]{1,0:T(8,128)S(1)}, u32[]{:S(2)}, u32[]{:S(2)}) collective-permute-start(f32[72,128]{1,0:T(8,128)S(1)} %add_add_fusion.mine_ref), channel_id=1, source_target_pairs={{8,0},{0,8},{24,16},{16,24},{40,32},{32,40},{56,48},{48,56},{72,64... | collective-permute-start | bytes 110600 | tf_op jit(solution)/shard_map/ppermute | solution.py:233
  95.1 6.2 %collective-permute-start.29 = (f32[72,128]{1,0:T(8,128)S(1)}, f32[72,128]{1,0:T(8,128)S(1)}, u32[]{:S(2)}, u32[]{:S(2)}) collective-permute-start(f32[72,128]{1,0:T(8,128)S(1)} %collective-permute-done.28.mine_ref), channel_id=1, source_target_pairs={{8,0},{0,8},{24,16},{16,24},{40,32},{32,40},{56,48},{48,56},{72,64... | collective-permute-start | bytes 110600 | tf_op jit(solution)/shard_map/ppermute | solution.py:233
  (2 other events, 32.0 us)

commit v2 on v1

--- a/solution.py
+++ b/solution.py
@@ -238,15 +238,15 @@
 
 
 def summed_halves(mine, other, y_last):
-    x = mine + from_row(other, lambda z, y, c: (z, y, 1 - c))
+    mate = from_row(other, lambda z, y, c: (z, y, 1 - c))
+    x = mine + mate
+    next_z = from_row(x, lambda z, y, c: (z ^ 1, y, c))
     if y_last:
-        x = x + from_row(x, lambda z, y, c: (z ^ 1, y, c))
+        x = x + next_z
     else:
-        x = (
-            (x + from_row(x, lambda z, y, c: (z ^ 1, y, c)))
-            + from_row(x, lambda z, y, c: (z, 1 - y, c))
-            + from_row(x, lambda z, y, c: (z ^ 1, 1 - y, c))
-        )
+        next_y = from_row(x, lambda z, y, c: (z, 1 - y, c))
+        next_zy = from_row(x, lambda z, y, c: (z ^ 1, 1 - y, c))
+        x = ((x + next_z) + next_y) + next_zy
     x = (
         (x + from_row(x, lambda z, y, c: (z + side(z), y, c)))
         + from_row(x, lambda z, y, c: (z - 2 * side(z), y, c))
@@ -274,16 +274,18 @@
     for step in range(STEPS):
         if step == 0:
             before = [shifted(panel)]
+        else:
+            before = [a_before, shifted(own[1])]
         mine, other = gram(core, own, n)
         half = summed_halves(mine, other, y_last=step == 0)
         hopped = shifted(half)
-        a = turn_first(core, with_other(half), own, n)
+        own_halves = with_other(half)
+        a = turn_first(core, own_halves, own, n)
         halves = with_other(hopped)
         if step + 1 == STEPS:
             return turn_last(core, halves, a, before)
         a_before, b = turn_both(core, halves, before, n)
         own = [a, b]
-        before = [a_before, shifted(b)]
 
 
 def solution(mesh):

time: 105 us -> 105 us (level)
  no operation moved by 1% of the time
where the time goes in v2:
time: 105 us
  starting transfers between devices  56.4 us (54%)
  waiting for transfers between devices  28.6 us (27%)
  Pallas kernels  18.5 us (18%)
  local copies, waits for them, and re-layouts  1.08 us (1%)
    ppermute x26, starting transfers between devices, from_row(): return lax.ppermute(x, 'row', route)  50.8 us
    ppermute x26, waiting for transfers between devices, from_row(): return lax.ppermute(x, 'row', route)  18.9 us
    ppermute x6, waiting for transfers between devices, shifted(): return lax.ppermute(block, 'pair', route)  9.79 us
    pallas_call x3, Pallas kernels, turn_first(): pl.pallas_call(first_kernel, out_shape=pltpu.VMEM((blocks[0].shape[0], n)...  8.22 us
    pallas_call x2, Pallas kernels, turn_both(): pl.pallas_call(both_kernel, out_shape=[pltpu.VMEM((blocks[0].shape[0], n)...  5.92 us
    ppermute x6, starting transfers between devices, shifted(): return lax.ppermute(block, 'pair', route)  5.59 us
    pallas_call x1, Pallas kernels, turn_last(): pl.pallas_call(last_kernel, out_shape=jax.ShapeDtypeStruct((rows, 2 * n),...  3.51 us
  transfers between devices with their start and end apart: 32, of which 20 were waited for; matrix products, arithmetic and copies ran while one was open for 0% of the time, Pallas kernels for 8%

profile of v2, /device:TPU:1, one launch (start us, length us, event | category | flops | bytes accessed | tf_op | source)
XLA Modules:
  0.0 105.0 jit_solution(1831372828588250011)
XLA Ops:
  0.0 3.7 %collective-permute-start.9 = (f32[512,256]{1,0:T(8,128)}, f32[512,256]{1,0:T(8,128)S(1)}, u32[]{:S(2)}, u32[]{:S(2)}) collective-permute-start(f32[512,256]{1,0:T(8,128)} %refs_0_.3), channel_id=1, source_target_pairs={{7,0},{0,1},{1,2},{2,3},{3,4},{4,5},{5,6},{6,7},{15,8},{8,9},{9,10... | collective-permute-start | bytes 1572872 | tf_op jit(solution)/shard_map/ppermute | solution.py:267
  7.0 1.6 %collective-permute-start.1 = (f32[72,128]{1,0:T(8,128)S(1)}, f32[72,128]{1,0:T(8,128)S(1)}, u32[]{:S(2)}, u32[]{:S(2)}) collective-permute-start(f32[72,128]{1,0:T(8,128)S(1)} %add.60), channel_id=1, source_target_pairs={{32,0},{40,8},{48,16},{56,24},{0,32},{8,40},{16,48},{24,56},{96,64... | collective-permute-start | bytes 110600 | tf_op jit(solution)/shard_map/ppermute | solution.py:233
  8.7 1.6 %collective-permute-done.1 = f32[72,128]{1,0:T(8,128)S(1)} collective-permute-done((f32[72,128]{1,0:T(8,128)S(1)}, f32[72,128]{1,0:T(8,128)S(1)}, u32[]{:S(2)}, u32[]{:S(2)}) %collective-permute-start.1) | collective-permute-done | bytes 36896 | tf_op jit(solution)/shard_map/ppermute | solution.py:233
  10.3 6.3 %collective-permute-start.4 = (f32[72,128]{1,0:T(8,128)S(1)}, f32[72,128]{1,0:T(8,128)S(1)}, u32[]{:S(2)}, u32[]{:S(2)}) collective-permute-start(f32[72,128]{1,0:T(8,128)S(1)} %add.61), channel_id=1, source_target_pairs={{160,0},{168,8},{176,16},{184,24},{128,32},{136,40},{144,48},{152,... | collective-permute-start | bytes 110600 | tf_op jit(solution)/shard_map/ppermute | solution.py:233
  16.9 2.8 %collective-permute-start.2 = (f32[72,128]{1,0:T(8,128)S(1)}, f32[72,128]{1,0:T(8,128)S(1)}, u32[]{:S(2)}, u32[]{:S(2)}) collective-permute-start(f32[72,128]{1,0:T(8,128)S(1)} %add.61), channel_id=1, source_target_pairs={{224,0},{232,8},{240,16},{248,24},{64,32},{72,40},{80,48},{88,56},... | collective-permute-start | bytes 110600 | tf_op jit(solution)/shard_map/ppermute | solution.py:233
  22.0 2.4 %collective-permute-done.5 = f32[72,128]{1,0:T(8,128)S(1)} collective-permute-done((f32[72,128]{1,0:T(8,128)S(1)}, f32[72,128]{1,0:T(8,128)S(1)}, u32[]{:S(2)}, u32[]{:S(2)}) %collective-permute-start.5) | collective-permute-done | bytes 36896 | tf_op jit(solution)/shard_map/ppermute | solution.py:233
  24.4 1.4 %collective-permute-start.7 = (f32[72,128]{1,0:T(8,128)S(1)}, f32[72,128]{1,0:T(8,128)S(1)}, u32[]{:S(2)}, u32[]{:S(2)}) collective-permute-start(f32[72,128]{1,0:T(8,128)S(1)} %add.65.mine_ref), channel_id=1, source_target_pairs={{7,0},{0,1},{1,2},{2,3},{3,4},{4,5},{5,6},{6,7},{15,8},{8,9},{9,10... | collective-permute-start | bytes 110600 | tf_op jit(solution)/shard_map/ppermute | solution.py:267
  25.8 3.8 %collective-permute-start.6 = (f32[72,128]{1,0:T(8,128)S(1)}, f32[72,128]{1,0:T(8,128)S(1)}, u32[]{:S(2)}, u32[]{:S(2)}) collective-permute-start(f32[72,128]{1,0:T(8,128)S(1)} %add.65.mine_ref), channel_id=1, source_target_pairs={{8,0},{0,8},{24,16},{16,24},{40,32},{32,40},{56,48},{48,56},{72,64... | collective-permute-start | bytes 110600 | tf_op jit(solution)/shard_map/ppermute | solution.py:233
  29.6 1.2 %collective-permute-done.7.mine_ref = f32[72,128]{1,0:T(8,128)S(1)} collective-permute-done((f32[72,128]{1,0:T(8,128)S(1)}, f32[72,128]{1,0:T(8,128)S(1)}, u32[]{:S(2)}, u32[]{:S(2)}) %collective-permute-start.7) | collective-permute-done | bytes 36896 | tf_op jit(solution)/shard_map/ppermute | solution.py:267
  30.8 4.9 %collective-permute-start.8 = (f32[72,128]{1,0:T(8,128)S(1)}, f32[72,128]{1,0:T(8,128)S(1)}, u32[]{:S(2)}, u32[]{:S(2)}) collective-permute-start(f32[72,128]{1,0:T(8,128)S(1)} %collective-permute-done.7.mine_ref), channel_id=1, source_target_pairs={{8,0},{0,8},{24,16},{16,24},{40,32},{32,40},{56,48},{48,56},{72,64... | collective-permute-start | bytes 110600 | tf_op jit(solution)/shard_map/ppermute | solution.py:233
  35.7 2.7 %turn_first.3.refs_0_ = f32[512,128]{1,0:T(8,128)S(1)} custom-call(s32[1]{0:T(128)} %bitcast.core_ref, f32[72,128]{1,0:T(8,128)S(1)} %add.65.mine_ref, f32[72,128]{1,0:T(8,128)S(1)} %collective-permute-done.6.other_ref, f32[512,256]{1,0:T(8,128)S(1)} %copy-done.1), custom_call_target="tpu_custom_call" | custom-call | tf_op jit(solution)/shard_map/turn_first/pallas_call | solution.py:197
  38.5 3.0 %turn_both.2 = (f32[512,128]{1,0:T(8,128)S(1)}, f32[512,128]{1,0:T(8,128)S(1)}) custom-call(s32[1]{0:T(128)} %bitcast.core_ref, f32[72,128]{1,0:T(8,128)S(1)} %collective-permute-done.7.mine_ref, f32[72,128]{1,0:T(8,128)S(1)} %collective-permute-done.8.other_ref, f32[512,256]{1,0:T(8,128)S(1)} %collective-permute-done.9.refs_0_), custom_call_target="tpu_custom_call" | custom-call | tf_op jit(solution)/shard_map/turn_both/pallas_call | solution.py:206
  41.9 1.2 %collective-permute-done.10 = f32[72,128]{1,0:T(8,128)S(1)} collective-permute-done((f32[72,128]{1,0:T(8,128)S(1)}, f32[72,128]{1,0:T(8,128)S(1)}, u32[]{:S(2)}, u32[]{:S(2)}) %collective-permute-start.10) | collective-permute-done | bytes 36896 | tf_op jit(solution)/shard_map/ppermute | solution.py:233
  46.8 1.2 %collective-permute-done.12 = f32[72,128]{1,0:T(8,128)S(1)} collective-permute-done((f32[72,128]{1,0:T(8,128)S(1)}, f32[72,128]{1,0:T(8,128)S(1)}, u32[]{:S(2)}, u32[]{:S(2)}) %collective-permute-start.12) | collective-permute-done | bytes 36896 | tf_op jit(solution)/shard_map/ppermute | solution.py:233
  48.2 3.5 %collective-permute-start.16 = (f32[72,128]{1,0:T(8,128)S(1)}, f32[72,128]{1,0:T(8,128)S(1)}, u32[]{:S(2)}, u32[]{:S(2)}) collective-permute-start(f32[72,128]{1,0:T(8,128)S(1)} %add_add_fusion.3), channel_id=1, source_target_pairs={{160,0},{168,8},{176,16},{184,24},{128,32},{136,40},{144,48},{152,... | collective-permute-start | bytes 110600 | tf_op jit(solution)/shard_map/ppermute | solution.py:233
  52.5 1.9 %collective-permute-start.14 = (f32[72,128]{1,0:T(8,128)S(1)}, f32[72,128]{1,0:T(8,128)S(1)}, u32[]{:S(2)}, u32[]{:S(2)}) collective-permute-start(f32[72,128]{1,0:T(8,128)S(1)} %add_add_fusion.3), channel_id=1, source_target_pairs={{224,0},{232,8},{240,16},{248,24},{64,32},{72,40},{80,48},{88,56},... | collective-permute-start | bytes 110600 | tf_op jit(solution)/shard_map/ppermute | solution.py:233
  54.4 1.3 %collective-permute-done.15 = f32[72,128]{1,0:T(8,128)S(1)} collective-permute-done((f32[72,128]{1,0:T(8,128)S(1)}, f32[72,128]{1,0:T(8,128)S(1)}, u32[]{:S(2)}, u32[]{:S(2)}) %collective-permute-start.15) | collective-permute-done | bytes 36896 | tf_op jit(solution)/shard_map/ppermute | solution.py:233
  55.6 1.4 %collective-permute-done.14 = f32[72,128]{1,0:T(8,128)S(1)} collective-permute-done((f32[72,128]{1,0:T(8,128)S(1)}, f32[72,128]{1,0:T(8,128)S(1)}, u32[]{:S(2)}, u32[]{:S(2)}) %collective-permute-start.14) | collective-permute-done | bytes 36896 | tf_op jit(solution)/shard_map/ppermute | solution.py:233
  57.2 2.8 %collective-permute-start.17 = (f32[72,128]{1,0:T(8,128)S(1)}, f32[72,128]{1,0:T(8,128)S(1)}, u32[]{:S(2)}, u32[]{:S(2)}) collective-permute-start(f32[72,128]{1,0:T(8,128)S(1)} %add_add_fusion.2.mine_ref), channel_id=1, source_target_pairs={{8,0},{0,8},{24,16},{16,24},{40,32},{32,40},{56,48},{48,56},{72,64... | collective-permute-start | bytes 110600 | tf_op jit(solution)/shard_map/ppermute | solution.py:233
  60.0 4.5 %collective-permute-done.18.mine_ref = f32[72,128]{1,0:T(8,128)S(1)} collective-permute-done((f32[72,128]{1,0:T(8,128)S(1)}, f32[72,128]{1,0:T(8,128)S(1)}, u32[]{:S(2)}, u32[]{:S(2)}) %collective-permute-start.18) | collective-permute-done | bytes 36896 | tf_op jit(solution)/shard_map/ppermute | solution.py:267
  64.5 3.0 %collective-permute-start.19 = (f32[72,128]{1,0:T(8,128)S(1)}, f32[72,128]{1,0:T(8,128)S(1)}, u32[]{:S(2)}, u32[]{:S(2)}) collective-permute-start(f32[72,128]{1,0:T(8,128)S(1)} %collective-permute-done.18.mine_ref), channel_id=1, source_target_pairs={{8,0},{0,8},{24,16},{16,24},{40,32},{32,40},{56,48},{48,56},{72,64... | collective-permute-start | bytes 110600 | tf_op jit(solution)/shard_map/ppermute | solution.py:233
  67.5 2.7 %turn_first.4.refs_0_ = f32[512,128]{1,0:T(8,128)S(1)} custom-call(s32[1]{0:T(128)} %bitcast.core_ref, f32[72,128]{1,0:T(8,128)S(1)} %add_add_fusion.2.mine_ref, f32[72,128]{1,0:T(8,128)S(1)} %collective-permute-done.17.other_ref, f32[512,128]{1,0:T(8,128)S(1)} %turn_first.3.refs_0_, f32[512,128]{1,0:T(8,128)S(1)} %get-tuple-element.17.refs_1_), custom_call_target="tpu_custom_call" | custom-call | tf_op jit(solution)/shard_map/turn_first/pallas_call | solution.py:197
  70.3 3.0 %turn_both.3 = (f32[512,128]{1,0:T(8,128)S(1)}, f32[512,128]{1,0:T(8,128)S(1)}) custom-call(s32[1]{0:T(128)} %bitcast.core_ref, f32[72,128]{1,0:T(8,128)S(1)} %collective-permute-done.18.mine_ref, f32[72,128]{1,0:T(8,128)S(1)} %collective-permute-done.19.other_ref, f32[512,128]{1,0:T(8,128)S(1)} %get-tuple-element.20.refs_0_, ...), custom_call_target="tpu_custom_call" | custom-call | tf_op jit(solution)/shard_map/turn_both/pallas_call | solution.py:206
  76.2 1.3 %collective-permute-start.22 = (f32[72,128]{1,0:T(8,128)S(1)}, f32[72,128]{1,0:T(8,128)S(1)}, u32[]{:S(2)}, u32[]{:S(2)}) collective-permute-start(f32[72,128]{1,0:T(8,128)S(1)} %add.73), channel_id=1, source_target_pairs={{32,0},{40,8},{48,16},{56,24},{0,32},{8,40},{16,48},{24,56},{96,64... | collective-permute-start | bytes 110600 | tf_op jit(solution)/shard_map/ppermute | solution.py:233
  79.3 2.9 %collective-permute-start.27 = (f32[72,128]{1,0:T(8,128)S(1)}, f32[72,128]{1,0:T(8,128)S(1)}, u32[]{:S(2)}, u32[]{:S(2)}) collective-permute-start(f32[72,128]{1,0:T(8,128)S(1)} %add_add_fusion.1), channel_id=1, source_target_pairs={{160,0},{168,8},{176,16},{184,24},{128,32},{136,40},{144,48},{152,... | collective-permute-start | bytes 110600 | tf_op jit(solution)/shard_map/ppermute | solution.py:233
  83.4 1.4 %collective-permute-start.25 = (f32[72,128]{1,0:T(8,128)S(1)}, f32[72,128]{1,0:T(8,128)S(1)}, u32[]{:S(2)}, u32[]{:S(2)}) collective-permute-start(f32[72,128]{1,0:T(8,128)S(1)} %add_add_fusion.1), channel_id=1, source_target_pairs={{224,0},{232,8},{240,16},{248,24},{64,32},{72,40},{80,48},{88,56},... | collective-permute-start | bytes 110600 | tf_op jit(solution)/shard_map/ppermute | solution.py:233
  85.2 1.4 %collective-permute-done.26 = f32[72,128]{1,0:T(8,128)S(1)} collective-permute-done((f32[72,128]{1,0:T(8,128)S(1)}, f32[72,128]{1,0:T(8,128)S(1)}, u32[]{:S(2)}, u32[]{:S(2)}) %collective-permute-start.26) | collective-permute-done | bytes 36896 | tf_op jit(solution)/shard_map/ppermute | solution.py:233
  88.0 3.1 %collective-permute-start.30 = (f32[72,128]{1,0:T(8,128)S(1)}, f32[72,128]{1,0:T(8,128)S(1)}, u32[]{:S(2)}, u32[]{:S(2)}) collective-permute-start(f32[72,128]{1,0:T(8,128)S(1)} %add_add_fusion.mine_ref), channel_id=1, source_target_pairs={{8,0},{0,8},{24,16},{16,24},{40,32},{32,40},{56,48},{48,56},{72,64... | collective-permute-start | bytes 110600 | tf_op jit(solution)/shard_map/ppermute | solution.py:233
  91.1 4.0 %collective-permute-done.28.mine_ref = f32[72,128]{1,0:T(8,128)S(1)} collective-permute-done((f32[72,128]{1,0:T(8,128)S(1)}, f32[72,128]{1,0:T(8,128)S(1)}, u32[]{:S(2)}, u32[]{:S(2)}) %collective-permute-start.28) | collective-permute-done | bytes 36896 | tf_op jit(solution)/shard_map/ppermute | solution.py:267
  95.1 3.4 %collective-permute-start.29 = (f32[72,128]{1,0:T(8,128)S(1)}, f32[72,128]{1,0:T(8,128)S(1)}, u32[]{:S(2)}, u32[]{:S(2)}) collective-permute-start(f32[72,128]{1,0:T(8,128)S(1)} %collective-permute-done.28.mine_ref), channel_id=1, source_target_pairs={{8,0},{0,8},{24,16},{16,24},{40,32},{32,40},{56,48},{48,56},{72,64... | collective-permute-start | bytes 110600 | tf_op jit(solution)/shard_map/ppermute | solution.py:233
  98.6 2.7 %turn_first.5.refs_0_ = f32[512,128]{1,0:T(8,128)S(1)} custom-call(s32[1]{0:T(128)} %bitcast.core_ref, f32[72,128]{1,0:T(8,128)S(1)} %add_add_fusion.mine_ref, f32[72,128]{1,0:T(8,128)S(1)} %collective-permute-done.30.other_ref, f32[512,128]{1,0:T(8,128)S(1)} %turn_first.4.refs_0_, f32[512,128]{1,0:T(8,128)S(1)} %get-tuple-element.21.refs_1_), custom_call_target="tpu_custom_call" | custom-call | tf_op jit(solution)/shard_map/turn_first/pallas_call | solution.py:197
  101.4 3.5 %turn_last.1 = f32[512,256]{1,0:T(8,128)} custom-call(s32[1]{0:T(128)} %bitcast.core_ref, f32[72,128]{1,0:T(8,128)S(1)} %collective-permute-done.28.mine_ref, f32[72,128]{1,0:T(8,128)S(1)} %collective-permute-done.29.other_ref, f32[512,128]{1,0:T(8,128)S(1)} %turn_first.5.refs_0_, f32[512,128]{1,0:T(8,128)S(1)} %get-tuple-element.24.refs_1_, ...), custom_call_target="tpu_custom_call" | custom-call | tf_op jit(solution)/shard_map/turn_last/pallas_call | solution.py:216
  (55 shorter events, 18.7 us)
Async XLA Ops:
  0.0 38.5 %collective-permute-start.9 = (f32[512,256]{1,0:T(8,128)}, f32[512,256]{1,0:T(8,128)S(1)}, u32[]{:S(2)}, u32[]{:S(2)}) collective-permute-start(f32[512,256]{1,0:T(8,128)} %refs_0_.3), channel_id=1, source_target_pairs={{7,0},{0,1},{1,2},{2,3},{3,4},{4,5},{5,6},{6,7},{15,8},{8,9},{9,10... | collective-permute-start | bytes 1572872 | tf_op jit(solution)/shard_map/ppermute | solution.py:267
  5.1 1.9 %collective-permute-start = (f32[72,128]{1,0:T(8,128)S(1)}, f32[72,128]{1,0:T(8,128)S(1)}, u32[]{:S(2)}, u32[]{:S(2)}) collective-permute-start(f32[72,128]{1,0:T(8,128)S(1)} %get-tuple-element.16), channel_id=1, source_target_pairs={{8,0},{0,8},{24,16},{16,24},{40,32},{32,40},{56,48},{48,56},{72,64... | collective-permute-start | bytes 110600 | tf_op jit(solution)/shard_map/ppermute | solution.py:233
  7.0 3.3 %collective-permute-start.1 = (f32[72,128]{1,0:T(8,128)S(1)}, f32[72,128]{1,0:T(8,128)S(1)}, u32[]{:S(2)}, u32[]{:S(2)}) collective-permute-start(f32[72,128]{1,0:T(8,128)S(1)} %add.60), channel_id=1, source_target_pairs={{32,0},{40,8},{48,16},{56,24},{0,32},{8,40},{16,48},{24,56},{96,64... | collective-permute-start | bytes 110600 | tf_op jit(solution)/shard_map/ppermute | solution.py:233
  10.3 9.4 %collective-permute-start.4 = (f32[72,128]{1,0:T(8,128)S(1)}, f32[72,128]{1,0:T(8,128)S(1)}, u32[]{:S(2)}, u32[]{:S(2)}) collective-permute-start(f32[72,128]{1,0:T(8,128)S(1)} %add.61), channel_id=1, source_target_pairs={{160,0},{168,8},{176,16},{184,24},{128,32},{136,40},{144,48},{152,... | collective-permute-start | bytes 110600 | tf_op jit(solution)/shard_map/ppermute | solution.py:233
  16.6 3.8 %collective-permute-start.3 = (f32[72,128]{1,0:T(8,128)S(1)}, f32[72,128]{1,0:T(8,128)S(1)}, u32[]{:S(2)}, u32[]{:S(2)}) collective-permute-start(f32[72,128]{1,0:T(8,128)S(1)} %add.61), channel_id=1, source_target_pairs={{64,0},{72,8},{80,16},{88,24},{224,32},{232,40},{240,48},{248,56},... | collective-permute-start | bytes 110600 | tf_op jit(solution)/shard_map/ppermute | solution.py:233
  16.9 4.6 %collective-permute-start.2 = (f32[72,128]{1,0:T(8,128)S(1)}, f32[72,128]{1,0:T(8,128)S(1)}, u32[]{:S(2)}, u32[]{:S(2)}) collective-permute-start(f32[72,128]{1,0:T(8,128)S(1)} %add.61), channel_id=1, source_target_pairs={{224,0},{232,8},{240,16},{248,24},{64,32},{72,40},{80,48},{88,56},... | collective-permute-start | bytes 110600 | tf_op jit(solution)/shard_map/ppermute | solution.py:233
  21.5 2.9 %collective-permute-start.5 = (f32[72,128]{1,0:T(8,128)S(1)}, f32[72,128]{1,0:T(8,128)S(1)}, u32[]{:S(2)}, u32[]{:S(2)}) collective-permute-start(f32[72,128]{1,0:T(8,128)S(1)} %add_add_fusion.4), channel_id=1, source_target_pairs={{16,0},{24,8},{0,16},{8,24},{48,32},{56,40},{32,48},{40,56},{80,64... | collective-permute-start | bytes 110600 | tf_op jit(solution)/shard_map/ppermute | solution.py:233
  24.4 6.4 %collective-permute-start.7 = (f32[72,128]{1,0:T(8,128)S(1)}, f32[72,128]{1,0:T(8,128)S(1)}, u32[]{:S(2)}, u32[]{:S(2)}) collective-permute-start(f32[72,128]{1,0:T(8,128)S(1)} %add.65.mine_ref), channel_id=1, source_target_pairs={{7,0},{0,1},{1,2},{2,3},{3,4},{4,5},{5,6},{6,7},{15,8},{8,9},{9,10... | collective-permute-start | bytes 110600 | tf_op jit(solution)/shard_map/ppermute | solution.py:267
  25.8 9.9 %collective-permute-start.6 = (f32[72,128]{1,0:T(8,128)S(1)}, f32[72,128]{1,0:T(8,128)S(1)}, u32[]{:S(2)}, u32[]{:S(2)}) collective-permute-start(f32[72,128]{1,0:T(8,128)S(1)} %add.65.mine_ref), channel_id=1, source_target_pairs={{8,0},{0,8},{24,16},{16,24},{40,32},{32,40},{56,48},{48,56},{72,64... | collective-permute-start | bytes 110600 | tf_op jit(solution)/shard_map/ppermute | solution.py:233
  30.8 7.7 %collective-permute-start.8 = (f32[72,128]{1,0:T(8,128)S(1)}, f32[72,128]{1,0:T(8,128)S(1)}, u32[]{:S(2)}, u32[]{:S(2)}) collective-permute-start(f32[72,128]{1,0:T(8,128)S(1)} %collective-permute-done.7.mine_ref), channel_id=1, source_target_pairs={{8,0},{0,8},{24,16},{16,24},{40,32},{32,40},{56,48},{48,56},{72,64... | collective-permute-start | bytes 110600 | tf_op jit(solution)/shard_map/ppermute | solution.py:233
  41.8 1.3 %collective-permute-start.10 = (f32[72,128]{1,0:T(8,128)S(1)}, f32[72,128]{1,0:T(8,128)S(1)}, u32[]{:S(2)}, u32[]{:S(2)}) collective-permute-start(f32[72,128]{1,0:T(8,128)S(1)} %get-tuple-element.19), channel_id=1, source_target_pairs={{8,0},{0,8},{24,16},{16,24},{40,32},{32,40},{56,48},{48,56},{72,64... | collective-permute-start | bytes 110600 | tf_op jit(solution)/shard_map/ppermute | solution.py:233
  43.1 3.7 %collective-permute-start.13 = (f32[72,128]{1,0:T(8,128)S(1)}, f32[72,128]{1,0:T(8,128)S(1)}, u32[]{:S(2)}, u32[]{:S(2)}) collective-permute-start(f32[72,128]{1,0:T(8,128)S(1)} %add.66), channel_id=1, source_target_pairs={{48,0},{56,8},{32,16},{40,24},{16,32},{24,40},{0,48},{8,56},{112,6... | collective-permute-start | bytes 110600 | tf_op jit(solution)/shard_map/ppermute | solution.py:233
  44.0 4.1 %collective-permute-start.12 = (f32[72,128]{1,0:T(8,128)S(1)}, f32[72,128]{1,0:T(8,128)S(1)}, u32[]{:S(2)}, u32[]{:S(2)}) collective-permute-start(f32[72,128]{1,0:T(8,128)S(1)} %add.66), channel_id=1, source_target_pairs={{16,0},{24,8},{0,16},{8,24},{48,32},{56,40},{32,48},{40,56},{80,64... | collective-permute-start | bytes 110600 | tf_op jit(solution)/shard_map/ppermute | solution.py:233
  45.0 3.1 %collective-permute-start.11 = (f32[72,128]{1,0:T(8,128)S(1)}, f32[72,128]{1,0:T(8,128)S(1)}, u32[]{:S(2)}, u32[]{:S(2)}) collective-permute-start(f32[72,128]{1,0:T(8,128)S(1)} %add.66), channel_id=1, source_target_pairs={{32,0},{40,8},{48,16},{56,24},{0,32},{8,40},{16,48},{24,56},{96,64... | collective-permute-start | bytes 110600 | tf_op jit(solution)/shard_map/ppermute | solution.py:233
  48.2 6.2 %collective-permute-start.16 = (f32[72,128]{1,0:T(8,128)S(1)}, f32[72,128]{1,0:T(8,128)S(1)}, u32[]{:S(2)}, u32[]{:S(2)}) collective-permute-start(f32[72,128]{1,0:T(8,128)S(1)} %add_add_fusion.3), channel_id=1, source_target_pairs={{160,0},{168,8},{176,16},{184,24},{128,32},{136,40},{144,48},{152,... | collective-permute-start | bytes 110600 | tf_op jit(solution)/shard_map/ppermute | solution.py:233
  51.7 4.0 %collective-permute-start.15 = (f32[72,128]{1,0:T(8,128)S(1)}, f32[72,128]{1,0:T(8,128)S(1)}, u32[]{:S(2)}, u32[]{:S(2)}) collective-permute-start(f32[72,128]{1,0:T(8,128)S(1)} %add_add_fusion.3), channel_id=1, source_target_pairs={{64,0},{72,8},{80,16},{88,24},{224,32},{232,40},{240,48},{248,56},... | collective-permute-start | bytes 110600 | tf_op jit(solution)/shard_map/ppermute | solution.py:233
  52.5 4.6 %collective-permute-start.14 = (f32[72,128]{1,0:T(8,128)S(1)}, f32[72,128]{1,0:T(8,128)S(1)}, u32[]{:S(2)}, u32[]{:S(2)}) collective-permute-start(f32[72,128]{1,0:T(8,128)S(1)} %add_add_fusion.3), channel_id=1, source_target_pairs={{224,0},{232,8},{240,16},{248,24},{64,32},{72,40},{80,48},{88,56},... | collective-permute-start | bytes 110600 | tf_op jit(solution)/shard_map/ppermute | solution.py:233
  54.4 15.9 %collective-permute-start.20 = (f32[512,128]{1,0:T(8,128)S(1)}, f32[512,128]{1,0:T(8,128)S(1)}, u32[]{:S(2)}, u32[]{:S(2)}) collective-permute-start(f32[512,128]{1,0:T(8,128)S(1)} %get-tuple-element.17.refs_1_), channel_id=1, source_target_pairs={{7,0},{0,1},{1,2},{2,3},{3,4},{4,5},{5,6},{6,7},{15,8},{8,9},{9,10... | collective-permute-start | bytes 786440 | tf_op jit(solution)/shard_map/ppermute | solution.py:267
  57.0 7.5 %collective-permute-start.18 = (f32[72,128]{1,0:T(8,128)S(1)}, f32[72,128]{1,0:T(8,128)S(1)}, u32[]{:S(2)}, u32[]{:S(2)}) collective-permute-start(f32[72,128]{1,0:T(8,128)S(1)} %add_add_fusion.2.mine_ref), channel_id=1, source_target_pairs={{7,0},{0,1},{1,2},{2,3},{3,4},{4,5},{5,6},{6,7},{15,8},{8,9},{9,10... | collective-permute-start | bytes 110600 | tf_op jit(solution)/shard_map/ppermute | solution.py:267
  57.2 10.3 %collective-permute-start.17 = (f32[72,128]{1,0:T(8,128)S(1)}, f32[72,128]{1,0:T(8,128)S(1)}, u32[]{:S(2)}, u32[]{:S(2)}) collective-permute-start(f32[72,128]{1,0:T(8,128)S(1)} %add_add_fusion.2.mine_ref), channel_id=1, source_target_pairs={{8,0},{0,8},{24,16},{16,24},{40,32},{32,40},{56,48},{48,56},{72,64... | collective-permute-start | bytes 110600 | tf_op jit(solution)/shard_map/ppermute | solution.py:233
  64.5 5.7 %collective-permute-start.19 = (f32[72,128]{1,0:T(8,128)S(1)}, f32[72,128]{1,0:T(8,128)S(1)}, u32[]{:S(2)}, u32[]{:S(2)}) collective-permute-start(f32[72,128]{1,0:T(8,128)S(1)} %collective-permute-done.18.mine_ref), channel_id=1, source_target_pairs={{8,0},{0,8},{24,16},{16,24},{40,32},{32,40},{56,48},{48,56},{72,64... | collective-permute-start | bytes 110600 | tf_op jit(solution)/shard_map/ppermute | solution.py:233
  73.5 1.3 %collective-permute-start.21 = (f32[72,128]{1,0:T(8,128)S(1)}, f32[72,128]{1,0:T(8,128)S(1)}, u32[]{:S(2)}, u32[]{:S(2)}) collective-permute-start(f32[72,128]{1,0:T(8,128)S(1)} %get-tuple-element.23), channel_id=1, source_target_pairs={{8,0},{0,8},{24,16},{16,24},{40,32},{32,40},{56,48},{48,56},{72,64... | collective-permute-start | bytes 110600 | tf_op jit(solution)/shard_map/ppermute | solution.py:233
  74.8 3.7 %collective-permute-start.24 = (f32[72,128]{1,0:T(8,128)S(1)}, f32[72,128]{1,0:T(8,128)S(1)}, u32[]{:S(2)}, u32[]{:S(2)}) collective-permute-start(f32[72,128]{1,0:T(8,128)S(1)} %add.73), channel_id=1, source_target_pairs={{48,0},{56,8},{32,16},{40,24},{16,32},{24,40},{0,48},{8,56},{112,6... | collective-permute-start | bytes 110600 | tf_op jit(solution)/shard_map/ppermute | solution.py:233
  75.1 3.4 %collective-permute-start.23 = (f32[72,128]{1,0:T(8,128)S(1)}, f32[72,128]{1,0:T(8,128)S(1)}, u32[]{:S(2)}, u32[]{:S(2)}) collective-permute-start(f32[72,128]{1,0:T(8,128)S(1)} %add.73), channel_id=1, source_target_pairs={{16,0},{24,8},{0,16},{8,24},{48,32},{56,40},{32,48},{40,56},{80,64... | collective-permute-start | bytes 110600 | tf_op jit(solution)/shard_map/ppermute | solution.py:233
  76.2 3.1 %collective-permute-start.22 = (f32[72,128]{1,0:T(8,128)S(1)}, f32[72,128]{1,0:T(8,128)S(1)}, u32[]{:S(2)}, u32[]{:S(2)}) collective-permute-start(f32[72,128]{1,0:T(8,128)S(1)} %add.73), channel_id=1, source_target_pairs={{32,0},{40,8},{48,16},{56,24},{0,32},{8,40},{16,48},{24,56},{96,64... | collective-permute-start | bytes 110600 | tf_op jit(solution)/shard_map/ppermute | solution.py:233
  79.3 6.0 %collective-permute-start.27 = (f32[72,128]{1,0:T(8,128)S(1)}, f32[72,128]{1,0:T(8,128)S(1)}, u32[]{:S(2)}, u32[]{:S(2)}) collective-permute-start(f32[72,128]{1,0:T(8,128)S(1)} %add_add_fusion.1), channel_id=1, source_target_pairs={{160,0},{168,8},{176,16},{184,24},{128,32},{136,40},{144,48},{152,... | collective-permute-start | bytes 110600 | tf_op jit(solution)/shard_map/ppermute | solution.py:233
  82.2 4.4 %collective-permute-start.26 = (f32[72,128]{1,0:T(8,128)S(1)}, f32[72,128]{1,0:T(8,128)S(1)}, u32[]{:S(2)}, u32[]{:S(2)}) collective-permute-start(f32[72,128]{1,0:T(8,128)S(1)} %add_add_fusion.1), channel_id=1, source_target_pairs={{64,0},{72,8},{80,16},{88,24},{224,32},{232,40},{240,48},{248,56},... | collective-permute-start | bytes 110600 | tf_op jit(solution)/shard_map/ppermute | solution.py:233
  83.4 4.3 %collective-permute-start.25 = (f32[72,128]{1,0:T(8,128)S(1)}, f32[72,128]{1,0:T(8,128)S(1)}, u32[]{:S(2)}, u32[]{:S(2)}) collective-permute-start(f32[72,128]{1,0:T(8,128)S(1)} %add_add_fusion.1), channel_id=1, source_target_pairs={{224,0},{232,8},{240,16},{248,24},{64,32},{72,40},{80,48},{88,56},... | collective-permute-start | bytes 110600 | tf_op jit(solution)/shard_map/ppermute | solution.py:233
  84.8 16.5 %collective-permute-start.31 = (f32[512,128]{1,0:T(8,128)S(1)}, f32[512,128]{1,0:T(8,128)S(1)}, u32[]{:S(2)}, u32[]{:S(2)}) collective-permute-start(f32[512,128]{1,0:T(8,128)S(1)} %get-tuple-element.21.refs_1_), channel_id=1, source_target_pairs={{7,0},{0,1},{1,2},{2,3},{3,4},{4,5},{5,6},{6,7},{15,8},{8,9},{9,10... | collective-permute-start | bytes 786440 | tf_op jit(solution)/shard_map/ppermute | solution.py:267
  87.7 7.4 %collective-permute-start.28 = (f32[72,128]{1,0:T(8,128)S(1)}, f32[72,128]{1,0:T(8,128)S(1)}, u32[]{:S(2)}, u32[]{:S(2)}) collective-permute-start(f32[72,128]{1,0:T(8,128)S(1)} %add_add_fusion.mine_ref), channel_id=1, source_target_pairs={{7,0},{0,1},{1,2},{2,3},{3,4},{4,5},{5,6},{6,7},{15,8},{8,9},{9,10... | collective-permute-start | bytes 110600 | tf_op jit(solution)/shard_map/ppermute | solution.py:267
  88.0 10.5 %collective-permute-start.30 = (f32[72,128]{1,0:T(8,128)S(1)}, f32[72,128]{1,0:T(8,128)S(1)}, u32[]{:S(2)}, u32[]{:S(2)}) collective-permute-start(f32[72,128]{1,0:T(8,128)S(1)} %add_add_fusion.mine_ref), channel_id=1, source_target_pairs={{8,0},{0,8},{24,16},{16,24},{40,32},{32,40},{56,48},{48,56},{72,64... | collective-permute-start | bytes 110600 | tf_op jit(solution)/shard_map/ppermute | solution.py:233
  95.1 6.2 %collective-permute-start.29 = (f32[72,128]{1,0:T(8,128)S(1)}, f32[72,128]{1,0:T(8,128)S(1)}, u32[]{:S(2)}, u32[]{:S(2)}) collective-permute-start(f32[72,128]{1,0:T(8,128)S(1)} %collective-permute-done.28.mine_ref), channel_id=1, source_target_pairs={{8,0},{0,8},{24,16},{16,24},{40,32},{32,40},{56,48},{48,56},{72,64... | collective-permute-start | bytes 110600 | tf_op jit(solution)/shard_map/ppermute | solution.py:233
  (2 other events, 32.0 us)

commit v3 on v2

v3 whole, which is shorter than its diff:
```python
import jax
import jax.numpy as jnp
from jax import lax
from jax.experimental import pallas as pl
from jax.experimental.pallas import tpu as pltpu
from jax.sharding import PartitionSpec as P


STEPS = 3

BF16 = jnp.bfloat16
F32 = jnp.float32
HIGH = lax.Precision.HIGHEST

QUAD = 4
PAD = 8
CHUNKS = 4


def split(x):
    hi = x.astype(BF16)
    return hi, (x - hi.astype(F32)).astype(BF16)


def left3(x):
    return jnp.concatenate(split(x), 1)


def right3(x):
    hi, lo = split(x)
    top = jnp.concatenate([hi, lo], 1)
    low = jnp.concatenate([hi, jnp.zeros_like(hi)], 1)
    return jnp.concatenate([top, low], 0)


def times3(left, right):
    out = jnp.dot(left, right, preferred_element_type=F32)
    n = out.shape[1] // 2
    return out[:, :n] + out[:, n:]


def times(a, b):
    return jnp.dot(a, b, precision=HIGH, preferred_element_type=F32)


def quarter_cosines(cross, diag_a, diag_b):
    shape = cross.shape
    scale_a = lax.rsqrt(diag_a + 1e-06)
    scale_b = lax.rsqrt(diag_b + 1e-06)
    return 0.25 * (cross * jnp.transpose(jnp.broadcast_to(scale_a, shape)) * scale_b)


def damped_inverse(d, dt):
    n = d.shape[0]
    shape = (n, n)
    eye = jnp.where(
        lax.broadcasted_iota(jnp.int32, shape, 0) == lax.broadcasted_iota(jnp.int32, shape, 1),
        1.0,
        0.0,
    ).astype(F32)
    base = eye + times(d, dt)
    top = 1.0 + 1.001 * (0.25 * n) ** 2
    start = 2.0 / (1.0 + top)
    gap = (top - 1.0) / (top + 1.0)
    y = start * base
    x = None
    while gap > 0.05:
        z = 2.0 * eye - y
        stretch = 2.0 / (2.0 - gap * gap)
        right = right3(z)
        if x is None:
            y = stretch * times3(left3(y), right)
            x = (stretch * start) * z
        else:
            both = stretch * times3(jnp.concatenate([left3(x), left3(y)], 0), right)
            x, y = both[:n], both[n:]
        gap = gap * gap / (2.0 - gap * gap)
    left = eye - times3(left3(x), right3(base))
    x = x + times3(left3(left), right3(x))
    wide = times(x, jnp.concatenate([base, d], 1))
    left = eye - wide[:, :n]
    both = jnp.concatenate([x, wide[:, n:]], 1)
    both = both + times3(left3(left), right3(both))
    return both[:, :n], both[:, n:]


def message(diag_a, diag_b, cross, core, cross_ref, mine_ref, other_ref):
    n = cross.shape[0]
    half = n // 2
    step = half + PAD
    cross_ref[:half] = cross[:half]
    cross_ref[step : step + half] = cross[half:]
    cross_ref[half:step] = jnp.broadcast_to(diag_a, (PAD, n))
    cross_ref[step + half :] = jnp.broadcast_to(diag_b, (PAD, n))
    mine_ref[...] = cross_ref[pl.ds(pl.multiple_of(core * step, 8), step), :]
    other_ref[...] = cross_ref[pl.ds(pl.multiple_of((1 - core) * step, 8), step), :]


def both_blocks(refs):
    if len(refs) == 1:
        n = refs[0].shape[1] // 2
        return refs[0][:, :n], refs[0][:, n:]
    return refs[0][...], refs[1][...]


def cross_of(a, b):
    n = a.shape[1]
    a_hi, a_lo = split(jnp.transpose(a))
    b_hi, b_lo = split(b)
    wide = jnp.dot(a_hi, jnp.concatenate([b_hi, b_lo], 1), preferred_element_type=F32)
    return wide[:, :n] + wide[:, n:] + jnp.dot(a_lo, b_hi, preferred_element_type=F32)


def squares(block):
    return jnp.sum(block * block, 0, keepdims=True)


def gram_kernel(core_ref, *refs):
    *blocks, mine_ref, other_ref, cross_ref = refs
    a, b = both_blocks(blocks)
    message(squares(a), squares(b), cross_of(a, b), core_ref[0], cross_ref, mine_ref, other_ref)


def cosines_of(core_ref, mine_ref, other_ref):
    half = mine_ref.shape[0] - PAD
    first = core_ref[0] == 0
    mine = mine_ref[...]
    other = other_ref[...]
    low = jnp.where(first, mine, other)
    high = jnp.where(first, other, mine)
    cross = jnp.concatenate([low[:half], high[:half]], 0)
    return quarter_cosines(cross, low[half : half + 1], high[half : half + 1])


def first_block(a, b, m, md):
    n = m.shape[0]
    x_hi, x_lo = split(jnp.concatenate([a, b], 1))
    c_hi, c_lo = split(jnp.concatenate([m, -jnp.transpose(md)], 0))
    wide = jnp.dot(x_hi, jnp.concatenate([c_hi, c_lo], 1), preferred_element_type=F32)
    low = jnp.dot(x_lo, c_hi, preferred_element_type=F32)
    return 2.0 * (wide[:, :n] + wide[:, n:] + low) - a


def first_kernel(core_ref, mine_ref, other_ref, *refs):
    *blocks, a_out = refs
    d = cosines_of(core_ref, mine_ref, other_ref)
    a, b = both_blocks(blocks)
    a_out[...] = first_block(a, b, *damped_inverse(d, jnp.transpose(d)))


def late_kernel(m_ref, md_ref, *refs):
    *blocks, a_out = refs
    a, b = both_blocks(blocks)
    a_out[...] = first_block(a, b, m_ref[...], md_ref[...])


def second_kernel(core_ref, mine_ref, other_ref, own_ref, *refs):
    *blocks, b_out, m_out, md_out, mine_out, other_out, cross_ref = refs
    d = cosines_of(core_ref, mine_ref, other_ref)
    dt = jnp.transpose(d)
    a, b = both_blocks(blocks)
    turned = left3(a - times3(left3(b), right3(dt)))
    own = own_ref[...]
    m, md = damped_inverse(d, dt)
    b = b + 2.0 * times3(turned, right3(md))
    message(
        squares(own), squares(b), cross_of(own, b), core_ref[0], cross_ref, mine_out, other_out
    )
    b_out[...] = b
    m_out[...] = m
    md_out[...] = md


def last_kernel(core_ref, mine_ref, other_ref, own_ref, *refs):
    *blocks, out_ref, b_ref, sems = refs
    rows, n = own_ref.shape
    copies = [pltpu.make_async_copy(own_ref, out_ref.at[:, :n], sems.at[CHUNKS])]
    copies[0].start()
    d = cosines_of(core_ref, mine_ref, other_ref)
    dt = jnp.transpose(d)
    a, b = both_blocks(blocks)
    turned = left3(a - times3(left3(b), right3(dt)))
    _, md = damped_inverse(d, dt)
    right = right3(md)
    size = rows // CHUNKS
    for i in range(CHUNKS):
        part = slice(i * size, (i + 1) * size)
        b_ref[part] = b[part] + 2.0 * times3(turned[part], right)
        copy = pltpu.make_async_copy(b_ref.at[part], out_ref.at[part, n:], sems.at[i])
        copy.start()
        copies.append(copy)
    for copy in copies:
        copy.wait()


def near(x):
    return pltpu.with_memory_space_constraint(x, pltpu.VMEM)


def vmem_call(kernel, shapes, arrays, core=None, scratch=(), **options):
    specs = [pl.BlockSpec(memory_space=pltpu.VMEM)] * len(arrays)
    arrays = [near(x) for x in arrays]
    if core is not None:
        specs = [pl.BlockSpec(memory_space=pltpu.SMEM)] + specs
        arrays = [core] + arrays
    return pl.pallas_call(
        kernel, out_shape=shapes, in_specs=specs, scratch_shapes=scratch, **options
    )(*arrays)


def message_shapes(n):
    half = pltpu.VMEM((n // 2 + PAD, n), F32)
    return [half, half], [pltpu.VMEM((n + 2 * PAD, n), F32)]


def gram(core, blocks, n):
    halves, scratch = message_shapes(n)
    return vmem_call(gram_kernel, halves, blocks, core, scratch)


def turn_first(core, halves, blocks, n):
    block = pltpu.VMEM((blocks[0].shape[0], n), F32)
    return vmem_call(first_kernel, block, [*halves, *blocks], core)


def turn_late(m, md, blocks, n):
    block = pltpu.VMEM((blocks[0].shape[0], n), F32)
    return vmem_call(late_kernel, block, [m, md, *blocks])


def turn_second(core, halves, own, blocks, n):
    message_out, scratch = message_shapes(n)
    square = pltpu.VMEM((n, n), F32)
    shapes = [pltpu.VMEM(own.shape, F32), square, square, *message_out]
    arrays = [*halves, own, *blocks]
    return vmem_call(second_kernel, shapes, arrays, core, scratch)


def turn_last(core, halves, own, blocks):
    rows, n = own.shape
    return vmem_call(
        last_kernel,
        jax.ShapeDtypeStruct((rows, 2 * n), F32),
        [*halves, own, *blocks],
        core,
        [pltpu.VMEM((rows, n), F32), pltpu.SemaphoreType.DMA((CHUNKS + 1,))],
        out_specs=pl.BlockSpec(memory_space=pl.ANY),
    )


def from_row(x, source):
    devices = range(lax.axis_size("row"))
    line = len(devices) // QUAD
    route = []
    for i in devices:
        z, y_lo, core = source(i // QUAD, i // 2 % 2, i % 2)
        route.append((z % line * QUAD + y_lo * 2 + core, i))
    return lax.ppermute(x, "row", route)


def side(z):
    return 1 if z % 2 else -1


def summed_halves(mine, other, y_last):
    mate = from_row(other, lambda z, y, c: (z, y, 1 - c))
    x = mine + mate
    next_z = from_row(x, lambda z, y, c: (z ^ 1, y, c))
    if y_last:
        x = x + next_z
    else:
        next_y = from_row(x, lambda z, y, c: (z, 1 - y, c))
        next_zy = from_row(x, lambda z, y, c: (z ^ 1, 1 - y, c))
        x = ((x + next_z) + next_y) + next_zy
    by_one = from_row(x, lambda z, y, c: (z + side(z), y, c))
    by_two = from_row(x, lambda z, y, c: (z - 2 * side(z), y, c))
    by_three = from_row(x, lambda z, y, c: (z + 3 * side(z), y, c))
    x = ((x + by_one) + by_two) + by_three
    if y_last:
        x = x + from_row(x, lambda z, y, c: (z, 1 - y, c))
    return x


def with_other(half):
    return [half, from_row(half, lambda z, y, c: (z, y, 1 - c))]


def shifted(block):
    devices = range(lax.axis_size("pair"))
    route = [((i - 1) % len(devices), i) for i in devices]
    return lax.ppermute(block, "pair", route)


def local(panel):
    n = panel.shape[1] // 2
    core = (lax.axis_index("row") & 1).astype(jnp.int32).reshape(1)
    own = [panel]
    for step in range(STEPS):
        if step == 0:
            before = [shifted(panel)]
            mine, other = gram(core, own, n)
        else:
            second = shifted(b)
            before = [turn_late(m, md, before, n), second]
        half = summed_halves(mine, other, y_last=step == 0)
        hopped = shifted(half)
        own_halves = with_other(half)
        a = turn_first(core, own_halves, own, n)
        halves = with_other(hopped)
        if step + 1 == STEPS:
            return turn_last(core, halves, a, before)
        b, m, md, mine, other = turn_second(core, halves, a, before, n)
        own = [a, b]


def solution(mesh):
    return jax.shard_map(
        local,
        mesh=mesh,
        in_specs=(P("row", "pair"),),
        out_specs=P("row", "pair"),
        check_vma=False,
    )
```

time: 105 us -> 104 us (level)
  transfers between devices with their start and end apart: 32 -> 32, of which waited for: 20 -> 20; matrix products, arithmetic and copies ran while one was open for 0% -> 0% of each run, Pallas kernels for 8% -> 9%
where the time goes in v3:
time: 104 us
  starting transfers between devices  56.2 us (54%)
  waiting for transfers between devices  28.4 us (27%)
  Pallas kernels  18 us (17%)
  local copies, waits for them, and re-layouts  1.08 us (1%)
    ppermute x26, starting transfers between devices, from_row(): return lax.ppermute(x, 'row', route)  50.8 us
    ppermute x26, waiting for transfers between devices, from_row(): return lax.ppermute(x, 'row', route)  18.8 us
    pallas_call x9, Pallas kernels, vmem_call(): pl.pallas_call(kernel, out_shape=shapes, in_specs=specs, scratch_shapes=s...  18 us
    ppermute x6, waiting for transfers between devices, shifted(): return lax.ppermute(block, 'pair', route)  9.58 us
    ppermute x6, starting transfers between devices, shifted(): return lax.ppermute(block, 'pair', route)  5.38 us
  transfers between devices with their start and end apart: 32, of which 20 were waited for; matrix products, arithmetic and copies ran while one was open for 0% of the time, Pallas kernels for 9%

profile of v3, /device:TPU:1, one launch (start us, length us, event | category | flops | bytes accessed | tf_op | source)
XLA Modules:
  0.0 104.1 jit_solution(6623965785122034644)
XLA Ops:
  0.0 3.7 %collective-permute-start.9 = (f32[512,256]{1,0:T(8,128)}, f32[512,256]{1,0:T(8,128)S(1)}, u32[]{:S(2)}, u32[]{:S(2)}) collective-permute-start(f32[512,256]{1,0:T(8,128)} %refs_0_.3), channel_id=1, source_target_pairs={{7,0},{0,1},{1,2},{2,3},{3,4},{4,5},{5,6},{6,7},{15,8},{8,9},{9,10... | collective-permute-start | bytes 1572872 | tf_op jit(solution)/shard_map/ppermute | solution.py:291
  7.0 1.6 %collective-permute-start.1 = (f32[72,128]{1,0:T(8,128)S(1)}, f32[72,128]{1,0:T(8,128)S(1)}, u32[]{:S(2)}, u32[]{:S(2)}) collective-permute-start(f32[72,128]{1,0:T(8,128)S(1)} %add.60), channel_id=1, source_target_pairs={{32,0},{40,8},{48,16},{56,24},{0,32},{8,40},{16,48},{24,56},{96,64... | collective-permute-start | bytes 110600 | tf_op jit(solution)/shard_map/ppermute | solution.py:258
  8.7 1.6 %collective-permute-done.1 = f32[72,128]{1,0:T(8,128)S(1)} collective-permute-done((f32[72,128]{1,0:T(8,128)S(1)}, f32[72,128]{1,0:T(8,128)S(1)}, u32[]{:S(2)}, u32[]{:S(2)}) %collective-permute-start.1) | collective-permute-done | bytes 36896 | tf_op jit(solution)/shard_map/ppermute | solution.py:258
  10.3 6.3 %collective-permute-start.4 = (f32[72,128]{1,0:T(8,128)S(1)}, f32[72,128]{1,0:T(8,128)S(1)}, u32[]{:S(2)}, u32[]{:S(2)}) collective-permute-start(f32[72,128]{1,0:T(8,128)S(1)} %add.61), channel_id=1, source_target_pairs={{160,0},{168,8},{176,16},{184,24},{128,32},{136,40},{144,48},{152,... | collective-permute-start | bytes 110600 | tf_op jit(solution)/shard_map/ppermute | solution.py:258
  16.9 2.8 %collective-permute-start.2 = (f32[72,128]{1,0:T(8,128)S(1)}, f32[72,128]{1,0:T(8,128)S(1)}, u32[]{:S(2)}, u32[]{:S(2)}) collective-permute-start(f32[72,128]{1,0:T(8,128)S(1)} %add.61), channel_id=1, source_target_pairs={{224,0},{232,8},{240,16},{248,24},{64,32},{72,40},{80,48},{88,56},... | collective-permute-start | bytes 110600 | tf_op jit(solution)/shard_map/ppermute | solution.py:258
  22.0 2.4 %collective-permute-done.5 = f32[72,128]{1,0:T(8,128)S(1)} collective-permute-done((f32[72,128]{1,0:T(8,128)S(1)}, f32[72,128]{1,0:T(8,128)S(1)}, u32[]{:S(2)}, u32[]{:S(2)}) %collective-permute-start.5) | collective-permute-done | bytes 36896 | tf_op jit(solution)/shard_map/ppermute | solution.py:258
  24.4 1.4 %collective-permute-start.6 = (f32[72,128]{1,0:T(8,128)S(1)}, f32[72,128]{1,0:T(8,128)S(1)}, u32[]{:S(2)}, u32[]{:S(2)}) collective-permute-start(f32[72,128]{1,0:T(8,128)S(1)} %add.65.mine_ref), channel_id=1, source_target_pairs={{7,0},{0,1},{1,2},{2,3},{3,4},{4,5},{5,6},{6,7},{15,8},{8,9},{9,10... | collective-permute-start | bytes 110600 | tf_op jit(solution)/shard_map/ppermute | solution.py:291
  25.8 3.8 %collective-permute-start.8 = (f32[72,128]{1,0:T(8,128)S(1)}, f32[72,128]{1,0:T(8,128)S(1)}, u32[]{:S(2)}, u32[]{:S(2)}) collective-permute-start(f32[72,128]{1,0:T(8,128)S(1)} %add.65.mine_ref), channel_id=1, source_target_pairs={{8,0},{0,8},{24,16},{16,24},{40,32},{32,40},{56,48},{48,56},{72,64... | collective-permute-start | bytes 110600 | tf_op jit(solution)/shard_map/ppermute | solution.py:258
  29.6 1.2 %collective-permute-done.6.mine_ref = f32[72,128]{1,0:T(8,128)S(1)} collective-permute-done((f32[72,128]{1,0:T(8,128)S(1)}, f32[72,128]{1,0:T(8,128)S(1)}, u32[]{:S(2)}, u32[]{:S(2)}) %collective-permute-start.6) | collective-permute-done | bytes 36896 | tf_op jit(solution)/shard_map/ppermute | solution.py:291
  30.8 4.9 %collective-permute-start.7 = (f32[72,128]{1,0:T(8,128)S(1)}, f32[72,128]{1,0:T(8,128)S(1)}, u32[]{:S(2)}, u32[]{:S(2)}) collective-permute-start(f32[72,128]{1,0:T(8,128)S(1)} %collective-permute-done.6.mine_ref), channel_id=1, source_target_pairs={{8,0},{0,8},{24,16},{16,24},{40,32},{32,40},{56,48},{48,56},{72,64... | collective-permute-start | bytes 110600 | tf_op jit(solution)/shard_map/ppermute | solution.py:258
  35.7 2.7 %shard_map.18.own_ref.refs_0_ = f32[512,128]{1,0:T(8,128)S(1)} custom-call(s32[1]{0:T(128)} %bitcast.core_ref, f32[72,128]{1,0:T(8,128)S(1)} %add.65.mine_ref, f32[72,128]{1,0:T(8,128)S(1)} %collective-permute-done.8.other_ref, f32[512,256]{1,0:T(8,128)S(1)} %copy-done.1), custom_call_target="tpu_custom_call" | custom-call | tf_op jit(solution)/shard_map/pallas_call | solution.py:206
  38.4 2.8 %shard_map.19 = (f32[512,128]{1,0:T(8,128)S(1)}, f32[128,128]{1,0:T(8,128)S(1)}, f32[128,128]{1,0:T(8,128)S(1)}, f32[72,128]{1,0:T(8,128)S(1)}, f32[72,128]{1,0:T(8,128)S(1)}) custom-call(s32[1]{0:T(128)} %bitcast.core_ref, f32[72,128]{1,0:T(8,128)S(1)} %collective-permute-done.6.mine_ref, f32[72,128]{1,0:T(8,128)S(1)} %collective-permute-done.7.other_ref, ...), custom_call_target="tpu_custom_call" | custom-call | tf_op jit(solution)/shard_map/pallas_call | solution.py:206
  41.3 1.2 %collective-permute-done.10 = f32[72,128]{1,0:T(8,128)S(1)} collective-permute-done((f32[72,128]{1,0:T(8,128)S(1)}, f32[72,128]{1,0:T(8,128)S(1)}, u32[]{:S(2)}, u32[]{:S(2)}) %collective-permute-start.10) | collective-permute-done | bytes 36896 | tf_op jit(solution)/shard_map/ppermute | solution.py:258
  46.3 1.2 %collective-permute-done.12 = f32[72,128]{1,0:T(8,128)S(1)} collective-permute-done((f32[72,128]{1,0:T(8,128)S(1)}, f32[72,128]{1,0:T(8,128)S(1)}, u32[]{:S(2)}, u32[]{:S(2)}) %collective-permute-start.12) | collective-permute-done | bytes 36896 | tf_op jit(solution)/shard_map/ppermute | solution.py:258
  47.6 3.3 %collective-permute-start.16 = (f32[72,128]{1,0:T(8,128)S(1)}, f32[72,128]{1,0:T(8,128)S(1)}, u32[]{:S(2)}, u32[]{:S(2)}) collective-permute-start(f32[72,128]{1,0:T(8,128)S(1)} %add_add_fusion.3), channel_id=1, source_target_pairs={{160,0},{168,8},{176,16},{184,24},{128,32},{136,40},{144,48},{152,... | collective-permute-start | bytes 110600 | tf_op jit(solution)/shard_map/ppermute | solution.py:258
  51.8 1.9 %collective-permute-start.14 = (f32[72,128]{1,0:T(8,128)S(1)}, f32[72,128]{1,0:T(8,128)S(1)}, u32[]{:S(2)}, u32[]{:S(2)}) collective-permute-start(f32[72,128]{1,0:T(8,128)S(1)} %add_add_fusion.3), channel_id=1, source_target_pairs={{224,0},{232,8},{240,16},{248,24},{64,32},{72,40},{80,48},{88,56},... | collective-permute-start | bytes 110600 | tf_op jit(solution)/shard_map/ppermute | solution.py:258
  53.7 1.3 %collective-permute-done.15 = f32[72,128]{1,0:T(8,128)S(1)} collective-permute-done((f32[72,128]{1,0:T(8,128)S(1)}, f32[72,128]{1,0:T(8,128)S(1)}, u32[]{:S(2)}, u32[]{:S(2)}) %collective-permute-start.15) | collective-permute-done | bytes 36896 | tf_op jit(solution)/shard_map/ppermute | solution.py:258
  55.0 1.4 %collective-permute-done.14 = f32[72,128]{1,0:T(8,128)S(1)} collective-permute-done((f32[72,128]{1,0:T(8,128)S(1)}, f32[72,128]{1,0:T(8,128)S(1)}, u32[]{:S(2)}, u32[]{:S(2)}) %collective-permute-start.14) | collective-permute-done | bytes 36896 | tf_op jit(solution)/shard_map/ppermute | solution.py:258
  56.5 2.8 %collective-permute-start.19 = (f32[72,128]{1,0:T(8,128)S(1)}, f32[72,128]{1,0:T(8,128)S(1)}, u32[]{:S(2)}, u32[]{:S(2)}) collective-permute-start(f32[72,128]{1,0:T(8,128)S(1)} %add_add_fusion.2.mine_ref), channel_id=1, source_target_pairs={{8,0},{0,8},{24,16},{16,24},{40,32},{32,40},{56,48},{48,56},{72,64... | collective-permute-start | bytes 110600 | tf_op jit(solution)/shard_map/ppermute | solution.py:258
  59.3 4.5 %collective-permute-done.17.mine_ref = f32[72,128]{1,0:T(8,128)S(1)} collective-permute-done((f32[72,128]{1,0:T(8,128)S(1)}, f32[72,128]{1,0:T(8,128)S(1)}, u32[]{:S(2)}, u32[]{:S(2)}) %collective-permute-start.17) | collective-permute-done | bytes 36896 | tf_op jit(solution)/shard_map/ppermute | solution.py:291
  63.8 3.0 %collective-permute-start.18 = (f32[72,128]{1,0:T(8,128)S(1)}, f32[72,128]{1,0:T(8,128)S(1)}, u32[]{:S(2)}, u32[]{:S(2)}) collective-permute-start(f32[72,128]{1,0:T(8,128)S(1)} %collective-permute-done.17.mine_ref), channel_id=1, source_target_pairs={{8,0},{0,8},{24,16},{16,24},{40,32},{32,40},{56,48},{48,56},{72,64... | collective-permute-start | bytes 110600 | tf_op jit(solution)/shard_map/ppermute | solution.py:258
  67.2 2.7 %shard_map.20.own_ref.refs_0_ = f32[512,128]{1,0:T(8,128)S(1)} custom-call(s32[1]{0:T(128)} %bitcast.core_ref, f32[72,128]{1,0:T(8,128)S(1)} %add_add_fusion.2.mine_ref, f32[72,128]{1,0:T(8,128)S(1)} %collective-permute-done.19.other_ref, f32[512,128]{1,0:T(8,128)S(1)} %shard_map.18.own_ref.refs_0_, f32[512,128]{1,0:T(8,128)S(1)} %get-tuple-element.21.refs_1_), custom_call_target="tpu_custom_call" | custom-call | tf_op jit(solution)/shard_map/pallas_call | solution.py:206
  69.9 2.8 %shard_map.22 = (f32[512,128]{1,0:T(8,128)S(1)}, f32[128,128]{1,0:T(8,128)S(1)}, f32[128,128]{1,0:T(8,128)S(1)}, f32[72,128]{1,0:T(8,128)S(1)}, f32[72,128]{1,0:T(8,128)S(1)}) custom-call(s32[1]{0:T(128)} %bitcast.core_ref, f32[72,128]{1,0:T(8,128)S(1)} %collective-permute-done.17.mine_ref, f32[72,128]{1,0:T(8,128)S(1)} %collective-permute-done.18.other_ref, ...), custom_call_target="tpu_custom_call" | custom-call | tf_op jit(solution)/shard_map/pallas_call | solution.py:206
  75.3 1.3 %collective-permute-start.22 = (f32[72,128]{1,0:T(8,128)S(1)}, f32[72,128]{1,0:T(8,128)S(1)}, u32[]{:S(2)}, u32[]{:S(2)}) collective-permute-start(f32[72,128]{1,0:T(8,128)S(1)} %add.73), channel_id=1, source_target_pairs={{32,0},{40,8},{48,16},{56,24},{0,32},{8,40},{16,48},{24,56},{96,64... | collective-permute-start | bytes 110600 | tf_op jit(solution)/shard_map/ppermute | solution.py:258
  78.5 2.9 %collective-permute-start.27 = (f32[72,128]{1,0:T(8,128)S(1)}, f32[72,128]{1,0:T(8,128)S(1)}, u32[]{:S(2)}, u32[]{:S(2)}) collective-permute-start(f32[72,128]{1,0:T(8,128)S(1)} %add_add_fusion.1), channel_id=1, source_target_pairs={{160,0},{168,8},{176,16},{184,24},{128,32},{136,40},{144,48},{152,... | collective-permute-start | bytes 110600 | tf_op jit(solution)/shard_map/ppermute | solution.py:258
  82.6 1.4 %collective-permute-start.25 = (f32[72,128]{1,0:T(8,128)S(1)}, f32[72,128]{1,0:T(8,128)S(1)}, u32[]{:S(2)}, u32[]{:S(2)}) collective-permute-start(f32[72,128]{1,0:T(8,128)S(1)} %add_add_fusion.1), channel_id=1, source_target_pairs={{224,0},{232,8},{240,16},{248,24},{64,32},{72,40},{80,48},{88,56},... | collective-permute-start | bytes 110600 | tf_op jit(solution)/shard_map/ppermute | solution.py:258
  84.4 1.4 %collective-permute-done.26 = f32[72,128]{1,0:T(8,128)S(1)} collective-permute-done((f32[72,128]{1,0:T(8,128)S(1)}, f32[72,128]{1,0:T(8,128)S(1)}, u32[]{:S(2)}, u32[]{:S(2)}) %collective-permute-start.26) | collective-permute-done | bytes 36896 | tf_op jit(solution)/shard_map/ppermute | solution.py:258
  87.0 3.3 %collective-permute-start.30 = (f32[72,128]{1,0:T(8,128)S(1)}, f32[72,128]{1,0:T(8,128)S(1)}, u32[]{:S(2)}, u32[]{:S(2)}) collective-permute-start(f32[72,128]{1,0:T(8,128)S(1)} %add_add_fusion.mine_ref), channel_id=1, source_target_pairs={{8,0},{0,8},{24,16},{16,24},{40,32},{32,40},{56,48},{48,56},{72,64... | collective-permute-start | bytes 110600 | tf_op jit(solution)/shard_map/ppermute | solution.py:258
  90.3 3.8 %collective-permute-done.28.mine_ref = f32[72,128]{1,0:T(8,128)S(1)} collective-permute-done((f32[72,128]{1,0:T(8,128)S(1)}, f32[72,128]{1,0:T(8,128)S(1)}, u32[]{:S(2)}, u32[]{:S(2)}) %collective-permute-start.28) | collective-permute-done | bytes 36896 | tf_op jit(solution)/shard_map/ppermute | solution.py:291
  94.1 3.4 %collective-permute-start.29 = (f32[72,128]{1,0:T(8,128)S(1)}, f32[72,128]{1,0:T(8,128)S(1)}, u32[]{:S(2)}, u32[]{:S(2)}) collective-permute-start(f32[72,128]{1,0:T(8,128)S(1)} %collective-permute-done.28.mine_ref), channel_id=1, source_target_pairs={{8,0},{0,8},{24,16},{16,24},{40,32},{32,40},{56,48},{48,56},{72,64... | collective-permute-start | bytes 110600 | tf_op jit(solution)/shard_map/ppermute | solution.py:258
  97.9 2.7 %shard_map.23.own_ref = f32[512,128]{1,0:T(8,128)S(1)} custom-call(s32[1]{0:T(128)} %bitcast.core_ref, f32[72,128]{1,0:T(8,128)S(1)} %add_add_fusion.mine_ref, f32[72,128]{1,0:T(8,128)S(1)} %collective-permute-done.30.other_ref, f32[512,128]{1,0:T(8,128)S(1)} %shard_map.20.own_ref.refs_0_, f32[512,128]{1,0:T(8,128)S(1)} %get-tuple-element.26.refs_1_), custom_call_target="tpu_custom_call" | custom-call | tf_op jit(solution)/shard_map/pallas_call | solution.py:206
  100.7 3.3 %shard_map.25 = f32[512,256]{1,0:T(8,128)} custom-call(s32[1]{0:T(128)} %bitcast.core_ref, f32[72,128]{1,0:T(8,128)S(1)} %collective-permute-done.28.mine_ref, f32[72,128]{1,0:T(8,128)S(1)} %collective-permute-done.29.other_ref, f32[512,128]{1,0:T(8,128)S(1)} %shard_map.23.own_ref, f32[512,128]{1,0:T(8,128)S(1)} %shard_map.24.refs_0_, ...), custom_call_target="tpu_custom_call" | custom-call | tf_op jit(solution)/shard_map/pallas_call | solution.py:206
  (55 shorter events, 18.7 us)
Async XLA Ops:
  0.0 38.4 %collective-permute-start.9 = (f32[512,256]{1,0:T(8,128)}, f32[512,256]{1,0:T(8,128)S(1)}, u32[]{:S(2)}, u32[]{:S(2)}) collective-permute-start(f32[512,256]{1,0:T(8,128)} %refs_0_.3), channel_id=1, source_target_pairs={{7,0},{0,1},{1,2},{2,3},{3,4},{4,5},{5,6},{6,7},{15,8},{8,9},{9,10... | collective-permute-start | bytes 1572872 | tf_op jit(solution)/shard_map/ppermute | solution.py:291
  5.1 1.9 %collective-permute-start = (f32[72,128]{1,0:T(8,128)S(1)}, f32[72,128]{1,0:T(8,128)S(1)}, u32[]{:S(2)}, u32[]{:S(2)}) collective-permute-start(f32[72,128]{1,0:T(8,128)S(1)} %get-tuple-element.18), channel_id=1, source_target_pairs={{8,0},{0,8},{24,16},{16,24},{40,32},{32,40},{56,48},{48,56},{72,64... | collective-permute-start | bytes 110600 | tf_op jit(solution)/shard_map/ppermute | solution.py:258
  7.0 3.3 %collective-permute-start.1 = (f32[72,128]{1,0:T(8,128)S(1)}, f32[72,128]{1,0:T(8,128)S(1)}, u32[]{:S(2)}, u32[]{:S(2)}) collective-permute-start(f32[72,128]{1,0:T(8,128)S(1)} %add.60), channel_id=1, source_target_pairs={{32,0},{40,8},{48,16},{56,24},{0,32},{8,40},{16,48},{24,56},{96,64... | collective-permute-start | bytes 110600 | tf_op jit(solution)/shard_map/ppermute | solution.py:258
  10.3 9.4 %collective-permute-start.4 = (f32[72,128]{1,0:T(8,128)S(1)}, f32[72,128]{1,0:T(8,128)S(1)}, u32[]{:S(2)}, u32[]{:S(2)}) collective-permute-start(f32[72,128]{1,0:T(8,128)S(1)} %add.61), channel_id=1, source_target_pairs={{160,0},{168,8},{176,16},{184,24},{128,32},{136,40},{144,48},{152,... | collective-permute-start | bytes 110600 | tf_op jit(solution)/shard_map/ppermute | solution.py:258
  16.6 3.8 %collective-permute-start.3 = (f32[72,128]{1,0:T(8,128)S(1)}, f32[72,128]{1,0:T(8,128)S(1)}, u32[]{:S(2)}, u32[]{:S(2)}) collective-permute-start(f32[72,128]{1,0:T(8,128)S(1)} %add.61), channel_id=1, source_target_pairs={{64,0},{72,8},{80,16},{88,24},{224,32},{232,40},{240,48},{248,56},... | collective-permute-start | bytes 110600 | tf_op jit(solution)/shard_map/ppermute | solution.py:258
  16.9 4.6 %collective-permute-start.2 = (f32[72,128]{1,0:T(8,128)S(1)}, f32[72,128]{1,0:T(8,128)S(1)}, u32[]{:S(2)}, u32[]{:S(2)}) collective-permute-start(f32[72,128]{1,0:T(8,128)S(1)} %add.61), channel_id=1, source_target_pairs={{224,0},{232,8},{240,16},{248,24},{64,32},{72,40},{80,48},{88,56},... | collective-permute-start | bytes 110600 | tf_op jit(solution)/shard_map/ppermute | solution.py:258
  21.5 2.9 %collective-permute-start.5 = (f32[72,128]{1,0:T(8,128)S(1)}, f32[72,128]{1,0:T(8,128)S(1)}, u32[]{:S(2)}, u32[]{:S(2)}) collective-permute-start(f32[72,128]{1,0:T(8,128)S(1)} %add_add_fusion.4), channel_id=1, source_target_pairs={{16,0},{24,8},{0,16},{8,24},{48,32},{56,40},{32,48},{40,56},{80,64... | collective-permute-start | bytes 110600 | tf_op jit(solution)/shard_map/ppermute | solution.py:258
  24.4 6.4 %collective-permute-start.6 = (f32[72,128]{1,0:T(8,128)S(1)}, f32[72,128]{1,0:T(8,128)S(1)}, u32[]{:S(2)}, u32[]{:S(2)}) collective-permute-start(f32[72,128]{1,0:T(8,128)S(1)} %add.65.mine_ref), channel_id=1, source_target_pairs={{7,0},{0,1},{1,2},{2,3},{3,4},{4,5},{5,6},{6,7},{15,8},{8,9},{9,10... | collective-permute-start | bytes 110600 | tf_op jit(solution)/shard_map/ppermute | solution.py:291
  25.8 9.9 %collective-permute-start.8 = (f32[72,128]{1,0:T(8,128)S(1)}, f32[72,128]{1,0:T(8,128)S(1)}, u32[]{:S(2)}, u32[]{:S(2)}) collective-permute-start(f32[72,128]{1,0:T(8,128)S(1)} %add.65.mine_ref), channel_id=1, source_target_pairs={{8,0},{0,8},{24,16},{16,24},{40,32},{32,40},{56,48},{48,56},{72,64... | collective-permute-start | bytes 110600 | tf_op jit(solution)/shard_map/ppermute | solution.py:258
  30.8 7.6 %collective-permute-start.7 = (f32[72,128]{1,0:T(8,128)S(1)}, f32[72,128]{1,0:T(8,128)S(1)}, u32[]{:S(2)}, u32[]{:S(2)}) collective-permute-start(f32[72,128]{1,0:T(8,128)S(1)} %collective-permute-done.6.mine_ref), channel_id=1, source_target_pairs={{8,0},{0,8},{24,16},{16,24},{40,32},{32,40},{56,48},{48,56},{72,64... | collective-permute-start | bytes 110600 | tf_op jit(solution)/shard_map/ppermute | solution.py:258
  41.2 1.3 %collective-permute-start.10 = (f32[72,128]{1,0:T(8,128)S(1)}, f32[72,128]{1,0:T(8,128)S(1)}, u32[]{:S(2)}, u32[]{:S(2)}) collective-permute-start(f32[72,128]{1,0:T(8,128)S(1)} %get-tuple-element.20), channel_id=1, source_target_pairs={{8,0},{0,8},{24,16},{16,24},{40,32},{32,40},{56,48},{48,56},{72,64... | collective-permute-start | bytes 110600 | tf_op jit(solution)/shard_map/ppermute | solution.py:258
  42.5 3.7 %collective-permute-start.13 = (f32[72,128]{1,0:T(8,128)S(1)}, f32[72,128]{1,0:T(8,128)S(1)}, u32[]{:S(2)}, u32[]{:S(2)}) collective-permute-start(f32[72,128]{1,0:T(8,128)S(1)} %add.66), channel_id=1, source_target_pairs={{48,0},{56,8},{32,16},{40,24},{16,32},{24,40},{0,48},{8,56},{112,6... | collective-permute-start | bytes 110600 | tf_op jit(solution)/shard_map/ppermute | solution.py:258
  43.5 4.1 %collective-permute-start.12 = (f32[72,128]{1,0:T(8,128)S(1)}, f32[72,128]{1,0:T(8,128)S(1)}, u32[]{:S(2)}, u32[]{:S(2)}) collective-permute-start(f32[72,128]{1,0:T(8,128)S(1)} %add.66), channel_id=1, source_target_pairs={{16,0},{24,8},{0,16},{8,24},{48,32},{56,40},{32,48},{40,56},{80,64... | collective-permute-start | bytes 110600 | tf_op jit(solution)/shard_map/ppermute | solution.py:258
  44.5 3.1 %collective-permute-start.11 = (f32[72,128]{1,0:T(8,128)S(1)}, f32[72,128]{1,0:T(8,128)S(1)}, u32[]{:S(2)}, u32[]{:S(2)}) collective-permute-start(f32[72,128]{1,0:T(8,128)S(1)} %add.66), channel_id=1, source_target_pairs={{32,0},{40,8},{48,16},{56,24},{0,32},{8,40},{16,48},{24,56},{96,64... | collective-permute-start | bytes 110600 | tf_op jit(solution)/shard_map/ppermute | solution.py:258
  47.6 6.0 %collective-permute-start.16 = (f32[72,128]{1,0:T(8,128)S(1)}, f32[72,128]{1,0:T(8,128)S(1)}, u32[]{:S(2)}, u32[]{:S(2)}) collective-permute-start(f32[72,128]{1,0:T(8,128)S(1)} %add_add_fusion.3), channel_id=1, source_target_pairs={{160,0},{168,8},{176,16},{184,24},{128,32},{136,40},{144,48},{152,... | collective-permute-start | bytes 110600 | tf_op jit(solution)/shard_map/ppermute | solution.py:258
  51.0 4.0 %collective-permute-start.15 = (f32[72,128]{1,0:T(8,128)S(1)}, f32[72,128]{1,0:T(8,128)S(1)}, u32[]{:S(2)}, u32[]{:S(2)}) collective-permute-start(f32[72,128]{1,0:T(8,128)S(1)} %add_add_fusion.3), channel_id=1, source_target_pairs={{64,0},{72,8},{80,16},{88,24},{224,32},{232,40},{240,48},{248,56},... | collective-permute-start | bytes 110600 | tf_op jit(solution)/shard_map/ppermute | solution.py:258
  51.8 4.6 %collective-permute-start.14 = (f32[72,128]{1,0:T(8,128)S(1)}, f32[72,128]{1,0:T(8,128)S(1)}, u32[]{:S(2)}, u32[]{:S(2)}) collective-permute-start(f32[72,128]{1,0:T(8,128)S(1)} %add_add_fusion.3), channel_id=1, source_target_pairs={{224,0},{232,8},{240,16},{248,24},{64,32},{72,40},{80,48},{88,56},... | collective-permute-start | bytes 110600 | tf_op jit(solution)/shard_map/ppermute | solution.py:258
  53.7 16.2 %collective-permute-start.20 = (f32[512,128]{1,0:T(8,128)S(1)}, f32[512,128]{1,0:T(8,128)S(1)}, u32[]{:S(2)}, u32[]{:S(2)}) collective-permute-start(f32[512,128]{1,0:T(8,128)S(1)} %get-tuple-element.21.refs_1_), channel_id=1, source_target_pairs={{7,0},{0,1},{1,2},{2,3},{3,4},{4,5},{5,6},{6,7},{15,8},{8,9},{9,10... | collective-permute-start | bytes 786440 | tf_op jit(solution)/shard_map/ppermute | solution.py:291
  56.3 7.5 %collective-permute-start.17 = (f32[72,128]{1,0:T(8,128)S(1)}, f32[72,128]{1,0:T(8,128)S(1)}, u32[]{:S(2)}, u32[]{:S(2)}) collective-permute-start(f32[72,128]{1,0:T(8,128)S(1)} %add_add_fusion.2.mine_ref), channel_id=1, source_target_pairs={{7,0},{0,1},{1,2},{2,3},{3,4},{4,5},{5,6},{6,7},{15,8},{8,9},{9,10... | collective-permute-start | bytes 110600 | tf_op jit(solution)/shard_map/ppermute | solution.py:291
  56.5 10.7 %collective-permute-start.19 = (f32[72,128]{1,0:T(8,128)S(1)}, f32[72,128]{1,0:T(8,128)S(1)}, u32[]{:S(2)}, u32[]{:S(2)}) collective-permute-start(f32[72,128]{1,0:T(8,128)S(1)} %add_add_fusion.2.mine_ref), channel_id=1, source_target_pairs={{8,0},{0,8},{24,16},{16,24},{40,32},{32,40},{56,48},{48,56},{72,64... | collective-permute-start | bytes 110600 | tf_op jit(solution)/shard_map/ppermute | solution.py:258
  63.8 6.1 %collective-permute-start.18 = (f32[72,128]{1,0:T(8,128)S(1)}, f32[72,128]{1,0:T(8,128)S(1)}, u32[]{:S(2)}, u32[]{:S(2)}) collective-permute-start(f32[72,128]{1,0:T(8,128)S(1)} %collective-permute-done.17.mine_ref), channel_id=1, source_target_pairs={{8,0},{0,8},{24,16},{16,24},{40,32},{32,40},{56,48},{48,56},{72,64... | collective-permute-start | bytes 110600 | tf_op jit(solution)/shard_map/ppermute | solution.py:258
  72.7 1.3 %collective-permute-start.21 = (f32[72,128]{1,0:T(8,128)S(1)}, f32[72,128]{1,0:T(8,128)S(1)}, u32[]{:S(2)}, u32[]{:S(2)}) collective-permute-start(f32[72,128]{1,0:T(8,128)S(1)} %get-tuple-element.25), channel_id=1, source_target_pairs={{8,0},{0,8},{24,16},{16,24},{40,32},{32,40},{56,48},{48,56},{72,64... | collective-permute-start | bytes 110600 | tf_op jit(solution)/shard_map/ppermute | solution.py:258
  74.0 3.7 %collective-permute-start.24 = (f32[72,128]{1,0:T(8,128)S(1)}, f32[72,128]{1,0:T(8,128)S(1)}, u32[]{:S(2)}, u32[]{:S(2)}) collective-permute-start(f32[72,128]{1,0:T(8,128)S(1)} %add.73), channel_id=1, source_target_pairs={{48,0},{56,8},{32,16},{40,24},{16,32},{24,40},{0,48},{8,56},{112,6... | collective-permute-start | bytes 110600 | tf_op jit(solution)/shard_map/ppermute | solution.py:258
  74.3 3.5 %collective-permute-start.23 = (f32[72,128]{1,0:T(8,128)S(1)}, f32[72,128]{1,0:T(8,128)S(1)}, u32[]{:S(2)}, u32[]{:S(2)}) collective-permute-start(f32[72,128]{1,0:T(8,128)S(1)} %add.73), channel_id=1, source_target_pairs={{16,0},{24,8},{0,16},{8,24},{48,32},{56,40},{32,48},{40,56},{80,64... | collective-permute-start | bytes 110600 | tf_op jit(solution)/shard_map/ppermute | solution.py:258
  75.3 3.1 %collective-permute-start.22 = (f32[72,128]{1,0:T(8,128)S(1)}, f32[72,128]{1,0:T(8,128)S(1)}, u32[]{:S(2)}, u32[]{:S(2)}) collective-permute-start(f32[72,128]{1,0:T(8,128)S(1)} %add.73), channel_id=1, source_target_pairs={{32,0},{40,8},{48,16},{56,24},{0,32},{8,40},{16,48},{24,56},{96,64... | collective-permute-start | bytes 110600 | tf_op jit(solution)/shard_map/ppermute | solution.py:258
  78.5 6.0 %collective-permute-start.27 = (f32[72,128]{1,0:T(8,128)S(1)}, f32[72,128]{1,0:T(8,128)S(1)}, u32[]{:S(2)}, u32[]{:S(2)}) collective-permute-start(f32[72,128]{1,0:T(8,128)S(1)} %add_add_fusion.1), channel_id=1, source_target_pairs={{160,0},{168,8},{176,16},{184,24},{128,32},{136,40},{144,48},{152,... | collective-permute-start | bytes 110600 | tf_op jit(solution)/shard_map/ppermute | solution.py:258
  81.4 4.4 %collective-permute-start.26 = (f32[72,128]{1,0:T(8,128)S(1)}, f32[72,128]{1,0:T(8,128)S(1)}, u32[]{:S(2)}, u32[]{:S(2)}) collective-permute-start(f32[72,128]{1,0:T(8,128)S(1)} %add_add_fusion.1), channel_id=1, source_target_pairs={{64,0},{72,8},{80,16},{88,24},{224,32},{232,40},{240,48},{248,56},... | collective-permute-start | bytes 110600 | tf_op jit(solution)/shard_map/ppermute | solution.py:258
  82.6 4.3 %collective-permute-start.25 = (f32[72,128]{1,0:T(8,128)S(1)}, f32[72,128]{1,0:T(8,128)S(1)}, u32[]{:S(2)}, u32[]{:S(2)}) collective-permute-start(f32[72,128]{1,0:T(8,128)S(1)} %add_add_fusion.1), channel_id=1, source_target_pairs={{224,0},{232,8},{240,16},{248,24},{64,32},{72,40},{80,48},{88,56},... | collective-permute-start | bytes 110600 | tf_op jit(solution)/shard_map/ppermute | solution.py:258
  84.0 16.7 %collective-permute-start.31 = (f32[512,128]{1,0:T(8,128)S(1)}, f32[512,128]{1,0:T(8,128)S(1)}, u32[]{:S(2)}, u32[]{:S(2)}) collective-permute-start(f32[512,128]{1,0:T(8,128)S(1)} %get-tuple-element.26.refs_1_), channel_id=1, source_target_pairs={{7,0},{0,1},{1,2},{2,3},{3,4},{4,5},{5,6},{6,7},{15,8},{8,9},{9,10... | collective-permute-start | bytes 786440 | tf_op jit(solution)/shard_map/ppermute | solution.py:291
  86.9 7.2 %collective-permute-start.28 = (f32[72,128]{1,0:T(8,128)S(1)}, f32[72,128]{1,0:T(8,128)S(1)}, u32[]{:S(2)}, u32[]{:S(2)}) collective-permute-start(f32[72,128]{1,0:T(8,128)S(1)} %add_add_fusion.mine_ref), channel_id=1, source_target_pairs={{7,0},{0,1},{1,2},{2,3},{3,4},{4,5},{5,6},{6,7},{15,8},{8,9},{9,10... | collective-permute-start | bytes 110600 | tf_op jit(solution)/shard_map/ppermute | solution.py:291
  87.0 10.9 %collective-permute-start.30 = (f32[72,128]{1,0:T(8,128)S(1)}, f32[72,128]{1,0:T(8,128)S(1)}, u32[]{:S(2)}, u32[]{:S(2)}) collective-permute-start(f32[72,128]{1,0:T(8,128)S(1)} %add_add_fusion.mine_ref), channel_id=1, source_target_pairs={{8,0},{0,8},{24,16},{16,24},{40,32},{32,40},{56,48},{48,56},{72,64... | collective-permute-start | bytes 110600 | tf_op jit(solution)/shard_map/ppermute | solution.py:258
  94.1 6.5 %collective-permute-start.29 = (f32[72,128]{1,0:T(8,128)S(1)}, f32[72,128]{1,0:T(8,128)S(1)}, u32[]{:S(2)}, u32[]{:S(2)}) collective-permute-start(f32[72,128]{1,0:T(8,128)S(1)} %collective-permute-done.28.mine_ref), channel_id=1, source_target_pairs={{8,0},{0,8},{24,16},{16,24},{40,32},{32,40},{56,48},{48,56},{72,64... | collective-permute-start | bytes 110600 | tf_op jit(solution)/shard_map/ppermute | solution.py:258
  (2 other events, 32.0 us)

commit v4 on v3

--- a/solution.py
+++ b/solution.py
@@ -50,14 +50,15 @@
     return 0.25 * (cross * jnp.transpose(jnp.broadcast_to(scale_a, shape)) * scale_b)
 
 
-def damped_inverse(d, dt):
+def identity(n):
+    row = lax.broadcasted_iota(jnp.int32, (n, n), 0)
+    column = lax.broadcasted_iota(jnp.int32, (n, n), 1)
+    return jnp.where(row == column, 1.0, 0.0).astype(F32)
+
+
+def rough_inverse(d, dt):
     n = d.shape[0]
-    shape = (n, n)
-    eye = jnp.where(
-        lax.broadcasted_iota(jnp.int32, shape, 0) == lax.broadcasted_iota(jnp.int32, shape, 1),
-        1.0,
-        0.0,
-    ).astype(F32)
+    eye = identity(n)
     base = eye + times(d, dt)
     top = 1.0 + 1.001 * (0.25 * n) ** 2
     start = 2.0 / (1.0 + top)
@@ -77,8 +78,13 @@
         gap = gap * gap / (2.0 - gap * gap)
     left = eye - times3(left3(x), right3(base))
     x = x + times3(left3(left), right3(x))
+    return base, x
+
+
+def corrected(base, x, d):
+    n = d.shape[0]
     wide = times(x, jnp.concatenate([base, d], 1))
-    left = eye - wide[:, :n]
+    left = identity(n) - wide[:, :n]
     both = jnp.concatenate([x, wide[:, n:]], 1)
     both = both + times3(left3(left), right3(both))
     return both[:, :n], both[:, n:]
@@ -115,10 +121,23 @@
     return jnp.sum(block * block, 0, keepdims=True)
 
 
-def gram_kernel(core_ref, *refs):
-    *blocks, mine_ref, other_ref, cross_ref = refs
-    a, b = both_blocks(blocks)
-    message(squares(a), squares(b), cross_of(a, b), core_ref[0], cross_ref, mine_ref, other_ref)
+def load_kernel(core_ref, panel_ref, near_ref, mine_ref, other_ref, cross_ref, sems):
+    rows, n = near_ref.shape[0], near_ref.shape[1] // 2
+    size = rows // CHUNKS
+    parts = [slice(i * size, (i + 1) * size) for i in range(CHUNKS)]
+    copies = [
+        pltpu.make_async_copy(panel_ref.at[part], near_ref.at[part], sems.at[i])
+        for i, part in enumerate(parts)
+    ]
+    for copy in copies:
+        copy.start()
+    sums = []
+    for copy, part in zip(copies, parts):
+        copy.wait()
+        a, b = near_ref[part, :n], near_ref[part, n:]
+        sums.append((squares(a), squares(b), cross_of(a, b)))
+    diag_a, diag_b, cross = (sum(terms[1:], terms[0]) for terms in zip(*sums))
+    message(diag_a, diag_b, cross, core_ref[0], cross_ref, mine_ref, other_ref)
 
 
 def cosines_of(core_ref, mine_ref, other_ref):
@@ -141,11 +160,16 @@
     return 2.0 * (wide[:, :n] + wide[:, n:] + low) - a
 
 
-def first_kernel(core_ref, mine_ref, other_ref, *refs):
+def head_kernel(core_ref, mine_ref, other_ref, base_out, x_out, d_out):
+    d = cosines_of(core_ref, mine_ref, other_ref)
+    d_out[...] = d
+    base_out[...], x_out[...] = rough_inverse(d, jnp.transpose(d))
+
+
+def tail_kernel(base_ref, x_ref, d_ref, *refs):
     *blocks, a_out = refs
-    d = cosines_of(core_ref, mine_ref, other_ref)
     a, b = both_blocks(blocks)
-    a_out[...] = first_block(a, b, *damped_inverse(d, jnp.transpose(d)))
+    a_out[...] = first_block(a, b, *corrected(base_ref[...], x_ref[...], d_ref[...]))
 
 
 def late_kernel(m_ref, md_ref, *refs):
@@ -161,7 +185,7 @@
     a, b = both_blocks(blocks)
     turned = left3(a - times3(left3(b), right3(dt)))
     own = own_ref[...]
-    m, md = damped_inverse(d, dt)
+    m, md = corrected(*rough_inverse(d, dt), d)
     b = b + 2.0 * times3(turned, right3(md))
     message(
         squares(own), squares(b), cross_of(own, b), core_ref[0], cross_ref, mine_out, other_out
@@ -180,7 +204,7 @@
     dt = jnp.transpose(d)
     a, b = both_blocks(blocks)
     turned = left3(a - times3(left3(b), right3(dt)))
-    _, md = damped_inverse(d, dt)
+    _, md = corrected(*rough_inverse(d, dt), d)
     right = right3(md)
     size = rows // CHUNKS
     for i in range(CHUNKS):
@@ -213,14 +237,25 @@
     return [half, half], [pltpu.VMEM((n + 2 * PAD, n), F32)]
 
 
-def gram(core, blocks, n):
+def load(core, panel, n):
     halves, scratch = message_shapes(n)
-    return vmem_call(gram_kernel, halves, blocks, core, scratch)
-
-
-def turn_first(core, halves, blocks, n):
+    return pl.pallas_call(
+        load_kernel,
+        out_shape=[pltpu.VMEM(panel.shape, F32), *halves],
+        in_specs=[pl.BlockSpec(memory_space=pltpu.SMEM), pl.BlockSpec(memory_space=pl.ANY)],
+        scratch_shapes=[*scratch, pltpu.SemaphoreType.DMA((CHUNKS,))],
+        name="load",
+    )(core, panel)
+
+
+def turn_head(core, halves, n):
+    squares = [pltpu.VMEM((n, n), F32)] * 3
+    return vmem_call(head_kernel, squares, halves, core)
+
+
+def turn_tail(squares, blocks, n):
     block = pltpu.VMEM((blocks[0].shape[0], n), F32)
-    return vmem_call(first_kernel, block, [*halves, *blocks], core)
+    return vmem_call(tail_kernel, block, [*squares, *blocks])
 
 
 def turn_late(m, md, blocks, n):
@@ -294,19 +329,20 @@
 def local(panel):
     n = panel.shape[1] // 2
     core = (lax.axis_index("row") & 1).astype(jnp.int32).reshape(1)
-    own = [panel]
     for step in range(STEPS):
         if step == 0:
             before = [shifted(panel)]
-            mine, other = gram(core, own, n)
+            own, mine, other = load(core, panel, n)
+            own = [own]
         else:
             second = shifted(b)
             before = [turn_late(m, md, before, n), second]
         half = summed_halves(mine, other, y_last=step == 0)
         hopped = shifted(half)
         own_halves = with_other(half)
-        a = turn_first(core, own_halves, own, n)
+        squares = turn_head(core, own_halves, n)
         halves = with_other(hopped)
+        a = turn_tail(squares, own, n)
         if step + 1 == STEPS:
             return turn_last(core, halves, a, before)
         b, m, md, mine, other = turn_second(core, halves, a, before, n)

time: 104 us -> 109 us (1.048)
  waiting for transfers between devices: 28.4 us -> 32.4 us
  Pallas kernels: 18 us -> 19.8 us
    ppermute x26, waiting for transfers between devices: 18.8 us -> 24.4 us  [from_row(): return lax.ppermute(x, 'row', route)]
    pallas_call x0 -> x1, Pallas kernels: none -> 1.88 us  [load(): pl.pallas_call(load_kernel, out_shape=[pltpu.VMEM(panel.shape, F32), *hal...]
    ppermute x6, waiting for transfers between devices: 9.58 us -> 7.98 us  [shifted(): return lax.ppermute(block, 'pair', route)]
    ppermute x6, starting transfers between devices: 5.38 us -> 6.67 us  [shifted(): return lax.ppermute(block, 'pair', route)]
    pallas_call x9 -> x11, Pallas kernels: 18 us -> 18 us  [vmem_call(): pl.pallas_call(kernel, out_shape=shapes, in_specs=specs, scratch_shapes=s...]
  transfers between devices with their start and end apart: 32 -> 32, of which waited for: 20 -> 19; matrix products, arithmetic and copies ran while one was open for 0% -> 0% of each run, Pallas kernels for 9% -> 10%
where the time goes in v4:
time: 109 us
  starting transfers between devices  56.6 us (52%)
  waiting for transfers between devices  32.4 us (30%)
  Pallas kernels  19.8 us (18%)
    ppermute x26, starting transfers between devices, from_row(): return lax.ppermute(x, 'row', route)  50 us
    ppermute x26, waiting for transfers between devices, from_row(): return lax.ppermute(x, 'row', route)  24.4 us
    pallas_call x11, Pallas kernels, vmem_call(): pl.pallas_call(kernel, out_shape=shapes, in_specs=specs, scratch_shapes=s...  18 us
    ppermute x6, waiting for transfers between devices, shifted(): return lax.ppermute(block, 'pair', route)  7.98 us
    ppermute x6, starting transfers between devices, shifted(): return lax.ppermute(block, 'pair', route)  6.67 us
  transfers between devices with their start and end apart: 32, of which 19 were waited for; matrix products, arithmetic and copies ran while one was open for 0% of the time, Pallas kernels for 10%

profile of v4, /device:TPU:1, one launch (start us, length us, event | category | flops | bytes accessed | tf_op | source)
XLA Modules:
  0.0 109.3 jit_solution(9395001205936676321)
XLA Ops:
  0.0 3.7 %collective-permute-start.9 = (f32[512,256]{1,0:T(8,128)}, f32[512,256]{1,0:T(8,128)S(1)}, u32[]{:S(2)}, u32[]{:S(2)}) collective-permute-start(f32[512,256]{1,0:T(8,128)} %panel_ref.1), channel_id=1, source_target_pairs={{7,0},{0,1},{1,2},{2,3},{3,4},{4,5},{5,6},{6,7},{15,8},{8,9},{9,10... | collective-permute-start | bytes 1572872 | tf_op jit(solution)/shard_map/ppermute | solution.py:326
  3.7 1.9 %load.1 = (f32[512,256]{1,0:T(8,128)S(1)}, f32[72,128]{1,0:T(8,128)S(1)}, f32[72,128]{1,0:T(8,128)S(1)}) custom-call(s32[1]{0:T(128)} %bitcast.core_ref, f32[512,256]{1,0:T(8,128)} %panel_ref.1), custom_call_target="tpu_custom_call" | custom-call | tf_op jit(solution)/shard_map/load/pallas_call | solution.py:242
  7.5 1.6 %collective-permute-start.1 = (f32[72,128]{1,0:T(8,128)S(1)}, f32[72,128]{1,0:T(8,128)S(1)}, u32[]{:S(2)}, u32[]{:S(2)}) collective-permute-start(f32[72,128]{1,0:T(8,128)S(1)} %add.60), channel_id=1, source_target_pairs={{32,0},{40,8},{48,16},{56,24},{0,32},{8,40},{16,48},{24,56},{96,64... | collective-permute-start | bytes 110600 | tf_op jit(solution)/shard_map/ppermute | solution.py:293
  9.2 1.6 %collective-permute-done.1 = f32[72,128]{1,0:T(8,128)S(1)} collective-permute-done((f32[72,128]{1,0:T(8,128)S(1)}, f32[72,128]{1,0:T(8,128)S(1)}, u32[]{:S(2)}, u32[]{:S(2)}) %collective-permute-start.1) | collective-permute-done | bytes 36896 | tf_op jit(solution)/shard_map/ppermute | solution.py:293
  10.8 5.4 %collective-permute-start.2 = (f32[72,128]{1,0:T(8,128)S(1)}, f32[72,128]{1,0:T(8,128)S(1)}, u32[]{:S(2)}, u32[]{:S(2)}) collective-permute-start(f32[72,128]{1,0:T(8,128)S(1)} %add.61), channel_id=1, source_target_pairs={{224,0},{232,8},{240,16},{248,24},{64,32},{72,40},{80,48},{88,56},... | collective-permute-start | bytes 110600 | tf_op jit(solution)/shard_map/ppermute | solution.py:293
  18.4 1.5 %collective-permute-done.3 = f32[72,128]{1,0:T(8,128)S(1)} collective-permute-done((f32[72,128]{1,0:T(8,128)S(1)}, f32[72,128]{1,0:T(8,128)S(1)}, u32[]{:S(2)}, u32[]{:S(2)}) %collective-permute-start.3) | collective-permute-done | bytes 36896 | tf_op jit(solution)/shard_map/ppermute | solution.py:293
  19.9 3.7 %collective-permute-done.4 = f32[72,128]{1,0:T(8,128)S(1)} collective-permute-done((f32[72,128]{1,0:T(8,128)S(1)}, f32[72,128]{1,0:T(8,128)S(1)}, u32[]{:S(2)}, u32[]{:S(2)}) %collective-permute-start.4) | collective-permute-done | bytes 36896 | tf_op jit(solution)/shard_map/ppermute | solution.py:293
  24.1 2.4 %collective-permute-done.5 = f32[72,128]{1,0:T(8,128)S(1)} collective-permute-done((f32[72,128]{1,0:T(8,128)S(1)}, f32[72,128]{1,0:T(8,128)S(1)}, u32[]{:S(2)}, u32[]{:S(2)}) %collective-permute-start.5) | collective-permute-done | bytes 36896 | tf_op jit(solution)/shard_map/ppermute | solution.py:293
  26.5 1.4 %collective-permute-start.6 = (f32[72,128]{1,0:T(8,128)S(1)}, f32[72,128]{1,0:T(8,128)S(1)}, u32[]{:S(2)}, u32[]{:S(2)}) collective-permute-start(f32[72,128]{1,0:T(8,128)S(1)} %add.65.mine_ref), channel_id=1, source_target_pairs={{7,0},{0,1},{1,2},{2,3},{3,4},{4,5},{5,6},{6,7},{15,8},{8,9},{9,10... | collective-permute-start | bytes 110600 | tf_op jit(solution)/shard_map/ppermute | solution.py:326
  28.0 4.0 %collective-permute-start.8 = (f32[72,128]{1,0:T(8,128)S(1)}, f32[72,128]{1,0:T(8,128)S(1)}, u32[]{:S(2)}, u32[]{:S(2)}) collective-permute-start(f32[72,128]{1,0:T(8,128)S(1)} %add.65.mine_ref), channel_id=1, source_target_pairs={{8,0},{0,8},{24,16},{16,24},{40,32},{32,40},{56,48},{48,56},{72,64... | collective-permute-start | bytes 110600 | tf_op jit(solution)/shard_map/ppermute | solution.py:293
  32.9 5.3 %collective-permute-start.7 = (f32[72,128]{1,0:T(8,128)S(1)}, f32[72,128]{1,0:T(8,128)S(1)}, u32[]{:S(2)}, u32[]{:S(2)}) collective-permute-start(f32[72,128]{1,0:T(8,128)S(1)} %collective-permute-done.6.mine_ref), channel_id=1, source_target_pairs={{8,0},{0,8},{24,16},{16,24},{40,32},{32,40},{56,48},{48,56},{72,64... | collective-permute-start | bytes 110600 | tf_op jit(solution)/shard_map/ppermute | solution.py:293
  38.3 1.8 %shard_map.17 = (f32[128,128]{1,0:T(8,128)S(1)}, f32[128,128]{1,0:T(8,128)S(1)}, f32[128,128]{1,0:T(8,128)S(1)}) custom-call(s32[1]{0:T(128)} %bitcast.core_ref, f32[72,128]{1,0:T(8,128)S(1)} %add.65.mine_ref, f32[72,128]{1,0:T(8,128)S(1)} %collective-permute-done.8.other_ref), custom_call_target="tpu_custom_call" | custom-call | tf_op jit(solution)/shard_map/pallas_call | solution.py:230
  41.1 2.8 %shard_map.19 = (f32[512,128]{1,0:T(8,128)S(1)}, f32[128,128]{1,0:T(8,128)S(1)}, f32[128,128]{1,0:T(8,128)S(1)}, f32[72,128]{1,0:T(8,128)S(1)}, f32[72,128]{1,0:T(8,128)S(1)}) custom-call(s32[1]{0:T(128)} %bitcast.core_ref, f32[72,128]{1,0:T(8,128)S(1)} %collective-permute-done.6.mine_ref, f32[72,128]{1,0:T(8,128)S(1)} %collective-permute-done.7.other_ref, ...), custom_call_target="tpu_custom_call" | custom-call | tf_op jit(solution)/shard_map/pallas_call | solution.py:230
  44.0 1.2 %collective-permute-done.10 = f32[72,128]{1,0:T(8,128)S(1)} collective-permute-done((f32[72,128]{1,0:T(8,128)S(1)}, f32[72,128]{1,0:T(8,128)S(1)}, u32[]{:S(2)}, u32[]{:S(2)}) %collective-permute-start.10) | collective-permute-done | bytes 36896 | tf_op jit(solution)/shard_map/ppermute | solution.py:293
  45.8 2.0 %collective-permute-start.13 = (f32[72,128]{1,0:T(8,128)S(1)}, f32[72,128]{1,0:T(8,128)S(1)}, u32[]{:S(2)}, u32[]{:S(2)}) collective-permute-start(f32[72,128]{1,0:T(8,128)S(1)} %add.66), channel_id=1, source_target_pairs={{48,0},{56,8},{32,16},{40,24},{16,32},{24,40},{0,48},{8,56},{112,6... | collective-permute-start | bytes 110600 | tf_op jit(solution)/shard_map/ppermute | solution.py:293
  50.3 4.4 %collective-permute-start.16 = (f32[72,128]{1,0:T(8,128)S(1)}, f32[72,128]{1,0:T(8,128)S(1)}, u32[]{:S(2)}, u32[]{:S(2)}) collective-permute-start(f32[72,128]{1,0:T(8,128)S(1)} %add_add_fusion.3), channel_id=1, source_target_pairs={{160,0},{168,8},{176,16},{184,24},{128,32},{136,40},{144,48},{152,... | collective-permute-start | bytes 110600 | tf_op jit(solution)/shard_map/ppermute | solution.py:293
  54.9 1.6 %collective-permute-done.16 = f32[72,128]{1,0:T(8,128)S(1)} collective-permute-done((f32[72,128]{1,0:T(8,128)S(1)}, f32[72,128]{1,0:T(8,128)S(1)}, u32[]{:S(2)}, u32[]{:S(2)}) %collective-permute-start.16) | collective-permute-done | bytes 36896 | tf_op jit(solution)/shard_map/ppermute | solution.py:293
  57.5 3.2 %collective-permute-start.19 = (f32[72,128]{1,0:T(8,128)S(1)}, f32[72,128]{1,0:T(8,128)S(1)}, u32[]{:S(2)}, u32[]{:S(2)}) collective-permute-start(f32[72,128]{1,0:T(8,128)S(1)} %add_add_fusion.2.mine_ref), channel_id=1, source_target_pairs={{8,0},{0,8},{24,16},{16,24},{40,32},{32,40},{56,48},{48,56},{72,64... | collective-permute-start | bytes 110600 | tf_op jit(solution)/shard_map/ppermute | solution.py:293
  60.6 3.7 %collective-permute-done.17.mine_ref = f32[72,128]{1,0:T(8,128)S(1)} collective-permute-done((f32[72,128]{1,0:T(8,128)S(1)}, f32[72,128]{1,0:T(8,128)S(1)}, u32[]{:S(2)}, u32[]{:S(2)}) %collective-permute-start.17) | collective-permute-done | bytes 36896 | tf_op jit(solution)/shard_map/ppermute | solution.py:326
  64.3 3.5 %collective-permute-start.18 = (f32[72,128]{1,0:T(8,128)S(1)}, f32[72,128]{1,0:T(8,128)S(1)}, u32[]{:S(2)}, u32[]{:S(2)}) collective-permute-start(f32[72,128]{1,0:T(8,128)S(1)} %collective-permute-done.17.mine_ref), channel_id=1, source_target_pairs={{8,0},{0,8},{24,16},{16,24},{40,32},{32,40},{56,48},{48,56},{72,64... | collective-permute-start | bytes 110600 | tf_op jit(solution)/shard_map/ppermute | solution.py:293
  68.2 1.8 %shard_map.20 = (f32[128,128]{1,0:T(8,128)S(1)}, f32[128,128]{1,0:T(8,128)S(1)}, f32[128,128]{1,0:T(8,128)S(1)}) custom-call(s32[1]{0:T(128)} %bitcast.core_ref, f32[72,128]{1,0:T(8,128)S(1)} %add_add_fusion.2.mine_ref, f32[72,128]{1,0:T(8,128)S(1)} %collective-permute-done.19.other_ref), custom_call_target="tpu_custom_call" | custom-call | tf_op jit(solution)/shard_map/pallas_call | solution.py:230
  71.0 2.8 %shard_map.23 = (f32[512,128]{1,0:T(8,128)S(1)}, f32[128,128]{1,0:T(8,128)S(1)}, f32[128,128]{1,0:T(8,128)S(1)}, f32[72,128]{1,0:T(8,128)S(1)}, f32[72,128]{1,0:T(8,128)S(1)}) custom-call(s32[1]{0:T(128)} %bitcast.core_ref, f32[72,128]{1,0:T(8,128)S(1)} %collective-permute-done.17.mine_ref, f32[72,128]{1,0:T(8,128)S(1)} %collective-permute-done.18.other_ref, ...), custom_call_target="tpu_custom_call" | custom-call | tf_op jit(solution)/shard_map/pallas_call | solution.py:230
  79.0 2.0 %collective-permute-done.24 = f32[72,128]{1,0:T(8,128)S(1)} collective-permute-done((f32[72,128]{1,0:T(8,128)S(1)}, f32[72,128]{1,0:T(8,128)S(1)}, u32[]{:S(2)}, u32[]{:S(2)}) %collective-permute-start.24) | collective-permute-done | bytes 36896 | tf_op jit(solution)/shard_map/ppermute | solution.py:293
  81.0 2.8 %collective-permute-start.25 = (f32[72,128]{1,0:T(8,128)S(1)}, f32[72,128]{1,0:T(8,128)S(1)}, u32[]{:S(2)}, u32[]{:S(2)}) collective-permute-start(f32[72,128]{1,0:T(8,128)S(1)} %add_add_fusion.1), channel_id=1, source_target_pairs={{224,0},{232,8},{240,16},{248,24},{64,32},{72,40},{80,48},{88,56},... | collective-permute-start | bytes 110600 | tf_op jit(solution)/shard_map/ppermute | solution.py:293
  83.8 1.6 %collective-permute-start.26 = (f32[72,128]{1,0:T(8,128)S(1)}, f32[72,128]{1,0:T(8,128)S(1)}, u32[]{:S(2)}, u32[]{:S(2)}) collective-permute-start(f32[72,128]{1,0:T(8,128)S(1)} %add_add_fusion.1), channel_id=1, source_target_pairs={{64,0},{72,8},{80,16},{88,24},{224,32},{232,40},{240,48},{248,56},... | collective-permute-start | bytes 110600 | tf_op jit(solution)/shard_map/ppermute | solution.py:293
  86.0 1.8 %collective-permute-done.26 = f32[72,128]{1,0:T(8,128)S(1)} collective-permute-done((f32[72,128]{1,0:T(8,128)S(1)}, f32[72,128]{1,0:T(8,128)S(1)}, u32[]{:S(2)}, u32[]{:S(2)}) %collective-permute-start.26) | collective-permute-done | bytes 36896 | tf_op jit(solution)/shard_map/ppermute | solution.py:293
  87.8 3.5 %collective-permute-done.27 = f32[72,128]{1,0:T(8,128)S(1)} collective-permute-done((f32[72,128]{1,0:T(8,128)S(1)}, f32[72,128]{1,0:T(8,128)S(1)}, u32[]{:S(2)}, u32[]{:S(2)}) %collective-permute-start.27) | collective-permute-done | bytes 36896 | tf_op jit(solution)/shard_map/ppermute | solution.py:293
  91.5 3.6 %collective-permute-start.30 = (f32[72,128]{1,0:T(8,128)S(1)}, f32[72,128]{1,0:T(8,128)S(1)}, u32[]{:S(2)}, u32[]{:S(2)}) collective-permute-start(f32[72,128]{1,0:T(8,128)S(1)} %add_add_fusion.mine_ref), channel_id=1, source_target_pairs={{8,0},{0,8},{24,16},{16,24},{40,32},{32,40},{56,48},{48,56},{72,64... | collective-permute-start | bytes 110600 | tf_op jit(solution)/shard_map/ppermute | solution.py:293
  95.2 3.3 %collective-permute-done.28.mine_ref = f32[72,128]{1,0:T(8,128)S(1)} collective-permute-done((f32[72,128]{1,0:T(8,128)S(1)}, f32[72,128]{1,0:T(8,128)S(1)}, u32[]{:S(2)}, u32[]{:S(2)}) %collective-permute-start.28) | collective-permute-done | bytes 36896 | tf_op jit(solution)/shard_map/ppermute | solution.py:326
  98.5 4.2 %collective-permute-start.29 = (f32[72,128]{1,0:T(8,128)S(1)}, f32[72,128]{1,0:T(8,128)S(1)}, u32[]{:S(2)}, u32[]{:S(2)}) collective-permute-start(f32[72,128]{1,0:T(8,128)S(1)} %collective-permute-done.28.mine_ref), channel_id=1, source_target_pairs={{8,0},{0,8},{24,16},{16,24},{40,32},{32,40},{56,48},{48,56},{72,64... | collective-permute-start | bytes 110600 | tf_op jit(solution)/shard_map/ppermute | solution.py:293
  103.0 1.8 %shard_map.24 = (f32[128,128]{1,0:T(8,128)S(1)}, f32[128,128]{1,0:T(8,128)S(1)}, f32[128,128]{1,0:T(8,128)S(1)}) custom-call(s32[1]{0:T(128)} %bitcast.core_ref, f32[72,128]{1,0:T(8,128)S(1)} %add_add_fusion.mine_ref, f32[72,128]{1,0:T(8,128)S(1)} %collective-permute-done.30.other_ref), custom_call_target="tpu_custom_call" | custom-call | tf_op jit(solution)/shard_map/pallas_call | solution.py:230
  105.9 3.3 %shard_map.27 = f32[512,256]{1,0:T(8,128)} custom-call(s32[1]{0:T(128)} %bitcast.core_ref, f32[72,128]{1,0:T(8,128)S(1)} %collective-permute-done.28.mine_ref, f32[72,128]{1,0:T(8,128)S(1)} %collective-permute-done.29.other_ref, f32[512,128]{1,0:T(8,128)S(1)} %shard_map.25.own_ref, f32[512,128]{1,0:T(8,128)S(1)} %shard_map.26.refs_0_, ...), custom_call_target="tpu_custom_call" | custom-call | tf_op jit(solution)/shard_map/pallas_call | solution.py:230
  (54 shorter events, 19.7 us)
Async XLA Ops:
  0.0 41.1 %collective-permute-start.9 = (f32[512,256]{1,0:T(8,128)}, f32[512,256]{1,0:T(8,128)S(1)}, u32[]{:S(2)}, u32[]{:S(2)}) collective-permute-start(f32[512,256]{1,0:T(8,128)} %panel_ref.1), channel_id=1, source_target_pairs={{7,0},{0,1},{1,2},{2,3},{3,4},{4,5},{5,6},{6,7},{15,8},{8,9},{9,10... | collective-permute-start | bytes 1572872 | tf_op jit(solution)/shard_map/ppermute | solution.py:326
  5.6 1.9 %collective-permute-start = (f32[72,128]{1,0:T(8,128)S(1)}, f32[72,128]{1,0:T(8,128)S(1)}, u32[]{:S(2)}, u32[]{:S(2)}) collective-permute-start(f32[72,128]{1,0:T(8,128)S(1)} %get-tuple-element.28), channel_id=1, source_target_pairs={{8,0},{0,8},{24,16},{16,24},{40,32},{32,40},{56,48},{48,56},{72,64... | collective-permute-start | bytes 110600 | tf_op jit(solution)/shard_map/ppermute | solution.py:293
  7.5 3.3 %collective-permute-start.1 = (f32[72,128]{1,0:T(8,128)S(1)}, f32[72,128]{1,0:T(8,128)S(1)}, u32[]{:S(2)}, u32[]{:S(2)}) collective-permute-start(f32[72,128]{1,0:T(8,128)S(1)} %add.60), channel_id=1, source_target_pairs={{32,0},{40,8},{48,16},{56,24},{0,32},{8,40},{16,48},{24,56},{96,64... | collective-permute-start | bytes 110600 | tf_op jit(solution)/shard_map/ppermute | solution.py:293
  10.8 7.6 %collective-permute-start.2 = (f32[72,128]{1,0:T(8,128)S(1)}, f32[72,128]{1,0:T(8,128)S(1)}, u32[]{:S(2)}, u32[]{:S(2)}) collective-permute-start(f32[72,128]{1,0:T(8,128)S(1)} %add.61), channel_id=1, source_target_pairs={{224,0},{232,8},{240,16},{248,24},{64,32},{72,40},{80,48},{88,56},... | collective-permute-start | bytes 110600 | tf_op jit(solution)/shard_map/ppermute | solution.py:293
  16.2 3.7 %collective-permute-start.3 = (f32[72,128]{1,0:T(8,128)S(1)}, f32[72,128]{1,0:T(8,128)S(1)}, u32[]{:S(2)}, u32[]{:S(2)}) collective-permute-start(f32[72,128]{1,0:T(8,128)S(1)} %add.61), channel_id=1, source_target_pairs={{64,0},{72,8},{80,16},{88,24},{224,32},{232,40},{240,48},{248,56},... | collective-permute-start | bytes 110600 | tf_op jit(solution)/shard_map/ppermute | solution.py:293
  17.4 6.2 %collective-permute-start.4 = (f32[72,128]{1,0:T(8,128)S(1)}, f32[72,128]{1,0:T(8,128)S(1)}, u32[]{:S(2)}, u32[]{:S(2)}) collective-permute-start(f32[72,128]{1,0:T(8,128)S(1)} %add.61), channel_id=1, source_target_pairs={{160,0},{168,8},{176,16},{184,24},{128,32},{136,40},{144,48},{152,... | collective-permute-start | bytes 110600 | tf_op jit(solution)/shard_map/ppermute | solution.py:293
  23.6 2.9 %collective-permute-start.5 = (f32[72,128]{1,0:T(8,128)S(1)}, f32[72,128]{1,0:T(8,128)S(1)}, u32[]{:S(2)}, u32[]{:S(2)}) collective-permute-start(f32[72,128]{1,0:T(8,128)S(1)} %add_add_fusion.4), channel_id=1, source_target_pairs={{16,0},{24,8},{0,16},{8,24},{48,32},{56,40},{32,48},{40,56},{80,64... | collective-permute-start | bytes 110600 | tf_op jit(solution)/shard_map/ppermute | solution.py:293
  26.5 6.4 %collective-permute-start.6 = (f32[72,128]{1,0:T(8,128)S(1)}, f32[72,128]{1,0:T(8,128)S(1)}, u32[]{:S(2)}, u32[]{:S(2)}) collective-permute-start(f32[72,128]{1,0:T(8,128)S(1)} %add.65.mine_ref), channel_id=1, source_target_pairs={{7,0},{0,1},{1,2},{2,3},{3,4},{4,5},{5,6},{6,7},{15,8},{8,9},{9,10... | collective-permute-start | bytes 110600 | tf_op jit(solution)/shard_map/ppermute | solution.py:326
  28.0 10.3 %collective-permute-start.8 = (f32[72,128]{1,0:T(8,128)S(1)}, f32[72,128]{1,0:T(8,128)S(1)}, u32[]{:S(2)}, u32[]{:S(2)}) collective-permute-start(f32[72,128]{1,0:T(8,128)S(1)} %add.65.mine_ref), channel_id=1, source_target_pairs={{8,0},{0,8},{24,16},{16,24},{40,32},{32,40},{56,48},{48,56},{72,64... | collective-permute-start | bytes 110600 | tf_op jit(solution)/shard_map/ppermute | solution.py:293
  32.9 8.1 %collective-permute-start.7 = (f32[72,128]{1,0:T(8,128)S(1)}, f32[72,128]{1,0:T(8,128)S(1)}, u32[]{:S(2)}, u32[]{:S(2)}) collective-permute-start(f32[72,128]{1,0:T(8,128)S(1)} %collective-permute-done.6.mine_ref), channel_id=1, source_target_pairs={{8,0},{0,8},{24,16},{16,24},{40,32},{32,40},{56,48},{48,56},{72,64... | collective-permute-start | bytes 110600 | tf_op jit(solution)/shard_map/ppermute | solution.py:293
  43.9 1.3 %collective-permute-start.10 = (f32[72,128]{1,0:T(8,128)S(1)}, f32[72,128]{1,0:T(8,128)S(1)}, u32[]{:S(2)}, u32[]{:S(2)}) collective-permute-start(f32[72,128]{1,0:T(8,128)S(1)} %get-tuple-element.34), channel_id=1, source_target_pairs={{8,0},{0,8},{24,16},{16,24},{40,32},{32,40},{56,48},{48,56},{72,64... | collective-permute-start | bytes 110600 | tf_op jit(solution)/shard_map/ppermute | solution.py:293
  45.2 2.8 %collective-permute-start.11 = (f32[72,128]{1,0:T(8,128)S(1)}, f32[72,128]{1,0:T(8,128)S(1)}, u32[]{:S(2)}, u32[]{:S(2)}) collective-permute-start(f32[72,128]{1,0:T(8,128)S(1)} %add.66), channel_id=1, source_target_pairs={{32,0},{40,8},{48,16},{56,24},{0,32},{8,40},{16,48},{24,56},{96,64... | collective-permute-start | bytes 110600 | tf_op jit(solution)/shard_map/ppermute | solution.py:293
  45.6 3.1 %collective-permute-start.12 = (f32[72,128]{1,0:T(8,128)S(1)}, f32[72,128]{1,0:T(8,128)S(1)}, u32[]{:S(2)}, u32[]{:S(2)}) collective-permute-start(f32[72,128]{1,0:T(8,128)S(1)} %add.66), channel_id=1, source_target_pairs={{16,0},{24,8},{0,16},{8,24},{48,32},{56,40},{32,48},{40,56},{80,64... | collective-permute-start | bytes 110600 | tf_op jit(solution)/shard_map/ppermute | solution.py:293
  45.8 3.8 %collective-permute-start.13 = (f32[72,128]{1,0:T(8,128)S(1)}, f32[72,128]{1,0:T(8,128)S(1)}, u32[]{:S(2)}, u32[]{:S(2)}) collective-permute-start(f32[72,128]{1,0:T(8,128)S(1)} %add.66), channel_id=1, source_target_pairs={{48,0},{56,8},{32,16},{40,24},{16,32},{24,40},{0,48},{8,56},{112,6... | collective-permute-start | bytes 110600 | tf_op jit(solution)/shard_map/ppermute | solution.py:293
  49.6 5.3 %collective-permute-start.14 = (f32[72,128]{1,0:T(8,128)S(1)}, f32[72,128]{1,0:T(8,128)S(1)}, u32[]{:S(2)}, u32[]{:S(2)}) collective-permute-start(f32[72,128]{1,0:T(8,128)S(1)} %add_add_fusion.3), channel_id=1, source_target_pairs={{224,0},{232,8},{240,16},{248,24},{64,32},{72,40},{80,48},{88,56},... | collective-permute-start | bytes 110600 | tf_op jit(solution)/shard_map/ppermute | solution.py:293
  50.1 4.8 %collective-permute-start.15 = (f32[72,128]{1,0:T(8,128)S(1)}, f32[72,128]{1,0:T(8,128)S(1)}, u32[]{:S(2)}, u32[]{:S(2)}) collective-permute-start(f32[72,128]{1,0:T(8,128)S(1)} %add_add_fusion.3), channel_id=1, source_target_pairs={{64,0},{72,8},{80,16},{88,24},{224,32},{232,40},{240,48},{248,56},... | collective-permute-start | bytes 110600 | tf_op jit(solution)/shard_map/ppermute | solution.py:293
  50.3 6.2 %collective-permute-start.16 = (f32[72,128]{1,0:T(8,128)S(1)}, f32[72,128]{1,0:T(8,128)S(1)}, u32[]{:S(2)}, u32[]{:S(2)}) collective-permute-start(f32[72,128]{1,0:T(8,128)S(1)} %add_add_fusion.3), channel_id=1, source_target_pairs={{160,0},{168,8},{176,16},{184,24},{128,32},{136,40},{144,48},{152,... | collective-permute-start | bytes 110600 | tf_op jit(solution)/shard_map/ppermute | solution.py:293
  54.7 16.3 %collective-permute-start.20 = (f32[512,128]{1,0:T(8,128)S(1)}, f32[512,128]{1,0:T(8,128)S(1)}, u32[]{:S(2)}, u32[]{:S(2)}) collective-permute-start(f32[512,128]{1,0:T(8,128)S(1)} %get-tuple-element.38.refs_1_), channel_id=1, source_target_pairs={{7,0},{0,1},{1,2},{2,3},{3,4},{4,5},{5,6},{6,7},{15,8},{8,9},{9,10... | collective-permute-start | bytes 786440 | tf_op jit(solution)/shard_map/ppermute | solution.py:326
  56.5 7.8 %collective-permute-start.17 = (f32[72,128]{1,0:T(8,128)S(1)}, f32[72,128]{1,0:T(8,128)S(1)}, u32[]{:S(2)}, u32[]{:S(2)}) collective-permute-start(f32[72,128]{1,0:T(8,128)S(1)} %add_add_fusion.2.mine_ref), channel_id=1, source_target_pairs={{7,0},{0,1},{1,2},{2,3},{3,4},{4,5},{5,6},{6,7},{15,8},{8,9},{9,10... | collective-permute-start | bytes 110600 | tf_op jit(solution)/shard_map/ppermute | solution.py:326
  57.5 10.7 %collective-permute-start.19 = (f32[72,128]{1,0:T(8,128)S(1)}, f32[72,128]{1,0:T(8,128)S(1)}, u32[]{:S(2)}, u32[]{:S(2)}) collective-permute-start(f32[72,128]{1,0:T(8,128)S(1)} %add_add_fusion.2.mine_ref), channel_id=1, source_target_pairs={{8,0},{0,8},{24,16},{16,24},{40,32},{32,40},{56,48},{48,56},{72,64... | collective-permute-start | bytes 110600 | tf_op jit(solution)/shard_map/ppermute | solution.py:293
  64.3 6.7 %collective-permute-start.18 = (f32[72,128]{1,0:T(8,128)S(1)}, f32[72,128]{1,0:T(8,128)S(1)}, u32[]{:S(2)}, u32[]{:S(2)}) collective-permute-start(f32[72,128]{1,0:T(8,128)S(1)} %collective-permute-done.17.mine_ref), channel_id=1, source_target_pairs={{8,0},{0,8},{24,16},{16,24},{40,32},{32,40},{56,48},{48,56},{72,64... | collective-permute-start | bytes 110600 | tf_op jit(solution)/shard_map/ppermute | solution.py:293
  73.8 1.3 %collective-permute-start.21 = (f32[72,128]{1,0:T(8,128)S(1)}, f32[72,128]{1,0:T(8,128)S(1)}, u32[]{:S(2)}, u32[]{:S(2)}) collective-permute-start(f32[72,128]{1,0:T(8,128)S(1)} %get-tuple-element.42), channel_id=1, source_target_pairs={{8,0},{0,8},{24,16},{16,24},{40,32},{32,40},{56,48},{48,56},{72,64... | collective-permute-start | bytes 110600 | tf_op jit(solution)/shard_map/ppermute | solution.py:293
  75.1 2.8 %collective-permute-start.22 = (f32[72,128]{1,0:T(8,128)S(1)}, f32[72,128]{1,0:T(8,128)S(1)}, u32[]{:S(2)}, u32[]{:S(2)}) collective-permute-start(f32[72,128]{1,0:T(8,128)S(1)} %add.73), channel_id=1, source_target_pairs={{32,0},{40,8},{48,16},{56,24},{0,32},{8,40},{16,48},{24,56},{96,64... | collective-permute-start | bytes 110600 | tf_op jit(solution)/shard_map/ppermute | solution.py:293
  76.2 2.8 %collective-permute-start.23 = (f32[72,128]{1,0:T(8,128)S(1)}, f32[72,128]{1,0:T(8,128)S(1)}, u32[]{:S(2)}, u32[]{:S(2)}) collective-permute-start(f32[72,128]{1,0:T(8,128)S(1)} %add.73), channel_id=1, source_target_pairs={{16,0},{24,8},{0,16},{8,24},{48,32},{56,40},{32,48},{40,56},{80,64... | collective-permute-start | bytes 110600 | tf_op jit(solution)/shard_map/ppermute | solution.py:293
  77.3 3.7 %collective-permute-start.24 = (f32[72,128]{1,0:T(8,128)S(1)}, f32[72,128]{1,0:T(8,128)S(1)}, u32[]{:S(2)}, u32[]{:S(2)}) collective-permute-start(f32[72,128]{1,0:T(8,128)S(1)} %add.73), channel_id=1, source_target_pairs={{48,0},{56,8},{32,16},{40,24},{16,32},{24,40},{0,48},{8,56},{112,6... | collective-permute-start | bytes 110600 | tf_op jit(solution)/shard_map/ppermute | solution.py:293
  81.0 5.0 %collective-permute-start.25 = (f32[72,128]{1,0:T(8,128)S(1)}, f32[72,128]{1,0:T(8,128)S(1)}, u32[]{:S(2)}, u32[]{:S(2)}) collective-permute-start(f32[72,128]{1,0:T(8,128)S(1)} %add_add_fusion.1), channel_id=1, source_target_pairs={{224,0},{232,8},{240,16},{248,24},{64,32},{72,40},{80,48},{88,56},... | collective-permute-start | bytes 110600 | tf_op jit(solution)/shard_map/ppermute | solution.py:293
  83.8 4.0 %collective-permute-start.26 = (f32[72,128]{1,0:T(8,128)S(1)}, f32[72,128]{1,0:T(8,128)S(1)}, u32[]{:S(2)}, u32[]{:S(2)}) collective-permute-start(f32[72,128]{1,0:T(8,128)S(1)} %add_add_fusion.1), channel_id=1, source_target_pairs={{64,0},{72,8},{80,16},{88,24},{224,32},{232,40},{240,48},{248,56},... | collective-permute-start | bytes 110600 | tf_op jit(solution)/shard_map/ppermute | solution.py:293
  85.4 5.8 %collective-permute-start.27 = (f32[72,128]{1,0:T(8,128)S(1)}, f32[72,128]{1,0:T(8,128)S(1)}, u32[]{:S(2)}, u32[]{:S(2)}) collective-permute-start(f32[72,128]{1,0:T(8,128)S(1)} %add_add_fusion.1), channel_id=1, source_target_pairs={{160,0},{168,8},{176,16},{184,24},{128,32},{136,40},{144,48},{152,... | collective-permute-start | bytes 110600 | tf_op jit(solution)/shard_map/ppermute | solution.py:293
  86.0 19.9 %collective-permute-start.31 = (f32[512,128]{1,0:T(8,128)S(1)}, f32[512,128]{1,0:T(8,128)S(1)}, u32[]{:S(2)}, u32[]{:S(2)}) collective-permute-start(f32[512,128]{1,0:T(8,128)S(1)} %get-tuple-element.46.refs_1_), channel_id=1, source_target_pairs={{7,0},{0,1},{1,2},{2,3},{3,4},{4,5},{5,6},{6,7},{15,8},{8,9},{9,10... | collective-permute-start | bytes 786440 | tf_op jit(solution)/shard_map/ppermute | solution.py:326
  91.2 7.3 %collective-permute-start.28 = (f32[72,128]{1,0:T(8,128)S(1)}, f32[72,128]{1,0:T(8,128)S(1)}, u32[]{:S(2)}, u32[]{:S(2)}) collective-permute-start(f32[72,128]{1,0:T(8,128)S(1)} %add_add_fusion.mine_ref), channel_id=1, source_target_pairs={{7,0},{0,1},{1,2},{2,3},{3,4},{4,5},{5,6},{6,7},{15,8},{8,9},{9,10... | collective-permute-start | bytes 110600 | tf_op jit(solution)/shard_map/ppermute | solution.py:326
  91.5 11.5 %collective-permute-start.30 = (f32[72,128]{1,0:T(8,128)S(1)}, f32[72,128]{1,0:T(8,128)S(1)}, u32[]{:S(2)}, u32[]{:S(2)}) collective-permute-start(f32[72,128]{1,0:T(8,128)S(1)} %add_add_fusion.mine_ref), channel_id=1, source_target_pairs={{8,0},{0,8},{24,16},{16,24},{40,32},{32,40},{56,48},{48,56},{72,64... | collective-permute-start | bytes 110600 | tf_op jit(solution)/shard_map/ppermute | solution.py:293
  98.5 7.4 %collective-permute-start.29 = (f32[72,128]{1,0:T(8,128)S(1)}, f32[72,128]{1,0:T(8,128)S(1)}, u32[]{:S(2)}, u32[]{:S(2)}) collective-permute-start(f32[72,128]{1,0:T(8,128)S(1)} %collective-permute-done.28.mine_ref), channel_id=1, source_target_pairs={{8,0},{0,8},{24,16},{16,24},{40,32},{32,40},{56,48},{48,56},{72,64... | collective-permute-start | bytes 110600 | tf_op jit(solution)/shard_map/ppermute | solution.py:293

commit v5 on v4

--- a/solution.py
+++ b/solution.py
@@ -121,23 +121,12 @@
     return jnp.sum(block * block, 0, keepdims=True)
 
 
-def load_kernel(core_ref, panel_ref, near_ref, mine_ref, other_ref, cross_ref, sems):
-    rows, n = near_ref.shape[0], near_ref.shape[1] // 2
-    size = rows // CHUNKS
-    parts = [slice(i * size, (i + 1) * size) for i in range(CHUNKS)]
-    copies = [
-        pltpu.make_async_copy(panel_ref.at[part], near_ref.at[part], sems.at[i])
-        for i, part in enumerate(parts)
-    ]
-    for copy in copies:
-        copy.start()
-    sums = []
-    for copy, part in zip(copies, parts):
-        copy.wait()
-        a, b = near_ref[part, :n], near_ref[part, n:]
-        sums.append((squares(a), squares(b), cross_of(a, b)))
-    diag_a, diag_b, cross = (sum(terms[1:], terms[0]) for terms in zip(*sums))
-    message(diag_a, diag_b, cross, core_ref[0], cross_ref, mine_ref, other_ref)
+def load_kernel(core_ref, panel_ref, near_ref, mine_ref, other_ref, cross_ref, sem):
+    copy = pltpu.make_async_copy(panel_ref, near_ref, sem)
+    copy.start()
+    copy.wait()
+    a, b = both_blocks([near_ref])
+    message(squares(a), squares(b), cross_of(a, b), core_ref[0], cross_ref, mine_ref, other_ref)
 
 
 def cosines_of(core_ref, mine_ref, other_ref):
@@ -243,7 +232,7 @@
         load_kernel,
         out_shape=[pltpu.VMEM(panel.shape, F32), *halves],
         in_specs=[pl.BlockSpec(memory_space=pltpu.SMEM), pl.BlockSpec(memory_space=pl.ANY)],
-        scratch_shapes=[*scratch, pltpu.SemaphoreType.DMA((CHUNKS,))],
+        scratch_shapes=[*scratch, pltpu.SemaphoreType.DMA],
         name="load",
     )(core, panel)
 
@@ -331,8 +320,8 @@
     core = (lax.axis_index("row") & 1).astype(jnp.int32).reshape(1)
     for step in range(STEPS):
         if step == 0:
-            before = [shifted(panel)]
             own, mine, other = load(core, panel, n)
+            before = [shifted(own)]
             own = [own]
         else:
             second = shifted(b)

time: 109 us -> 105 us (0.963)
  waiting for transfers between devices: 32.4 us -> 28.8 us
    ppermute x26, waiting for transfers between devices: 24.4 us -> 19.1 us  [from_row(): return lax.ppermute(x, 'row', route)]
    ppermute x6, waiting for transfers between devices: 7.98 us -> 9.7 us  [shifted(): return lax.ppermute(block, 'pair', route)]
  transfers between devices with their start and end apart: 32 -> 32, of which waited for: 19 -> 20; matrix products, arithmetic and copies ran while one was open for 0% -> 0% of each run, Pallas kernels for 10% -> 9%
where the time goes in v5:
time: 105 us
  starting transfers between devices  56 us (53%)
  waiting for transfers between devices  28.8 us (27%)
  Pallas kernels  19.3 us (18%)
    ppermute x26, starting transfers between devices, from_row(): return lax.ppermute(x, 'row', route)  50.3 us
    ppermute x26, waiting for transfers between devices, from_row(): return lax.ppermute(x, 'row', route)  19.1 us
    pallas_call x11, Pallas kernels, vmem_call(): pl.pallas_call(kernel, out_shape=shapes, in_specs=specs, scratch_shapes=s...  18 us
    ppermute x6, waiting for transfers between devices, shifted(): return lax.ppermute(block, 'pair', route)  9.7 us
    ppermute x6, starting transfers between devices, shifted(): return lax.ppermute(block, 'pair', route)  5.63 us
  transfers between devices with their start and end apart: 32, of which 20 were waited for; matrix products, arithmetic and copies ran while one was open for 0% of the time, Pallas kernels for 9%

profile of v5, /device:TPU:1, one launch (start us, length us, event | category | flops | bytes accessed | tf_op | source)
XLA Modules:
  0.0 104.6 jit_solution(14982776716661147923)
XLA Ops:
  0.0 1.3 %load.1 = (f32[512,256]{1,0:T(8,128)S(1)}, f32[72,128]{1,0:T(8,128)S(1)}, f32[72,128]{1,0:T(8,128)S(1)}) custom-call(s32[1]{0:T(128)} %bitcast.core_ref, f32[512,256]{1,0:T(8,128)} %panel_ref.1), custom_call_target="tpu_custom_call" | custom-call | tf_op jit(solution)/shard_map/load/pallas_call | solution.py:231
  1.4 3.8 %collective-permute-start.9 = (f32[512,256]{1,0:T(8,128)S(1)}, f32[512,256]{1,0:T(8,128)S(1)}, u32[]{:S(2)}, u32[]{:S(2)}) collective-permute-start(f32[512,256]{1,0:T(8,128)S(1)} %get-tuple-element.32.refs_0_), channel_id=1, source_target_pairs={{7,0},{0,1},{1,2},{2,3},{3,4},{4,5},{5,6},{6,7},{15,8},{8,9},{9,10... | collective-permute-start | bytes 1572872 | tf_op jit(solution)/shard_map/ppermute | solution.py:315
  7.0 1.6 %collective-permute-start.1 = (f32[72,128]{1,0:T(8,128)S(1)}, f32[72,128]{1,0:T(8,128)S(1)}, u32[]{:S(2)}, u32[]{:S(2)}) collective-permute-start(f32[72,128]{1,0:T(8,128)S(1)} %add.60), channel_id=1, source_target_pairs={{32,0},{40,8},{48,16},{56,24},{0,32},{8,40},{16,48},{24,56},{96,64... | collective-permute-start | bytes 110600 | tf_op jit(solution)/shard_map/ppermute | solution.py:282
  8.6 1.3 %collective-permute-done.1 = f32[72,128]{1,0:T(8,128)S(1)} collective-permute-done((f32[72,128]{1,0:T(8,128)S(1)}, f32[72,128]{1,0:T(8,128)S(1)}, u32[]{:S(2)}, u32[]{:S(2)}) %collective-permute-start.1) | collective-permute-done | bytes 36896 | tf_op jit(solution)/shard_map/ppermute | solution.py:282
  10.0 6.6 %collective-permute-start.4 = (f32[72,128]{1,0:T(8,128)S(1)}, f32[72,128]{1,0:T(8,128)S(1)}, u32[]{:S(2)}, u32[]{:S(2)}) collective-permute-start(f32[72,128]{1,0:T(8,128)S(1)} %add.61), channel_id=1, source_target_pairs={{160,0},{168,8},{176,16},{184,24},{128,32},{136,40},{144,48},{152,... | collective-permute-start | bytes 110600 | tf_op jit(solution)/shard_map/ppermute | solution.py:282
  16.8 2.8 %collective-permute-start.2 = (f32[72,128]{1,0:T(8,128)S(1)}, f32[72,128]{1,0:T(8,128)S(1)}, u32[]{:S(2)}, u32[]{:S(2)}) collective-permute-start(f32[72,128]{1,0:T(8,128)S(1)} %add.61), channel_id=1, source_target_pairs={{224,0},{232,8},{240,16},{248,24},{64,32},{72,40},{80,48},{88,56},... | collective-permute-start | bytes 110600 | tf_op jit(solution)/shard_map/ppermute | solution.py:282
  21.6 2.7 %collective-permute-done.5 = f32[72,128]{1,0:T(8,128)S(1)} collective-permute-done((f32[72,128]{1,0:T(8,128)S(1)}, f32[72,128]{1,0:T(8,128)S(1)}, u32[]{:S(2)}, u32[]{:S(2)}) %collective-permute-start.5) | collective-permute-done | bytes 36896 | tf_op jit(solution)/shard_map/ppermute | solution.py:282
  24.3 1.4 %collective-permute-start.6 = (f32[72,128]{1,0:T(8,128)S(1)}, f32[72,128]{1,0:T(8,128)S(1)}, u32[]{:S(2)}, u32[]{:S(2)}) collective-permute-start(f32[72,128]{1,0:T(8,128)S(1)} %add.65.mine_ref), channel_id=1, source_target_pairs={{7,0},{0,1},{1,2},{2,3},{3,4},{4,5},{5,6},{6,7},{15,8},{8,9},{9,10... | collective-permute-start | bytes 110600 | tf_op jit(solution)/shard_map/ppermute | solution.py:315
  25.8 3.8 %collective-permute-start.8 = (f32[72,128]{1,0:T(8,128)S(1)}, f32[72,128]{1,0:T(8,128)S(1)}, u32[]{:S(2)}, u32[]{:S(2)}) collective-permute-start(f32[72,128]{1,0:T(8,128)S(1)} %add.65.mine_ref), channel_id=1, source_target_pairs={{8,0},{0,8},{24,16},{16,24},{40,32},{32,40},{56,48},{48,56},{72,64... | collective-permute-start | bytes 110600 | tf_op jit(solution)/shard_map/ppermute | solution.py:282
  29.5 1.2 %collective-permute-done.6.mine_ref = f32[72,128]{1,0:T(8,128)S(1)} collective-permute-done((f32[72,128]{1,0:T(8,128)S(1)}, f32[72,128]{1,0:T(8,128)S(1)}, u32[]{:S(2)}, u32[]{:S(2)}) %collective-permute-start.6) | collective-permute-done | bytes 36896 | tf_op jit(solution)/shard_map/ppermute | solution.py:315
  30.8 4.9 %collective-permute-start.7 = (f32[72,128]{1,0:T(8,128)S(1)}, f32[72,128]{1,0:T(8,128)S(1)}, u32[]{:S(2)}, u32[]{:S(2)}) collective-permute-start(f32[72,128]{1,0:T(8,128)S(1)} %collective-permute-done.6.mine_ref), channel_id=1, source_target_pairs={{8,0},{0,8},{24,16},{16,24},{40,32},{32,40},{56,48},{48,56},{72,64... | collective-permute-start | bytes 110600 | tf_op jit(solution)/shard_map/ppermute | solution.py:282
  35.7 1.8 %shard_map.17 = (f32[128,128]{1,0:T(8,128)S(1)}, f32[128,128]{1,0:T(8,128)S(1)}, f32[128,128]{1,0:T(8,128)S(1)}) custom-call(s32[1]{0:T(128)} %bitcast.core_ref, f32[72,128]{1,0:T(8,128)S(1)} %add.65.mine_ref, f32[72,128]{1,0:T(8,128)S(1)} %collective-permute-done.8.other_ref), custom_call_target="tpu_custom_call" | custom-call | tf_op jit(solution)/shard_map/pallas_call | solution.py:219
  38.5 2.8 %shard_map.19 = (f32[512,128]{1,0:T(8,128)S(1)}, f32[128,128]{1,0:T(8,128)S(1)}, f32[128,128]{1,0:T(8,128)S(1)}, f32[72,128]{1,0:T(8,128)S(1)}, f32[72,128]{1,0:T(8,128)S(1)}) custom-call(s32[1]{0:T(128)} %bitcast.core_ref, f32[72,128]{1,0:T(8,128)S(1)} %collective-permute-done.6.mine_ref, f32[72,128]{1,0:T(8,128)S(1)} %collective-permute-done.7.other_ref, ...), custom_call_target="tpu_custom_call" | custom-call | tf_op jit(solution)/shard_map/pallas_call | solution.py:219
  47.7 3.3 %collective-permute-start.16 = (f32[72,128]{1,0:T(8,128)S(1)}, f32[72,128]{1,0:T(8,128)S(1)}, u32[]{:S(2)}, u32[]{:S(2)}) collective-permute-start(f32[72,128]{1,0:T(8,128)S(1)} %add_add_fusion.3), channel_id=1, source_target_pairs={{160,0},{168,8},{176,16},{184,24},{128,32},{136,40},{144,48},{152,... | collective-permute-start | bytes 110600 | tf_op jit(solution)/shard_map/ppermute | solution.py:282
  51.8 1.8 %collective-permute-start.14 = (f32[72,128]{1,0:T(8,128)S(1)}, f32[72,128]{1,0:T(8,128)S(1)}, u32[]{:S(2)}, u32[]{:S(2)}) collective-permute-start(f32[72,128]{1,0:T(8,128)S(1)} %add_add_fusion.3), channel_id=1, source_target_pairs={{224,0},{232,8},{240,16},{248,24},{64,32},{72,40},{80,48},{88,56},... | collective-permute-start | bytes 110600 | tf_op jit(solution)/shard_map/ppermute | solution.py:282
  53.6 1.5 %collective-permute-done.15 = f32[72,128]{1,0:T(8,128)S(1)} collective-permute-done((f32[72,128]{1,0:T(8,128)S(1)}, f32[72,128]{1,0:T(8,128)S(1)}, u32[]{:S(2)}, u32[]{:S(2)}) %collective-permute-start.15) | collective-permute-done | bytes 36896 | tf_op jit(solution)/shard_map/ppermute | solution.py:282
  55.1 1.3 %collective-permute-done.14 = f32[72,128]{1,0:T(8,128)S(1)} collective-permute-done((f32[72,128]{1,0:T(8,128)S(1)}, f32[72,128]{1,0:T(8,128)S(1)}, u32[]{:S(2)}, u32[]{:S(2)}) %collective-permute-start.14) | collective-permute-done | bytes 36896 | tf_op jit(solution)/shard_map/ppermute | solution.py:282
  56.5 2.8 %collective-permute-start.19 = (f32[72,128]{1,0:T(8,128)S(1)}, f32[72,128]{1,0:T(8,128)S(1)}, u32[]{:S(2)}, u32[]{:S(2)}) collective-permute-start(f32[72,128]{1,0:T(8,128)S(1)} %add_add_fusion.2.mine_ref), channel_id=1, source_target_pairs={{8,0},{0,8},{24,16},{16,24},{40,32},{32,40},{56,48},{48,56},{72,64... | collective-permute-start | bytes 110600 | tf_op jit(solution)/shard_map/ppermute | solution.py:282
  59.3 4.4 %collective-permute-done.17.mine_ref = f32[72,128]{1,0:T(8,128)S(1)} collective-permute-done((f32[72,128]{1,0:T(8,128)S(1)}, f32[72,128]{1,0:T(8,128)S(1)}, u32[]{:S(2)}, u32[]{:S(2)}) %collective-permute-start.17) | collective-permute-done | bytes 36896 | tf_op jit(solution)/shard_map/ppermute | solution.py:315
  63.7 3.1 %collective-permute-start.18 = (f32[72,128]{1,0:T(8,128)S(1)}, f32[72,128]{1,0:T(8,128)S(1)}, u32[]{:S(2)}, u32[]{:S(2)}) collective-permute-start(f32[72,128]{1,0:T(8,128)S(1)} %collective-permute-done.17.mine_ref), channel_id=1, source_target_pairs={{8,0},{0,8},{24,16},{16,24},{40,32},{32,40},{56,48},{48,56},{72,64... | collective-permute-start | bytes 110600 | tf_op jit(solution)/shard_map/ppermute | solution.py:282
  67.2 1.8 %shard_map.20 = (f32[128,128]{1,0:T(8,128)S(1)}, f32[128,128]{1,0:T(8,128)S(1)}, f32[128,128]{1,0:T(8,128)S(1)}) custom-call(s32[1]{0:T(128)} %bitcast.core_ref, f32[72,128]{1,0:T(8,128)S(1)} %add_add_fusion.2.mine_ref, f32[72,128]{1,0:T(8,128)S(1)} %collective-permute-done.19.other_ref), custom_call_target="tpu_custom_call" | custom-call | tf_op jit(solution)/shard_map/pallas_call | solution.py:219
  70.0 2.8 %shard_map.23 = (f32[512,128]{1,0:T(8,128)S(1)}, f32[128,128]{1,0:T(8,128)S(1)}, f32[128,128]{1,0:T(8,128)S(1)}, f32[72,128]{1,0:T(8,128)S(1)}, f32[72,128]{1,0:T(8,128)S(1)}) custom-call(s32[1]{0:T(128)} %bitcast.core_ref, f32[72,128]{1,0:T(8,128)S(1)} %collective-permute-done.17.mine_ref, f32[72,128]{1,0:T(8,128)S(1)} %collective-permute-done.18.other_ref, ...), custom_call_target="tpu_custom_call" | custom-call | tf_op jit(solution)/shard_map/pallas_call | solution.py:219
  75.5 1.3 %collective-permute-start.22 = (f32[72,128]{1,0:T(8,128)S(1)}, f32[72,128]{1,0:T(8,128)S(1)}, u32[]{:S(2)}, u32[]{:S(2)}) collective-permute-start(f32[72,128]{1,0:T(8,128)S(1)} %add.73), channel_id=1, source_target_pairs={{32,0},{40,8},{48,16},{56,24},{0,32},{8,40},{16,48},{24,56},{96,64... | collective-permute-start | bytes 110600 | tf_op jit(solution)/shard_map/ppermute | solution.py:282
  78.6 2.9 %collective-permute-start.27 = (f32[72,128]{1,0:T(8,128)S(1)}, f32[72,128]{1,0:T(8,128)S(1)}, u32[]{:S(2)}, u32[]{:S(2)}) collective-permute-start(f32[72,128]{1,0:T(8,128)S(1)} %add_add_fusion.1), channel_id=1, source_target_pairs={{160,0},{168,8},{176,16},{184,24},{128,32},{136,40},{144,48},{152,... | collective-permute-start | bytes 110600 | tf_op jit(solution)/shard_map/ppermute | solution.py:282
  81.5 1.2 %collective-permute-start.26 = (f32[72,128]{1,0:T(8,128)S(1)}, f32[72,128]{1,0:T(8,128)S(1)}, u32[]{:S(2)}, u32[]{:S(2)}) collective-permute-start(f32[72,128]{1,0:T(8,128)S(1)} %add_add_fusion.1), channel_id=1, source_target_pairs={{64,0},{72,8},{80,16},{88,24},{224,32},{232,40},{240,48},{248,56},... | collective-permute-start | bytes 110600 | tf_op jit(solution)/shard_map/ppermute | solution.py:282
  82.7 1.3 %collective-permute-start.25 = (f32[72,128]{1,0:T(8,128)S(1)}, f32[72,128]{1,0:T(8,128)S(1)}, u32[]{:S(2)}, u32[]{:S(2)}) collective-permute-start(f32[72,128]{1,0:T(8,128)S(1)} %add_add_fusion.1), channel_id=1, source_target_pairs={{224,0},{232,8},{240,16},{248,24},{64,32},{72,40},{80,48},{88,56},... | collective-permute-start | bytes 110600 | tf_op jit(solution)/shard_map/ppermute | solution.py:282
  84.5 1.4 %collective-permute-done.26 = f32[72,128]{1,0:T(8,128)S(1)} collective-permute-done((f32[72,128]{1,0:T(8,128)S(1)}, f32[72,128]{1,0:T(8,128)S(1)}, u32[]{:S(2)}, u32[]{:S(2)}) %collective-permute-start.26) | collective-permute-done | bytes 36896 | tf_op jit(solution)/shard_map/ppermute | solution.py:282
  87.4 3.0 %collective-permute-start.30 = (f32[72,128]{1,0:T(8,128)S(1)}, f32[72,128]{1,0:T(8,128)S(1)}, u32[]{:S(2)}, u32[]{:S(2)}) collective-permute-start(f32[72,128]{1,0:T(8,128)S(1)} %add_add_fusion.mine_ref), channel_id=1, source_target_pairs={{8,0},{0,8},{24,16},{16,24},{40,32},{32,40},{56,48},{48,56},{72,64... | collective-permute-start | bytes 110600 | tf_op jit(solution)/shard_map/ppermute | solution.py:282
  90.4 4.1 %collective-permute-done.28.mine_ref = f32[72,128]{1,0:T(8,128)S(1)} collective-permute-done((f32[72,128]{1,0:T(8,128)S(1)}, f32[72,128]{1,0:T(8,128)S(1)}, u32[]{:S(2)}, u32[]{:S(2)}) %collective-permute-start.28) | collective-permute-done | bytes 36896 | tf_op jit(solution)/shard_map/ppermute | solution.py:315
  94.5 3.4 %collective-permute-start.29 = (f32[72,128]{1,0:T(8,128)S(1)}, f32[72,128]{1,0:T(8,128)S(1)}, u32[]{:S(2)}, u32[]{:S(2)}) collective-permute-start(f32[72,128]{1,0:T(8,128)S(1)} %collective-permute-done.28.mine_ref), channel_id=1, source_target_pairs={{8,0},{0,8},{24,16},{16,24},{40,32},{32,40},{56,48},{48,56},{72,64... | collective-permute-start | bytes 110600 | tf_op jit(solution)/shard_map/ppermute | solution.py:282
  98.3 1.8 %shard_map.24 = (f32[128,128]{1,0:T(8,128)S(1)}, f32[128,128]{1,0:T(8,128)S(1)}, f32[128,128]{1,0:T(8,128)S(1)}) custom-call(s32[1]{0:T(128)} %bitcast.core_ref, f32[72,128]{1,0:T(8,128)S(1)} %add_add_fusion.mine_ref, f32[72,128]{1,0:T(8,128)S(1)} %collective-permute-done.30.other_ref), custom_call_target="tpu_custom_call" | custom-call | tf_op jit(solution)/shard_map/pallas_call | solution.py:219
  101.1 3.3 %shard_map.27 = f32[512,256]{1,0:T(8,128)} custom-call(s32[1]{0:T(128)} %bitcast.core_ref, f32[72,128]{1,0:T(8,128)S(1)} %collective-permute-done.28.mine_ref, f32[72,128]{1,0:T(8,128)S(1)} %collective-permute-done.29.other_ref, f32[512,128]{1,0:T(8,128)S(1)} %shard_map.25.own_ref, f32[512,128]{1,0:T(8,128)S(1)} %shard_map.26.refs_0_, ...), custom_call_target="tpu_custom_call" | custom-call | tf_op jit(solution)/shard_map/pallas_call | solution.py:219
  (54 shorter events, 21.4 us)
Async XLA Ops:
  1.4 37.1 %collective-permute-start.9 = (f32[512,256]{1,0:T(8,128)S(1)}, f32[512,256]{1,0:T(8,128)S(1)}, u32[]{:S(2)}, u32[]{:S(2)}) collective-permute-start(f32[512,256]{1,0:T(8,128)S(1)} %get-tuple-element.32.refs_0_), channel_id=1, source_target_pairs={{7,0},{0,1},{1,2},{2,3},{3,4},{4,5},{5,6},{6,7},{15,8},{8,9},{9,10... | collective-permute-start | bytes 1572872 | tf_op jit(solution)/shard_map/ppermute | solution.py:315
  5.2 1.8 %collective-permute-start = (f32[72,128]{1,0:T(8,128)S(1)}, f32[72,128]{1,0:T(8,128)S(1)}, u32[]{:S(2)}, u32[]{:S(2)}) collective-permute-start(f32[72,128]{1,0:T(8,128)S(1)} %get-tuple-element.28), channel_id=1, source_target_pairs={{8,0},{0,8},{24,16},{16,24},{40,32},{32,40},{56,48},{48,56},{72,64... | collective-permute-start | bytes 110600 | tf_op jit(solution)/shard_map/ppermute | solution.py:282
  7.0 3.0 %collective-permute-start.1 = (f32[72,128]{1,0:T(8,128)S(1)}, f32[72,128]{1,0:T(8,128)S(1)}, u32[]{:S(2)}, u32[]{:S(2)}) collective-permute-start(f32[72,128]{1,0:T(8,128)S(1)} %add.60), channel_id=1, source_target_pairs={{32,0},{40,8},{48,16},{56,24},{0,32},{8,40},{16,48},{24,56},{96,64... | collective-permute-start | bytes 110600 | tf_op jit(solution)/shard_map/ppermute | solution.py:282
  10.0 9.7 %collective-permute-start.4 = (f32[72,128]{1,0:T(8,128)S(1)}, f32[72,128]{1,0:T(8,128)S(1)}, u32[]{:S(2)}, u32[]{:S(2)}) collective-permute-start(f32[72,128]{1,0:T(8,128)S(1)} %add.61), channel_id=1, source_target_pairs={{160,0},{168,8},{176,16},{184,24},{128,32},{136,40},{144,48},{152,... | collective-permute-start | bytes 110600 | tf_op jit(solution)/shard_map/ppermute | solution.py:282
  16.6 3.8 %collective-permute-start.3 = (f32[72,128]{1,0:T(8,128)S(1)}, f32[72,128]{1,0:T(8,128)S(1)}, u32[]{:S(2)}, u32[]{:S(2)}) collective-permute-start(f32[72,128]{1,0:T(8,128)S(1)} %add.61), channel_id=1, source_target_pairs={{64,0},{72,8},{80,16},{88,24},{224,32},{232,40},{240,48},{248,56},... | collective-permute-start | bytes 110600 | tf_op jit(solution)/shard_map/ppermute | solution.py:282
  16.8 4.6 %collective-permute-start.2 = (f32[72,128]{1,0:T(8,128)S(1)}, f32[72,128]{1,0:T(8,128)S(1)}, u32[]{:S(2)}, u32[]{:S(2)}) collective-permute-start(f32[72,128]{1,0:T(8,128)S(1)} %add.61), channel_id=1, source_target_pairs={{224,0},{232,8},{240,16},{248,24},{64,32},{72,40},{80,48},{88,56},... | collective-permute-start | bytes 110600 | tf_op jit(solution)/shard_map/ppermute | solution.py:282
  21.4 2.9 %collective-permute-start.5 = (f32[72,128]{1,0:T(8,128)S(1)}, f32[72,128]{1,0:T(8,128)S(1)}, u32[]{:S(2)}, u32[]{:S(2)}) collective-permute-start(f32[72,128]{1,0:T(8,128)S(1)} %add_add_fusion.4), channel_id=1, source_target_pairs={{16,0},{24,8},{0,16},{8,24},{48,32},{56,40},{32,48},{40,56},{80,64... | collective-permute-start | bytes 110600 | tf_op jit(solution)/shard_map/ppermute | solution.py:282
  24.3 6.4 %collective-permute-start.6 = (f32[72,128]{1,0:T(8,128)S(1)}, f32[72,128]{1,0:T(8,128)S(1)}, u32[]{:S(2)}, u32[]{:S(2)}) collective-permute-start(f32[72,128]{1,0:T(8,128)S(1)} %add.65.mine_ref), channel_id=1, source_target_pairs={{7,0},{0,1},{1,2},{2,3},{3,4},{4,5},{5,6},{6,7},{15,8},{8,9},{9,10... | collective-permute-start | bytes 110600 | tf_op jit(solution)/shard_map/ppermute | solution.py:315
  25.8 9.9 %collective-permute-start.8 = (f32[72,128]{1,0:T(8,128)S(1)}, f32[72,128]{1,0:T(8,128)S(1)}, u32[]{:S(2)}, u32[]{:S(2)}) collective-permute-start(f32[72,128]{1,0:T(8,128)S(1)} %add.65.mine_ref), channel_id=1, source_target_pairs={{8,0},{0,8},{24,16},{16,24},{40,32},{32,40},{56,48},{48,56},{72,64... | collective-permute-start | bytes 110600 | tf_op jit(solution)/shard_map/ppermute | solution.py:282
  30.8 7.7 %collective-permute-start.7 = (f32[72,128]{1,0:T(8,128)S(1)}, f32[72,128]{1,0:T(8,128)S(1)}, u32[]{:S(2)}, u32[]{:S(2)}) collective-permute-start(f32[72,128]{1,0:T(8,128)S(1)} %collective-permute-done.6.mine_ref), channel_id=1, source_target_pairs={{8,0},{0,8},{24,16},{16,24},{40,32},{32,40},{56,48},{48,56},{72,64... | collective-permute-start | bytes 110600 | tf_op jit(solution)/shard_map/ppermute | solution.py:282
  41.3 1.3 %collective-permute-start.10 = (f32[72,128]{1,0:T(8,128)S(1)}, f32[72,128]{1,0:T(8,128)S(1)}, u32[]{:S(2)}, u32[]{:S(2)}) collective-permute-start(f32[72,128]{1,0:T(8,128)S(1)} %get-tuple-element.34), channel_id=1, source_target_pairs={{8,0},{0,8},{24,16},{16,24},{40,32},{32,40},{56,48},{48,56},{72,64... | collective-permute-start | bytes 110600 | tf_op jit(solution)/shard_map/ppermute | solution.py:282
  42.6 3.7 %collective-permute-start.13 = (f32[72,128]{1,0:T(8,128)S(1)}, f32[72,128]{1,0:T(8,128)S(1)}, u32[]{:S(2)}, u32[]{:S(2)}) collective-permute-start(f32[72,128]{1,0:T(8,128)S(1)} %add.66), channel_id=1, source_target_pairs={{48,0},{56,8},{32,16},{40,24},{16,32},{24,40},{0,48},{8,56},{112,6... | collective-permute-start | bytes 110600 | tf_op jit(solution)/shard_map/ppermute | solution.py:282
  43.5 4.0 %collective-permute-start.12 = (f32[72,128]{1,0:T(8,128)S(1)}, f32[72,128]{1,0:T(8,128)S(1)}, u32[]{:S(2)}, u32[]{:S(2)}) collective-permute-start(f32[72,128]{1,0:T(8,128)S(1)} %add.66), channel_id=1, source_target_pairs={{16,0},{24,8},{0,16},{8,24},{48,32},{56,40},{32,48},{40,56},{80,64... | collective-permute-start | bytes 110600 | tf_op jit(solution)/shard_map/ppermute | solution.py:282
  44.6 3.1 %collective-permute-start.11 = (f32[72,128]{1,0:T(8,128)S(1)}, f32[72,128]{1,0:T(8,128)S(1)}, u32[]{:S(2)}, u32[]{:S(2)}) collective-permute-start(f32[72,128]{1,0:T(8,128)S(1)} %add.66), channel_id=1, source_target_pairs={{32,0},{40,8},{48,16},{56,24},{0,32},{8,40},{16,48},{24,56},{96,64... | collective-permute-start | bytes 110600 | tf_op jit(solution)/shard_map/ppermute | solution.py:282
  47.7 5.9 %collective-permute-start.16 = (f32[72,128]{1,0:T(8,128)S(1)}, f32[72,128]{1,0:T(8,128)S(1)}, u32[]{:S(2)}, u32[]{:S(2)}) collective-permute-start(f32[72,128]{1,0:T(8,128)S(1)} %add_add_fusion.3), channel_id=1, source_target_pairs={{160,0},{168,8},{176,16},{184,24},{128,32},{136,40},{144,48},{152,... | collective-permute-start | bytes 110600 | tf_op jit(solution)/shard_map/ppermute | solution.py:282
  51.0 4.1 %collective-permute-start.15 = (f32[72,128]{1,0:T(8,128)S(1)}, f32[72,128]{1,0:T(8,128)S(1)}, u32[]{:S(2)}, u32[]{:S(2)}) collective-permute-start(f32[72,128]{1,0:T(8,128)S(1)} %add_add_fusion.3), channel_id=1, source_target_pairs={{64,0},{72,8},{80,16},{88,24},{224,32},{232,40},{240,48},{248,56},... | collective-permute-start | bytes 110600 | tf_op jit(solution)/shard_map/ppermute | solution.py:282
  51.8 4.6 %collective-permute-start.14 = (f32[72,128]{1,0:T(8,128)S(1)}, f32[72,128]{1,0:T(8,128)S(1)}, u32[]{:S(2)}, u32[]{:S(2)}) collective-permute-start(f32[72,128]{1,0:T(8,128)S(1)} %add_add_fusion.3), channel_id=1, source_target_pairs={{224,0},{232,8},{240,16},{248,24},{64,32},{72,40},{80,48},{88,56},... | collective-permute-start | bytes 110600 | tf_op jit(solution)/shard_map/ppermute | solution.py:282
  53.6 16.4 %collective-permute-start.20 = (f32[512,128]{1,0:T(8,128)S(1)}, f32[512,128]{1,0:T(8,128)S(1)}, u32[]{:S(2)}, u32[]{:S(2)}) collective-permute-start(f32[512,128]{1,0:T(8,128)S(1)} %get-tuple-element.38.refs_1_), channel_id=1, source_target_pairs={{7,0},{0,1},{1,2},{2,3},{3,4},{4,5},{5,6},{6,7},{15,8},{8,9},{9,10... | collective-permute-start | bytes 786440 | tf_op jit(solution)/shard_map/ppermute | solution.py:315
  56.4 7.3 %collective-permute-start.17 = (f32[72,128]{1,0:T(8,128)S(1)}, f32[72,128]{1,0:T(8,128)S(1)}, u32[]{:S(2)}, u32[]{:S(2)}) collective-permute-start(f32[72,128]{1,0:T(8,128)S(1)} %add_add_fusion.2.mine_ref), channel_id=1, source_target_pairs={{7,0},{0,1},{1,2},{2,3},{3,4},{4,5},{5,6},{6,7},{15,8},{8,9},{9,10... | collective-permute-start | bytes 110600 | tf_op jit(solution)/shard_map/ppermute | solution.py:315
  56.5 10.7 %collective-permute-start.19 = (f32[72,128]{1,0:T(8,128)S(1)}, f32[72,128]{1,0:T(8,128)S(1)}, u32[]{:S(2)}, u32[]{:S(2)}) collective-permute-start(f32[72,128]{1,0:T(8,128)S(1)} %add_add_fusion.2.mine_ref), channel_id=1, source_target_pairs={{8,0},{0,8},{24,16},{16,24},{40,32},{32,40},{56,48},{48,56},{72,64... | collective-permute-start | bytes 110600 | tf_op jit(solution)/shard_map/ppermute | solution.py:282
  63.7 6.3 %collective-permute-start.18 = (f32[72,128]{1,0:T(8,128)S(1)}, f32[72,128]{1,0:T(8,128)S(1)}, u32[]{:S(2)}, u32[]{:S(2)}) collective-permute-start(f32[72,128]{1,0:T(8,128)S(1)} %collective-permute-done.17.mine_ref), channel_id=1, source_target_pairs={{8,0},{0,8},{24,16},{16,24},{40,32},{32,40},{56,48},{48,56},{72,64... | collective-permute-start | bytes 110600 | tf_op jit(solution)/shard_map/ppermute | solution.py:282
  72.8 1.3 %collective-permute-start.21 = (f32[72,128]{1,0:T(8,128)S(1)}, f32[72,128]{1,0:T(8,128)S(1)}, u32[]{:S(2)}, u32[]{:S(2)}) collective-permute-start(f32[72,128]{1,0:T(8,128)S(1)} %get-tuple-element.42), channel_id=1, source_target_pairs={{8,0},{0,8},{24,16},{16,24},{40,32},{32,40},{56,48},{48,56},{72,64... | collective-permute-start | bytes 110600 | tf_op jit(solution)/shard_map/ppermute | solution.py:282
  74.1 3.7 %collective-permute-start.24 = (f32[72,128]{1,0:T(8,128)S(1)}, f32[72,128]{1,0:T(8,128)S(1)}, u32[]{:S(2)}, u32[]{:S(2)}) collective-permute-start(f32[72,128]{1,0:T(8,128)S(1)} %add.73), channel_id=1, source_target_pairs={{48,0},{56,8},{32,16},{40,24},{16,32},{24,40},{0,48},{8,56},{112,6... | collective-permute-start | bytes 110600 | tf_op jit(solution)/shard_map/ppermute | solution.py:282
  74.4 3.4 %collective-permute-start.23 = (f32[72,128]{1,0:T(8,128)S(1)}, f32[72,128]{1,0:T(8,128)S(1)}, u32[]{:S(2)}, u32[]{:S(2)}) collective-permute-start(f32[72,128]{1,0:T(8,128)S(1)} %add.73), channel_id=1, source_target_pairs={{16,0},{24,8},{0,16},{8,24},{48,32},{56,40},{32,48},{40,56},{80,64... | collective-permute-start | bytes 110600 | tf_op jit(solution)/shard_map/ppermute | solution.py:282
  75.5 3.1 %collective-permute-start.22 = (f32[72,128]{1,0:T(8,128)S(1)}, f32[72,128]{1,0:T(8,128)S(1)}, u32[]{:S(2)}, u32[]{:S(2)}) collective-permute-start(f32[72,128]{1,0:T(8,128)S(1)} %add.73), channel_id=1, source_target_pairs={{32,0},{40,8},{48,16},{56,24},{0,32},{8,40},{16,48},{24,56},{96,64... | collective-permute-start | bytes 110600 | tf_op jit(solution)/shard_map/ppermute | solution.py:282
  78.6 5.9 %collective-permute-start.27 = (f32[72,128]{1,0:T(8,128)S(1)}, f32[72,128]{1,0:T(8,128)S(1)}, u32[]{:S(2)}, u32[]{:S(2)}) collective-permute-start(f32[72,128]{1,0:T(8,128)S(1)} %add_add_fusion.1), channel_id=1, source_target_pairs={{160,0},{168,8},{176,16},{184,24},{128,32},{136,40},{144,48},{152,... | collective-permute-start | bytes 110600 | tf_op jit(solution)/shard_map/ppermute | solution.py:282
  81.5 4.5 %collective-permute-start.26 = (f32[72,128]{1,0:T(8,128)S(1)}, f32[72,128]{1,0:T(8,128)S(1)}, u32[]{:S(2)}, u32[]{:S(2)}) collective-permute-start(f32[72,128]{1,0:T(8,128)S(1)} %add_add_fusion.1), channel_id=1, source_target_pairs={{64,0},{72,8},{80,16},{88,24},{224,32},{232,40},{240,48},{248,56},... | collective-permute-start | bytes 110600 | tf_op jit(solution)/shard_map/ppermute | solution.py:282
  82.7 4.4 %collective-permute-start.25 = (f32[72,128]{1,0:T(8,128)S(1)}, f32[72,128]{1,0:T(8,128)S(1)}, u32[]{:S(2)}, u32[]{:S(2)}) collective-permute-start(f32[72,128]{1,0:T(8,128)S(1)} %add_add_fusion.1), channel_id=1, source_target_pairs={{224,0},{232,8},{240,16},{248,24},{64,32},{72,40},{80,48},{88,56},... | collective-permute-start | bytes 110600 | tf_op jit(solution)/shard_map/ppermute | solution.py:282
  84.0 17.1 %collective-permute-start.31 = (f32[512,128]{1,0:T(8,128)S(1)}, f32[512,128]{1,0:T(8,128)S(1)}, u32[]{:S(2)}, u32[]{:S(2)}) collective-permute-start(f32[512,128]{1,0:T(8,128)S(1)} %get-tuple-element.46.refs_1_), channel_id=1, source_target_pairs={{7,0},{0,1},{1,2},{2,3},{3,4},{4,5},{5,6},{6,7},{15,8},{8,9},{9,10... | collective-permute-start | bytes 786440 | tf_op jit(solution)/shard_map/ppermute | solution.py:315
  87.1 7.4 %collective-permute-start.28 = (f32[72,128]{1,0:T(8,128)S(1)}, f32[72,128]{1,0:T(8,128)S(1)}, u32[]{:S(2)}, u32[]{:S(2)}) collective-permute-start(f32[72,128]{1,0:T(8,128)S(1)} %add_add_fusion.mine_ref), channel_id=1, source_target_pairs={{7,0},{0,1},{1,2},{2,3},{3,4},{4,5},{5,6},{6,7},{15,8},{8,9},{9,10... | collective-permute-start | bytes 110600 | tf_op jit(solution)/shard_map/ppermute | solution.py:315
  87.4 10.9 %collective-permute-start.30 = (f32[72,128]{1,0:T(8,128)S(1)}, f32[72,128]{1,0:T(8,128)S(1)}, u32[]{:S(2)}, u32[]{:S(2)}) collective-permute-start(f32[72,128]{1,0:T(8,128)S(1)} %add_add_fusion.mine_ref), channel_id=1, source_target_pairs={{8,0},{0,8},{24,16},{16,24},{40,32},{32,40},{56,48},{48,56},{72,64... | collective-permute-start | bytes 110600 | tf_op jit(solution)/shard_map/ppermute | solution.py:282
  94.5 6.6 %collective-permute-start.29 = (f32[72,128]{1,0:T(8,128)S(1)}, f32[72,128]{1,0:T(8,128)S(1)}, u32[]{:S(2)}, u32[]{:S(2)}) collective-permute-start(f32[72,128]{1,0:T(8,128)S(1)} %collective-permute-done.28.mine_ref), channel_id=1, source_target_pairs={{8,0},{0,8},{24,16},{16,24},{40,32},{32,40},{56,48},{48,56},{72,64... | collective-permute-start | bytes 110600 | tf_op jit(solution)/shard_map/ppermute | solution.py:282

commit v6 on v5

--- a/solution.py
+++ b/solution.py
@@ -282,31 +282,47 @@
     return lax.ppermute(x, "row", route)
 
 
+def mate(z, y, c):
+    return z, y, 1 - c
+
+
+def owner(chip):
+    def source(z, y, c):
+        other_z, other_y = chip(z, y)
+        return other_z, other_y, (c + z + y + other_z + other_y) % 2
+
+    return source
+
+
+def owned_half(row):
+    return (row + row // 2 + row // QUAD) % 2
+
+
 def side(z):
     return 1 if z % 2 else -1
 
 
 def summed_halves(mine, other, y_last):
-    mate = from_row(other, lambda z, y, c: (z, y, 1 - c))
-    x = mine + mate
-    next_z = from_row(x, lambda z, y, c: (z ^ 1, y, c))
+    incoming = from_row(other, mate)
+    x = mine + incoming
+    next_z = from_row(x, owner(lambda z, y: (z ^ 1, y)))
     if y_last:
         x = x + next_z
     else:
-        next_y = from_row(x, lambda z, y, c: (z, 1 - y, c))
-        next_zy = from_row(x, lambda z, y, c: (z ^ 1, 1 - y, c))
+        next_y = from_row(x, owner(lambda z, y: (z, 1 - y)))
+        next_zy = from_row(x, owner(lambda z, y: (z ^ 1, 1 - y)))
         x = ((x + next_z) + next_y) + next_zy
-    by_one = from_row(x, lambda z, y, c: (z + side(z), y, c))
-    by_two = from_row(x, lambda z, y, c: (z - 2 * side(z), y, c))
-    by_three = from_row(x, lambda z, y, c: (z + 3 * side(z), y, c))
+    by_one = from_row(x, owner(lambda z, y: (z + side(z), y)))
+    by_two = from_row(x, owner(lambda z, y: (z - 2 * side(z), y)))
+    by_three = from_row(x, owner(lambda z, y: (z + 3 * side(z), y)))
     x = ((x + by_one) + by_two) + by_three
     if y_last:
-        x = x + from_row(x, lambda z, y, c: (z, 1 - y, c))
+        x = x + from_row(x, owner(lambda z, y: (z, 1 - y)))
     return x
 
 
 def with_other(half):
-    return [half, from_row(half, lambda z, y, c: (z, y, 1 - c))]
+    return [half, from_row(half, mate)]
 
 
 def shifted(block):
@@ -317,7 +333,7 @@
 
 def local(panel):
     n = panel.shape[1] // 2
-    core = (lax.axis_index("row") & 1).astype(jnp.int32).reshape(1)
+    core = owned_half(lax.axis_index("row")).astype(jnp.int32).reshape(1)
     for step in range(STEPS):
         if step == 0:
             own, mine, other = load(core, panel, n)

time: 105 us -> 104 us (level)
  starting transfers between devices: 56 us -> 41.2 us
  waiting for transfers between devices: 28.8 us -> 43.4 us
    ppermute x26, starting transfers between devices: 50.3 us -> 35.6 us  [from_row(): return lax.ppermute(x, 'row', route)]
    ppermute x6, waiting for transfers between devices: 9.7 us -> 20.6 us  [shifted(): return lax.ppermute(block, 'pair', route)]
    ppermute x26, waiting for transfers between devices: 19.1 us -> 22.8 us  [from_row(): return lax.ppermute(x, 'row', route)]
where the time goes in v6:
time: 104 us
  waiting for transfers between devices  43.4 us (42%)
  starting transfers between devices  41.2 us (40%)
  Pallas kernels  19.3 us (19%)
    ppermute x26, starting transfers between devices, from_row(): return lax.ppermute(x, 'row', route)  35.6 us
    ppermute x26, waiting for transfers between devices, from_row(): return lax.ppermute(x, 'row', route)  22.8 us
    ppermute x6, waiting for transfers between devices, shifted(): return lax.ppermute(block, 'pair', route)  20.6 us
    pallas_call x11, Pallas kernels, vmem_call(): pl.pallas_call(kernel, out_shape=shapes, in_specs=specs, scratch_shapes=s...  18 us
    ppermute x6, starting transfers between devices, shifted(): return lax.ppermute(block, 'pair', route)  5.62 us
  transfers between devices with their start and end apart: 32, of which 20 were waited for; matrix products, arithmetic and copies ran while one was open for 0% of the time, Pallas kernels for 9%

profile of v6, /device:TPU:1, one launch (start us, length us, event | category | flops | bytes accessed | tf_op | source)
XLA Modules:
  0.0 104.3 jit_solution(14221766770878059072)
XLA Ops:
  0.0 1.3 %load.1 = (f32[512,256]{1,0:T(8,128)S(1)}, f32[72,128]{1,0:T(8,128)S(1)}, f32[72,128]{1,0:T(8,128)S(1)}) custom-call(s32[1]{0:T(128)} %bitcast.core_ref, f32[512,256]{1,0:T(8,128)} %panel_ref.1), custom_call_target="tpu_custom_call" | custom-call | tf_op jit(solution)/shard_map/load/pallas_call | solution.py:231
  1.4 3.8 %collective-permute-start.9 = (f32[512,256]{1,0:T(8,128)S(1)}, f32[512,256]{1,0:T(8,128)S(1)}, u32[]{:S(2)}, u32[]{:S(2)}) collective-permute-start(f32[512,256]{1,0:T(8,128)S(1)} %get-tuple-element.32.refs_0_), channel_id=1, source_target_pairs={{7,0},{0,1},{1,2},{2,3},{3,4},{4,5},{5,6},{6,7},{15,8},{8,9},{9,10... | collective-permute-start | bytes 1572872 | tf_op jit(solution)/shard_map/ppermute | solution.py:331
  7.0 1.9 %collective-permute-start.1 = (f32[72,128]{1,0:T(8,128)S(1)}, f32[72,128]{1,0:T(8,128)S(1)}, u32[]{:S(2)}, u32[]{:S(2)}) collective-permute-start(f32[72,128]{1,0:T(8,128)S(1)} %add.75), channel_id=1, source_target_pairs={{40,0},{32,8},{56,16},{48,24},{8,32},{0,40},{24,48},{16,56},{104,6... | collective-permute-start | bytes 110600 | tf_op jit(solution)/shard_map/ppermute | solution.py:282
  8.9 1.6 %collective-permute-done.1 = f32[72,128]{1,0:T(8,128)S(1)} collective-permute-done((f32[72,128]{1,0:T(8,128)S(1)}, f32[72,128]{1,0:T(8,128)S(1)}, u32[]{:S(2)}, u32[]{:S(2)}) %collective-permute-start.1) | collective-permute-done | bytes 36896 | tf_op jit(solution)/shard_map/ppermute | solution.py:282
  10.5 6.6 %collective-permute-start.4 = (f32[72,128]{1,0:T(8,128)S(1)}, f32[72,128]{1,0:T(8,128)S(1)}, u32[]{:S(2)}, u32[]{:S(2)}) collective-permute-start(f32[72,128]{1,0:T(8,128)S(1)} %add.76), channel_id=1, source_target_pairs={{168,0},{160,8},{184,16},{176,24},{136,32},{128,40},{152,48},{144,... | collective-permute-start | bytes 110600 | tf_op jit(solution)/shard_map/ppermute | solution.py:282
  17.4 3.5 %collective-permute-start.2 = (f32[72,128]{1,0:T(8,128)S(1)}, f32[72,128]{1,0:T(8,128)S(1)}, u32[]{:S(2)}, u32[]{:S(2)}) collective-permute-start(f32[72,128]{1,0:T(8,128)S(1)} %add.76), channel_id=1, source_target_pairs={{232,0},{224,8},{248,16},{240,24},{72,32},{64,40},{88,48},{80,56},... | collective-permute-start | bytes 110600 | tf_op jit(solution)/shard_map/ppermute | solution.py:282
  20.9 2.0 %collective-permute-done.2 = f32[72,128]{1,0:T(8,128)S(1)} collective-permute-done((f32[72,128]{1,0:T(8,128)S(1)}, f32[72,128]{1,0:T(8,128)S(1)}, u32[]{:S(2)}, u32[]{:S(2)}) %collective-permute-start.2) | collective-permute-done | bytes 36896 | tf_op jit(solution)/shard_map/ppermute | solution.py:282
  23.1 3.3 %collective-permute-done.5 = f32[72,128]{1,0:T(8,128)S(1)} collective-permute-done((f32[72,128]{1,0:T(8,128)S(1)}, f32[72,128]{1,0:T(8,128)S(1)}, u32[]{:S(2)}, u32[]{:S(2)}) %collective-permute-start.5) | collective-permute-done | bytes 36896 | tf_op jit(solution)/shard_map/ppermute | solution.py:282
  26.4 1.4 %collective-permute-start.6 = (f32[72,128]{1,0:T(8,128)S(1)}, f32[72,128]{1,0:T(8,128)S(1)}, u32[]{:S(2)}, u32[]{:S(2)}) collective-permute-start(f32[72,128]{1,0:T(8,128)S(1)} %add.80.mine_ref), channel_id=1, source_target_pairs={{7,0},{0,1},{1,2},{2,3},{3,4},{4,5},{5,6},{6,7},{15,8},{8,9},{9,10... | collective-permute-start | bytes 110600 | tf_op jit(solution)/shard_map/ppermute | solution.py:331
  28.5 4.7 %collective-permute-done.6.mine_ref = f32[72,128]{1,0:T(8,128)S(1)} collective-permute-done((f32[72,128]{1,0:T(8,128)S(1)}, f32[72,128]{1,0:T(8,128)S(1)}, u32[]{:S(2)}, u32[]{:S(2)}) %collective-permute-start.6) | collective-permute-done | bytes 36896 | tf_op jit(solution)/shard_map/ppermute | solution.py:331
  33.9 1.8 %shard_map.17 = (f32[128,128]{1,0:T(8,128)S(1)}, f32[128,128]{1,0:T(8,128)S(1)}, f32[128,128]{1,0:T(8,128)S(1)}) custom-call(s32[1]{0:T(128)} %bitcast.core_ref, f32[72,128]{1,0:T(8,128)S(1)} %add.80.mine_ref, f32[72,128]{1,0:T(8,128)S(1)} %collective-permute-done.8.other_ref), custom_call_target="tpu_custom_call" | custom-call | tf_op jit(solution)/shard_map/pallas_call | solution.py:219
  36.7 2.8 %shard_map.19 = (f32[512,128]{1,0:T(8,128)S(1)}, f32[128,128]{1,0:T(8,128)S(1)}, f32[128,128]{1,0:T(8,128)S(1)}, f32[72,128]{1,0:T(8,128)S(1)}, f32[72,128]{1,0:T(8,128)S(1)}) custom-call(s32[1]{0:T(128)} %bitcast.core_ref, f32[72,128]{1,0:T(8,128)S(1)} %collective-permute-done.6.mine_ref, f32[72,128]{1,0:T(8,128)S(1)} %collective-permute-done.7.other_ref, ...), custom_call_target="tpu_custom_call" | custom-call | tf_op jit(solution)/shard_map/pallas_call | solution.py:219
  39.6 1.2 %collective-permute-done.10 = f32[72,128]{1,0:T(8,128)S(1)} collective-permute-done((f32[72,128]{1,0:T(8,128)S(1)}, f32[72,128]{1,0:T(8,128)S(1)}, u32[]{:S(2)}, u32[]{:S(2)}) %collective-permute-start.10) | collective-permute-done | bytes 36896 | tf_op jit(solution)/shard_map/ppermute | solution.py:282
  40.8 2.0 %collective-permute-start.13 = (f32[72,128]{1,0:T(8,128)S(1)}, f32[72,128]{1,0:T(8,128)S(1)}, u32[]{:S(2)}, u32[]{:S(2)}) collective-permute-start(f32[72,128]{1,0:T(8,128)S(1)} %add.81), channel_id=1, source_target_pairs={{48,0},{56,8},{32,16},{40,24},{16,32},{24,40},{0,48},{8,56},{112,6... | collective-permute-start | bytes 110600 | tf_op jit(solution)/shard_map/ppermute | solution.py:282
  44.5 2.1 %collective-permute-done.12 = f32[72,128]{1,0:T(8,128)S(1)} collective-permute-done((f32[72,128]{1,0:T(8,128)S(1)}, f32[72,128]{1,0:T(8,128)S(1)}, u32[]{:S(2)}, u32[]{:S(2)}) %collective-permute-start.12) | collective-permute-done | bytes 36896 | tf_op jit(solution)/shard_map/ppermute | solution.py:282
  47.3 3.4 %collective-permute-start.16 = (f32[72,128]{1,0:T(8,128)S(1)}, f32[72,128]{1,0:T(8,128)S(1)}, u32[]{:S(2)}, u32[]{:S(2)}) collective-permute-start(f32[72,128]{1,0:T(8,128)S(1)} %add_add_fusion.3), channel_id=1, source_target_pairs={{168,0},{160,8},{184,16},{176,24},{136,32},{128,40},{152,48},{144,... | collective-permute-start | bytes 110600 | tf_op jit(solution)/shard_map/ppermute | solution.py:282
  51.4 2.3 %collective-permute-start.14 = (f32[72,128]{1,0:T(8,128)S(1)}, f32[72,128]{1,0:T(8,128)S(1)}, u32[]{:S(2)}, u32[]{:S(2)}) collective-permute-start(f32[72,128]{1,0:T(8,128)S(1)} %add_add_fusion.3), channel_id=1, source_target_pairs={{232,0},{224,8},{248,16},{240,24},{72,32},{64,40},{88,48},{80,56},... | collective-permute-start | bytes 110600 | tf_op jit(solution)/shard_map/ppermute | solution.py:282
  54.4 2.2 %collective-permute-done.14 = f32[72,128]{1,0:T(8,128)S(1)} collective-permute-done((f32[72,128]{1,0:T(8,128)S(1)}, f32[72,128]{1,0:T(8,128)S(1)}, u32[]{:S(2)}, u32[]{:S(2)}) %collective-permute-start.14) | collective-permute-done | bytes 36896 | tf_op jit(solution)/shard_map/ppermute | solution.py:282
  57.2 8.6 %collective-permute-done.17.mine_ref = f32[72,128]{1,0:T(8,128)S(1)} collective-permute-done((f32[72,128]{1,0:T(8,128)S(1)}, f32[72,128]{1,0:T(8,128)S(1)}, u32[]{:S(2)}, u32[]{:S(2)}) %collective-permute-start.17) | collective-permute-done | bytes 36896 | tf_op jit(solution)/shard_map/ppermute | solution.py:331
  67.2 1.8 %shard_map.20 = (f32[128,128]{1,0:T(8,128)S(1)}, f32[128,128]{1,0:T(8,128)S(1)}, f32[128,128]{1,0:T(8,128)S(1)}) custom-call(s32[1]{0:T(128)} %bitcast.core_ref, f32[72,128]{1,0:T(8,128)S(1)} %add_add_fusion.2.mine_ref, f32[72,128]{1,0:T(8,128)S(1)} %collective-permute-done.19.other_ref), custom_call_target="tpu_custom_call" | custom-call | tf_op jit(solution)/shard_map/pallas_call | solution.py:219
  70.0 2.8 %shard_map.23 = (f32[512,128]{1,0:T(8,128)S(1)}, f32[128,128]{1,0:T(8,128)S(1)}, f32[128,128]{1,0:T(8,128)S(1)}, f32[72,128]{1,0:T(8,128)S(1)}, f32[72,128]{1,0:T(8,128)S(1)}) custom-call(s32[1]{0:T(128)} %bitcast.core_ref, f32[72,128]{1,0:T(8,128)S(1)} %collective-permute-done.17.mine_ref, f32[72,128]{1,0:T(8,128)S(1)} %collective-permute-done.18.other_ref, ...), custom_call_target="tpu_custom_call" | custom-call | tf_op jit(solution)/shard_map/pallas_call | solution.py:219
  72.9 1.2 %collective-permute-done.21 = f32[72,128]{1,0:T(8,128)S(1)} collective-permute-done((f32[72,128]{1,0:T(8,128)S(1)}, f32[72,128]{1,0:T(8,128)S(1)}, u32[]{:S(2)}, u32[]{:S(2)}) %collective-permute-start.21) | collective-permute-done | bytes 36896 | tf_op jit(solution)/shard_map/ppermute | solution.py:282
  74.5 1.4 %collective-permute-start.23 = (f32[72,128]{1,0:T(8,128)S(1)}, f32[72,128]{1,0:T(8,128)S(1)}, u32[]{:S(2)}, u32[]{:S(2)}) collective-permute-start(f32[72,128]{1,0:T(8,128)S(1)} %add.88), channel_id=1, source_target_pairs={{24,0},{16,8},{8,16},{0,24},{56,32},{48,40},{40,48},{32,56},{88,64... | collective-permute-start | bytes 110600 | tf_op jit(solution)/shard_map/ppermute | solution.py:282
  75.9 1.2 %collective-permute-start.22 = (f32[72,128]{1,0:T(8,128)S(1)}, f32[72,128]{1,0:T(8,128)S(1)}, u32[]{:S(2)}, u32[]{:S(2)}) collective-permute-start(f32[72,128]{1,0:T(8,128)S(1)} %add.88), channel_id=1, source_target_pairs={{40,0},{32,8},{56,16},{48,24},{8,32},{0,40},{24,48},{16,56},{104,6... | collective-permute-start | bytes 110600 | tf_op jit(solution)/shard_map/ppermute | solution.py:282
  79.3 2.4 %collective-permute-start.27 = (f32[72,128]{1,0:T(8,128)S(1)}, f32[72,128]{1,0:T(8,128)S(1)}, u32[]{:S(2)}, u32[]{:S(2)}) collective-permute-start(f32[72,128]{1,0:T(8,128)S(1)} %add_add_fusion.1), channel_id=1, source_target_pairs={{168,0},{160,8},{184,16},{176,24},{136,32},{128,40},{152,48},{144,... | collective-permute-start | bytes 110600 | tf_op jit(solution)/shard_map/ppermute | solution.py:282
  81.7 1.7 %collective-permute-start.26 = (f32[72,128]{1,0:T(8,128)S(1)}, f32[72,128]{1,0:T(8,128)S(1)}, u32[]{:S(2)}, u32[]{:S(2)}) collective-permute-start(f32[72,128]{1,0:T(8,128)S(1)} %add_add_fusion.1), channel_id=1, source_target_pairs={{64,0},{72,8},{80,16},{88,24},{224,32},{232,40},{240,48},{248,56},... | collective-permute-start | bytes 110600 | tf_op jit(solution)/shard_map/ppermute | solution.py:282
  83.3 1.2 %collective-permute-start.25 = (f32[72,128]{1,0:T(8,128)S(1)}, f32[72,128]{1,0:T(8,128)S(1)}, u32[]{:S(2)}, u32[]{:S(2)}) collective-permute-start(f32[72,128]{1,0:T(8,128)S(1)} %add_add_fusion.1), channel_id=1, source_target_pairs={{232,0},{224,8},{248,16},{240,24},{72,32},{64,40},{88,48},{80,56},... | collective-permute-start | bytes 110600 | tf_op jit(solution)/shard_map/ppermute | solution.py:282
  84.5 1.2 %collective-permute-done.27 = f32[72,128]{1,0:T(8,128)S(1)} collective-permute-done((f32[72,128]{1,0:T(8,128)S(1)}, f32[72,128]{1,0:T(8,128)S(1)}, u32[]{:S(2)}, u32[]{:S(2)}) %collective-permute-start.27) | collective-permute-done | bytes 36896 | tf_op jit(solution)/shard_map/ppermute | solution.py:282
  85.7 2.8 %collective-permute-done.25 = f32[72,128]{1,0:T(8,128)S(1)} collective-permute-done((f32[72,128]{1,0:T(8,128)S(1)}, f32[72,128]{1,0:T(8,128)S(1)}, u32[]{:S(2)}, u32[]{:S(2)}) %collective-permute-start.25) | collective-permute-done | bytes 36896 | tf_op jit(solution)/shard_map/ppermute | solution.py:282
  89.4 7.3 %collective-permute-done.28.mine_ref = f32[72,128]{1,0:T(8,128)S(1)} collective-permute-done((f32[72,128]{1,0:T(8,128)S(1)}, f32[72,128]{1,0:T(8,128)S(1)}, u32[]{:S(2)}, u32[]{:S(2)}) %collective-permute-start.28) | collective-permute-done | bytes 36896 | tf_op jit(solution)/shard_map/ppermute | solution.py:331
  98.0 1.8 %shard_map.24 = (f32[128,128]{1,0:T(8,128)S(1)}, f32[128,128]{1,0:T(8,128)S(1)}, f32[128,128]{1,0:T(8,128)S(1)}) custom-call(s32[1]{0:T(128)} %bitcast.core_ref, f32[72,128]{1,0:T(8,128)S(1)} %add_add_fusion.mine_ref, f32[72,128]{1,0:T(8,128)S(1)} %collective-permute-done.30.other_ref), custom_call_target="tpu_custom_call" | custom-call | tf_op jit(solution)/shard_map/pallas_call | solution.py:219
  100.9 3.3 %shard_map.27 = f32[512,256]{1,0:T(8,128)} custom-call(s32[1]{0:T(128)} %bitcast.core_ref, f32[72,128]{1,0:T(8,128)S(1)} %collective-permute-done.28.mine_ref, f32[72,128]{1,0:T(8,128)S(1)} %collective-permute-done.29.other_ref, f32[512,128]{1,0:T(8,128)S(1)} %shard_map.25.own_ref, f32[512,128]{1,0:T(8,128)S(1)} %shard_map.26.refs_0_, ...), custom_call_target="tpu_custom_call" | custom-call | tf_op jit(solution)/shard_map/pallas_call | solution.py:219
  (54 shorter events, 17.3 us)
Async XLA Ops:
  1.4 35.4 %collective-permute-start.9 = (f32[512,256]{1,0:T(8,128)S(1)}, f32[512,256]{1,0:T(8,128)S(1)}, u32[]{:S(2)}, u32[]{:S(2)}) collective-permute-start(f32[512,256]{1,0:T(8,128)S(1)} %get-tuple-element.32.refs_0_), channel_id=1, source_target_pairs={{7,0},{0,1},{1,2},{2,3},{3,4},{4,5},{5,6},{6,7},{15,8},{8,9},{9,10... | collective-permute-start | bytes 1572872 | tf_op jit(solution)/shard_map/ppermute | solution.py:331
  5.2 1.8 %collective-permute-start = (f32[72,128]{1,0:T(8,128)S(1)}, f32[72,128]{1,0:T(8,128)S(1)}, u32[]{:S(2)}, u32[]{:S(2)}) collective-permute-start(f32[72,128]{1,0:T(8,128)S(1)} %get-tuple-element.28), channel_id=1, source_target_pairs={{8,0},{0,8},{24,16},{16,24},{40,32},{32,40},{56,48},{48,56},{72,64... | collective-permute-start | bytes 110600 | tf_op jit(solution)/shard_map/ppermute | solution.py:282
  7.0 3.5 %collective-permute-start.1 = (f32[72,128]{1,0:T(8,128)S(1)}, f32[72,128]{1,0:T(8,128)S(1)}, u32[]{:S(2)}, u32[]{:S(2)}) collective-permute-start(f32[72,128]{1,0:T(8,128)S(1)} %add.75), channel_id=1, source_target_pairs={{40,0},{32,8},{56,16},{48,24},{8,32},{0,40},{24,48},{16,56},{104,6... | collective-permute-start | bytes 110600 | tf_op jit(solution)/shard_map/ppermute | solution.py:282
  10.5 10.4 %collective-permute-start.4 = (f32[72,128]{1,0:T(8,128)S(1)}, f32[72,128]{1,0:T(8,128)S(1)}, u32[]{:S(2)}, u32[]{:S(2)}) collective-permute-start(f32[72,128]{1,0:T(8,128)S(1)} %add.76), channel_id=1, source_target_pairs={{168,0},{160,8},{184,16},{176,24},{136,32},{128,40},{152,48},{144,... | collective-permute-start | bytes 110600 | tf_op jit(solution)/shard_map/ppermute | solution.py:282
  17.1 3.7 %collective-permute-start.3 = (f32[72,128]{1,0:T(8,128)S(1)}, f32[72,128]{1,0:T(8,128)S(1)}, u32[]{:S(2)}, u32[]{:S(2)}) collective-permute-start(f32[72,128]{1,0:T(8,128)S(1)} %add.76), channel_id=1, source_target_pairs={{64,0},{72,8},{80,16},{88,24},{224,32},{232,40},{240,48},{248,56},... | collective-permute-start | bytes 110600 | tf_op jit(solution)/shard_map/ppermute | solution.py:282
  17.4 5.5 %collective-permute-start.2 = (f32[72,128]{1,0:T(8,128)S(1)}, f32[72,128]{1,0:T(8,128)S(1)}, u32[]{:S(2)}, u32[]{:S(2)}) collective-permute-start(f32[72,128]{1,0:T(8,128)S(1)} %add.76), channel_id=1, source_target_pairs={{232,0},{224,8},{248,16},{240,24},{72,32},{64,40},{88,48},{80,56},... | collective-permute-start | bytes 110600 | tf_op jit(solution)/shard_map/ppermute | solution.py:282
  22.9 3.5 %collective-permute-start.5 = (f32[72,128]{1,0:T(8,128)S(1)}, f32[72,128]{1,0:T(8,128)S(1)}, u32[]{:S(2)}, u32[]{:S(2)}) collective-permute-start(f32[72,128]{1,0:T(8,128)S(1)} %add_add_fusion.4), channel_id=1, source_target_pairs={{24,0},{16,8},{8,16},{0,24},{56,32},{48,40},{40,48},{32,56},{88,64... | collective-permute-start | bytes 110600 | tf_op jit(solution)/shard_map/ppermute | solution.py:282
  26.4 6.8 %collective-permute-start.6 = (f32[72,128]{1,0:T(8,128)S(1)}, f32[72,128]{1,0:T(8,128)S(1)}, u32[]{:S(2)}, u32[]{:S(2)}) collective-permute-start(f32[72,128]{1,0:T(8,128)S(1)} %add.80.mine_ref), channel_id=1, source_target_pairs={{7,0},{0,1},{1,2},{2,3},{3,4},{4,5},{5,6},{6,7},{15,8},{8,9},{9,10... | collective-permute-start | bytes 110600 | tf_op jit(solution)/shard_map/ppermute | solution.py:331
  27.8 6.1 %collective-permute-start.8 = (f32[72,128]{1,0:T(8,128)S(1)}, f32[72,128]{1,0:T(8,128)S(1)}, u32[]{:S(2)}, u32[]{:S(2)}) collective-permute-start(f32[72,128]{1,0:T(8,128)S(1)} %add.80.mine_ref), channel_id=1, source_target_pairs={{8,0},{0,8},{24,16},{16,24},{40,32},{32,40},{56,48},{48,56},{72,64... | collective-permute-start | bytes 110600 | tf_op jit(solution)/shard_map/ppermute | solution.py:282
  33.2 3.5 %collective-permute-start.7 = (f32[72,128]{1,0:T(8,128)S(1)}, f32[72,128]{1,0:T(8,128)S(1)}, u32[]{:S(2)}, u32[]{:S(2)}) collective-permute-start(f32[72,128]{1,0:T(8,128)S(1)} %collective-permute-done.6.mine_ref), channel_id=1, source_target_pairs={{8,0},{0,8},{24,16},{16,24},{40,32},{32,40},{56,48},{48,56},{72,64... | collective-permute-start | bytes 110600 | tf_op jit(solution)/shard_map/ppermute | solution.py:282
  39.5 1.3 %collective-permute-start.10 = (f32[72,128]{1,0:T(8,128)S(1)}, f32[72,128]{1,0:T(8,128)S(1)}, u32[]{:S(2)}, u32[]{:S(2)}) collective-permute-start(f32[72,128]{1,0:T(8,128)S(1)} %get-tuple-element.34), channel_id=1, source_target_pairs={{8,0},{0,8},{24,16},{16,24},{40,32},{32,40},{56,48},{48,56},{72,64... | collective-permute-start | bytes 110600 | tf_op jit(solution)/shard_map/ppermute | solution.py:282
  40.8 3.7 %collective-permute-start.13 = (f32[72,128]{1,0:T(8,128)S(1)}, f32[72,128]{1,0:T(8,128)S(1)}, u32[]{:S(2)}, u32[]{:S(2)}) collective-permute-start(f32[72,128]{1,0:T(8,128)S(1)} %add.81), channel_id=1, source_target_pairs={{48,0},{56,8},{32,16},{40,24},{16,32},{24,40},{0,48},{8,56},{112,6... | collective-permute-start | bytes 110600 | tf_op jit(solution)/shard_map/ppermute | solution.py:282
  42.8 3.8 %collective-permute-start.12 = (f32[72,128]{1,0:T(8,128)S(1)}, f32[72,128]{1,0:T(8,128)S(1)}, u32[]{:S(2)}, u32[]{:S(2)}) collective-permute-start(f32[72,128]{1,0:T(8,128)S(1)} %add.81), channel_id=1, source_target_pairs={{24,0},{16,8},{8,16},{0,24},{56,32},{48,40},{40,48},{32,56},{88,64... | collective-permute-start | bytes 110600 | tf_op jit(solution)/shard_map/ppermute | solution.py:282
  43.9 3.4 %collective-permute-start.11 = (f32[72,128]{1,0:T(8,128)S(1)}, f32[72,128]{1,0:T(8,128)S(1)}, u32[]{:S(2)}, u32[]{:S(2)}) collective-permute-start(f32[72,128]{1,0:T(8,128)S(1)} %add.81), channel_id=1, source_target_pairs={{40,0},{32,8},{56,16},{48,24},{8,32},{0,40},{24,48},{16,56},{104,6... | collective-permute-start | bytes 110600 | tf_op jit(solution)/shard_map/ppermute | solution.py:282
  47.3 6.8 %collective-permute-start.16 = (f32[72,128]{1,0:T(8,128)S(1)}, f32[72,128]{1,0:T(8,128)S(1)}, u32[]{:S(2)}, u32[]{:S(2)}) collective-permute-start(f32[72,128]{1,0:T(8,128)S(1)} %add_add_fusion.3), channel_id=1, source_target_pairs={{168,0},{160,8},{184,16},{176,24},{136,32},{128,40},{152,48},{144,... | collective-permute-start | bytes 110600 | tf_op jit(solution)/shard_map/ppermute | solution.py:282
  50.7 3.7 %collective-permute-start.15 = (f32[72,128]{1,0:T(8,128)S(1)}, f32[72,128]{1,0:T(8,128)S(1)}, u32[]{:S(2)}, u32[]{:S(2)}) collective-permute-start(f32[72,128]{1,0:T(8,128)S(1)} %add_add_fusion.3), channel_id=1, source_target_pairs={{64,0},{72,8},{80,16},{88,24},{224,32},{232,40},{240,48},{248,56},... | collective-permute-start | bytes 110600 | tf_op jit(solution)/shard_map/ppermute | solution.py:282
  51.4 5.3 %collective-permute-start.14 = (f32[72,128]{1,0:T(8,128)S(1)}, f32[72,128]{1,0:T(8,128)S(1)}, u32[]{:S(2)}, u32[]{:S(2)}) collective-permute-start(f32[72,128]{1,0:T(8,128)S(1)} %add_add_fusion.3), channel_id=1, source_target_pairs={{232,0},{224,8},{248,16},{240,24},{72,32},{64,40},{88,48},{80,56},... | collective-permute-start | bytes 110600 | tf_op jit(solution)/shard_map/ppermute | solution.py:282
  53.7 16.3 %collective-permute-start.20 = (f32[512,128]{1,0:T(8,128)S(1)}, f32[512,128]{1,0:T(8,128)S(1)}, u32[]{:S(2)}, u32[]{:S(2)}) collective-permute-start(f32[512,128]{1,0:T(8,128)S(1)} %get-tuple-element.38.refs_1_), channel_id=1, source_target_pairs={{7,0},{0,1},{1,2},{2,3},{3,4},{4,5},{5,6},{6,7},{15,8},{8,9},{9,10... | collective-permute-start | bytes 786440 | tf_op jit(solution)/shard_map/ppermute | solution.py:331
  56.6 9.2 %collective-permute-start.17 = (f32[72,128]{1,0:T(8,128)S(1)}, f32[72,128]{1,0:T(8,128)S(1)}, u32[]{:S(2)}, u32[]{:S(2)}) collective-permute-start(f32[72,128]{1,0:T(8,128)S(1)} %add_add_fusion.2.mine_ref), channel_id=1, source_target_pairs={{7,0},{0,1},{1,2},{2,3},{3,4},{4,5},{5,6},{6,7},{15,8},{8,9},{9,10... | collective-permute-start | bytes 110600 | tf_op jit(solution)/shard_map/ppermute | solution.py:331
  56.7 10.5 %collective-permute-start.19 = (f32[72,128]{1,0:T(8,128)S(1)}, f32[72,128]{1,0:T(8,128)S(1)}, u32[]{:S(2)}, u32[]{:S(2)}) collective-permute-start(f32[72,128]{1,0:T(8,128)S(1)} %add_add_fusion.2.mine_ref), channel_id=1, source_target_pairs={{8,0},{0,8},{24,16},{16,24},{40,32},{32,40},{56,48},{48,56},{72,64... | collective-permute-start | bytes 110600 | tf_op jit(solution)/shard_map/ppermute | solution.py:282
  65.8 4.2 %collective-permute-start.18 = (f32[72,128]{1,0:T(8,128)S(1)}, f32[72,128]{1,0:T(8,128)S(1)}, u32[]{:S(2)}, u32[]{:S(2)}) collective-permute-start(f32[72,128]{1,0:T(8,128)S(1)} %collective-permute-done.17.mine_ref), channel_id=1, source_target_pairs={{8,0},{0,8},{24,16},{16,24},{40,32},{32,40},{56,48},{48,56},{72,64... | collective-permute-start | bytes 110600 | tf_op jit(solution)/shard_map/ppermute | solution.py:282
  72.8 1.3 %collective-permute-start.21 = (f32[72,128]{1,0:T(8,128)S(1)}, f32[72,128]{1,0:T(8,128)S(1)}, u32[]{:S(2)}, u32[]{:S(2)}) collective-permute-start(f32[72,128]{1,0:T(8,128)S(1)} %get-tuple-element.42), channel_id=1, source_target_pairs={{8,0},{0,8},{24,16},{16,24},{40,32},{32,40},{56,48},{48,56},{72,64... | collective-permute-start | bytes 110600 | tf_op jit(solution)/shard_map/ppermute | solution.py:282
  74.1 3.8 %collective-permute-start.24 = (f32[72,128]{1,0:T(8,128)S(1)}, f32[72,128]{1,0:T(8,128)S(1)}, u32[]{:S(2)}, u32[]{:S(2)}) collective-permute-start(f32[72,128]{1,0:T(8,128)S(1)} %add.88), channel_id=1, source_target_pairs={{48,0},{56,8},{32,16},{40,24},{16,32},{24,40},{0,48},{8,56},{112,6... | collective-permute-start | bytes 110600 | tf_op jit(solution)/shard_map/ppermute | solution.py:282
  74.5 4.4 %collective-permute-start.23 = (f32[72,128]{1,0:T(8,128)S(1)}, f32[72,128]{1,0:T(8,128)S(1)}, u32[]{:S(2)}, u32[]{:S(2)}) collective-permute-start(f32[72,128]{1,0:T(8,128)S(1)} %add.88), channel_id=1, source_target_pairs={{24,0},{16,8},{8,16},{0,24},{56,32},{48,40},{40,48},{32,56},{88,64... | collective-permute-start | bytes 110600 | tf_op jit(solution)/shard_map/ppermute | solution.py:282
  75.9 3.4 %collective-permute-start.22 = (f32[72,128]{1,0:T(8,128)S(1)}, f32[72,128]{1,0:T(8,128)S(1)}, u32[]{:S(2)}, u32[]{:S(2)}) collective-permute-start(f32[72,128]{1,0:T(8,128)S(1)} %add.88), channel_id=1, source_target_pairs={{40,0},{32,8},{56,16},{48,24},{8,32},{0,40},{24,48},{16,56},{104,6... | collective-permute-start | bytes 110600 | tf_op jit(solution)/shard_map/ppermute | solution.py:282
  79.3 6.5 %collective-permute-start.27 = (f32[72,128]{1,0:T(8,128)S(1)}, f32[72,128]{1,0:T(8,128)S(1)}, u32[]{:S(2)}, u32[]{:S(2)}) collective-permute-start(f32[72,128]{1,0:T(8,128)S(1)} %add_add_fusion.1), channel_id=1, source_target_pairs={{168,0},{160,8},{184,16},{176,24},{136,32},{128,40},{152,48},{144,... | collective-permute-start | bytes 110600 | tf_op jit(solution)/shard_map/ppermute | solution.py:282
  81.7 4.1 %collective-permute-start.26 = (f32[72,128]{1,0:T(8,128)S(1)}, f32[72,128]{1,0:T(8,128)S(1)}, u32[]{:S(2)}, u32[]{:S(2)}) collective-permute-start(f32[72,128]{1,0:T(8,128)S(1)} %add_add_fusion.1), channel_id=1, source_target_pairs={{64,0},{72,8},{80,16},{88,24},{224,32},{232,40},{240,48},{248,56},... | collective-permute-start | bytes 110600 | tf_op jit(solution)/shard_map/ppermute | solution.py:282
  83.3 5.3 %collective-permute-start.25 = (f32[72,128]{1,0:T(8,128)S(1)}, f32[72,128]{1,0:T(8,128)S(1)}, u32[]{:S(2)}, u32[]{:S(2)}) collective-permute-start(f32[72,128]{1,0:T(8,128)S(1)} %add_add_fusion.1), channel_id=1, source_target_pairs={{232,0},{224,8},{248,16},{240,24},{72,32},{64,40},{88,48},{80,56},... | collective-permute-start | bytes 110600 | tf_op jit(solution)/shard_map/ppermute | solution.py:282
  84.5 16.3 %collective-permute-start.31 = (f32[512,128]{1,0:T(8,128)S(1)}, f32[512,128]{1,0:T(8,128)S(1)}, u32[]{:S(2)}, u32[]{:S(2)}) collective-permute-start(f32[512,128]{1,0:T(8,128)S(1)} %get-tuple-element.46.refs_1_), channel_id=1, source_target_pairs={{7,0},{0,1},{1,2},{2,3},{3,4},{4,5},{5,6},{6,7},{15,8},{8,9},{9,10... | collective-permute-start | bytes 786440 | tf_op jit(solution)/shard_map/ppermute | solution.py:331
  88.6 8.1 %collective-permute-start.28 = (f32[72,128]{1,0:T(8,128)S(1)}, f32[72,128]{1,0:T(8,128)S(1)}, u32[]{:S(2)}, u32[]{:S(2)}) collective-permute-start(f32[72,128]{1,0:T(8,128)S(1)} %add_add_fusion.mine_ref), channel_id=1, source_target_pairs={{7,0},{0,1},{1,2},{2,3},{3,4},{4,5},{5,6},{6,7},{15,8},{8,9},{9,10... | collective-permute-start | bytes 110600 | tf_op jit(solution)/shard_map/ppermute | solution.py:331
  88.9 9.1 %collective-permute-start.30 = (f32[72,128]{1,0:T(8,128)S(1)}, f32[72,128]{1,0:T(8,128)S(1)}, u32[]{:S(2)}, u32[]{:S(2)}) collective-permute-start(f32[72,128]{1,0:T(8,128)S(1)} %add_add_fusion.mine_ref), channel_id=1, source_target_pairs={{8,0},{0,8},{24,16},{16,24},{40,32},{32,40},{56,48},{48,56},{72,64... | collective-permute-start | bytes 110600 | tf_op jit(solution)/shard_map/ppermute | solution.py:282
  96.7 4.2 %collective-permute-start.29 = (f32[72,128]{1,0:T(8,128)S(1)}, f32[72,128]{1,0:T(8,128)S(1)}, u32[]{:S(2)}, u32[]{:S(2)}) collective-permute-start(f32[72,128]{1,0:T(8,128)S(1)} %collective-permute-done.28.mine_ref), channel_id=1, source_target_pairs={{8,0},{0,8},{24,16},{16,24},{40,32},{32,40},{56,48},{48,56},{72,64... | collective-permute-start | bytes 110600 | tf_op jit(solution)/shard_map/ppermute | solution.py:282

commit v7 on v6

--- a/solution.py
+++ b/solution.py
@@ -294,10 +294,6 @@
     return source
 
 
-def owned_half(row):
-    return (row + row // 2 + row // QUAD) % 2
-
-
 def side(z):
     return 1 if z % 2 else -1
 
@@ -333,7 +329,8 @@
 
 def local(panel):
     n = panel.shape[1] // 2
-    core = owned_half(lax.axis_index("row")).astype(jnp.int32).reshape(1)
+    row = lax.axis_index("row")
+    core = ((row ^ (row >> 1) ^ (row >> 2)) & 1).astype(jnp.int32).reshape(1)
     for step in range(STEPS):
         if step == 0:
             own, mine, other = load(core, panel, n)

time: 104 us -> 104 us (level)
  no operation moved by 1% of the time
where the time goes in v7:
time: 104 us
  waiting for transfers between devices  43.4 us (42%)
  starting transfers between devices  41.2 us (40%)
  Pallas kernels  19.3 us (19%)
    ppermute x26, starting transfers between devices, from_row(): return lax.ppermute(x, 'row', route)  35.6 us
    ppermute x26, waiting for transfers between devices, from_row(): return lax.ppermute(x, 'row', route)  22.8 us
    ppermute x6, waiting for transfers between devices, shifted(): return lax.ppermute(block, 'pair', route)  20.6 us
    pallas_call x11, Pallas kernels, vmem_call(): pl.pallas_call(kernel, out_shape=shapes, in_specs=specs, scratch_shapes=s...  18 us
    ppermute x6, starting transfers between devices, shifted(): return lax.ppermute(block, 'pair', route)  5.62 us
  transfers between devices with their start and end apart: 32, of which 20 were waited for; matrix products, arithmetic and copies ran while one was open for 0% of the time, Pallas kernels for 9%

profile of v7, /device:TPU:1, one launch (start us, length us, event | category | flops | bytes accessed | tf_op | source)
XLA Modules:
  0.0 104.3 jit_solution(10586146445458618237)
XLA Ops:
  0.0 1.3 %load.1 = (f32[512,256]{1,0:T(8,128)S(1)}, f32[72,128]{1,0:T(8,128)S(1)}, f32[72,128]{1,0:T(8,128)S(1)}) custom-call(s32[1]{0:T(128)} %bitcast.core_ref, f32[512,256]{1,0:T(8,128)} %panel_ref.1), custom_call_target="tpu_custom_call" | custom-call | tf_op jit(solution)/shard_map/load/pallas_call | solution.py:231
  1.4 3.8 %collective-permute-start.9 = (f32[512,256]{1,0:T(8,128)S(1)}, f32[512,256]{1,0:T(8,128)S(1)}, u32[]{:S(2)}, u32[]{:S(2)}) collective-permute-start(f32[512,256]{1,0:T(8,128)S(1)} %get-tuple-element.32.refs_0_), channel_id=1, source_target_pairs={{7,0},{0,1},{1,2},{2,3},{3,4},{4,5},{5,6},{6,7},{15,8},{8,9},{9,10... | collective-permute-start | bytes 1572872 | tf_op jit(solution)/shard_map/ppermute | solution.py:327
  7.0 1.9 %collective-permute-start.1 = (f32[72,128]{1,0:T(8,128)S(1)}, f32[72,128]{1,0:T(8,128)S(1)}, u32[]{:S(2)}, u32[]{:S(2)}) collective-permute-start(f32[72,128]{1,0:T(8,128)S(1)} %add.60), channel_id=1, source_target_pairs={{40,0},{32,8},{56,16},{48,24},{8,32},{0,40},{24,48},{16,56},{104,6... | collective-permute-start | bytes 110600 | tf_op jit(solution)/shard_map/ppermute | solution.py:282
  8.9 1.6 %collective-permute-done.1 = f32[72,128]{1,0:T(8,128)S(1)} collective-permute-done((f32[72,128]{1,0:T(8,128)S(1)}, f32[72,128]{1,0:T(8,128)S(1)}, u32[]{:S(2)}, u32[]{:S(2)}) %collective-permute-start.1) | collective-permute-done | bytes 36896 | tf_op jit(solution)/shard_map/ppermute | solution.py:282
  10.5 6.6 %collective-permute-start.4 = (f32[72,128]{1,0:T(8,128)S(1)}, f32[72,128]{1,0:T(8,128)S(1)}, u32[]{:S(2)}, u32[]{:S(2)}) collective-permute-start(f32[72,128]{1,0:T(8,128)S(1)} %add.61), channel_id=1, source_target_pairs={{168,0},{160,8},{184,16},{176,24},{136,32},{128,40},{152,48},{144,... | collective-permute-start | bytes 110600 | tf_op jit(solution)/shard_map/ppermute | solution.py:282
  17.4 3.5 %collective-permute-start.2 = (f32[72,128]{1,0:T(8,128)S(1)}, f32[72,128]{1,0:T(8,128)S(1)}, u32[]{:S(2)}, u32[]{:S(2)}) collective-permute-start(f32[72,128]{1,0:T(8,128)S(1)} %add.61), channel_id=1, source_target_pairs={{232,0},{224,8},{248,16},{240,24},{72,32},{64,40},{88,48},{80,56},... | collective-permute-start | bytes 110600 | tf_op jit(solution)/shard_map/ppermute | solution.py:282
  20.9 2.0 %collective-permute-done.2 = f32[72,128]{1,0:T(8,128)S(1)} collective-permute-done((f32[72,128]{1,0:T(8,128)S(1)}, f32[72,128]{1,0:T(8,128)S(1)}, u32[]{:S(2)}, u32[]{:S(2)}) %collective-permute-start.2) | collective-permute-done | bytes 36896 | tf_op jit(solution)/shard_map/ppermute | solution.py:282
  23.1 3.3 %collective-permute-done.5 = f32[72,128]{1,0:T(8,128)S(1)} collective-permute-done((f32[72,128]{1,0:T(8,128)S(1)}, f32[72,128]{1,0:T(8,128)S(1)}, u32[]{:S(2)}, u32[]{:S(2)}) %collective-permute-start.5) | collective-permute-done | bytes 36896 | tf_op jit(solution)/shard_map/ppermute | solution.py:282
  26.4 1.4 %collective-permute-start.6 = (f32[72,128]{1,0:T(8,128)S(1)}, f32[72,128]{1,0:T(8,128)S(1)}, u32[]{:S(2)}, u32[]{:S(2)}) collective-permute-start(f32[72,128]{1,0:T(8,128)S(1)} %add.65.mine_ref), channel_id=1, source_target_pairs={{7,0},{0,1},{1,2},{2,3},{3,4},{4,5},{5,6},{6,7},{15,8},{8,9},{9,10... | collective-permute-start | bytes 110600 | tf_op jit(solution)/shard_map/ppermute | solution.py:327
  28.5 4.7 %collective-permute-done.6.mine_ref = f32[72,128]{1,0:T(8,128)S(1)} collective-permute-done((f32[72,128]{1,0:T(8,128)S(1)}, f32[72,128]{1,0:T(8,128)S(1)}, u32[]{:S(2)}, u32[]{:S(2)}) %collective-permute-start.6) | collective-permute-done | bytes 36896 | tf_op jit(solution)/shard_map/ppermute | solution.py:327
  33.9 1.8 %shard_map.17 = (f32[128,128]{1,0:T(8,128)S(1)}, f32[128,128]{1,0:T(8,128)S(1)}, f32[128,128]{1,0:T(8,128)S(1)}) custom-call(s32[1]{0:T(128)} %bitcast.core_ref, f32[72,128]{1,0:T(8,128)S(1)} %add.65.mine_ref, f32[72,128]{1,0:T(8,128)S(1)} %collective-permute-done.8.other_ref), custom_call_target="tpu_custom_call" | custom-call | tf_op jit(solution)/shard_map/pallas_call | solution.py:219
  36.7 2.8 %shard_map.19 = (f32[512,128]{1,0:T(8,128)S(1)}, f32[128,128]{1,0:T(8,128)S(1)}, f32[128,128]{1,0:T(8,128)S(1)}, f32[72,128]{1,0:T(8,128)S(1)}, f32[72,128]{1,0:T(8,128)S(1)}) custom-call(s32[1]{0:T(128)} %bitcast.core_ref, f32[72,128]{1,0:T(8,128)S(1)} %collective-permute-done.6.mine_ref, f32[72,128]{1,0:T(8,128)S(1)} %collective-permute-done.7.other_ref, ...), custom_call_target="tpu_custom_call" | custom-call | tf_op jit(solution)/shard_map/pallas_call | solution.py:219
  39.6 1.2 %collective-permute-done.10 = f32[72,128]{1,0:T(8,128)S(1)} collective-permute-done((f32[72,128]{1,0:T(8,128)S(1)}, f32[72,128]{1,0:T(8,128)S(1)}, u32[]{:S(2)}, u32[]{:S(2)}) %collective-permute-start.10) | collective-permute-done | bytes 36896 | tf_op jit(solution)/shard_map/ppermute | solution.py:282
  40.8 2.0 %collective-permute-start.13 = (f32[72,128]{1,0:T(8,128)S(1)}, f32[72,128]{1,0:T(8,128)S(1)}, u32[]{:S(2)}, u32[]{:S(2)}) collective-permute-start(f32[72,128]{1,0:T(8,128)S(1)} %add.66), channel_id=1, source_target_pairs={{48,0},{56,8},{32,16},{40,24},{16,32},{24,40},{0,48},{8,56},{112,6... | collective-permute-start | bytes 110600 | tf_op jit(solution)/shard_map/ppermute | solution.py:282
  44.5 2.1 %collective-permute-done.12 = f32[72,128]{1,0:T(8,128)S(1)} collective-permute-done((f32[72,128]{1,0:T(8,128)S(1)}, f32[72,128]{1,0:T(8,128)S(1)}, u32[]{:S(2)}, u32[]{:S(2)}) %collective-permute-start.12) | collective-permute-done | bytes 36896 | tf_op jit(solution)/shard_map/ppermute | solution.py:282
  47.3 3.4 %collective-permute-start.16 = (f32[72,128]{1,0:T(8,128)S(1)}, f32[72,128]{1,0:T(8,128)S(1)}, u32[]{:S(2)}, u32[]{:S(2)}) collective-permute-start(f32[72,128]{1,0:T(8,128)S(1)} %add_add_fusion.3), channel_id=1, source_target_pairs={{168,0},{160,8},{184,16},{176,24},{136,32},{128,40},{152,48},{144,... | collective-permute-start | bytes 110600 | tf_op jit(solution)/shard_map/ppermute | solution.py:282
  51.4 2.3 %collective-permute-start.14 = (f32[72,128]{1,0:T(8,128)S(1)}, f32[72,128]{1,0:T(8,128)S(1)}, u32[]{:S(2)}, u32[]{:S(2)}) collective-permute-start(f32[72,128]{1,0:T(8,128)S(1)} %add_add_fusion.3), channel_id=1, source_target_pairs={{232,0},{224,8},{248,16},{240,24},{72,32},{64,40},{88,48},{80,56},... | collective-permute-start | bytes 110600 | tf_op jit(solution)/shard_map/ppermute | solution.py:282
  54.4 2.2 %collective-permute-done.14 = f32[72,128]{1,0:T(8,128)S(1)} collective-permute-done((f32[72,128]{1,0:T(8,128)S(1)}, f32[72,128]{1,0:T(8,128)S(1)}, u32[]{:S(2)}, u32[]{:S(2)}) %collective-permute-start.14) | collective-permute-done | bytes 36896 | tf_op jit(solution)/shard_map/ppermute | solution.py:282
  57.2 8.6 %collective-permute-done.17.mine_ref = f32[72,128]{1,0:T(8,128)S(1)} collective-permute-done((f32[72,128]{1,0:T(8,128)S(1)}, f32[72,128]{1,0:T(8,128)S(1)}, u32[]{:S(2)}, u32[]{:S(2)}) %collective-permute-start.17) | collective-permute-done | bytes 36896 | tf_op jit(solution)/shard_map/ppermute | solution.py:327
  67.2 1.8 %shard_map.20 = (f32[128,128]{1,0:T(8,128)S(1)}, f32[128,128]{1,0:T(8,128)S(1)}, f32[128,128]{1,0:T(8,128)S(1)}) custom-call(s32[1]{0:T(128)} %bitcast.core_ref, f32[72,128]{1,0:T(8,128)S(1)} %add_add_fusion.2.mine_ref, f32[72,128]{1,0:T(8,128)S(1)} %collective-permute-done.19.other_ref), custom_call_target="tpu_custom_call" | custom-call | tf_op jit(solution)/shard_map/pallas_call | solution.py:219
  70.0 2.8 %shard_map.23 = (f32[512,128]{1,0:T(8,128)S(1)}, f32[128,128]{1,0:T(8,128)S(1)}, f32[128,128]{1,0:T(8,128)S(1)}, f32[72,128]{1,0:T(8,128)S(1)}, f32[72,128]{1,0:T(8,128)S(1)}) custom-call(s32[1]{0:T(128)} %bitcast.core_ref, f32[72,128]{1,0:T(8,128)S(1)} %collective-permute-done.17.mine_ref, f32[72,128]{1,0:T(8,128)S(1)} %collective-permute-done.18.other_ref, ...), custom_call_target="tpu_custom_call" | custom-call | tf_op jit(solution)/shard_map/pallas_call | solution.py:219
  72.9 1.2 %collective-permute-done.21 = f32[72,128]{1,0:T(8,128)S(1)} collective-permute-done((f32[72,128]{1,0:T(8,128)S(1)}, f32[72,128]{1,0:T(8,128)S(1)}, u32[]{:S(2)}, u32[]{:S(2)}) %collective-permute-start.21) | collective-permute-done | bytes 36896 | tf_op jit(solution)/shard_map/ppermute | solution.py:282
  74.5 1.4 %collective-permute-start.23 = (f32[72,128]{1,0:T(8,128)S(1)}, f32[72,128]{1,0:T(8,128)S(1)}, u32[]{:S(2)}, u32[]{:S(2)}) collective-permute-start(f32[72,128]{1,0:T(8,128)S(1)} %add.73), channel_id=1, source_target_pairs={{24,0},{16,8},{8,16},{0,24},{56,32},{48,40},{40,48},{32,56},{88,64... | collective-permute-start | bytes 110600 | tf_op jit(solution)/shard_map/ppermute | solution.py:282
  75.9 1.2 %collective-permute-start.22 = (f32[72,128]{1,0:T(8,128)S(1)}, f32[72,128]{1,0:T(8,128)S(1)}, u32[]{:S(2)}, u32[]{:S(2)}) collective-permute-start(f32[72,128]{1,0:T(8,128)S(1)} %add.73), channel_id=1, source_target_pairs={{40,0},{32,8},{56,16},{48,24},{8,32},{0,40},{24,48},{16,56},{104,6... | collective-permute-start | bytes 110600 | tf_op jit(solution)/shard_map/ppermute | solution.py:282
  79.3 2.4 %collective-permute-start.27 = (f32[72,128]{1,0:T(8,128)S(1)}, f32[72,128]{1,0:T(8,128)S(1)}, u32[]{:S(2)}, u32[]{:S(2)}) collective-permute-start(f32[72,128]{1,0:T(8,128)S(1)} %add_add_fusion.1), channel_id=1, source_target_pairs={{168,0},{160,8},{184,16},{176,24},{136,32},{128,40},{152,48},{144,... | collective-permute-start | bytes 110600 | tf_op jit(solution)/shard_map/ppermute | solution.py:282
  81.7 1.7 %collective-permute-start.26 = (f32[72,128]{1,0:T(8,128)S(1)}, f32[72,128]{1,0:T(8,128)S(1)}, u32[]{:S(2)}, u32[]{:S(2)}) collective-permute-start(f32[72,128]{1,0:T(8,128)S(1)} %add_add_fusion.1), channel_id=1, source_target_pairs={{64,0},{72,8},{80,16},{88,24},{224,32},{232,40},{240,48},{248,56},... | collective-permute-start | bytes 110600 | tf_op jit(solution)/shard_map/ppermute | solution.py:282
  83.3 1.2 %collective-permute-start.25 = (f32[72,128]{1,0:T(8,128)S(1)}, f32[72,128]{1,0:T(8,128)S(1)}, u32[]{:S(2)}, u32[]{:S(2)}) collective-permute-start(f32[72,128]{1,0:T(8,128)S(1)} %add_add_fusion.1), channel_id=1, source_target_pairs={{232,0},{224,8},{248,16},{240,24},{72,32},{64,40},{88,48},{80,56},... | collective-permute-start | bytes 110600 | tf_op jit(solution)/shard_map/ppermute | solution.py:282
  84.5 1.2 %collective-permute-done.27 = f32[72,128]{1,0:T(8,128)S(1)} collective-permute-done((f32[72,128]{1,0:T(8,128)S(1)}, f32[72,128]{1,0:T(8,128)S(1)}, u32[]{:S(2)}, u32[]{:S(2)}) %collective-permute-start.27) | collective-permute-done | bytes 36896 | tf_op jit(solution)/shard_map/ppermute | solution.py:282
  85.7 2.8 %collective-permute-done.25 = f32[72,128]{1,0:T(8,128)S(1)} collective-permute-done((f32[72,128]{1,0:T(8,128)S(1)}, f32[72,128]{1,0:T(8,128)S(1)}, u32[]{:S(2)}, u32[]{:S(2)}) %collective-permute-start.25) | collective-permute-done | bytes 36896 | tf_op jit(solution)/shard_map/ppermute | solution.py:282
  89.4 7.3 %collective-permute-done.28.mine_ref = f32[72,128]{1,0:T(8,128)S(1)} collective-permute-done((f32[72,128]{1,0:T(8,128)S(1)}, f32[72,128]{1,0:T(8,128)S(1)}, u32[]{:S(2)}, u32[]{:S(2)}) %collective-permute-start.28) | collective-permute-done | bytes 36896 | tf_op jit(solution)/shard_map/ppermute | solution.py:327
  98.0 1.8 %shard_map.24 = (f32[128,128]{1,0:T(8,128)S(1)}, f32[128,128]{1,0:T(8,128)S(1)}, f32[128,128]{1,0:T(8,128)S(1)}) custom-call(s32[1]{0:T(128)} %bitcast.core_ref, f32[72,128]{1,0:T(8,128)S(1)} %add_add_fusion.mine_ref, f32[72,128]{1,0:T(8,128)S(1)} %collective-permute-done.30.other_ref), custom_call_target="tpu_custom_call" | custom-call | tf_op jit(solution)/shard_map/pallas_call | solution.py:219
  100.9 3.3 %shard_map.27 = f32[512,256]{1,0:T(8,128)} custom-call(s32[1]{0:T(128)} %bitcast.core_ref, f32[72,128]{1,0:T(8,128)S(1)} %collective-permute-done.28.mine_ref, f32[72,128]{1,0:T(8,128)S(1)} %collective-permute-done.29.other_ref, f32[512,128]{1,0:T(8,128)S(1)} %shard_map.25.own_ref, f32[512,128]{1,0:T(8,128)S(1)} %shard_map.26.refs_0_, ...), custom_call_target="tpu_custom_call" | custom-call | tf_op jit(solution)/shard_map/pallas_call | solution.py:219
  (54 shorter events, 17.3 us)
Async XLA Ops:
  1.4 35.4 %collective-permute-start.9 = (f32[512,256]{1,0:T(8,128)S(1)}, f32[512,256]{1,0:T(8,128)S(1)}, u32[]{:S(2)}, u32[]{:S(2)}) collective-permute-start(f32[512,256]{1,0:T(8,128)S(1)} %get-tuple-element.32.refs_0_), channel_id=1, source_target_pairs={{7,0},{0,1},{1,2},{2,3},{3,4},{4,5},{5,6},{6,7},{15,8},{8,9},{9,10... | collective-permute-start | bytes 1572872 | tf_op jit(solution)/shard_map/ppermute | solution.py:327
  5.2 1.8 %collective-permute-start = (f32[72,128]{1,0:T(8,128)S(1)}, f32[72,128]{1,0:T(8,128)S(1)}, u32[]{:S(2)}, u32[]{:S(2)}) collective-permute-start(f32[72,128]{1,0:T(8,128)S(1)} %get-tuple-element.28), channel_id=1, source_target_pairs={{8,0},{0,8},{24,16},{16,24},{40,32},{32,40},{56,48},{48,56},{72,64... | collective-permute-start | bytes 110600 | tf_op jit(solution)/shard_map/ppermute | solution.py:282
  7.0 3.5 %collective-permute-start.1 = (f32[72,128]{1,0:T(8,128)S(1)}, f32[72,128]{1,0:T(8,128)S(1)}, u32[]{:S(2)}, u32[]{:S(2)}) collective-permute-start(f32[72,128]{1,0:T(8,128)S(1)} %add.60), channel_id=1, source_target_pairs={{40,0},{32,8},{56,16},{48,24},{8,32},{0,40},{24,48},{16,56},{104,6... | collective-permute-start | bytes 110600 | tf_op jit(solution)/shard_map/ppermute | solution.py:282
  10.5 10.4 %collective-permute-start.4 = (f32[72,128]{1,0:T(8,128)S(1)}, f32[72,128]{1,0:T(8,128)S(1)}, u32[]{:S(2)}, u32[]{:S(2)}) collective-permute-start(f32[72,128]{1,0:T(8,128)S(1)} %add.61), channel_id=1, source_target_pairs={{168,0},{160,8},{184,16},{176,24},{136,32},{128,40},{152,48},{144,... | collective-permute-start | bytes 110600 | tf_op jit(solution)/shard_map/ppermute | solution.py:282
  17.1 3.7 %collective-permute-start.3 = (f32[72,128]{1,0:T(8,128)S(1)}, f32[72,128]{1,0:T(8,128)S(1)}, u32[]{:S(2)}, u32[]{:S(2)}) collective-permute-start(f32[72,128]{1,0:T(8,128)S(1)} %add.61), channel_id=1, source_target_pairs={{64,0},{72,8},{80,16},{88,24},{224,32},{232,40},{240,48},{248,56},... | collective-permute-start | bytes 110600 | tf_op jit(solution)/shard_map/ppermute | solution.py:282
  17.4 5.5 %collective-permute-start.2 = (f32[72,128]{1,0:T(8,128)S(1)}, f32[72,128]{1,0:T(8,128)S(1)}, u32[]{:S(2)}, u32[]{:S(2)}) collective-permute-start(f32[72,128]{1,0:T(8,128)S(1)} %add.61), channel_id=1, source_target_pairs={{232,0},{224,8},{248,16},{240,24},{72,32},{64,40},{88,48},{80,56},... | collective-permute-start | bytes 110600 | tf_op jit(solution)/shard_map/ppermute | solution.py:282
  22.9 3.5 %collective-permute-start.5 = (f32[72,128]{1,0:T(8,128)S(1)}, f32[72,128]{1,0:T(8,128)S(1)}, u32[]{:S(2)}, u32[]{:S(2)}) collective-permute-start(f32[72,128]{1,0:T(8,128)S(1)} %add_add_fusion.4), channel_id=1, source_target_pairs={{24,0},{16,8},{8,16},{0,24},{56,32},{48,40},{40,48},{32,56},{88,64... | collective-permute-start | bytes 110600 | tf_op jit(solution)/shard_map/ppermute | solution.py:282
  26.4 6.8 %collective-permute-start.6 = (f32[72,128]{1,0:T(8,128)S(1)}, f32[72,128]{1,0:T(8,128)S(1)}, u32[]{:S(2)}, u32[]{:S(2)}) collective-permute-start(f32[72,128]{1,0:T(8,128)S(1)} %add.65.mine_ref), channel_id=1, source_target_pairs={{7,0},{0,1},{1,2},{2,3},{3,4},{4,5},{5,6},{6,7},{15,8},{8,9},{9,10... | collective-permute-start | bytes 110600 | tf_op jit(solution)/shard_map/ppermute | solution.py:327
  27.8 6.1 %collective-permute-start.8 = (f32[72,128]{1,0:T(8,128)S(1)}, f32[72,128]{1,0:T(8,128)S(1)}, u32[]{:S(2)}, u32[]{:S(2)}) collective-permute-start(f32[72,128]{1,0:T(8,128)S(1)} %add.65.mine_ref), channel_id=1, source_target_pairs={{8,0},{0,8},{24,16},{16,24},{40,32},{32,40},{56,48},{48,56},{72,64... | collective-permute-start | bytes 110600 | tf_op jit(solution)/shard_map/ppermute | solution.py:282
  33.2 3.5 %collective-permute-start.7 = (f32[72,128]{1,0:T(8,128)S(1)}, f32[72,128]{1,0:T(8,128)S(1)}, u32[]{:S(2)}, u32[]{:S(2)}) collective-permute-start(f32[72,128]{1,0:T(8,128)S(1)} %collective-permute-done.6.mine_ref), channel_id=1, source_target_pairs={{8,0},{0,8},{24,16},{16,24},{40,32},{32,40},{56,48},{48,56},{72,64... | collective-permute-start | bytes 110600 | tf_op jit(solution)/shard_map/ppermute | solution.py:282
  39.5 1.3 %collective-permute-start.10 = (f32[72,128]{1,0:T(8,128)S(1)}, f32[72,128]{1,0:T(8,128)S(1)}, u32[]{:S(2)}, u32[]{:S(2)}) collective-permute-start(f32[72,128]{1,0:T(8,128)S(1)} %get-tuple-element.34), channel_id=1, source_target_pairs={{8,0},{0,8},{24,16},{16,24},{40,32},{32,40},{56,48},{48,56},{72,64... | collective-permute-start | bytes 110600 | tf_op jit(solution)/shard_map/ppermute | solution.py:282
  40.8 3.7 %collective-permute-start.13 = (f32[72,128]{1,0:T(8,128)S(1)}, f32[72,128]{1,0:T(8,128)S(1)}, u32[]{:S(2)}, u32[]{:S(2)}) collective-permute-start(f32[72,128]{1,0:T(8,128)S(1)} %add.66), channel_id=1, source_target_pairs={{48,0},{56,8},{32,16},{40,24},{16,32},{24,40},{0,48},{8,56},{112,6... | collective-permute-start | bytes 110600 | tf_op jit(solution)/shard_map/ppermute | solution.py:282
  42.8 3.8 %collective-permute-start.12 = (f32[72,128]{1,0:T(8,128)S(1)}, f32[72,128]{1,0:T(8,128)S(1)}, u32[]{:S(2)}, u32[]{:S(2)}) collective-permute-start(f32[72,128]{1,0:T(8,128)S(1)} %add.66), channel_id=1, source_target_pairs={{24,0},{16,8},{8,16},{0,24},{56,32},{48,40},{40,48},{32,56},{88,64... | collective-permute-start | bytes 110600 | tf_op jit(solution)/shard_map/ppermute | solution.py:282
  43.9 3.4 %collective-permute-start.11 = (f32[72,128]{1,0:T(8,128)S(1)}, f32[72,128]{1,0:T(8,128)S(1)}, u32[]{:S(2)}, u32[]{:S(2)}) collective-permute-start(f32[72,128]{1,0:T(8,128)S(1)} %add.66), channel_id=1, source_target_pairs={{40,0},{32,8},{56,16},{48,24},{8,32},{0,40},{24,48},{16,56},{104,6... | collective-permute-start | bytes 110600 | tf_op jit(solution)/shard_map/ppermute | solution.py:282
  47.3 6.8 %collective-permute-start.16 = (f32[72,128]{1,0:T(8,128)S(1)}, f32[72,128]{1,0:T(8,128)S(1)}, u32[]{:S(2)}, u32[]{:S(2)}) collective-permute-start(f32[72,128]{1,0:T(8,128)S(1)} %add_add_fusion.3), channel_id=1, source_target_pairs={{168,0},{160,8},{184,16},{176,24},{136,32},{128,40},{152,48},{144,... | collective-permute-start | bytes 110600 | tf_op jit(solution)/shard_map/ppermute | solution.py:282
  50.7 3.7 %collective-permute-start.15 = (f32[72,128]{1,0:T(8,128)S(1)}, f32[72,128]{1,0:T(8,128)S(1)}, u32[]{:S(2)}, u32[]{:S(2)}) collective-permute-start(f32[72,128]{1,0:T(8,128)S(1)} %add_add_fusion.3), channel_id=1, source_target_pairs={{64,0},{72,8},{80,16},{88,24},{224,32},{232,40},{240,48},{248,56},... | collective-permute-start | bytes 110600 | tf_op jit(solution)/shard_map/ppermute | solution.py:282
  51.4 5.3 %collective-permute-start.14 = (f32[72,128]{1,0:T(8,128)S(1)}, f32[72,128]{1,0:T(8,128)S(1)}, u32[]{:S(2)}, u32[]{:S(2)}) collective-permute-start(f32[72,128]{1,0:T(8,128)S(1)} %add_add_fusion.3), channel_id=1, source_target_pairs={{232,0},{224,8},{248,16},{240,24},{72,32},{64,40},{88,48},{80,56},... | collective-permute-start | bytes 110600 | tf_op jit(solution)/shard_map/ppermute | solution.py:282
  53.7 16.3 %collective-permute-start.20 = (f32[512,128]{1,0:T(8,128)S(1)}, f32[512,128]{1,0:T(8,128)S(1)}, u32[]{:S(2)}, u32[]{:S(2)}) collective-permute-start(f32[512,128]{1,0:T(8,128)S(1)} %get-tuple-element.38.refs_1_), channel_id=1, source_target_pairs={{7,0},{0,1},{1,2},{2,3},{3,4},{4,5},{5,6},{6,7},{15,8},{8,9},{9,10... | collective-permute-start | bytes 786440 | tf_op jit(solution)/shard_map/ppermute | solution.py:327
  56.6 9.2 %collective-permute-start.17 = (f32[72,128]{1,0:T(8,128)S(1)}, f32[72,128]{1,0:T(8,128)S(1)}, u32[]{:S(2)}, u32[]{:S(2)}) collective-permute-start(f32[72,128]{1,0:T(8,128)S(1)} %add_add_fusion.2.mine_ref), channel_id=1, source_target_pairs={{7,0},{0,1},{1,2},{2,3},{3,4},{4,5},{5,6},{6,7},{15,8},{8,9},{9,10... | collective-permute-start | bytes 110600 | tf_op jit(solution)/shard_map/ppermute | solution.py:327
  56.7 10.5 %collective-permute-start.19 = (f32[72,128]{1,0:T(8,128)S(1)}, f32[72,128]{1,0:T(8,128)S(1)}, u32[]{:S(2)}, u32[]{:S(2)}) collective-permute-start(f32[72,128]{1,0:T(8,128)S(1)} %add_add_fusion.2.mine_ref), channel_id=1, source_target_pairs={{8,0},{0,8},{24,16},{16,24},{40,32},{32,40},{56,48},{48,56},{72,64... | collective-permute-start | bytes 110600 | tf_op jit(solution)/shard_map/ppermute | solution.py:282
  65.8 4.2 %collective-permute-start.18 = (f32[72,128]{1,0:T(8,128)S(1)}, f32[72,128]{1,0:T(8,128)S(1)}, u32[]{:S(2)}, u32[]{:S(2)}) collective-permute-start(f32[72,128]{1,0:T(8,128)S(1)} %collective-permute-done.17.mine_ref), channel_id=1, source_target_pairs={{8,0},{0,8},{24,16},{16,24},{40,32},{32,40},{56,48},{48,56},{72,64... | collective-permute-start | bytes 110600 | tf_op jit(solution)/shard_map/ppermute | solution.py:282
  72.8 1.3 %collective-permute-start.21 = (f32[72,128]{1,0:T(8,128)S(1)}, f32[72,128]{1,0:T(8,128)S(1)}, u32[]{:S(2)}, u32[]{:S(2)}) collective-permute-start(f32[72,128]{1,0:T(8,128)S(1)} %get-tuple-element.42), channel_id=1, source_target_pairs={{8,0},{0,8},{24,16},{16,24},{40,32},{32,40},{56,48},{48,56},{72,64... | collective-permute-start | bytes 110600 | tf_op jit(solution)/shard_map/ppermute | solution.py:282
  74.1 3.8 %collective-permute-start.24 = (f32[72,128]{1,0:T(8,128)S(1)}, f32[72,128]{1,0:T(8,128)S(1)}, u32[]{:S(2)}, u32[]{:S(2)}) collective-permute-start(f32[72,128]{1,0:T(8,128)S(1)} %add.73), channel_id=1, source_target_pairs={{48,0},{56,8},{32,16},{40,24},{16,32},{24,40},{0,48},{8,56},{112,6... | collective-permute-start | bytes 110600 | tf_op jit(solution)/shard_map/ppermute | solution.py:282
  74.5 4.4 %collective-permute-start.23 = (f32[72,128]{1,0:T(8,128)S(1)}, f32[72,128]{1,0:T(8,128)S(1)}, u32[]{:S(2)}, u32[]{:S(2)}) collective-permute-start(f32[72,128]{1,0:T(8,128)S(1)} %add.73), channel_id=1, source_target_pairs={{24,0},{16,8},{8,16},{0,24},{56,32},{48,40},{40,48},{32,56},{88,64... | collective-permute-start | bytes 110600 | tf_op jit(solution)/shard_map/ppermute | solution.py:282
  75.9 3.4 %collective-permute-start.22 = (f32[72,128]{1,0:T(8,128)S(1)}, f32[72,128]{1,0:T(8,128)S(1)}, u32[]{:S(2)}, u32[]{:S(2)}) collective-permute-start(f32[72,128]{1,0:T(8,128)S(1)} %add.73), channel_id=1, source_target_pairs={{40,0},{32,8},{56,16},{48,24},{8,32},{0,40},{24,48},{16,56},{104,6... | collective-permute-start | bytes 110600 | tf_op jit(solution)/shard_map/ppermute | solution.py:282
  79.3 6.5 %collective-permute-start.27 = (f32[72,128]{1,0:T(8,128)S(1)}, f32[72,128]{1,0:T(8,128)S(1)}, u32[]{:S(2)}, u32[]{:S(2)}) collective-permute-start(f32[72,128]{1,0:T(8,128)S(1)} %add_add_fusion.1), channel_id=1, source_target_pairs={{168,0},{160,8},{184,16},{176,24},{136,32},{128,40},{152,48},{144,... | collective-permute-start | bytes 110600 | tf_op jit(solution)/shard_map/ppermute | solution.py:282
  81.7 4.1 %collective-permute-start.26 = (f32[72,128]{1,0:T(8,128)S(1)}, f32[72,128]{1,0:T(8,128)S(1)}, u32[]{:S(2)}, u32[]{:S(2)}) collective-permute-start(f32[72,128]{1,0:T(8,128)S(1)} %add_add_fusion.1), channel_id=1, source_target_pairs={{64,0},{72,8},{80,16},{88,24},{224,32},{232,40},{240,48},{248,56},... | collective-permute-start | bytes 110600 | tf_op jit(solution)/shard_map/ppermute | solution.py:282
  83.3 5.3 %collective-permute-start.25 = (f32[72,128]{1,0:T(8,128)S(1)}, f32[72,128]{1,0:T(8,128)S(1)}, u32[]{:S(2)}, u32[]{:S(2)}) collective-permute-start(f32[72,128]{1,0:T(8,128)S(1)} %add_add_fusion.1), channel_id=1, source_target_pairs={{232,0},{224,8},{248,16},{240,24},{72,32},{64,40},{88,48},{80,56},... | collective-permute-start | bytes 110600 | tf_op jit(solution)/shard_map/ppermute | solution.py:282
  84.5 16.3 %collective-permute-start.31 = (f32[512,128]{1,0:T(8,128)S(1)}, f32[512,128]{1,0:T(8,128)S(1)}, u32[]{:S(2)}, u32[]{:S(2)}) collective-permute-start(f32[512,128]{1,0:T(8,128)S(1)} %get-tuple-element.46.refs_1_), channel_id=1, source_target_pairs={{7,0},{0,1},{1,2},{2,3},{3,4},{4,5},{5,6},{6,7},{15,8},{8,9},{9,10... | collective-permute-start | bytes 786440 | tf_op jit(solution)/shard_map/ppermute | solution.py:327
  88.6 8.1 %collective-permute-start.28 = (f32[72,128]{1,0:T(8,128)S(1)}, f32[72,128]{1,0:T(8,128)S(1)}, u32[]{:S(2)}, u32[]{:S(2)}) collective-permute-start(f32[72,128]{1,0:T(8,128)S(1)} %add_add_fusion.mine_ref), channel_id=1, source_target_pairs={{7,0},{0,1},{1,2},{2,3},{3,4},{4,5},{5,6},{6,7},{15,8},{8,9},{9,10... | collective-permute-start | bytes 110600 | tf_op jit(solution)/shard_map/ppermute | solution.py:327
  88.9 9.1 %collective-permute-start.30 = (f32[72,128]{1,0:T(8,128)S(1)}, f32[72,128]{1,0:T(8,128)S(1)}, u32[]{:S(2)}, u32[]{:S(2)}) collective-permute-start(f32[72,128]{1,0:T(8,128)S(1)} %add_add_fusion.mine_ref), channel_id=1, source_target_pairs={{8,0},{0,8},{24,16},{16,24},{40,32},{32,40},{56,48},{48,56},{72,64... | collective-permute-start | bytes 110600 | tf_op jit(solution)/shard_map/ppermute | solution.py:282
  96.7 4.2 %collective-permute-start.29 = (f32[72,128]{1,0:T(8,128)S(1)}, f32[72,128]{1,0:T(8,128)S(1)}, u32[]{:S(2)}, u32[]{:S(2)}) collective-permute-start(f32[72,128]{1,0:T(8,128)S(1)} %collective-permute-done.28.mine_ref), channel_id=1, source_target_pairs={{8,0},{0,8},{24,16},{16,24},{40,32},{32,40},{56,48},{48,56},{72,64... | collective-permute-start | bytes 110600 | tf_op jit(solution)/shard_map/ppermute | solution.py:282

commit v8 on v7

--- a/solution.py
+++ b/solution.py
@@ -129,9 +129,9 @@
     message(squares(a), squares(b), cross_of(a, b), core_ref[0], cross_ref, mine_ref, other_ref)
 
 
-def cosines_of(core_ref, mine_ref, other_ref):
+def cosines_of(owned, mine_ref, other_ref):
     half = mine_ref.shape[0] - PAD
-    first = core_ref[0] == 0
+    first = owned == 0
     mine = mine_ref[...]
     other = other_ref[...]
     low = jnp.where(first, mine, other)
@@ -150,7 +150,7 @@
 
 
 def head_kernel(core_ref, mine_ref, other_ref, base_out, x_out, d_out):
-    d = cosines_of(core_ref, mine_ref, other_ref)
+    d = cosines_of(core_ref[0], mine_ref, other_ref)
     d_out[...] = d
     base_out[...], x_out[...] = rough_inverse(d, jnp.transpose(d))
 
@@ -169,7 +169,7 @@
 
 def second_kernel(core_ref, mine_ref, other_ref, own_ref, *refs):
     *blocks, b_out, m_out, md_out, mine_out, other_out, cross_ref = refs
-    d = cosines_of(core_ref, mine_ref, other_ref)
+    d = cosines_of(1 - core_ref[0], mine_ref, other_ref)
     dt = jnp.transpose(d)
     a, b = both_blocks(blocks)
     turned = left3(a - times3(left3(b), right3(dt)))
@@ -189,7 +189,7 @@
     rows, n = own_ref.shape
     copies = [pltpu.make_async_copy(own_ref, out_ref.at[:, :n], sems.at[CHUNKS])]
     copies[0].start()
-    d = cosines_of(core_ref, mine_ref, other_ref)
+    d = cosines_of(1 - core_ref[0], mine_ref, other_ref)
     dt = jnp.transpose(d)
     a, b = both_blocks(blocks)
     turned = left3(a - times3(left3(b), right3(dt)))
@@ -301,16 +301,16 @@
 def summed_halves(mine, other, y_last):
     incoming = from_row(other, mate)
     x = mine + incoming
-    next_z = from_row(x, owner(lambda z, y: (z ^ 1, y)))
+    next_z = from_row(x, owner(lambda z, y: (z + side(z), y)))
     if y_last:
         x = x + next_z
     else:
         next_y = from_row(x, owner(lambda z, y: (z, 1 - y)))
-        next_zy = from_row(x, owner(lambda z, y: (z ^ 1, 1 - y)))
+        next_zy = from_row(x, owner(lambda z, y: (z + side(z), 1 - y)))
         x = ((x + next_z) + next_y) + next_zy
-    by_one = from_row(x, owner(lambda z, y: (z + side(z), y)))
-    by_two = from_row(x, owner(lambda z, y: (z - 2 * side(z), y)))
-    by_three = from_row(x, owner(lambda z, y: (z + 3 * side(z), y)))
+    by_one = from_row(x, owner(lambda z, y: (z - side(z), y)))
+    by_two = from_row(x, owner(lambda z, y: (z + 2 * side(z), y)))
+    by_three = from_row(x, owner(lambda z, y: (z - 3 * side(z), y)))
     x = ((x + by_one) + by_two) + by_three
     if y_last:
         x = x + from_row(x, owner(lambda z, y: (z, 1 - y)))
@@ -325,6 +325,16 @@
     devices = range(lax.axis_size("pair"))
     route = [((i - 1) % len(devices), i) for i in devices]
     return lax.ppermute(block, "pair", route)
+
+
+def hopped_over(half):
+    pairs = lax.axis_size("pair")
+    route = []
+    for row in range(lax.axis_size("row")):
+        for pair in range(pairs):
+            source = (row ^ 1) * pairs + (pair - 1) % pairs
+            route.append((source, row * pairs + pair))
+    return lax.ppermute(half, ("row", "pair"), route)
 
 
 def local(panel):
@@ -340,7 +350,7 @@
             second = shifted(b)
             before = [turn_late(m, md, before, n), second]
         half = summed_halves(mine, other, y_last=step == 0)
-        hopped = shifted(half)
+        hopped = hopped_over(half)
         own_halves = with_other(half)
         squares = turn_head(core, own_halves, n)
         halves = with_other(hopped)

time: 104 us -> 106 us (1.019)
  waiting for transfers between devices: 43.4 us -> 45.1 us
    ppermute x0 -> x3, waiting for transfers between devices: none -> 22.2 us  [hopped_over(): return lax.ppermute(half, ('row', 'pair'), route)]
    ppermute x6 -> x3, waiting for transfers between devices: 20.6 us -> 0.01 us  [shifted(): return lax.ppermute(block, 'pair', route)]
    ppermute x0 -> x3, starting transfers between devices: none -> 2.05 us  [hopped_over(): return lax.ppermute(half, ('row', 'pair'), route)]
    ppermute x6 -> x3, starting transfers between devices: 5.62 us -> 3.81 us  [shifted(): return lax.ppermute(block, 'pair', route)]
  transfers between devices with their start and end apart: 32 -> 32, of which waited for: 20 -> 22; matrix products, arithmetic and copies ran while one was open for 0% -> 0% of each run, Pallas kernels for 9% -> 9%
where the time goes in v8:
time: 106 us
  waiting for transfers between devices  45.1 us (43%)
  starting transfers between devices  40.8 us (38%)
  Pallas kernels  19.3 us (18%)
    ppermute x26, starting transfers between devices, from_row(): return lax.ppermute(x, 'row', route)  34.9 us
    ppermute x26, waiting for transfers between devices, from_row(): return lax.ppermute(x, 'row', route)  22.8 us
    ppermute x3, waiting for transfers between devices, hopped_over(): return lax.ppermute(half, ('row', 'pair'), route)  22.2 us
    pallas_call x11, Pallas kernels, vmem_call(): pl.pallas_call(kernel, out_shape=shapes, in_specs=specs, scratch_shapes=s...  18 us
    ppermute x3, starting transfers between devices, shifted(): return lax.ppermute(block, 'pair', route)  3.81 us
  transfers between devices with their start and end apart: 32, of which 22 were waited for; matrix products, arithmetic and copies ran while one was open for 0% of the time, Pallas kernels for 9%

profile of v8, /device:TPU:1, one launch (start us, length us, event | category | flops | bytes accessed | tf_op | source)
XLA Modules:
  0.0 105.6 jit_solution(5469310549371261215)
XLA Ops:
  0.0 1.3 %load.1 = (f32[512,256]{1,0:T(8,128)S(1)}, f32[72,128]{1,0:T(8,128)S(1)}, f32[72,128]{1,0:T(8,128)S(1)}) custom-call(s32[1]{0:T(128)} %bitcast.core_ref, f32[512,256]{1,0:T(8,128)} %panel_ref.1), custom_call_target="tpu_custom_call" | custom-call | tf_op jit(solution)/shard_map/load/pallas_call | solution.py:231
  1.4 3.8 %collective-permute-start.9 = (f32[512,256]{1,0:T(8,128)S(1)}, f32[512,256]{1,0:T(8,128)S(1)}, u32[]{:S(2)}, u32[]{:S(2)}) collective-permute-start(f32[512,256]{1,0:T(8,128)S(1)} %get-tuple-element.32.refs_0_), channel_id=1, source_target_pairs={{7,0},{0,1},{1,2},{2,3},{3,4},{4,5},{5,6},{6,7},{15,8},{8,9},{9,10... | collective-permute-start | bytes 1572872 | tf_op jit(solution)/shard_map/ppermute | solution.py:327
  7.0 5.8 %collective-permute-start.1 = (f32[72,128]{1,0:T(8,128)S(1)}, f32[72,128]{1,0:T(8,128)S(1)}, u32[]{:S(2)}, u32[]{:S(2)}) collective-permute-start(f32[72,128]{1,0:T(8,128)S(1)} %add.60), channel_id=1, source_target_pairs={{232,0},{224,8},{248,16},{240,24},{72,32},{64,40},{88,48},{80,56},... | collective-permute-start | bytes 110600 | tf_op jit(solution)/shard_map/ppermute | solution.py:282
  12.8 1.9 %collective-permute-done.1 = f32[72,128]{1,0:T(8,128)S(1)} collective-permute-done((f32[72,128]{1,0:T(8,128)S(1)}, f32[72,128]{1,0:T(8,128)S(1)}, u32[]{:S(2)}, u32[]{:S(2)}) %collective-permute-start.1) | collective-permute-done | bytes 36896 | tf_op jit(solution)/shard_map/ppermute | solution.py:282
  14.7 1.4 %collective-permute-start.4 = (f32[72,128]{1,0:T(8,128)S(1)}, f32[72,128]{1,0:T(8,128)S(1)}, u32[]{:S(2)}, u32[]{:S(2)}) collective-permute-start(f32[72,128]{1,0:T(8,128)S(1)} %add.61), channel_id=1, source_target_pairs={{104,0},{96,8},{120,16},{112,24},{200,32},{192,40},{216,48},{208,5... | collective-permute-start | bytes 110600 | tf_op jit(solution)/shard_map/ppermute | solution.py:282
  16.2 2.1 %collective-permute-start.3 = (f32[72,128]{1,0:T(8,128)S(1)}, f32[72,128]{1,0:T(8,128)S(1)}, u32[]{:S(2)}, u32[]{:S(2)}) collective-permute-start(f32[72,128]{1,0:T(8,128)S(1)} %add.61), channel_id=1, source_target_pairs={{192,0},{200,8},{208,16},{216,24},{96,32},{104,40},{112,48},{120,5... | collective-permute-start | bytes 110600 | tf_op jit(solution)/shard_map/ppermute | solution.py:282
  18.3 2.6 %collective-permute-start.2 = (f32[72,128]{1,0:T(8,128)S(1)}, f32[72,128]{1,0:T(8,128)S(1)}, u32[]{:S(2)}, u32[]{:S(2)}) collective-permute-start(f32[72,128]{1,0:T(8,128)S(1)} %add.61), channel_id=1, source_target_pairs={{40,0},{32,8},{56,16},{48,24},{8,32},{0,40},{24,48},{16,56},{104,6... | collective-permute-start | bytes 110600 | tf_op jit(solution)/shard_map/ppermute | solution.py:282
  21.1 2.1 %collective-permute-done.2 = f32[72,128]{1,0:T(8,128)S(1)} collective-permute-done((f32[72,128]{1,0:T(8,128)S(1)}, f32[72,128]{1,0:T(8,128)S(1)}, u32[]{:S(2)}, u32[]{:S(2)}) %collective-permute-start.2) | collective-permute-done | bytes 36896 | tf_op jit(solution)/shard_map/ppermute | solution.py:282
  24.0 2.9 %collective-permute-done.5 = f32[72,128]{1,0:T(8,128)S(1)} collective-permute-done((f32[72,128]{1,0:T(8,128)S(1)}, f32[72,128]{1,0:T(8,128)S(1)}, u32[]{:S(2)}, u32[]{:S(2)}) %collective-permute-start.5) | collective-permute-done | bytes 36896 | tf_op jit(solution)/shard_map/ppermute | solution.py:282
  26.9 1.2 %collective-permute-start.6 = (f32[72,128]{1,0:T(8,128)S(1)}, f32[72,128]{1,0:T(8,128)S(1)}, u32[]{:S(2)}, u32[]{:S(2)}) collective-permute-start(f32[72,128]{1,0:T(8,128)S(1)} %add.65.mine_ref), channel_id=1, source_target_pairs={{15,0},{8,1},{9,2},{10,3},{11,4},{12,5},{13,6},{14,7},{7,8},{0,9},... | collective-permute-start | bytes 110600 | tf_op jit(solution)/shard_map/ppermute | solution.py:337
  28.6 5.4 %collective-permute-done.6.mine_ref = f32[72,128]{1,0:T(8,128)S(1)} collective-permute-done((f32[72,128]{1,0:T(8,128)S(1)}, f32[72,128]{1,0:T(8,128)S(1)}, u32[]{:S(2)}, u32[]{:S(2)}) %collective-permute-start.6) | collective-permute-done | bytes 36896 | tf_op jit(solution)/shard_map/ppermute | solution.py:337
  34.4 1.8 %shard_map.17 = (f32[128,128]{1,0:T(8,128)S(1)}, f32[128,128]{1,0:T(8,128)S(1)}, f32[128,128]{1,0:T(8,128)S(1)}) custom-call(s32[1]{0:T(128)} %bitcast.core_ref, f32[72,128]{1,0:T(8,128)S(1)} %add.65.mine_ref, f32[72,128]{1,0:T(8,128)S(1)} %collective-permute-done.8.other_ref), custom_call_target="tpu_custom_call" | custom-call | tf_op jit(solution)/shard_map/pallas_call | solution.py:219
  37.2 2.8 %shard_map.19 = (f32[512,128]{1,0:T(8,128)S(1)}, f32[128,128]{1,0:T(8,128)S(1)}, f32[128,128]{1,0:T(8,128)S(1)}, f32[72,128]{1,0:T(8,128)S(1)}, f32[72,128]{1,0:T(8,128)S(1)}) custom-call(s32[1]{0:T(128)} %bitcast.core_ref, f32[72,128]{1,0:T(8,128)S(1)} %collective-permute-done.6.mine_ref, f32[72,128]{1,0:T(8,128)S(1)} %collective-permute-done.7.other_ref, ...), custom_call_target="tpu_custom_call" | custom-call | tf_op jit(solution)/shard_map/pallas_call | solution.py:219
  41.3 2.3 %collective-permute-start.13 = (f32[72,128]{1,0:T(8,128)S(1)}, f32[72,128]{1,0:T(8,128)S(1)}, u32[]{:S(2)}, u32[]{:S(2)}) collective-permute-start(f32[72,128]{1,0:T(8,128)S(1)} %add.66), channel_id=1, source_target_pairs={{240,0},{248,8},{224,16},{232,24},{80,32},{88,40},{64,48},{72,56},... | collective-permute-start | bytes 110600 | tf_op jit(solution)/shard_map/ppermute | solution.py:282
  46.2 1.4 %collective-permute-done.12 = f32[72,128]{1,0:T(8,128)S(1)} collective-permute-done((f32[72,128]{1,0:T(8,128)S(1)}, f32[72,128]{1,0:T(8,128)S(1)}, u32[]{:S(2)}, u32[]{:S(2)}) %collective-permute-start.12) | collective-permute-done | bytes 36896 | tf_op jit(solution)/shard_map/ppermute | solution.py:282
  47.6 1.5 %collective-permute-done.11 = f32[72,128]{1,0:T(8,128)S(1)} collective-permute-done((f32[72,128]{1,0:T(8,128)S(1)}, f32[72,128]{1,0:T(8,128)S(1)}, u32[]{:S(2)}, u32[]{:S(2)}) %collective-permute-start.11) | collective-permute-done | bytes 36896 | tf_op jit(solution)/shard_map/ppermute | solution.py:282
  49.1 1.7 %collective-permute-start.16 = (f32[72,128]{1,0:T(8,128)S(1)}, f32[72,128]{1,0:T(8,128)S(1)}, u32[]{:S(2)}, u32[]{:S(2)}) collective-permute-start(f32[72,128]{1,0:T(8,128)S(1)} %add_add_fusion.3), channel_id=1, source_target_pairs={{104,0},{96,8},{120,16},{112,24},{200,32},{192,40},{216,48},{208,5... | collective-permute-start | bytes 110600 | tf_op jit(solution)/shard_map/ppermute | solution.py:282
  50.8 2.7 %collective-permute-start.14 = (f32[72,128]{1,0:T(8,128)S(1)}, f32[72,128]{1,0:T(8,128)S(1)}, u32[]{:S(2)}, u32[]{:S(2)}) collective-permute-start(f32[72,128]{1,0:T(8,128)S(1)} %add_add_fusion.3), channel_id=1, source_target_pairs={{40,0},{32,8},{56,16},{48,24},{8,32},{0,40},{24,48},{16,56},{104,6... | collective-permute-start | bytes 110600 | tf_op jit(solution)/shard_map/ppermute | solution.py:282
  53.5 1.8 %collective-permute-done.16 = f32[72,128]{1,0:T(8,128)S(1)} collective-permute-done((f32[72,128]{1,0:T(8,128)S(1)}, f32[72,128]{1,0:T(8,128)S(1)}, u32[]{:S(2)}, u32[]{:S(2)}) %collective-permute-start.16) | collective-permute-done | bytes 36896 | tf_op jit(solution)/shard_map/ppermute | solution.py:282
  57.5 8.5 %collective-permute-done.17.mine_ref = f32[72,128]{1,0:T(8,128)S(1)} collective-permute-done((f32[72,128]{1,0:T(8,128)S(1)}, f32[72,128]{1,0:T(8,128)S(1)}, u32[]{:S(2)}, u32[]{:S(2)}) %collective-permute-start.17) | collective-permute-done | bytes 36896 | tf_op jit(solution)/shard_map/ppermute | solution.py:337
  66.8 1.8 %shard_map.20 = (f32[128,128]{1,0:T(8,128)S(1)}, f32[128,128]{1,0:T(8,128)S(1)}, f32[128,128]{1,0:T(8,128)S(1)}) custom-call(s32[1]{0:T(128)} %bitcast.core_ref, f32[72,128]{1,0:T(8,128)S(1)} %add_add_fusion.2.mine_ref, f32[72,128]{1,0:T(8,128)S(1)} %collective-permute-done.19.other_ref), custom_call_target="tpu_custom_call" | custom-call | tf_op jit(solution)/shard_map/pallas_call | solution.py:219
  69.6 2.8 %shard_map.23 = (f32[512,128]{1,0:T(8,128)S(1)}, f32[128,128]{1,0:T(8,128)S(1)}, f32[128,128]{1,0:T(8,128)S(1)}, f32[72,128]{1,0:T(8,128)S(1)}, f32[72,128]{1,0:T(8,128)S(1)}) custom-call(s32[1]{0:T(128)} %bitcast.core_ref, f32[72,128]{1,0:T(8,128)S(1)} %collective-permute-done.17.mine_ref, f32[72,128]{1,0:T(8,128)S(1)} %collective-permute-done.18.other_ref, ...), custom_call_target="tpu_custom_call" | custom-call | tf_op jit(solution)/shard_map/pallas_call | solution.py:219
  73.7 2.4 %collective-permute-start.24 = (f32[72,128]{1,0:T(8,128)S(1)}, f32[72,128]{1,0:T(8,128)S(1)}, u32[]{:S(2)}, u32[]{:S(2)}) collective-permute-start(f32[72,128]{1,0:T(8,128)S(1)} %add.73), channel_id=1, source_target_pairs={{240,0},{248,8},{224,16},{232,24},{80,32},{88,40},{64,48},{72,56},... | collective-permute-start | bytes 110600 | tf_op jit(solution)/shard_map/ppermute | solution.py:282
  78.6 1.5 %collective-permute-done.23 = f32[72,128]{1,0:T(8,128)S(1)} collective-permute-done((f32[72,128]{1,0:T(8,128)S(1)}, f32[72,128]{1,0:T(8,128)S(1)}, u32[]{:S(2)}, u32[]{:S(2)}) %collective-permute-start.23) | collective-permute-done | bytes 36896 | tf_op jit(solution)/shard_map/ppermute | solution.py:282
  80.2 1.4 %collective-permute-done.22 = f32[72,128]{1,0:T(8,128)S(1)} collective-permute-done((f32[72,128]{1,0:T(8,128)S(1)}, f32[72,128]{1,0:T(8,128)S(1)}, u32[]{:S(2)}, u32[]{:S(2)}) %collective-permute-start.22) | collective-permute-done | bytes 36896 | tf_op jit(solution)/shard_map/ppermute | solution.py:282
  81.6 1.7 %collective-permute-start.27 = (f32[72,128]{1,0:T(8,128)S(1)}, f32[72,128]{1,0:T(8,128)S(1)}, u32[]{:S(2)}, u32[]{:S(2)}) collective-permute-start(f32[72,128]{1,0:T(8,128)S(1)} %add_add_fusion.1), channel_id=1, source_target_pairs={{104,0},{96,8},{120,16},{112,24},{200,32},{192,40},{216,48},{208,5... | collective-permute-start | bytes 110600 | tf_op jit(solution)/shard_map/ppermute | solution.py:282
  83.2 2.8 %collective-permute-start.25 = (f32[72,128]{1,0:T(8,128)S(1)}, f32[72,128]{1,0:T(8,128)S(1)}, u32[]{:S(2)}, u32[]{:S(2)}) collective-permute-start(f32[72,128]{1,0:T(8,128)S(1)} %add_add_fusion.1), channel_id=1, source_target_pairs={{40,0},{32,8},{56,16},{48,24},{8,32},{0,40},{24,48},{16,56},{104,6... | collective-permute-start | bytes 110600 | tf_op jit(solution)/shard_map/ppermute | solution.py:282
  86.0 1.1 %collective-permute-done.27 = f32[72,128]{1,0:T(8,128)S(1)} collective-permute-done((f32[72,128]{1,0:T(8,128)S(1)}, f32[72,128]{1,0:T(8,128)S(1)}, u32[]{:S(2)}, u32[]{:S(2)}) %collective-permute-start.27) | collective-permute-done | bytes 36896 | tf_op jit(solution)/shard_map/ppermute | solution.py:282
  88.9 1.2 %collective-permute-start.30 = (f32[72,128]{1,0:T(8,128)S(1)}, f32[72,128]{1,0:T(8,128)S(1)}, u32[]{:S(2)}, u32[]{:S(2)}) collective-permute-start(f32[72,128]{1,0:T(8,128)S(1)} %add_add_fusion.mine_ref), channel_id=1, source_target_pairs={{8,0},{0,8},{24,16},{16,24},{40,32},{32,40},{56,48},{48,56},{72,64... | collective-permute-start | bytes 110600 | tf_op jit(solution)/shard_map/ppermute | solution.py:282
  90.2 8.3 %collective-permute-done.28.mine_ref = f32[72,128]{1,0:T(8,128)S(1)} collective-permute-done((f32[72,128]{1,0:T(8,128)S(1)}, f32[72,128]{1,0:T(8,128)S(1)}, u32[]{:S(2)}, u32[]{:S(2)}) %collective-permute-start.28) | collective-permute-done | bytes 36896 | tf_op jit(solution)/shard_map/ppermute | solution.py:337
  99.3 1.8 %shard_map.24 = (f32[128,128]{1,0:T(8,128)S(1)}, f32[128,128]{1,0:T(8,128)S(1)}, f32[128,128]{1,0:T(8,128)S(1)}) custom-call(s32[1]{0:T(128)} %bitcast.core_ref, f32[72,128]{1,0:T(8,128)S(1)} %add_add_fusion.mine_ref, f32[72,128]{1,0:T(8,128)S(1)} %collective-permute-done.30.other_ref), custom_call_target="tpu_custom_call" | custom-call | tf_op jit(solution)/shard_map/pallas_call | solution.py:219
  102.1 3.3 %shard_map.27 = f32[512,256]{1,0:T(8,128)} custom-call(s32[1]{0:T(128)} %bitcast.core_ref, f32[72,128]{1,0:T(8,128)S(1)} %collective-permute-done.28.mine_ref, f32[72,128]{1,0:T(8,128)S(1)} %collective-permute-done.29.other_ref, f32[512,128]{1,0:T(8,128)S(1)} %shard_map.25.own_ref, f32[512,128]{1,0:T(8,128)S(1)} %shard_map.26.refs_0_, ...), custom_call_target="tpu_custom_call" | custom-call | tf_op jit(solution)/shard_map/pallas_call | solution.py:219
  (54 shorter events, 19.9 us)
Async XLA Ops:
  1.4 35.9 %collective-permute-start.9 = (f32[512,256]{1,0:T(8,128)S(1)}, f32[512,256]{1,0:T(8,128)S(1)}, u32[]{:S(2)}, u32[]{:S(2)}) collective-permute-start(f32[512,256]{1,0:T(8,128)S(1)} %get-tuple-element.32.refs_0_), channel_id=1, source_target_pairs={{7,0},{0,1},{1,2},{2,3},{3,4},{4,5},{5,6},{6,7},{15,8},{8,9},{9,10... | collective-permute-start | bytes 1572872 | tf_op jit(solution)/shard_map/ppermute | solution.py:327
  5.2 1.8 %collective-permute-start = (f32[72,128]{1,0:T(8,128)S(1)}, f32[72,128]{1,0:T(8,128)S(1)}, u32[]{:S(2)}, u32[]{:S(2)}) collective-permute-start(f32[72,128]{1,0:T(8,128)S(1)} %get-tuple-element.28), channel_id=1, source_target_pairs={{8,0},{0,8},{24,16},{16,24},{40,32},{32,40},{56,48},{48,56},{72,64... | collective-permute-start | bytes 110600 | tf_op jit(solution)/shard_map/ppermute | solution.py:282
  7.0 7.7 %collective-permute-start.1 = (f32[72,128]{1,0:T(8,128)S(1)}, f32[72,128]{1,0:T(8,128)S(1)}, u32[]{:S(2)}, u32[]{:S(2)}) collective-permute-start(f32[72,128]{1,0:T(8,128)S(1)} %add.60), channel_id=1, source_target_pairs={{232,0},{224,8},{248,16},{240,24},{72,32},{64,40},{88,48},{80,56},... | collective-permute-start | bytes 110600 | tf_op jit(solution)/shard_map/ppermute | solution.py:282
  14.7 6.1 %collective-permute-start.4 = (f32[72,128]{1,0:T(8,128)S(1)}, f32[72,128]{1,0:T(8,128)S(1)}, u32[]{:S(2)}, u32[]{:S(2)}) collective-permute-start(f32[72,128]{1,0:T(8,128)S(1)} %add.61), channel_id=1, source_target_pairs={{104,0},{96,8},{120,16},{112,24},{200,32},{192,40},{216,48},{208,5... | collective-permute-start | bytes 110600 | tf_op jit(solution)/shard_map/ppermute | solution.py:282
  16.2 4.9 %collective-permute-start.3 = (f32[72,128]{1,0:T(8,128)S(1)}, f32[72,128]{1,0:T(8,128)S(1)}, u32[]{:S(2)}, u32[]{:S(2)}) collective-permute-start(f32[72,128]{1,0:T(8,128)S(1)} %add.61), channel_id=1, source_target_pairs={{192,0},{200,8},{208,16},{216,24},{96,32},{104,40},{112,48},{120,5... | collective-permute-start | bytes 110600 | tf_op jit(solution)/shard_map/ppermute | solution.py:282
  18.3 4.9 %collective-permute-start.2 = (f32[72,128]{1,0:T(8,128)S(1)}, f32[72,128]{1,0:T(8,128)S(1)}, u32[]{:S(2)}, u32[]{:S(2)}) collective-permute-start(f32[72,128]{1,0:T(8,128)S(1)} %add.61), channel_id=1, source_target_pairs={{40,0},{32,8},{56,16},{48,24},{8,32},{0,40},{24,48},{16,56},{104,6... | collective-permute-start | bytes 110600 | tf_op jit(solution)/shard_map/ppermute | solution.py:282
  23.2 3.7 %collective-permute-start.5 = (f32[72,128]{1,0:T(8,128)S(1)}, f32[72,128]{1,0:T(8,128)S(1)}, u32[]{:S(2)}, u32[]{:S(2)}) collective-permute-start(f32[72,128]{1,0:T(8,128)S(1)} %add_add_fusion.4), channel_id=1, source_target_pairs={{24,0},{16,8},{8,16},{0,24},{56,32},{48,40},{40,48},{32,56},{88,64... | collective-permute-start | bytes 110600 | tf_op jit(solution)/shard_map/ppermute | solution.py:282
  26.9 7.1 %collective-permute-start.6 = (f32[72,128]{1,0:T(8,128)S(1)}, f32[72,128]{1,0:T(8,128)S(1)}, u32[]{:S(2)}, u32[]{:S(2)}) collective-permute-start(f32[72,128]{1,0:T(8,128)S(1)} %add.65.mine_ref), channel_id=1, source_target_pairs={{15,0},{8,1},{9,2},{10,3},{11,4},{12,5},{13,6},{14,7},{7,8},{0,9},... | collective-permute-start | bytes 110600 | tf_op jit(solution)/shard_map/ppermute | solution.py:337
  28.1 6.3 %collective-permute-start.8 = (f32[72,128]{1,0:T(8,128)S(1)}, f32[72,128]{1,0:T(8,128)S(1)}, u32[]{:S(2)}, u32[]{:S(2)}) collective-permute-start(f32[72,128]{1,0:T(8,128)S(1)} %add.65.mine_ref), channel_id=1, source_target_pairs={{8,0},{0,8},{24,16},{16,24},{40,32},{32,40},{56,48},{48,56},{72,64... | collective-permute-start | bytes 110600 | tf_op jit(solution)/shard_map/ppermute | solution.py:282
  34.0 3.2 %collective-permute-start.7 = (f32[72,128]{1,0:T(8,128)S(1)}, f32[72,128]{1,0:T(8,128)S(1)}, u32[]{:S(2)}, u32[]{:S(2)}) collective-permute-start(f32[72,128]{1,0:T(8,128)S(1)} %collective-permute-done.6.mine_ref), channel_id=1, source_target_pairs={{8,0},{0,8},{24,16},{16,24},{40,32},{32,40},{56,48},{48,56},{72,64... | collective-permute-start | bytes 110600 | tf_op jit(solution)/shard_map/ppermute | solution.py:282
  40.0 1.3 %collective-permute-start.10 = (f32[72,128]{1,0:T(8,128)S(1)}, f32[72,128]{1,0:T(8,128)S(1)}, u32[]{:S(2)}, u32[]{:S(2)}) collective-permute-start(f32[72,128]{1,0:T(8,128)S(1)} %get-tuple-element.34), channel_id=1, source_target_pairs={{8,0},{0,8},{24,16},{16,24},{40,32},{32,40},{56,48},{48,56},{72,64... | collective-permute-start | bytes 110600 | tf_op jit(solution)/shard_map/ppermute | solution.py:282
  41.3 4.9 %collective-permute-start.13 = (f32[72,128]{1,0:T(8,128)S(1)}, f32[72,128]{1,0:T(8,128)S(1)}, u32[]{:S(2)}, u32[]{:S(2)}) collective-permute-start(f32[72,128]{1,0:T(8,128)S(1)} %add.66), channel_id=1, source_target_pairs={{240,0},{248,8},{224,16},{232,24},{80,32},{88,40},{64,48},{72,56},... | collective-permute-start | bytes 110600 | tf_op jit(solution)/shard_map/ppermute | solution.py:282
  43.6 4.0 %collective-permute-start.12 = (f32[72,128]{1,0:T(8,128)S(1)}, f32[72,128]{1,0:T(8,128)S(1)}, u32[]{:S(2)}, u32[]{:S(2)}) collective-permute-start(f32[72,128]{1,0:T(8,128)S(1)} %add.66), channel_id=1, source_target_pairs={{24,0},{16,8},{8,16},{0,24},{56,32},{48,40},{40,48},{32,56},{88,64... | collective-permute-start | bytes 110600 | tf_op jit(solution)/shard_map/ppermute | solution.py:282
  44.5 4.6 %collective-permute-start.11 = (f32[72,128]{1,0:T(8,128)S(1)}, f32[72,128]{1,0:T(8,128)S(1)}, u32[]{:S(2)}, u32[]{:S(2)}) collective-permute-start(f32[72,128]{1,0:T(8,128)S(1)} %add.66), channel_id=1, source_target_pairs={{232,0},{224,8},{248,16},{240,24},{72,32},{64,40},{88,48},{80,56},... | collective-permute-start | bytes 110600 | tf_op jit(solution)/shard_map/ppermute | solution.py:282
  49.1 6.2 %collective-permute-start.16 = (f32[72,128]{1,0:T(8,128)S(1)}, f32[72,128]{1,0:T(8,128)S(1)}, u32[]{:S(2)}, u32[]{:S(2)}) collective-permute-start(f32[72,128]{1,0:T(8,128)S(1)} %add_add_fusion.3), channel_id=1, source_target_pairs={{104,0},{96,8},{120,16},{112,24},{200,32},{192,40},{216,48},{208,5... | collective-permute-start | bytes 110600 | tf_op jit(solution)/shard_map/ppermute | solution.py:282
  50.8 5.0 %collective-permute-start.15 = (f32[72,128]{1,0:T(8,128)S(1)}, f32[72,128]{1,0:T(8,128)S(1)}, u32[]{:S(2)}, u32[]{:S(2)}) collective-permute-start(f32[72,128]{1,0:T(8,128)S(1)} %add_add_fusion.3), channel_id=1, source_target_pairs={{192,0},{200,8},{208,16},{216,24},{96,32},{104,40},{112,48},{120,5... | collective-permute-start | bytes 110600 | tf_op jit(solution)/shard_map/ppermute | solution.py:282
  50.8 5.3 %collective-permute-start.14 = (f32[72,128]{1,0:T(8,128)S(1)}, f32[72,128]{1,0:T(8,128)S(1)}, u32[]{:S(2)}, u32[]{:S(2)}) collective-permute-start(f32[72,128]{1,0:T(8,128)S(1)} %add_add_fusion.3), channel_id=1, source_target_pairs={{40,0},{32,8},{56,16},{48,24},{8,32},{0,40},{24,48},{16,56},{104,6... | collective-permute-start | bytes 110600 | tf_op jit(solution)/shard_map/ppermute | solution.py:282
  53.5 16.1 %collective-permute-start.20 = (f32[512,128]{1,0:T(8,128)S(1)}, f32[512,128]{1,0:T(8,128)S(1)}, u32[]{:S(2)}, u32[]{:S(2)}) collective-permute-start(f32[512,128]{1,0:T(8,128)S(1)} %get-tuple-element.38.refs_1_), channel_id=1, source_target_pairs={{7,0},{0,1},{1,2},{2,3},{3,4},{4,5},{5,6},{6,7},{15,8},{8,9},{9,10... | collective-permute-start | bytes 786440 | tf_op jit(solution)/shard_map/ppermute | solution.py:327
  56.2 9.8 %collective-permute-start.17 = (f32[72,128]{1,0:T(8,128)S(1)}, f32[72,128]{1,0:T(8,128)S(1)}, u32[]{:S(2)}, u32[]{:S(2)}) collective-permute-start(f32[72,128]{1,0:T(8,128)S(1)} %add_add_fusion.2.mine_ref), channel_id=1, source_target_pairs={{15,0},{8,1},{9,2},{10,3},{11,4},{12,5},{13,6},{14,7},{7,8},{0,9},... | collective-permute-start | bytes 110600 | tf_op jit(solution)/shard_map/ppermute | solution.py:337
  56.7 10.1 %collective-permute-start.19 = (f32[72,128]{1,0:T(8,128)S(1)}, f32[72,128]{1,0:T(8,128)S(1)}, u32[]{:S(2)}, u32[]{:S(2)}) collective-permute-start(f32[72,128]{1,0:T(8,128)S(1)} %add_add_fusion.2.mine_ref), channel_id=1, source_target_pairs={{8,0},{0,8},{24,16},{16,24},{40,32},{32,40},{56,48},{48,56},{72,64... | collective-permute-start | bytes 110600 | tf_op jit(solution)/shard_map/ppermute | solution.py:282
  66.0 3.6 %collective-permute-start.18 = (f32[72,128]{1,0:T(8,128)S(1)}, f32[72,128]{1,0:T(8,128)S(1)}, u32[]{:S(2)}, u32[]{:S(2)}) collective-permute-start(f32[72,128]{1,0:T(8,128)S(1)} %collective-permute-done.17.mine_ref), channel_id=1, source_target_pairs={{8,0},{0,8},{24,16},{16,24},{40,32},{32,40},{56,48},{48,56},{72,64... | collective-permute-start | bytes 110600 | tf_op jit(solution)/shard_map/ppermute | solution.py:282
  72.4 1.3 %collective-permute-start.21 = (f32[72,128]{1,0:T(8,128)S(1)}, f32[72,128]{1,0:T(8,128)S(1)}, u32[]{:S(2)}, u32[]{:S(2)}) collective-permute-start(f32[72,128]{1,0:T(8,128)S(1)} %get-tuple-element.42), channel_id=1, source_target_pairs={{8,0},{0,8},{24,16},{16,24},{40,32},{32,40},{56,48},{48,56},{72,64... | collective-permute-start | bytes 110600 | tf_op jit(solution)/shard_map/ppermute | solution.py:282
  73.7 4.9 %collective-permute-start.24 = (f32[72,128]{1,0:T(8,128)S(1)}, f32[72,128]{1,0:T(8,128)S(1)}, u32[]{:S(2)}, u32[]{:S(2)}) collective-permute-start(f32[72,128]{1,0:T(8,128)S(1)} %add.73), channel_id=1, source_target_pairs={{240,0},{248,8},{224,16},{232,24},{80,32},{88,40},{64,48},{72,56},... | collective-permute-start | bytes 110600 | tf_op jit(solution)/shard_map/ppermute | solution.py:282
  76.1 4.1 %collective-permute-start.23 = (f32[72,128]{1,0:T(8,128)S(1)}, f32[72,128]{1,0:T(8,128)S(1)}, u32[]{:S(2)}, u32[]{:S(2)}) collective-permute-start(f32[72,128]{1,0:T(8,128)S(1)} %add.73), channel_id=1, source_target_pairs={{24,0},{16,8},{8,16},{0,24},{56,32},{48,40},{40,48},{32,56},{88,64... | collective-permute-start | bytes 110600 | tf_op jit(solution)/shard_map/ppermute | solution.py:282
  77.0 4.6 %collective-permute-start.22 = (f32[72,128]{1,0:T(8,128)S(1)}, f32[72,128]{1,0:T(8,128)S(1)}, u32[]{:S(2)}, u32[]{:S(2)}) collective-permute-start(f32[72,128]{1,0:T(8,128)S(1)} %add.73), channel_id=1, source_target_pairs={{232,0},{224,8},{248,16},{240,24},{72,32},{64,40},{88,48},{80,56},... | collective-permute-start | bytes 110600 | tf_op jit(solution)/shard_map/ppermute | solution.py:282
  81.6 5.5 %collective-permute-start.27 = (f32[72,128]{1,0:T(8,128)S(1)}, f32[72,128]{1,0:T(8,128)S(1)}, u32[]{:S(2)}, u32[]{:S(2)}) collective-permute-start(f32[72,128]{1,0:T(8,128)S(1)} %add_add_fusion.1), channel_id=1, source_target_pairs={{104,0},{96,8},{120,16},{112,24},{200,32},{192,40},{216,48},{208,5... | collective-permute-start | bytes 110600 | tf_op jit(solution)/shard_map/ppermute | solution.py:282
  83.2 5.0 %collective-permute-start.26 = (f32[72,128]{1,0:T(8,128)S(1)}, f32[72,128]{1,0:T(8,128)S(1)}, u32[]{:S(2)}, u32[]{:S(2)}) collective-permute-start(f32[72,128]{1,0:T(8,128)S(1)} %add_add_fusion.1), channel_id=1, source_target_pairs={{192,0},{200,8},{208,16},{216,24},{96,32},{104,40},{112,48},{120,5... | collective-permute-start | bytes 110600 | tf_op jit(solution)/shard_map/ppermute | solution.py:282
  83.2 5.4 %collective-permute-start.25 = (f32[72,128]{1,0:T(8,128)S(1)}, f32[72,128]{1,0:T(8,128)S(1)}, u32[]{:S(2)}, u32[]{:S(2)}) collective-permute-start(f32[72,128]{1,0:T(8,128)S(1)} %add_add_fusion.1), channel_id=1, source_target_pairs={{40,0},{32,8},{56,16},{48,24},{8,32},{0,40},{24,48},{16,56},{104,6... | collective-permute-start | bytes 110600 | tf_op jit(solution)/shard_map/ppermute | solution.py:282
  86.0 16.1 %collective-permute-start.31 = (f32[512,128]{1,0:T(8,128)S(1)}, f32[512,128]{1,0:T(8,128)S(1)}, u32[]{:S(2)}, u32[]{:S(2)}) collective-permute-start(f32[512,128]{1,0:T(8,128)S(1)} %get-tuple-element.46.refs_1_), channel_id=1, source_target_pairs={{7,0},{0,1},{1,2},{2,3},{3,4},{4,5},{5,6},{6,7},{15,8},{8,9},{9,10... | collective-permute-start | bytes 786440 | tf_op jit(solution)/shard_map/ppermute | solution.py:327
  88.6 9.9 %collective-permute-start.28 = (f32[72,128]{1,0:T(8,128)S(1)}, f32[72,128]{1,0:T(8,128)S(1)}, u32[]{:S(2)}, u32[]{:S(2)}) collective-permute-start(f32[72,128]{1,0:T(8,128)S(1)} %add_add_fusion.mine_ref), channel_id=1, source_target_pairs={{15,0},{8,1},{9,2},{10,3},{11,4},{12,5},{13,6},{14,7},{7,8},{0,9},... | collective-permute-start | bytes 110600 | tf_op jit(solution)/shard_map/ppermute | solution.py:337
  88.9 10.3 %collective-permute-start.30 = (f32[72,128]{1,0:T(8,128)S(1)}, f32[72,128]{1,0:T(8,128)S(1)}, u32[]{:S(2)}, u32[]{:S(2)}) collective-permute-start(f32[72,128]{1,0:T(8,128)S(1)} %add_add_fusion.mine_ref), channel_id=1, source_target_pairs={{8,0},{0,8},{24,16},{16,24},{40,32},{32,40},{56,48},{48,56},{72,64... | collective-permute-start | bytes 110600 | tf_op jit(solution)/shard_map/ppermute | solution.py:282
  98.5 3.6 %collective-permute-start.29 = (f32[72,128]{1,0:T(8,128)S(1)}, f32[72,128]{1,0:T(8,128)S(1)}, u32[]{:S(2)}, u32[]{:S(2)}) collective-permute-start(f32[72,128]{1,0:T(8,128)S(1)} %collective-permute-done.28.mine_ref), channel_id=1, source_target_pairs={{8,0},{0,8},{24,16},{16,24},{40,32},{32,40},{56,48},{48,56},{72,64... | collective-permute-start | bytes 110600 | tf_op jit(solution)/shard_map/ppermute | solution.py:282

commit v9 on v8

--- a/solution.py
+++ b/solution.py
@@ -301,16 +301,16 @@
 def summed_halves(mine, other, y_last):
     incoming = from_row(other, mate)
     x = mine + incoming
-    next_z = from_row(x, owner(lambda z, y: (z + side(z), y)))
+    next_z = from_row(x, owner(lambda z, y: (z ^ 1, y)))
     if y_last:
         x = x + next_z
     else:
         next_y = from_row(x, owner(lambda z, y: (z, 1 - y)))
-        next_zy = from_row(x, owner(lambda z, y: (z + side(z), 1 - y)))
+        next_zy = from_row(x, owner(lambda z, y: (z ^ 1, 1 - y)))
         x = ((x + next_z) + next_y) + next_zy
-    by_one = from_row(x, owner(lambda z, y: (z - side(z), y)))
-    by_two = from_row(x, owner(lambda z, y: (z + 2 * side(z), y)))
-    by_three = from_row(x, owner(lambda z, y: (z - 3 * side(z), y)))
+    by_one = from_row(x, owner(lambda z, y: (z + side(z), y)))
+    by_two = from_row(x, owner(lambda z, y: (z - 2 * side(z), y)))
+    by_three = from_row(x, owner(lambda z, y: (z + 3 * side(z), y)))
     x = ((x + by_one) + by_two) + by_three
     if y_last:
         x = x + from_row(x, owner(lambda z, y: (z, 1 - y)))

time: 106 us -> 103 us (0.972)
  starting transfers between devices: 40.8 us -> 39.5 us
  waiting for transfers between devices: 45.1 us -> 43.9 us
    ppermute x26, starting transfers between devices: 34.9 us -> 33.4 us  [from_row(): return lax.ppermute(x, 'row', route)]
  transfers between devices with their start and end apart: 32 -> 32, of which waited for: 22 -> 19; matrix products, arithmetic and copies ran while one was open for 0% -> 0% of each run, Pallas kernels for 9% -> 9%
where the time goes in v9:
time: 103 us
  waiting for transfers between devices  43.9 us (43%)
  starting transfers between devices  39.5 us (38%)
  Pallas kernels  19.3 us (19%)
    ppermute x26, starting transfers between devices, from_row(): return lax.ppermute(x, 'row', route)  33.4 us
    ppermute x26, waiting for transfers between devices, from_row(): return lax.ppermute(x, 'row', route)  22 us
    ppermute x3, waiting for transfers between devices, hopped_over(): return lax.ppermute(half, ('row', 'pair'), route)  21.9 us
    pallas_call x11, Pallas kernels, vmem_call(): pl.pallas_call(kernel, out_shape=shapes, in_specs=specs, scratch_shapes=s...  18 us
    ppermute x3, starting transfers between devices, shifted(): return lax.ppermute(block, 'pair', route)  3.81 us
    ppermute x3, starting transfers between devices, hopped_over(): return lax.ppermute(half, ('row', 'pair'), route)  2.23 us
  transfers between devices with their start and end apart: 32, of which 19 were waited for; matrix products, arithmetic and copies ran while one was open for 0% of the time, Pallas kernels for 9%

profile of v9, /device:TPU:1, one launch (start us, length us, event | category | flops | bytes accessed | tf_op | source)
XLA Modules:
  0.0 103.2 jit_solution(13589822065227072221)
XLA Ops:
  0.0 1.3 %load.1 = (f32[512,256]{1,0:T(8,128)S(1)}, f32[72,128]{1,0:T(8,128)S(1)}, f32[72,128]{1,0:T(8,128)S(1)}) custom-call(s32[1]{0:T(128)} %bitcast.core_ref, f32[512,256]{1,0:T(8,128)} %panel_ref.1), custom_call_target="tpu_custom_call" | custom-call | tf_op jit(solution)/shard_map/load/pallas_call | solution.py:231
  1.4 3.8 %collective-permute-start.9 = (f32[512,256]{1,0:T(8,128)S(1)}, f32[512,256]{1,0:T(8,128)S(1)}, u32[]{:S(2)}, u32[]{:S(2)}) collective-permute-start(f32[512,256]{1,0:T(8,128)S(1)} %get-tuple-element.32.refs_0_), channel_id=1, source_target_pairs={{7,0},{0,1},{1,2},{2,3},{3,4},{4,5},{5,6},{6,7},{15,8},{8,9},{9,10... | collective-permute-start | bytes 1572872 | tf_op jit(solution)/shard_map/ppermute | solution.py:327
  5.2 1.0 collective-permute-start
  7.0 1.9 %collective-permute-start.1 = (f32[72,128]{1,0:T(8,128)S(1)}, f32[72,128]{1,0:T(8,128)S(1)}, u32[]{:S(2)}, u32[]{:S(2)}) collective-permute-start(f32[72,128]{1,0:T(8,128)S(1)} %add.60), channel_id=1, source_target_pairs={{40,0},{32,8},{56,16},{48,24},{8,32},{0,40},{24,48},{16,56},{104,6... | collective-permute-start | bytes 110600 | tf_op jit(solution)/shard_map/ppermute | solution.py:282
  8.9 1.6 %collective-permute-done.1 = f32[72,128]{1,0:T(8,128)S(1)} collective-permute-done((f32[72,128]{1,0:T(8,128)S(1)}, f32[72,128]{1,0:T(8,128)S(1)}, u32[]{:S(2)}, u32[]{:S(2)}) %collective-permute-start.1) | collective-permute-done | bytes 36896 | tf_op jit(solution)/shard_map/ppermute | solution.py:282
  10.5 6.6 %collective-permute-start.4 = (f32[72,128]{1,0:T(8,128)S(1)}, f32[72,128]{1,0:T(8,128)S(1)}, u32[]{:S(2)}, u32[]{:S(2)}) collective-permute-start(f32[72,128]{1,0:T(8,128)S(1)} %add.61), channel_id=1, source_target_pairs={{168,0},{160,8},{184,16},{176,24},{136,32},{128,40},{152,48},{144,... | collective-permute-start | bytes 110600 | tf_op jit(solution)/shard_map/ppermute | solution.py:282
  17.4 3.5 %collective-permute-start.2 = (f32[72,128]{1,0:T(8,128)S(1)}, f32[72,128]{1,0:T(8,128)S(1)}, u32[]{:S(2)}, u32[]{:S(2)}) collective-permute-start(f32[72,128]{1,0:T(8,128)S(1)} %add.61), channel_id=1, source_target_pairs={{232,0},{224,8},{248,16},{240,24},{72,32},{64,40},{88,48},{80,56},... | collective-permute-start | bytes 110600 | tf_op jit(solution)/shard_map/ppermute | solution.py:282
  20.9 2.0 %collective-permute-done.2 = f32[72,128]{1,0:T(8,128)S(1)} collective-permute-done((f32[72,128]{1,0:T(8,128)S(1)}, f32[72,128]{1,0:T(8,128)S(1)}, u32[]{:S(2)}, u32[]{:S(2)}) %collective-permute-start.2) | collective-permute-done | bytes 36896 | tf_op jit(solution)/shard_map/ppermute | solution.py:282
  23.1 3.3 %collective-permute-done.5 = f32[72,128]{1,0:T(8,128)S(1)} collective-permute-done((f32[72,128]{1,0:T(8,128)S(1)}, f32[72,128]{1,0:T(8,128)S(1)}, u32[]{:S(2)}, u32[]{:S(2)}) %collective-permute-start.5) | collective-permute-done | bytes 36896 | tf_op jit(solution)/shard_map/ppermute | solution.py:282
  26.4 1.7 %collective-permute-start.6 = (f32[72,128]{1,0:T(8,128)S(1)}, f32[72,128]{1,0:T(8,128)S(1)}, u32[]{:S(2)}, u32[]{:S(2)}) collective-permute-start(f32[72,128]{1,0:T(8,128)S(1)} %add.65.mine_ref), channel_id=1, source_target_pairs={{15,0},{8,1},{9,2},{10,3},{11,4},{12,5},{13,6},{14,7},{7,8},{0,9},... | collective-permute-start | bytes 110600 | tf_op jit(solution)/shard_map/ppermute | solution.py:337
  28.2 5.2 %collective-permute-done.6.mine_ref = f32[72,128]{1,0:T(8,128)S(1)} collective-permute-done((f32[72,128]{1,0:T(8,128)S(1)}, f32[72,128]{1,0:T(8,128)S(1)}, u32[]{:S(2)}, u32[]{:S(2)}) %collective-permute-start.6) | collective-permute-done | bytes 36896 | tf_op jit(solution)/shard_map/ppermute | solution.py:337
  33.4 1.8 %shard_map.17 = (f32[128,128]{1,0:T(8,128)S(1)}, f32[128,128]{1,0:T(8,128)S(1)}, f32[128,128]{1,0:T(8,128)S(1)}) custom-call(s32[1]{0:T(128)} %bitcast.core_ref, f32[72,128]{1,0:T(8,128)S(1)} %add.65.mine_ref, f32[72,128]{1,0:T(8,128)S(1)} %collective-permute-done.8.other_ref), custom_call_target="tpu_custom_call" | custom-call | tf_op jit(solution)/shard_map/pallas_call | solution.py:219
  36.2 2.8 %shard_map.19 = (f32[512,128]{1,0:T(8,128)S(1)}, f32[128,128]{1,0:T(8,128)S(1)}, f32[128,128]{1,0:T(8,128)S(1)}, f32[72,128]{1,0:T(8,128)S(1)}, f32[72,128]{1,0:T(8,128)S(1)}) custom-call(s32[1]{0:T(128)} %bitcast.core_ref, f32[72,128]{1,0:T(8,128)S(1)} %collective-permute-done.6.mine_ref, f32[72,128]{1,0:T(8,128)S(1)} %collective-permute-done.7.other_ref, ...), custom_call_target="tpu_custom_call" | custom-call | tf_op jit(solution)/shard_map/pallas_call | solution.py:219
  40.5 1.9 %collective-permute-start.13 = (f32[72,128]{1,0:T(8,128)S(1)}, f32[72,128]{1,0:T(8,128)S(1)}, u32[]{:S(2)}, u32[]{:S(2)}) collective-permute-start(f32[72,128]{1,0:T(8,128)S(1)} %add.66), channel_id=1, source_target_pairs={{48,0},{56,8},{32,16},{40,24},{16,32},{24,40},{0,48},{8,56},{112,6... | collective-permute-start | bytes 110600 | tf_op jit(solution)/shard_map/ppermute | solution.py:282
  44.2 2.1 %collective-permute-done.12 = f32[72,128]{1,0:T(8,128)S(1)} collective-permute-done((f32[72,128]{1,0:T(8,128)S(1)}, f32[72,128]{1,0:T(8,128)S(1)}, u32[]{:S(2)}, u32[]{:S(2)}) %collective-permute-start.12) | collective-permute-done | bytes 36896 | tf_op jit(solution)/shard_map/ppermute | solution.py:282
  46.7 3.5 %collective-permute-start.16 = (f32[72,128]{1,0:T(8,128)S(1)}, f32[72,128]{1,0:T(8,128)S(1)}, u32[]{:S(2)}, u32[]{:S(2)}) collective-permute-start(f32[72,128]{1,0:T(8,128)S(1)} %add_add_fusion.3), channel_id=1, source_target_pairs={{168,0},{160,8},{184,16},{176,24},{136,32},{128,40},{152,48},{144,... | collective-permute-start | bytes 110600 | tf_op jit(solution)/shard_map/ppermute | solution.py:282
  50.8 2.4 %collective-permute-start.14 = (f32[72,128]{1,0:T(8,128)S(1)}, f32[72,128]{1,0:T(8,128)S(1)}, u32[]{:S(2)}, u32[]{:S(2)}) collective-permute-start(f32[72,128]{1,0:T(8,128)S(1)} %add_add_fusion.3), channel_id=1, source_target_pairs={{232,0},{224,8},{248,16},{240,24},{72,32},{64,40},{88,48},{80,56},... | collective-permute-start | bytes 110600 | tf_op jit(solution)/shard_map/ppermute | solution.py:282
  53.9 2.1 %collective-permute-done.14 = f32[72,128]{1,0:T(8,128)S(1)} collective-permute-done((f32[72,128]{1,0:T(8,128)S(1)}, f32[72,128]{1,0:T(8,128)S(1)}, u32[]{:S(2)}, u32[]{:S(2)}) %collective-permute-start.14) | collective-permute-done | bytes 36896 | tf_op jit(solution)/shard_map/ppermute | solution.py:282
  56.7 9.0 %collective-permute-done.17.mine_ref = f32[72,128]{1,0:T(8,128)S(1)} collective-permute-done((f32[72,128]{1,0:T(8,128)S(1)}, f32[72,128]{1,0:T(8,128)S(1)}, u32[]{:S(2)}, u32[]{:S(2)}) %collective-permute-start.17) | collective-permute-done | bytes 36896 | tf_op jit(solution)/shard_map/ppermute | solution.py:337
  66.1 1.8 %shard_map.20 = (f32[128,128]{1,0:T(8,128)S(1)}, f32[128,128]{1,0:T(8,128)S(1)}, f32[128,128]{1,0:T(8,128)S(1)}) custom-call(s32[1]{0:T(128)} %bitcast.core_ref, f32[72,128]{1,0:T(8,128)S(1)} %add_add_fusion.2.mine_ref, f32[72,128]{1,0:T(8,128)S(1)} %collective-permute-done.19.other_ref), custom_call_target="tpu_custom_call" | custom-call | tf_op jit(solution)/shard_map/pallas_call | solution.py:219
  68.0 0.9 shard_map.21.own_ref.refs_0_
  69.0 2.8 %shard_map.23 = (f32[512,128]{1,0:T(8,128)S(1)}, f32[128,128]{1,0:T(8,128)S(1)}, f32[128,128]{1,0:T(8,128)S(1)}, f32[72,128]{1,0:T(8,128)S(1)}, f32[72,128]{1,0:T(8,128)S(1)}) custom-call(s32[1]{0:T(128)} %bitcast.core_ref, f32[72,128]{1,0:T(8,128)S(1)} %collective-permute-done.17.mine_ref, f32[72,128]{1,0:T(8,128)S(1)} %collective-permute-done.18.other_ref, ...), custom_call_target="tpu_custom_call" | custom-call | tf_op jit(solution)/shard_map/pallas_call | solution.py:219
  73.7 1.4 %collective-permute-start.23 = (f32[72,128]{1,0:T(8,128)S(1)}, f32[72,128]{1,0:T(8,128)S(1)}, u32[]{:S(2)}, u32[]{:S(2)}) collective-permute-start(f32[72,128]{1,0:T(8,128)S(1)} %add.73), channel_id=1, source_target_pairs={{24,0},{16,8},{8,16},{0,24},{56,32},{48,40},{40,48},{32,56},{88,64... | collective-permute-start | bytes 110600 | tf_op jit(solution)/shard_map/ppermute | solution.py:282
  76.9 1.4 %collective-permute-done.23 = f32[72,128]{1,0:T(8,128)S(1)} collective-permute-done((f32[72,128]{1,0:T(8,128)S(1)}, f32[72,128]{1,0:T(8,128)S(1)}, u32[]{:S(2)}, u32[]{:S(2)}) %collective-permute-start.23) | collective-permute-done | bytes 36896 | tf_op jit(solution)/shard_map/ppermute | solution.py:282
  78.5 2.3 %collective-permute-start.27 = (f32[72,128]{1,0:T(8,128)S(1)}, f32[72,128]{1,0:T(8,128)S(1)}, u32[]{:S(2)}, u32[]{:S(2)}) collective-permute-start(f32[72,128]{1,0:T(8,128)S(1)} %add_add_fusion.1), channel_id=1, source_target_pairs={{168,0},{160,8},{184,16},{176,24},{136,32},{128,40},{152,48},{144,... | collective-permute-start | bytes 110600 | tf_op jit(solution)/shard_map/ppermute | solution.py:282
  80.8 1.8 %collective-permute-start.26 = (f32[72,128]{1,0:T(8,128)S(1)}, f32[72,128]{1,0:T(8,128)S(1)}, u32[]{:S(2)}, u32[]{:S(2)}) collective-permute-start(f32[72,128]{1,0:T(8,128)S(1)} %add_add_fusion.1), channel_id=1, source_target_pairs={{64,0},{72,8},{80,16},{88,24},{224,32},{232,40},{240,48},{248,56},... | collective-permute-start | bytes 110600 | tf_op jit(solution)/shard_map/ppermute | solution.py:282
  82.7 1.3 %collective-permute-start.25 = (f32[72,128]{1,0:T(8,128)S(1)}, f32[72,128]{1,0:T(8,128)S(1)}, u32[]{:S(2)}, u32[]{:S(2)}) collective-permute-start(f32[72,128]{1,0:T(8,128)S(1)} %add_add_fusion.1), channel_id=1, source_target_pairs={{232,0},{224,8},{248,16},{240,24},{72,32},{64,40},{88,48},{80,56},... | collective-permute-start | bytes 110600 | tf_op jit(solution)/shard_map/ppermute | solution.py:282
  83.9 1.1 %collective-permute-done.27 = f32[72,128]{1,0:T(8,128)S(1)} collective-permute-done((f32[72,128]{1,0:T(8,128)S(1)}, f32[72,128]{1,0:T(8,128)S(1)}, u32[]{:S(2)}, u32[]{:S(2)}) %collective-permute-start.27) | collective-permute-done | bytes 36896 | tf_op jit(solution)/shard_map/ppermute | solution.py:282
  85.0 2.8 %collective-permute-done.25 = f32[72,128]{1,0:T(8,128)S(1)} collective-permute-done((f32[72,128]{1,0:T(8,128)S(1)}, f32[72,128]{1,0:T(8,128)S(1)}, u32[]{:S(2)}, u32[]{:S(2)}) %collective-permute-start.25) | collective-permute-done | bytes 36896 | tf_op jit(solution)/shard_map/ppermute | solution.py:282
  88.6 7.7 %collective-permute-done.28.mine_ref = f32[72,128]{1,0:T(8,128)S(1)} collective-permute-done((f32[72,128]{1,0:T(8,128)S(1)}, f32[72,128]{1,0:T(8,128)S(1)}, u32[]{:S(2)}, u32[]{:S(2)}) %collective-permute-start.28) | collective-permute-done | bytes 36896 | tf_op jit(solution)/shard_map/ppermute | solution.py:337
  96.9 1.8 %shard_map.24 = (f32[128,128]{1,0:T(8,128)S(1)}, f32[128,128]{1,0:T(8,128)S(1)}, f32[128,128]{1,0:T(8,128)S(1)}) custom-call(s32[1]{0:T(128)} %bitcast.core_ref, f32[72,128]{1,0:T(8,128)S(1)} %add_add_fusion.mine_ref, f32[72,128]{1,0:T(8,128)S(1)} %collective-permute-done.30.other_ref), custom_call_target="tpu_custom_call" | custom-call | tf_op jit(solution)/shard_map/pallas_call | solution.py:219
  99.7 3.3 %shard_map.27 = f32[512,256]{1,0:T(8,128)} custom-call(s32[1]{0:T(128)} %bitcast.core_ref, f32[72,128]{1,0:T(8,128)S(1)} %collective-permute-done.28.mine_ref, f32[72,128]{1,0:T(8,128)S(1)} %collective-permute-done.29.other_ref, f32[512,128]{1,0:T(8,128)S(1)} %shard_map.25.own_ref, f32[512,128]{1,0:T(8,128)S(1)} %shard_map.26.refs_0_, ...), custom_call_target="tpu_custom_call" | custom-call | tf_op jit(solution)/shard_map/pallas_call | solution.py:219
  (54 shorter events, 14.7 us)
Async XLA Ops:
  1.4 34.9 %collective-permute-start.9 = (f32[512,256]{1,0:T(8,128)S(1)}, f32[512,256]{1,0:T(8,128)S(1)}, u32[]{:S(2)}, u32[]{:S(2)}) collective-permute-start(f32[512,256]{1,0:T(8,128)S(1)} %get-tuple-element.32.refs_0_), channel_id=1, source_target_pairs={{7,0},{0,1},{1,2},{2,3},{3,4},{4,5},{5,6},{6,7},{15,8},{8,9},{9,10... | collective-permute-start | bytes 1572872 | tf_op jit(solution)/shard_map/ppermute | solution.py:327
  5.2 1.8 %collective-permute-start = (f32[72,128]{1,0:T(8,128)S(1)}, f32[72,128]{1,0:T(8,128)S(1)}, u32[]{:S(2)}, u32[]{:S(2)}) collective-permute-start(f32[72,128]{1,0:T(8,128)S(1)} %get-tuple-element.28), channel_id=1, source_target_pairs={{8,0},{0,8},{24,16},{16,24},{40,32},{32,40},{56,48},{48,56},{72,64... | collective-permute-start | bytes 110600 | tf_op jit(solution)/shard_map/ppermute | solution.py:282
  7.0 3.5 %collective-permute-start.1 = (f32[72,128]{1,0:T(8,128)S(1)}, f32[72,128]{1,0:T(8,128)S(1)}, u32[]{:S(2)}, u32[]{:S(2)}) collective-permute-start(f32[72,128]{1,0:T(8,128)S(1)} %add.60), channel_id=1, source_target_pairs={{40,0},{32,8},{56,16},{48,24},{8,32},{0,40},{24,48},{16,56},{104,6... | collective-permute-start | bytes 110600 | tf_op jit(solution)/shard_map/ppermute | solution.py:282
  10.5 10.4 %collective-permute-start.4 = (f32[72,128]{1,0:T(8,128)S(1)}, f32[72,128]{1,0:T(8,128)S(1)}, u32[]{:S(2)}, u32[]{:S(2)}) collective-permute-start(f32[72,128]{1,0:T(8,128)S(1)} %add.61), channel_id=1, source_target_pairs={{168,0},{160,8},{184,16},{176,24},{136,32},{128,40},{152,48},{144,... | collective-permute-start | bytes 110600 | tf_op jit(solution)/shard_map/ppermute | solution.py:282
  17.1 3.7 %collective-permute-start.3 = (f32[72,128]{1,0:T(8,128)S(1)}, f32[72,128]{1,0:T(8,128)S(1)}, u32[]{:S(2)}, u32[]{:S(2)}) collective-permute-start(f32[72,128]{1,0:T(8,128)S(1)} %add.61), channel_id=1, source_target_pairs={{64,0},{72,8},{80,16},{88,24},{224,32},{232,40},{240,48},{248,56},... | collective-permute-start | bytes 110600 | tf_op jit(solution)/shard_map/ppermute | solution.py:282
  17.4 5.5 %collective-permute-start.2 = (f32[72,128]{1,0:T(8,128)S(1)}, f32[72,128]{1,0:T(8,128)S(1)}, u32[]{:S(2)}, u32[]{:S(2)}) collective-permute-start(f32[72,128]{1,0:T(8,128)S(1)} %add.61), channel_id=1, source_target_pairs={{232,0},{224,8},{248,16},{240,24},{72,32},{64,40},{88,48},{80,56},... | collective-permute-start | bytes 110600 | tf_op jit(solution)/shard_map/ppermute | solution.py:282
  22.9 3.5 %collective-permute-start.5 = (f32[72,128]{1,0:T(8,128)S(1)}, f32[72,128]{1,0:T(8,128)S(1)}, u32[]{:S(2)}, u32[]{:S(2)}) collective-permute-start(f32[72,128]{1,0:T(8,128)S(1)} %add_add_fusion.4), channel_id=1, source_target_pairs={{24,0},{16,8},{8,16},{0,24},{56,32},{48,40},{40,48},{32,56},{88,64... | collective-permute-start | bytes 110600 | tf_op jit(solution)/shard_map/ppermute | solution.py:282
  26.4 7.0 %collective-permute-start.6 = (f32[72,128]{1,0:T(8,128)S(1)}, f32[72,128]{1,0:T(8,128)S(1)}, u32[]{:S(2)}, u32[]{:S(2)}) collective-permute-start(f32[72,128]{1,0:T(8,128)S(1)} %add.65.mine_ref), channel_id=1, source_target_pairs={{15,0},{8,1},{9,2},{10,3},{11,4},{12,5},{13,6},{14,7},{7,8},{0,9},... | collective-permute-start | bytes 110600 | tf_op jit(solution)/shard_map/ppermute | solution.py:337
  28.1 5.3 %collective-permute-start.8 = (f32[72,128]{1,0:T(8,128)S(1)}, f32[72,128]{1,0:T(8,128)S(1)}, u32[]{:S(2)}, u32[]{:S(2)}) collective-permute-start(f32[72,128]{1,0:T(8,128)S(1)} %add.65.mine_ref), channel_id=1, source_target_pairs={{8,0},{0,8},{24,16},{16,24},{40,32},{32,40},{56,48},{48,56},{72,64... | collective-permute-start | bytes 110600 | tf_op jit(solution)/shard_map/ppermute | solution.py:282
  33.4 2.8 %collective-permute-start.7 = (f32[72,128]{1,0:T(8,128)S(1)}, f32[72,128]{1,0:T(8,128)S(1)}, u32[]{:S(2)}, u32[]{:S(2)}) collective-permute-start(f32[72,128]{1,0:T(8,128)S(1)} %collective-permute-done.6.mine_ref), channel_id=1, source_target_pairs={{8,0},{0,8},{24,16},{16,24},{40,32},{32,40},{56,48},{48,56},{72,64... | collective-permute-start | bytes 110600 | tf_op jit(solution)/shard_map/ppermute | solution.py:282
  39.0 1.5 %collective-permute-start.10 = (f32[72,128]{1,0:T(8,128)S(1)}, f32[72,128]{1,0:T(8,128)S(1)}, u32[]{:S(2)}, u32[]{:S(2)}) collective-permute-start(f32[72,128]{1,0:T(8,128)S(1)} %get-tuple-element.34), channel_id=1, source_target_pairs={{8,0},{0,8},{24,16},{16,24},{40,32},{32,40},{56,48},{48,56},{72,64... | collective-permute-start | bytes 110600 | tf_op jit(solution)/shard_map/ppermute | solution.py:282
  40.5 3.7 %collective-permute-start.13 = (f32[72,128]{1,0:T(8,128)S(1)}, f32[72,128]{1,0:T(8,128)S(1)}, u32[]{:S(2)}, u32[]{:S(2)}) collective-permute-start(f32[72,128]{1,0:T(8,128)S(1)} %add.66), channel_id=1, source_target_pairs={{48,0},{56,8},{32,16},{40,24},{16,32},{24,40},{0,48},{8,56},{112,6... | collective-permute-start | bytes 110600 | tf_op jit(solution)/shard_map/ppermute | solution.py:282
  42.4 3.8 %collective-permute-start.12 = (f32[72,128]{1,0:T(8,128)S(1)}, f32[72,128]{1,0:T(8,128)S(1)}, u32[]{:S(2)}, u32[]{:S(2)}) collective-permute-start(f32[72,128]{1,0:T(8,128)S(1)} %add.66), channel_id=1, source_target_pairs={{24,0},{16,8},{8,16},{0,24},{56,32},{48,40},{40,48},{32,56},{88,64... | collective-permute-start | bytes 110600 | tf_op jit(solution)/shard_map/ppermute | solution.py:282
  43.3 3.4 %collective-permute-start.11 = (f32[72,128]{1,0:T(8,128)S(1)}, f32[72,128]{1,0:T(8,128)S(1)}, u32[]{:S(2)}, u32[]{:S(2)}) collective-permute-start(f32[72,128]{1,0:T(8,128)S(1)} %add.66), channel_id=1, source_target_pairs={{40,0},{32,8},{56,16},{48,24},{8,32},{0,40},{24,48},{16,56},{104,6... | collective-permute-start | bytes 110600 | tf_op jit(solution)/shard_map/ppermute | solution.py:282
  46.7 6.5 %collective-permute-start.16 = (f32[72,128]{1,0:T(8,128)S(1)}, f32[72,128]{1,0:T(8,128)S(1)}, u32[]{:S(2)}, u32[]{:S(2)}) collective-permute-start(f32[72,128]{1,0:T(8,128)S(1)} %add_add_fusion.3), channel_id=1, source_target_pairs={{168,0},{160,8},{184,16},{176,24},{136,32},{128,40},{152,48},{144,... | collective-permute-start | bytes 110600 | tf_op jit(solution)/shard_map/ppermute | solution.py:282
  50.2 3.7 %collective-permute-start.15 = (f32[72,128]{1,0:T(8,128)S(1)}, f32[72,128]{1,0:T(8,128)S(1)}, u32[]{:S(2)}, u32[]{:S(2)}) collective-permute-start(f32[72,128]{1,0:T(8,128)S(1)} %add_add_fusion.3), channel_id=1, source_target_pairs={{64,0},{72,8},{80,16},{88,24},{224,32},{232,40},{240,48},{248,56},... | collective-permute-start | bytes 110600 | tf_op jit(solution)/shard_map/ppermute | solution.py:282
  50.8 5.3 %collective-permute-start.14 = (f32[72,128]{1,0:T(8,128)S(1)}, f32[72,128]{1,0:T(8,128)S(1)}, u32[]{:S(2)}, u32[]{:S(2)}) collective-permute-start(f32[72,128]{1,0:T(8,128)S(1)} %add_add_fusion.3), channel_id=1, source_target_pairs={{232,0},{224,8},{248,16},{240,24},{72,32},{64,40},{88,48},{80,56},... | collective-permute-start | bytes 110600 | tf_op jit(solution)/shard_map/ppermute | solution.py:282
  53.2 15.8 %collective-permute-start.20 = (f32[512,128]{1,0:T(8,128)S(1)}, f32[512,128]{1,0:T(8,128)S(1)}, u32[]{:S(2)}, u32[]{:S(2)}) collective-permute-start(f32[512,128]{1,0:T(8,128)S(1)} %get-tuple-element.38.refs_1_), channel_id=1, source_target_pairs={{7,0},{0,1},{1,2},{2,3},{3,4},{4,5},{5,6},{6,7},{15,8},{8,9},{9,10... | collective-permute-start | bytes 786440 | tf_op jit(solution)/shard_map/ppermute | solution.py:327
  56.1 9.6 %collective-permute-start.17 = (f32[72,128]{1,0:T(8,128)S(1)}, f32[72,128]{1,0:T(8,128)S(1)}, u32[]{:S(2)}, u32[]{:S(2)}) collective-permute-start(f32[72,128]{1,0:T(8,128)S(1)} %add_add_fusion.2.mine_ref), channel_id=1, source_target_pairs={{15,0},{8,1},{9,2},{10,3},{11,4},{12,5},{13,6},{14,7},{7,8},{0,9},... | collective-permute-start | bytes 110600 | tf_op jit(solution)/shard_map/ppermute | solution.py:337
  56.3 9.9 %collective-permute-start.19 = (f32[72,128]{1,0:T(8,128)S(1)}, f32[72,128]{1,0:T(8,128)S(1)}, u32[]{:S(2)}, u32[]{:S(2)}) collective-permute-start(f32[72,128]{1,0:T(8,128)S(1)} %add_add_fusion.2.mine_ref), channel_id=1, source_target_pairs={{8,0},{0,8},{24,16},{16,24},{40,32},{32,40},{56,48},{48,56},{72,64... | collective-permute-start | bytes 110600 | tf_op jit(solution)/shard_map/ppermute | solution.py:282
  65.7 3.3 %collective-permute-start.18 = (f32[72,128]{1,0:T(8,128)S(1)}, f32[72,128]{1,0:T(8,128)S(1)}, u32[]{:S(2)}, u32[]{:S(2)}) collective-permute-start(f32[72,128]{1,0:T(8,128)S(1)} %collective-permute-done.17.mine_ref), channel_id=1, source_target_pairs={{8,0},{0,8},{24,16},{16,24},{40,32},{32,40},{56,48},{48,56},{72,64... | collective-permute-start | bytes 110600 | tf_op jit(solution)/shard_map/ppermute | solution.py:282
  71.8 1.4 %collective-permute-start.21 = (f32[72,128]{1,0:T(8,128)S(1)}, f32[72,128]{1,0:T(8,128)S(1)}, u32[]{:S(2)}, u32[]{:S(2)}) collective-permute-start(f32[72,128]{1,0:T(8,128)S(1)} %get-tuple-element.42), channel_id=1, source_target_pairs={{8,0},{0,8},{24,16},{16,24},{40,32},{32,40},{56,48},{48,56},{72,64... | collective-permute-start | bytes 110600 | tf_op jit(solution)/shard_map/ppermute | solution.py:282
  73.1 3.7 %collective-permute-start.24 = (f32[72,128]{1,0:T(8,128)S(1)}, f32[72,128]{1,0:T(8,128)S(1)}, u32[]{:S(2)}, u32[]{:S(2)}) collective-permute-start(f32[72,128]{1,0:T(8,128)S(1)} %add.73), channel_id=1, source_target_pairs={{48,0},{56,8},{32,16},{40,24},{16,32},{24,40},{0,48},{8,56},{112,6... | collective-permute-start | bytes 110600 | tf_op jit(solution)/shard_map/ppermute | solution.py:282
  73.7 4.6 %collective-permute-start.23 = (f32[72,128]{1,0:T(8,128)S(1)}, f32[72,128]{1,0:T(8,128)S(1)}, u32[]{:S(2)}, u32[]{:S(2)}) collective-permute-start(f32[72,128]{1,0:T(8,128)S(1)} %add.73), channel_id=1, source_target_pairs={{24,0},{16,8},{8,16},{0,24},{56,32},{48,40},{40,48},{32,56},{88,64... | collective-permute-start | bytes 110600 | tf_op jit(solution)/shard_map/ppermute | solution.py:282
  75.2 3.4 %collective-permute-start.22 = (f32[72,128]{1,0:T(8,128)S(1)}, f32[72,128]{1,0:T(8,128)S(1)}, u32[]{:S(2)}, u32[]{:S(2)}) collective-permute-start(f32[72,128]{1,0:T(8,128)S(1)} %add.73), channel_id=1, source_target_pairs={{40,0},{32,8},{56,16},{48,24},{8,32},{0,40},{24,48},{16,56},{104,6... | collective-permute-start | bytes 110600 | tf_op jit(solution)/shard_map/ppermute | solution.py:282
  78.5 6.5 %collective-permute-start.27 = (f32[72,128]{1,0:T(8,128)S(1)}, f32[72,128]{1,0:T(8,128)S(1)}, u32[]{:S(2)}, u32[]{:S(2)}) collective-permute-start(f32[72,128]{1,0:T(8,128)S(1)} %add_add_fusion.1), channel_id=1, source_target_pairs={{168,0},{160,8},{184,16},{176,24},{136,32},{128,40},{152,48},{144,... | collective-permute-start | bytes 110600 | tf_op jit(solution)/shard_map/ppermute | solution.py:282
  80.8 4.2 %collective-permute-start.26 = (f32[72,128]{1,0:T(8,128)S(1)}, f32[72,128]{1,0:T(8,128)S(1)}, u32[]{:S(2)}, u32[]{:S(2)}) collective-permute-start(f32[72,128]{1,0:T(8,128)S(1)} %add_add_fusion.1), channel_id=1, source_target_pairs={{64,0},{72,8},{80,16},{88,24},{224,32},{232,40},{240,48},{248,56},... | collective-permute-start | bytes 110600 | tf_op jit(solution)/shard_map/ppermute | solution.py:282
  82.7 5.2 %collective-permute-start.25 = (f32[72,128]{1,0:T(8,128)S(1)}, f32[72,128]{1,0:T(8,128)S(1)}, u32[]{:S(2)}, u32[]{:S(2)}) collective-permute-start(f32[72,128]{1,0:T(8,128)S(1)} %add_add_fusion.1), channel_id=1, source_target_pairs={{232,0},{224,8},{248,16},{240,24},{72,32},{64,40},{88,48},{80,56},... | collective-permute-start | bytes 110600 | tf_op jit(solution)/shard_map/ppermute | solution.py:282
  83.9 15.8 %collective-permute-start.31 = (f32[512,128]{1,0:T(8,128)S(1)}, f32[512,128]{1,0:T(8,128)S(1)}, u32[]{:S(2)}, u32[]{:S(2)}) collective-permute-start(f32[512,128]{1,0:T(8,128)S(1)} %get-tuple-element.46.refs_1_), channel_id=1, source_target_pairs={{7,0},{0,1},{1,2},{2,3},{3,4},{4,5},{5,6},{6,7},{15,8},{8,9},{9,10... | collective-permute-start | bytes 786440 | tf_op jit(solution)/shard_map/ppermute | solution.py:327
  87.9 8.5 %collective-permute-start.28 = (f32[72,128]{1,0:T(8,128)S(1)}, f32[72,128]{1,0:T(8,128)S(1)}, u32[]{:S(2)}, u32[]{:S(2)}) collective-permute-start(f32[72,128]{1,0:T(8,128)S(1)} %add_add_fusion.mine_ref), channel_id=1, source_target_pairs={{15,0},{8,1},{9,2},{10,3},{11,4},{12,5},{13,6},{14,7},{7,8},{0,9},... | collective-permute-start | bytes 110600 | tf_op jit(solution)/shard_map/ppermute | solution.py:337
  88.2 8.7 %collective-permute-start.30 = (f32[72,128]{1,0:T(8,128)S(1)}, f32[72,128]{1,0:T(8,128)S(1)}, u32[]{:S(2)}, u32[]{:S(2)}) collective-permute-start(f32[72,128]{1,0:T(8,128)S(1)} %add_add_fusion.mine_ref), channel_id=1, source_target_pairs={{8,0},{0,8},{24,16},{16,24},{40,32},{32,40},{56,48},{48,56},{72,64... | collective-permute-start | bytes 110600 | tf_op jit(solution)/shard_map/ppermute | solution.py:282
  96.4 3.3 %collective-permute-start.29 = (f32[72,128]{1,0:T(8,128)S(1)}, f32[72,128]{1,0:T(8,128)S(1)}, u32[]{:S(2)}, u32[]{:S(2)}) collective-permute-start(f32[72,128]{1,0:T(8,128)S(1)} %collective-permute-done.28.mine_ref), channel_id=1, source_target_pairs={{8,0},{0,8},{24,16},{16,24},{40,32},{32,40},{56,48},{48,56},{72,64... | collective-permute-start | bytes 110600 | tf_op jit(solution)/shard_map/ppermute | solution.py:282

commit v10 on v9

--- a/solution.py
+++ b/solution.py
@@ -169,7 +169,7 @@
 
 def second_kernel(core_ref, mine_ref, other_ref, own_ref, *refs):
     *blocks, b_out, m_out, md_out, mine_out, other_out, cross_ref = refs
-    d = cosines_of(1 - core_ref[0], mine_ref, other_ref)
+    d = cosines_of(core_ref[0], mine_ref, other_ref)
     dt = jnp.transpose(d)
     a, b = both_blocks(blocks)
     turned = left3(a - times3(left3(b), right3(dt)))
@@ -189,7 +189,7 @@
     rows, n = own_ref.shape
     copies = [pltpu.make_async_copy(own_ref, out_ref.at[:, :n], sems.at[CHUNKS])]
     copies[0].start()
-    d = cosines_of(1 - core_ref[0], mine_ref, other_ref)
+    d = cosines_of(core_ref[0], mine_ref, other_ref)
     dt = jnp.transpose(d)
     a, b = both_blocks(blocks)
     turned = left3(a - times3(left3(b), right3(dt)))
@@ -332,7 +332,7 @@
     route = []
     for row in range(lax.axis_size("row")):
         for pair in range(pairs):
-            source = (row ^ 1) * pairs + (pair - 1) % pairs
+            source = (row ^ 3) * pairs + (pair - 1) % pairs
             route.append((source, row * pairs + pair))
     return lax.ppermute(half, ("row", "pair"), route)
 

time: 103 us -> 103 us (level)
  no operation moved by 1% of the time
where the time goes in v10:
time: 103 us
  waiting for transfers between devices  43.1 us (42%)
  starting transfers between devices  39.8 us (39%)
  Pallas kernels  19.3 us (19%)
    ppermute x26, starting transfers between devices, from_row(): return lax.ppermute(x, 'row', route)  34.2 us
    ppermute x26, waiting for transfers between devices, from_row(): return lax.ppermute(x, 'row', route)  21.6 us
    ppermute x3, waiting for transfers between devices, hopped_over(): return lax.ppermute(half, ('row', 'pair'), route)  21.5 us
    pallas_call x11, Pallas kernels, vmem_call(): pl.pallas_call(kernel, out_shape=shapes, in_specs=specs, scratch_shapes=s...  18 us
    ppermute x3, starting transfers between devices, shifted(): return lax.ppermute(block, 'pair', route)  3.81 us
  transfers between devices with their start and end apart: 32, of which 19 were waited for; matrix products, arithmetic and copies ran while one was open for 0% of the time, Pallas kernels for 9%

profile of v10, /device:TPU:1, one launch (start us, length us, event | category | flops | bytes accessed | tf_op | source)
XLA Modules:
  0.0 102.7 jit_solution(10678029382598138507)
XLA Ops:
  0.0 1.3 %load.1 = (f32[512,256]{1,0:T(8,128)S(1)}, f32[72,128]{1,0:T(8,128)S(1)}, f32[72,128]{1,0:T(8,128)S(1)}) custom-call(s32[1]{0:T(128)} %bitcast.core_ref, f32[512,256]{1,0:T(8,128)} %panel_ref.1), custom_call_target="tpu_custom_call" | custom-call | tf_op jit(solution)/shard_map/load/pallas_call | solution.py:231
  1.4 3.8 %collective-permute-start.9 = (f32[512,256]{1,0:T(8,128)S(1)}, f32[512,256]{1,0:T(8,128)S(1)}, u32[]{:S(2)}, u32[]{:S(2)}) collective-permute-start(f32[512,256]{1,0:T(8,128)S(1)} %get-tuple-element.32.refs_0_), channel_id=1, source_target_pairs={{7,0},{0,1},{1,2},{2,3},{3,4},{4,5},{5,6},{6,7},{15,8},{8,9},{9,10... | collective-permute-start | bytes 1572872 | tf_op jit(solution)/shard_map/ppermute | solution.py:327
  7.0 1.9 %collective-permute-start.1 = (f32[72,128]{1,0:T(8,128)S(1)}, f32[72,128]{1,0:T(8,128)S(1)}, u32[]{:S(2)}, u32[]{:S(2)}) collective-permute-start(f32[72,128]{1,0:T(8,128)S(1)} %add.60), channel_id=1, source_target_pairs={{40,0},{32,8},{56,16},{48,24},{8,32},{0,40},{24,48},{16,56},{104,6... | collective-permute-start | bytes 110600 | tf_op jit(solution)/shard_map/ppermute | solution.py:282
  8.9 1.6 %collective-permute-done.1 = f32[72,128]{1,0:T(8,128)S(1)} collective-permute-done((f32[72,128]{1,0:T(8,128)S(1)}, f32[72,128]{1,0:T(8,128)S(1)}, u32[]{:S(2)}, u32[]{:S(2)}) %collective-permute-start.1) | collective-permute-done | bytes 36896 | tf_op jit(solution)/shard_map/ppermute | solution.py:282
  10.5 6.6 %collective-permute-start.4 = (f32[72,128]{1,0:T(8,128)S(1)}, f32[72,128]{1,0:T(8,128)S(1)}, u32[]{:S(2)}, u32[]{:S(2)}) collective-permute-start(f32[72,128]{1,0:T(8,128)S(1)} %add.61), channel_id=1, source_target_pairs={{168,0},{160,8},{184,16},{176,24},{136,32},{128,40},{152,48},{144,... | collective-permute-start | bytes 110600 | tf_op jit(solution)/shard_map/ppermute | solution.py:282
  17.4 3.5 %collective-permute-start.2 = (f32[72,128]{1,0:T(8,128)S(1)}, f32[72,128]{1,0:T(8,128)S(1)}, u32[]{:S(2)}, u32[]{:S(2)}) collective-permute-start(f32[72,128]{1,0:T(8,128)S(1)} %add.61), channel_id=1, source_target_pairs={{232,0},{224,8},{248,16},{240,24},{72,32},{64,40},{88,48},{80,56},... | collective-permute-start | bytes 110600 | tf_op jit(solution)/shard_map/ppermute | solution.py:282
  20.9 2.0 %collective-permute-done.2 = f32[72,128]{1,0:T(8,128)S(1)} collective-permute-done((f32[72,128]{1,0:T(8,128)S(1)}, f32[72,128]{1,0:T(8,128)S(1)}, u32[]{:S(2)}, u32[]{:S(2)}) %collective-permute-start.2) | collective-permute-done | bytes 36896 | tf_op jit(solution)/shard_map/ppermute | solution.py:282
  23.1 3.3 %collective-permute-done.5 = f32[72,128]{1,0:T(8,128)S(1)} collective-permute-done((f32[72,128]{1,0:T(8,128)S(1)}, f32[72,128]{1,0:T(8,128)S(1)}, u32[]{:S(2)}, u32[]{:S(2)}) %collective-permute-start.5) | collective-permute-done | bytes 36896 | tf_op jit(solution)/shard_map/ppermute | solution.py:282
  26.4 1.4 %collective-permute-start.6 = (f32[72,128]{1,0:T(8,128)S(1)}, f32[72,128]{1,0:T(8,128)S(1)}, u32[]{:S(2)}, u32[]{:S(2)}) collective-permute-start(f32[72,128]{1,0:T(8,128)S(1)} %add.65.mine_ref), channel_id=1, source_target_pairs={{31,0},{24,1},{25,2},{26,3},{27,4},{28,5},{29,6},{30,7},{23,8},{16... | collective-permute-start | bytes 110600 | tf_op jit(solution)/shard_map/ppermute | solution.py:337
  28.5 4.6 %collective-permute-done.6.mine_ref = f32[72,128]{1,0:T(8,128)S(1)} collective-permute-done((f32[72,128]{1,0:T(8,128)S(1)}, f32[72,128]{1,0:T(8,128)S(1)}, u32[]{:S(2)}, u32[]{:S(2)}) %collective-permute-start.6) | collective-permute-done | bytes 36896 | tf_op jit(solution)/shard_map/ppermute | solution.py:337
  33.1 1.8 %shard_map.17 = (f32[128,128]{1,0:T(8,128)S(1)}, f32[128,128]{1,0:T(8,128)S(1)}, f32[128,128]{1,0:T(8,128)S(1)}) custom-call(s32[1]{0:T(128)} %bitcast.core_ref, f32[72,128]{1,0:T(8,128)S(1)} %add.65.mine_ref, f32[72,128]{1,0:T(8,128)S(1)} %collective-permute-done.8.other_ref), custom_call_target="tpu_custom_call" | custom-call | tf_op jit(solution)/shard_map/pallas_call | solution.py:219
  35.9 2.8 %shard_map.19 = (f32[512,128]{1,0:T(8,128)S(1)}, f32[128,128]{1,0:T(8,128)S(1)}, f32[128,128]{1,0:T(8,128)S(1)}, f32[72,128]{1,0:T(8,128)S(1)}, f32[72,128]{1,0:T(8,128)S(1)}) custom-call(s32[1]{0:T(128)} %bitcast.core_ref, f32[72,128]{1,0:T(8,128)S(1)} %collective-permute-done.6.mine_ref, f32[72,128]{1,0:T(8,128)S(1)} %collective-permute-done.7.other_ref, ...), custom_call_target="tpu_custom_call" | custom-call | tf_op jit(solution)/shard_map/pallas_call | solution.py:219
  40.9 2.1 %collective-permute-start.12 = (f32[72,128]{1,0:T(8,128)S(1)}, f32[72,128]{1,0:T(8,128)S(1)}, u32[]{:S(2)}, u32[]{:S(2)}) collective-permute-start(f32[72,128]{1,0:T(8,128)S(1)} %add.66), channel_id=1, source_target_pairs={{24,0},{16,8},{8,16},{0,24},{56,32},{48,40},{40,48},{32,56},{88,64... | collective-permute-start | bytes 110600 | tf_op jit(solution)/shard_map/ppermute | solution.py:282
  43.9 1.2 %collective-permute-done.12 = f32[72,128]{1,0:T(8,128)S(1)} collective-permute-done((f32[72,128]{1,0:T(8,128)S(1)}, f32[72,128]{1,0:T(8,128)S(1)}, u32[]{:S(2)}, u32[]{:S(2)}) %collective-permute-start.12) | collective-permute-done | bytes 36896 | tf_op jit(solution)/shard_map/ppermute | solution.py:282
  45.1 1.3 %collective-permute-done.11 = f32[72,128]{1,0:T(8,128)S(1)} collective-permute-done((f32[72,128]{1,0:T(8,128)S(1)}, f32[72,128]{1,0:T(8,128)S(1)}, u32[]{:S(2)}, u32[]{:S(2)}) %collective-permute-start.11) | collective-permute-done | bytes 36896 | tf_op jit(solution)/shard_map/ppermute | solution.py:282
  46.4 3.5 %collective-permute-start.16 = (f32[72,128]{1,0:T(8,128)S(1)}, f32[72,128]{1,0:T(8,128)S(1)}, u32[]{:S(2)}, u32[]{:S(2)}) collective-permute-start(f32[72,128]{1,0:T(8,128)S(1)} %add_add_fusion.3), channel_id=1, source_target_pairs={{168,0},{160,8},{184,16},{176,24},{136,32},{128,40},{152,48},{144,... | collective-permute-start | bytes 110600 | tf_op jit(solution)/shard_map/ppermute | solution.py:282
  50.5 2.5 %collective-permute-start.14 = (f32[72,128]{1,0:T(8,128)S(1)}, f32[72,128]{1,0:T(8,128)S(1)}, u32[]{:S(2)}, u32[]{:S(2)}) collective-permute-start(f32[72,128]{1,0:T(8,128)S(1)} %add_add_fusion.3), channel_id=1, source_target_pairs={{232,0},{224,8},{248,16},{240,24},{72,32},{64,40},{88,48},{80,56},... | collective-permute-start | bytes 110600 | tf_op jit(solution)/shard_map/ppermute | solution.py:282
  53.7 2.1 %collective-permute-done.14 = f32[72,128]{1,0:T(8,128)S(1)} collective-permute-done((f32[72,128]{1,0:T(8,128)S(1)}, f32[72,128]{1,0:T(8,128)S(1)}, u32[]{:S(2)}, u32[]{:S(2)}) %collective-permute-start.14) | collective-permute-done | bytes 36896 | tf_op jit(solution)/shard_map/ppermute | solution.py:282
  56.4 9.1 %collective-permute-done.17.mine_ref = f32[72,128]{1,0:T(8,128)S(1)} collective-permute-done((f32[72,128]{1,0:T(8,128)S(1)}, f32[72,128]{1,0:T(8,128)S(1)}, u32[]{:S(2)}, u32[]{:S(2)}) %collective-permute-start.17) | collective-permute-done | bytes 36896 | tf_op jit(solution)/shard_map/ppermute | solution.py:337
  65.9 1.8 %shard_map.20 = (f32[128,128]{1,0:T(8,128)S(1)}, f32[128,128]{1,0:T(8,128)S(1)}, f32[128,128]{1,0:T(8,128)S(1)}) custom-call(s32[1]{0:T(128)} %bitcast.core_ref, f32[72,128]{1,0:T(8,128)S(1)} %add_add_fusion.2.mine_ref, f32[72,128]{1,0:T(8,128)S(1)} %collective-permute-done.19.other_ref), custom_call_target="tpu_custom_call" | custom-call | tf_op jit(solution)/shard_map/pallas_call | solution.py:219
  68.7 2.8 %shard_map.23 = (f32[512,128]{1,0:T(8,128)S(1)}, f32[128,128]{1,0:T(8,128)S(1)}, f32[128,128]{1,0:T(8,128)S(1)}, f32[72,128]{1,0:T(8,128)S(1)}, f32[72,128]{1,0:T(8,128)S(1)}) custom-call(s32[1]{0:T(128)} %bitcast.core_ref, f32[72,128]{1,0:T(8,128)S(1)} %collective-permute-done.17.mine_ref, f32[72,128]{1,0:T(8,128)S(1)} %collective-permute-done.18.other_ref, ...), custom_call_target="tpu_custom_call" | custom-call | tf_op jit(solution)/shard_map/pallas_call | solution.py:219
  72.9 1.7 %collective-permute-start.23 = (f32[72,128]{1,0:T(8,128)S(1)}, f32[72,128]{1,0:T(8,128)S(1)}, u32[]{:S(2)}, u32[]{:S(2)}) collective-permute-start(f32[72,128]{1,0:T(8,128)S(1)} %add.73), channel_id=1, source_target_pairs={{24,0},{16,8},{8,16},{0,24},{56,32},{48,40},{40,48},{32,56},{88,64... | collective-permute-start | bytes 110600 | tf_op jit(solution)/shard_map/ppermute | solution.py:282
  74.7 1.1 %collective-permute-start.22 = (f32[72,128]{1,0:T(8,128)S(1)}, f32[72,128]{1,0:T(8,128)S(1)}, u32[]{:S(2)}, u32[]{:S(2)}) collective-permute-start(f32[72,128]{1,0:T(8,128)S(1)} %add.73), channel_id=1, source_target_pairs={{40,0},{32,8},{56,16},{48,24},{8,32},{0,40},{24,48},{16,56},{104,6... | collective-permute-start | bytes 110600 | tf_op jit(solution)/shard_map/ppermute | solution.py:282
  76.9 1.2 %collective-permute-done.22 = f32[72,128]{1,0:T(8,128)S(1)} collective-permute-done((f32[72,128]{1,0:T(8,128)S(1)}, f32[72,128]{1,0:T(8,128)S(1)}, u32[]{:S(2)}, u32[]{:S(2)}) %collective-permute-start.22) | collective-permute-done | bytes 36896 | tf_op jit(solution)/shard_map/ppermute | solution.py:282
  78.1 2.1 %collective-permute-start.27 = (f32[72,128]{1,0:T(8,128)S(1)}, f32[72,128]{1,0:T(8,128)S(1)}, u32[]{:S(2)}, u32[]{:S(2)}) collective-permute-start(f32[72,128]{1,0:T(8,128)S(1)} %add_add_fusion.1), channel_id=1, source_target_pairs={{168,0},{160,8},{184,16},{176,24},{136,32},{128,40},{152,48},{144,... | collective-permute-start | bytes 110600 | tf_op jit(solution)/shard_map/ppermute | solution.py:282
  80.2 2.2 %collective-permute-start.26 = (f32[72,128]{1,0:T(8,128)S(1)}, f32[72,128]{1,0:T(8,128)S(1)}, u32[]{:S(2)}, u32[]{:S(2)}) collective-permute-start(f32[72,128]{1,0:T(8,128)S(1)} %add_add_fusion.1), channel_id=1, source_target_pairs={{64,0},{72,8},{80,16},{88,24},{224,32},{232,40},{240,48},{248,56},... | collective-permute-start | bytes 110600 | tf_op jit(solution)/shard_map/ppermute | solution.py:282
  82.4 1.0 collective-permute-start.25
  83.4 1.3 %collective-permute-done.27 = f32[72,128]{1,0:T(8,128)S(1)} collective-permute-done((f32[72,128]{1,0:T(8,128)S(1)}, f32[72,128]{1,0:T(8,128)S(1)}, u32[]{:S(2)}, u32[]{:S(2)}) %collective-permute-start.27) | collective-permute-done | bytes 36896 | tf_op jit(solution)/shard_map/ppermute | solution.py:282
  84.7 2.5 %collective-permute-done.25 = f32[72,128]{1,0:T(8,128)S(1)} collective-permute-done((f32[72,128]{1,0:T(8,128)S(1)}, f32[72,128]{1,0:T(8,128)S(1)}, u32[]{:S(2)}, u32[]{:S(2)}) %collective-permute-start.25) | collective-permute-done | bytes 36896 | tf_op jit(solution)/shard_map/ppermute | solution.py:282
  88.0 7.9 %collective-permute-done.28.mine_ref = f32[72,128]{1,0:T(8,128)S(1)} collective-permute-done((f32[72,128]{1,0:T(8,128)S(1)}, f32[72,128]{1,0:T(8,128)S(1)}, u32[]{:S(2)}, u32[]{:S(2)}) %collective-permute-start.28) | collective-permute-done | bytes 36896 | tf_op jit(solution)/shard_map/ppermute | solution.py:337
  96.4 1.8 %shard_map.24 = (f32[128,128]{1,0:T(8,128)S(1)}, f32[128,128]{1,0:T(8,128)S(1)}, f32[128,128]{1,0:T(8,128)S(1)}) custom-call(s32[1]{0:T(128)} %bitcast.core_ref, f32[72,128]{1,0:T(8,128)S(1)} %add_add_fusion.mine_ref, f32[72,128]{1,0:T(8,128)S(1)} %collective-permute-done.30.other_ref), custom_call_target="tpu_custom_call" | custom-call | tf_op jit(solution)/shard_map/pallas_call | solution.py:219
  99.2 3.3 %shard_map.27 = f32[512,256]{1,0:T(8,128)} custom-call(s32[1]{0:T(128)} %bitcast.core_ref, f32[72,128]{1,0:T(8,128)S(1)} %collective-permute-done.28.mine_ref, f32[72,128]{1,0:T(8,128)S(1)} %collective-permute-done.29.other_ref, f32[512,128]{1,0:T(8,128)S(1)} %shard_map.25.own_ref, f32[512,128]{1,0:T(8,128)S(1)} %shard_map.26.refs_0_, ...), custom_call_target="tpu_custom_call" | custom-call | tf_op jit(solution)/shard_map/pallas_call | solution.py:219
  (54 shorter events, 15.2 us)
Async XLA Ops:
  1.4 34.6 %collective-permute-start.9 = (f32[512,256]{1,0:T(8,128)S(1)}, f32[512,256]{1,0:T(8,128)S(1)}, u32[]{:S(2)}, u32[]{:S(2)}) collective-permute-start(f32[512,256]{1,0:T(8,128)S(1)} %get-tuple-element.32.refs_0_), channel_id=1, source_target_pairs={{7,0},{0,1},{1,2},{2,3},{3,4},{4,5},{5,6},{6,7},{15,8},{8,9},{9,10... | collective-permute-start | bytes 1572872 | tf_op jit(solution)/shard_map/ppermute | solution.py:327
  5.2 1.8 %collective-permute-start = (f32[72,128]{1,0:T(8,128)S(1)}, f32[72,128]{1,0:T(8,128)S(1)}, u32[]{:S(2)}, u32[]{:S(2)}) collective-permute-start(f32[72,128]{1,0:T(8,128)S(1)} %get-tuple-element.28), channel_id=1, source_target_pairs={{8,0},{0,8},{24,16},{16,24},{40,32},{32,40},{56,48},{48,56},{72,64... | collective-permute-start | bytes 110600 | tf_op jit(solution)/shard_map/ppermute | solution.py:282
  7.0 3.5 %collective-permute-start.1 = (f32[72,128]{1,0:T(8,128)S(1)}, f32[72,128]{1,0:T(8,128)S(1)}, u32[]{:S(2)}, u32[]{:S(2)}) collective-permute-start(f32[72,128]{1,0:T(8,128)S(1)} %add.60), channel_id=1, source_target_pairs={{40,0},{32,8},{56,16},{48,24},{8,32},{0,40},{24,48},{16,56},{104,6... | collective-permute-start | bytes 110600 | tf_op jit(solution)/shard_map/ppermute | solution.py:282
  10.5 10.4 %collective-permute-start.4 = (f32[72,128]{1,0:T(8,128)S(1)}, f32[72,128]{1,0:T(8,128)S(1)}, u32[]{:S(2)}, u32[]{:S(2)}) collective-permute-start(f32[72,128]{1,0:T(8,128)S(1)} %add.61), channel_id=1, source_target_pairs={{168,0},{160,8},{184,16},{176,24},{136,32},{128,40},{152,48},{144,... | collective-permute-start | bytes 110600 | tf_op jit(solution)/shard_map/ppermute | solution.py:282
  17.1 3.7 %collective-permute-start.3 = (f32[72,128]{1,0:T(8,128)S(1)}, f32[72,128]{1,0:T(8,128)S(1)}, u32[]{:S(2)}, u32[]{:S(2)}) collective-permute-start(f32[72,128]{1,0:T(8,128)S(1)} %add.61), channel_id=1, source_target_pairs={{64,0},{72,8},{80,16},{88,24},{224,32},{232,40},{240,48},{248,56},... | collective-permute-start | bytes 110600 | tf_op jit(solution)/shard_map/ppermute | solution.py:282
  17.4 5.5 %collective-permute-start.2 = (f32[72,128]{1,0:T(8,128)S(1)}, f32[72,128]{1,0:T(8,128)S(1)}, u32[]{:S(2)}, u32[]{:S(2)}) collective-permute-start(f32[72,128]{1,0:T(8,128)S(1)} %add.61), channel_id=1, source_target_pairs={{232,0},{224,8},{248,16},{240,24},{72,32},{64,40},{88,48},{80,56},... | collective-permute-start | bytes 110600 | tf_op jit(solution)/shard_map/ppermute | solution.py:282
  22.9 3.5 %collective-permute-start.5 = (f32[72,128]{1,0:T(8,128)S(1)}, f32[72,128]{1,0:T(8,128)S(1)}, u32[]{:S(2)}, u32[]{:S(2)}) collective-permute-start(f32[72,128]{1,0:T(8,128)S(1)} %add_add_fusion.4), channel_id=1, source_target_pairs={{24,0},{16,8},{8,16},{0,24},{56,32},{48,40},{40,48},{32,56},{88,64... | collective-permute-start | bytes 110600 | tf_op jit(solution)/shard_map/ppermute | solution.py:282
  26.4 6.7 %collective-permute-start.6 = (f32[72,128]{1,0:T(8,128)S(1)}, f32[72,128]{1,0:T(8,128)S(1)}, u32[]{:S(2)}, u32[]{:S(2)}) collective-permute-start(f32[72,128]{1,0:T(8,128)S(1)} %add.65.mine_ref), channel_id=1, source_target_pairs={{31,0},{24,1},{25,2},{26,3},{27,4},{28,5},{29,6},{30,7},{23,8},{16... | collective-permute-start | bytes 110600 | tf_op jit(solution)/shard_map/ppermute | solution.py:337
  27.8 5.3 %collective-permute-start.8 = (f32[72,128]{1,0:T(8,128)S(1)}, f32[72,128]{1,0:T(8,128)S(1)}, u32[]{:S(2)}, u32[]{:S(2)}) collective-permute-start(f32[72,128]{1,0:T(8,128)S(1)} %add.65.mine_ref), channel_id=1, source_target_pairs={{8,0},{0,8},{24,16},{16,24},{40,32},{32,40},{56,48},{48,56},{72,64... | collective-permute-start | bytes 110600 | tf_op jit(solution)/shard_map/ppermute | solution.py:282
  33.1 2.8 %collective-permute-start.7 = (f32[72,128]{1,0:T(8,128)S(1)}, f32[72,128]{1,0:T(8,128)S(1)}, u32[]{:S(2)}, u32[]{:S(2)}) collective-permute-start(f32[72,128]{1,0:T(8,128)S(1)} %collective-permute-done.6.mine_ref), channel_id=1, source_target_pairs={{8,0},{0,8},{24,16},{16,24},{40,32},{32,40},{56,48},{48,56},{72,64... | collective-permute-start | bytes 110600 | tf_op jit(solution)/shard_map/ppermute | solution.py:282
  38.7 1.5 %collective-permute-start.10 = (f32[72,128]{1,0:T(8,128)S(1)}, f32[72,128]{1,0:T(8,128)S(1)}, u32[]{:S(2)}, u32[]{:S(2)}) collective-permute-start(f32[72,128]{1,0:T(8,128)S(1)} %get-tuple-element.34), channel_id=1, source_target_pairs={{8,0},{0,8},{24,16},{16,24},{40,32},{32,40},{56,48},{48,56},{72,64... | collective-permute-start | bytes 110600 | tf_op jit(solution)/shard_map/ppermute | solution.py:282
  40.2 3.7 %collective-permute-start.13 = (f32[72,128]{1,0:T(8,128)S(1)}, f32[72,128]{1,0:T(8,128)S(1)}, u32[]{:S(2)}, u32[]{:S(2)}) collective-permute-start(f32[72,128]{1,0:T(8,128)S(1)} %add.66), channel_id=1, source_target_pairs={{48,0},{56,8},{32,16},{40,24},{16,32},{24,40},{0,48},{8,56},{112,6... | collective-permute-start | bytes 110600 | tf_op jit(solution)/shard_map/ppermute | solution.py:282
  40.9 4.2 %collective-permute-start.12 = (f32[72,128]{1,0:T(8,128)S(1)}, f32[72,128]{1,0:T(8,128)S(1)}, u32[]{:S(2)}, u32[]{:S(2)}) collective-permute-start(f32[72,128]{1,0:T(8,128)S(1)} %add.66), channel_id=1, source_target_pairs={{24,0},{16,8},{8,16},{0,24},{56,32},{48,40},{40,48},{32,56},{88,64... | collective-permute-start | bytes 110600 | tf_op jit(solution)/shard_map/ppermute | solution.py:282
  43.0 3.4 %collective-permute-start.11 = (f32[72,128]{1,0:T(8,128)S(1)}, f32[72,128]{1,0:T(8,128)S(1)}, u32[]{:S(2)}, u32[]{:S(2)}) collective-permute-start(f32[72,128]{1,0:T(8,128)S(1)} %add.66), channel_id=1, source_target_pairs={{40,0},{32,8},{56,16},{48,24},{8,32},{0,40},{24,48},{16,56},{104,6... | collective-permute-start | bytes 110600 | tf_op jit(solution)/shard_map/ppermute | solution.py:282
  46.4 6.6 %collective-permute-start.16 = (f32[72,128]{1,0:T(8,128)S(1)}, f32[72,128]{1,0:T(8,128)S(1)}, u32[]{:S(2)}, u32[]{:S(2)}) collective-permute-start(f32[72,128]{1,0:T(8,128)S(1)} %add_add_fusion.3), channel_id=1, source_target_pairs={{168,0},{160,8},{184,16},{176,24},{136,32},{128,40},{152,48},{144,... | collective-permute-start | bytes 110600 | tf_op jit(solution)/shard_map/ppermute | solution.py:282
  49.9 3.8 %collective-permute-start.15 = (f32[72,128]{1,0:T(8,128)S(1)}, f32[72,128]{1,0:T(8,128)S(1)}, u32[]{:S(2)}, u32[]{:S(2)}) collective-permute-start(f32[72,128]{1,0:T(8,128)S(1)} %add_add_fusion.3), channel_id=1, source_target_pairs={{64,0},{72,8},{80,16},{88,24},{224,32},{232,40},{240,48},{248,56},... | collective-permute-start | bytes 110600 | tf_op jit(solution)/shard_map/ppermute | solution.py:282
  50.5 5.3 %collective-permute-start.14 = (f32[72,128]{1,0:T(8,128)S(1)}, f32[72,128]{1,0:T(8,128)S(1)}, u32[]{:S(2)}, u32[]{:S(2)}) collective-permute-start(f32[72,128]{1,0:T(8,128)S(1)} %add_add_fusion.3), channel_id=1, source_target_pairs={{232,0},{224,8},{248,16},{240,24},{72,32},{64,40},{88,48},{80,56},... | collective-permute-start | bytes 110600 | tf_op jit(solution)/shard_map/ppermute | solution.py:282
  53.0 15.7 %collective-permute-start.20 = (f32[512,128]{1,0:T(8,128)S(1)}, f32[512,128]{1,0:T(8,128)S(1)}, u32[]{:S(2)}, u32[]{:S(2)}) collective-permute-start(f32[512,128]{1,0:T(8,128)S(1)} %get-tuple-element.38.refs_1_), channel_id=1, source_target_pairs={{7,0},{0,1},{1,2},{2,3},{3,4},{4,5},{5,6},{6,7},{15,8},{8,9},{9,10... | collective-permute-start | bytes 786440 | tf_op jit(solution)/shard_map/ppermute | solution.py:327
  55.8 9.7 %collective-permute-start.17 = (f32[72,128]{1,0:T(8,128)S(1)}, f32[72,128]{1,0:T(8,128)S(1)}, u32[]{:S(2)}, u32[]{:S(2)}) collective-permute-start(f32[72,128]{1,0:T(8,128)S(1)} %add_add_fusion.2.mine_ref), channel_id=1, source_target_pairs={{31,0},{24,1},{25,2},{26,3},{27,4},{28,5},{29,6},{30,7},{23,8},{16... | collective-permute-start | bytes 110600 | tf_op jit(solution)/shard_map/ppermute | solution.py:337
  55.8 10.0 %collective-permute-start.19 = (f32[72,128]{1,0:T(8,128)S(1)}, f32[72,128]{1,0:T(8,128)S(1)}, u32[]{:S(2)}, u32[]{:S(2)}) collective-permute-start(f32[72,128]{1,0:T(8,128)S(1)} %add_add_fusion.2.mine_ref), channel_id=1, source_target_pairs={{8,0},{0,8},{24,16},{16,24},{40,32},{32,40},{56,48},{48,56},{72,64... | collective-permute-start | bytes 110600 | tf_op jit(solution)/shard_map/ppermute | solution.py:282
  65.4 3.3 %collective-permute-start.18 = (f32[72,128]{1,0:T(8,128)S(1)}, f32[72,128]{1,0:T(8,128)S(1)}, u32[]{:S(2)}, u32[]{:S(2)}) collective-permute-start(f32[72,128]{1,0:T(8,128)S(1)} %collective-permute-done.17.mine_ref), channel_id=1, source_target_pairs={{8,0},{0,8},{24,16},{16,24},{40,32},{32,40},{56,48},{48,56},{72,64... | collective-permute-start | bytes 110600 | tf_op jit(solution)/shard_map/ppermute | solution.py:282
  71.5 1.4 %collective-permute-start.21 = (f32[72,128]{1,0:T(8,128)S(1)}, f32[72,128]{1,0:T(8,128)S(1)}, u32[]{:S(2)}, u32[]{:S(2)}) collective-permute-start(f32[72,128]{1,0:T(8,128)S(1)} %get-tuple-element.42), channel_id=1, source_target_pairs={{8,0},{0,8},{24,16},{16,24},{40,32},{32,40},{56,48},{48,56},{72,64... | collective-permute-start | bytes 110600 | tf_op jit(solution)/shard_map/ppermute | solution.py:282
  72.9 3.8 %collective-permute-start.24 = (f32[72,128]{1,0:T(8,128)S(1)}, f32[72,128]{1,0:T(8,128)S(1)}, u32[]{:S(2)}, u32[]{:S(2)}) collective-permute-start(f32[72,128]{1,0:T(8,128)S(1)} %add.73), channel_id=1, source_target_pairs={{48,0},{56,8},{32,16},{40,24},{16,32},{24,40},{0,48},{8,56},{112,6... | collective-permute-start | bytes 110600 | tf_op jit(solution)/shard_map/ppermute | solution.py:282
  72.9 3.9 %collective-permute-start.23 = (f32[72,128]{1,0:T(8,128)S(1)}, f32[72,128]{1,0:T(8,128)S(1)}, u32[]{:S(2)}, u32[]{:S(2)}) collective-permute-start(f32[72,128]{1,0:T(8,128)S(1)} %add.73), channel_id=1, source_target_pairs={{24,0},{16,8},{8,16},{0,24},{56,32},{48,40},{40,48},{32,56},{88,64... | collective-permute-start | bytes 110600 | tf_op jit(solution)/shard_map/ppermute | solution.py:282
  74.7 3.4 %collective-permute-start.22 = (f32[72,128]{1,0:T(8,128)S(1)}, f32[72,128]{1,0:T(8,128)S(1)}, u32[]{:S(2)}, u32[]{:S(2)}) collective-permute-start(f32[72,128]{1,0:T(8,128)S(1)} %add.73), channel_id=1, source_target_pairs={{40,0},{32,8},{56,16},{48,24},{8,32},{0,40},{24,48},{16,56},{104,6... | collective-permute-start | bytes 110600 | tf_op jit(solution)/shard_map/ppermute | solution.py:282
  78.1 6.6 %collective-permute-start.27 = (f32[72,128]{1,0:T(8,128)S(1)}, f32[72,128]{1,0:T(8,128)S(1)}, u32[]{:S(2)}, u32[]{:S(2)}) collective-permute-start(f32[72,128]{1,0:T(8,128)S(1)} %add_add_fusion.1), channel_id=1, source_target_pairs={{168,0},{160,8},{184,16},{176,24},{136,32},{128,40},{152,48},{144,... | collective-permute-start | bytes 110600 | tf_op jit(solution)/shard_map/ppermute | solution.py:282
  80.2 4.5 %collective-permute-start.26 = (f32[72,128]{1,0:T(8,128)S(1)}, f32[72,128]{1,0:T(8,128)S(1)}, u32[]{:S(2)}, u32[]{:S(2)}) collective-permute-start(f32[72,128]{1,0:T(8,128)S(1)} %add_add_fusion.1), channel_id=1, source_target_pairs={{64,0},{72,8},{80,16},{88,24},{224,32},{232,40},{240,48},{248,56},... | collective-permute-start | bytes 110600 | tf_op jit(solution)/shard_map/ppermute | solution.py:282
  82.4 4.8 %collective-permute-start.25 = (f32[72,128]{1,0:T(8,128)S(1)}, f32[72,128]{1,0:T(8,128)S(1)}, u32[]{:S(2)}, u32[]{:S(2)}) collective-permute-start(f32[72,128]{1,0:T(8,128)S(1)} %add_add_fusion.1), channel_id=1, source_target_pairs={{232,0},{224,8},{248,16},{240,24},{72,32},{64,40},{88,48},{80,56},... | collective-permute-start | bytes 110600 | tf_op jit(solution)/shard_map/ppermute | solution.py:282
  83.4 15.8 %collective-permute-start.31 = (f32[512,128]{1,0:T(8,128)S(1)}, f32[512,128]{1,0:T(8,128)S(1)}, u32[]{:S(2)}, u32[]{:S(2)}) collective-permute-start(f32[512,128]{1,0:T(8,128)S(1)} %get-tuple-element.46.refs_1_), channel_id=1, source_target_pairs={{7,0},{0,1},{1,2},{2,3},{3,4},{4,5},{5,6},{6,7},{15,8},{8,9},{9,10... | collective-permute-start | bytes 786440 | tf_op jit(solution)/shard_map/ppermute | solution.py:327
  87.2 8.7 %collective-permute-start.28 = (f32[72,128]{1,0:T(8,128)S(1)}, f32[72,128]{1,0:T(8,128)S(1)}, u32[]{:S(2)}, u32[]{:S(2)}) collective-permute-start(f32[72,128]{1,0:T(8,128)S(1)} %add_add_fusion.mine_ref), channel_id=1, source_target_pairs={{31,0},{24,1},{25,2},{26,3},{27,4},{28,5},{29,6},{30,7},{23,8},{16... | collective-permute-start | bytes 110600 | tf_op jit(solution)/shard_map/ppermute | solution.py:337
  87.5 8.9 %collective-permute-start.30 = (f32[72,128]{1,0:T(8,128)S(1)}, f32[72,128]{1,0:T(8,128)S(1)}, u32[]{:S(2)}, u32[]{:S(2)}) collective-permute-start(f32[72,128]{1,0:T(8,128)S(1)} %add_add_fusion.mine_ref), channel_id=1, source_target_pairs={{8,0},{0,8},{24,16},{16,24},{40,32},{32,40},{56,48},{48,56},{72,64... | collective-permute-start | bytes 110600 | tf_op jit(solution)/shard_map/ppermute | solution.py:282
  95.8 3.4 %collective-permute-start.29 = (f32[72,128]{1,0:T(8,128)S(1)}, f32[72,128]{1,0:T(8,128)S(1)}, u32[]{:S(2)}, u32[]{:S(2)}) collective-permute-start(f32[72,128]{1,0:T(8,128)S(1)} %collective-permute-done.28.mine_ref), channel_id=1, source_target_pairs={{8,0},{0,8},{24,16},{16,24},{40,32},{32,40},{56,48},{48,56},{72,64... | collective-permute-start | bytes 110600 | tf_op jit(solution)/shard_map/ppermute | solution.py:282

commit v11 on v10

--- a/solution.py
+++ b/solution.py
@@ -288,32 +288,30 @@
 
 def owner(chip):
     def source(z, y, c):
-        other_z, other_y = chip(z, y)
-        return other_z, other_y, (c + z + y + other_z + other_y) % 2
+        half = (c + z + y) % 2
+        side = 1 if (z + half) % 2 else -1
+        other_z, other_y = chip(z, y, side)
+        return other_z, other_y, (half + other_z + other_y) % 2
 
     return source
-
-
-def side(z):
-    return 1 if z % 2 else -1
 
 
 def summed_halves(mine, other, y_last):
     incoming = from_row(other, mate)
     x = mine + incoming
-    next_z = from_row(x, owner(lambda z, y: (z ^ 1, y)))
+    next_z = from_row(x, owner(lambda z, y, side: (z - side, y)))
     if y_last:
         x = x + next_z
     else:
-        next_y = from_row(x, owner(lambda z, y: (z, 1 - y)))
-        next_zy = from_row(x, owner(lambda z, y: (z ^ 1, 1 - y)))
+        next_y = from_row(x, owner(lambda z, y, side: (z, 1 - y)))
+        next_zy = from_row(x, owner(lambda z, y, side: (z - side, 1 - y)))
         x = ((x + next_z) + next_y) + next_zy
-    by_one = from_row(x, owner(lambda z, y: (z + side(z), y)))
-    by_two = from_row(x, owner(lambda z, y: (z - 2 * side(z), y)))
-    by_three = from_row(x, owner(lambda z, y: (z + 3 * side(z), y)))
+    by_one = from_row(x, owner(lambda z, y, side: (z + side, y)))
+    by_two = from_row(x, owner(lambda z, y, side: (z - 2 * side, y)))
+    by_three = from_row(x, owner(lambda z, y, side: (z + 3 * side, y)))
     x = ((x + by_one) + by_two) + by_three
     if y_last:
-        x = x + from_row(x, owner(lambda z, y: (z, 1 - y)))
+        x = x + from_row(x, owner(lambda z, y, side: (z, 1 - y)))
     return x
 
 

time: 103 us -> 103 us (level)
    ppermute x26, starting transfers between devices: 34.2 us -> 31.1 us  [from_row(): return lax.ppermute(x, 'row', route)]
    ppermute x3, starting transfers between devices: 1.8 us -> 3.94 us  [hopped_over(): return lax.ppermute(half, ('row', 'pair'), route)]
    ppermute x26, waiting for transfers between devices: 21.6 us -> 23.1 us  [from_row(): return lax.ppermute(x, 'row', route)]
  transfers between devices with their start and end apart: 32 -> 32, of which waited for: 19 -> 20; matrix products, arithmetic and copies ran while one was open for 0% -> 0% of each run, Pallas kernels for 9% -> 9%
where the time goes in v11:
time: 103 us
  waiting for transfers between devices  43.9 us (43%)
  starting transfers between devices  38.8 us (38%)
  Pallas kernels  19.3 us (19%)
    ppermute x26, starting transfers between devices, from_row(): return lax.ppermute(x, 'row', route)  31.1 us
    ppermute x26, waiting for transfers between devices, from_row(): return lax.ppermute(x, 'row', route)  23.1 us
    ppermute x3, waiting for transfers between devices, hopped_over(): return lax.ppermute(half, ('row', 'pair'), route)  20.8 us
    pallas_call x11, Pallas kernels, vmem_call(): pl.pallas_call(kernel, out_shape=shapes, in_specs=specs, scratch_shapes=s...  18 us
    ppermute x3, starting transfers between devices, hopped_over(): return lax.ppermute(half, ('row', 'pair'), route)  3.94 us
    ppermute x3, starting transfers between devices, shifted(): return lax.ppermute(block, 'pair', route)  3.81 us
  transfers between devices with their start and end apart: 32, of which 20 were waited for; matrix products, arithmetic and copies ran while one was open for 0% of the time, Pallas kernels for 9%

profile of v11, /device:TPU:1, one launch (start us, length us, event | category | flops | bytes accessed | tf_op | source)
XLA Modules:
  0.0 102.5 jit_solution(14027777988561643198)
XLA Ops:
  0.0 1.3 %load.1 = (f32[512,256]{1,0:T(8,128)S(1)}, f32[72,128]{1,0:T(8,128)S(1)}, f32[72,128]{1,0:T(8,128)S(1)}) custom-call(s32[1]{0:T(128)} %bitcast.core_ref, f32[512,256]{1,0:T(8,128)} %panel_ref.1), custom_call_target="tpu_custom_call" | custom-call | tf_op jit(solution)/shard_map/load/pallas_call | solution.py:231
  1.4 3.8 %collective-permute-start.9 = (f32[512,256]{1,0:T(8,128)S(1)}, f32[512,256]{1,0:T(8,128)S(1)}, u32[]{:S(2)}, u32[]{:S(2)}) collective-permute-start(f32[512,256]{1,0:T(8,128)S(1)} %get-tuple-element.32.refs_0_), channel_id=1, source_target_pairs={{7,0},{0,1},{1,2},{2,3},{3,4},{4,5},{5,6},{6,7},{15,8},{8,9},{9,10... | collective-permute-start | bytes 1572872 | tf_op jit(solution)/shard_map/ppermute | solution.py:325
  7.0 5.8 %collective-permute-start.1 = (f32[72,128]{1,0:T(8,128)S(1)}, f32[72,128]{1,0:T(8,128)S(1)}, u32[]{:S(2)}, u32[]{:S(2)}) collective-permute-start(f32[72,128]{1,0:T(8,128)S(1)} %add.60), channel_id=1, source_target_pairs={{40,0},{224,8},{248,16},{48,24},{72,32},{0,40},{24,48},{80,56},{10... | collective-permute-start | bytes 110600 | tf_op jit(solution)/shard_map/ppermute | solution.py:282
  12.8 1.9 %collective-permute-done.1 = f32[72,128]{1,0:T(8,128)S(1)} collective-permute-done((f32[72,128]{1,0:T(8,128)S(1)}, f32[72,128]{1,0:T(8,128)S(1)}, u32[]{:S(2)}, u32[]{:S(2)}) %collective-permute-start.1) | collective-permute-done | bytes 36896 | tf_op jit(solution)/shard_map/ppermute | solution.py:282
  14.7 1.4 %collective-permute-start.4 = (f32[72,128]{1,0:T(8,128)S(1)}, f32[72,128]{1,0:T(8,128)S(1)}, u32[]{:S(2)}, u32[]{:S(2)}) collective-permute-start(f32[72,128]{1,0:T(8,128)S(1)} %add.61), channel_id=1, source_target_pairs={{168,0},{96,8},{120,16},{176,24},{200,32},{128,40},{152,48},{208,5... | collective-permute-start | bytes 110600 | tf_op jit(solution)/shard_map/ppermute | solution.py:282
  16.2 2.1 %collective-permute-start.3 = (f32[72,128]{1,0:T(8,128)S(1)}, f32[72,128]{1,0:T(8,128)S(1)}, u32[]{:S(2)}, u32[]{:S(2)}) collective-permute-start(f32[72,128]{1,0:T(8,128)S(1)} %add.61), channel_id=1, source_target_pairs={{64,0},{200,8},{208,16},{88,24},{96,32},{232,40},{240,48},{120,56}... | collective-permute-start | bytes 110600 | tf_op jit(solution)/shard_map/ppermute | solution.py:282
  18.3 2.6 %collective-permute-start.2 = (f32[72,128]{1,0:T(8,128)S(1)}, f32[72,128]{1,0:T(8,128)S(1)}, u32[]{:S(2)}, u32[]{:S(2)}) collective-permute-start(f32[72,128]{1,0:T(8,128)S(1)} %add.61), channel_id=1, source_target_pairs={{232,0},{32,8},{56,16},{240,24},{8,32},{64,40},{88,48},{16,56},{40... | collective-permute-start | bytes 110600 | tf_op jit(solution)/shard_map/ppermute | solution.py:282
  21.1 1.8 %collective-permute-done.2 = f32[72,128]{1,0:T(8,128)S(1)} collective-permute-done((f32[72,128]{1,0:T(8,128)S(1)}, f32[72,128]{1,0:T(8,128)S(1)}, u32[]{:S(2)}, u32[]{:S(2)}) %collective-permute-start.2) | collective-permute-done | bytes 36896 | tf_op jit(solution)/shard_map/ppermute | solution.py:282
  23.7 2.6 %collective-permute-done.5 = f32[72,128]{1,0:T(8,128)S(1)} collective-permute-done((f32[72,128]{1,0:T(8,128)S(1)}, f32[72,128]{1,0:T(8,128)S(1)}, u32[]{:S(2)}, u32[]{:S(2)}) %collective-permute-start.5) | collective-permute-done | bytes 36896 | tf_op jit(solution)/shard_map/ppermute | solution.py:282
  26.3 2.1 %collective-permute-start.6 = (f32[72,128]{1,0:T(8,128)S(1)}, f32[72,128]{1,0:T(8,128)S(1)}, u32[]{:S(2)}, u32[]{:S(2)}) collective-permute-start(f32[72,128]{1,0:T(8,128)S(1)} %add.65.mine_ref), channel_id=1, source_target_pairs={{31,0},{24,1},{25,2},{26,3},{27,4},{28,5},{29,6},{30,7},{23,8},{16... | collective-permute-start | bytes 110600 | tf_op jit(solution)/shard_map/ppermute | solution.py:335
  28.6 4.4 %collective-permute-done.6.mine_ref = f32[72,128]{1,0:T(8,128)S(1)} collective-permute-done((f32[72,128]{1,0:T(8,128)S(1)}, f32[72,128]{1,0:T(8,128)S(1)}, u32[]{:S(2)}, u32[]{:S(2)}) %collective-permute-start.6) | collective-permute-done | bytes 36896 | tf_op jit(solution)/shard_map/ppermute | solution.py:335
  33.0 1.8 %shard_map.17 = (f32[128,128]{1,0:T(8,128)S(1)}, f32[128,128]{1,0:T(8,128)S(1)}, f32[128,128]{1,0:T(8,128)S(1)}) custom-call(s32[1]{0:T(128)} %bitcast.core_ref, f32[72,128]{1,0:T(8,128)S(1)} %add.65.mine_ref, f32[72,128]{1,0:T(8,128)S(1)} %collective-permute-done.8.other_ref), custom_call_target="tpu_custom_call" | custom-call | tf_op jit(solution)/shard_map/pallas_call | solution.py:219
  35.9 2.8 %shard_map.19 = (f32[512,128]{1,0:T(8,128)S(1)}, f32[128,128]{1,0:T(8,128)S(1)}, f32[128,128]{1,0:T(8,128)S(1)}, f32[72,128]{1,0:T(8,128)S(1)}, f32[72,128]{1,0:T(8,128)S(1)}) custom-call(s32[1]{0:T(128)} %bitcast.core_ref, f32[72,128]{1,0:T(8,128)S(1)} %collective-permute-done.6.mine_ref, f32[72,128]{1,0:T(8,128)S(1)} %collective-permute-done.7.other_ref, ...), custom_call_target="tpu_custom_call" | custom-call | tf_op jit(solution)/shard_map/pallas_call | solution.py:219
  40.1 1.9 %collective-permute-start.13 = (f32[72,128]{1,0:T(8,128)S(1)}, f32[72,128]{1,0:T(8,128)S(1)}, u32[]{:S(2)}, u32[]{:S(2)}) collective-permute-start(f32[72,128]{1,0:T(8,128)S(1)} %add.66), channel_id=1, source_target_pairs={{48,0},{248,8},{224,16},{40,24},{80,32},{24,40},{0,48},{72,56},{11... | collective-permute-start | bytes 110600 | tf_op jit(solution)/shard_map/ppermute | solution.py:282
  42.0 2.4 %collective-permute-start.12 = (f32[72,128]{1,0:T(8,128)S(1)}, f32[72,128]{1,0:T(8,128)S(1)}, u32[]{:S(2)}, u32[]{:S(2)}) collective-permute-start(f32[72,128]{1,0:T(8,128)S(1)} %add.66), channel_id=1, source_target_pairs={{24,0},{16,8},{8,16},{0,24},{56,32},{48,40},{40,48},{32,56},{88,64... | collective-permute-start | bytes 110600 | tf_op jit(solution)/shard_map/ppermute | solution.py:282
  46.0 3.0 %collective-permute-done.11 = f32[72,128]{1,0:T(8,128)S(1)} collective-permute-done((f32[72,128]{1,0:T(8,128)S(1)}, f32[72,128]{1,0:T(8,128)S(1)}, u32[]{:S(2)}, u32[]{:S(2)}) %collective-permute-start.11) | collective-permute-done | bytes 36896 | tf_op jit(solution)/shard_map/ppermute | solution.py:282
  49.0 1.5 %collective-permute-start.16 = (f32[72,128]{1,0:T(8,128)S(1)}, f32[72,128]{1,0:T(8,128)S(1)}, u32[]{:S(2)}, u32[]{:S(2)}) collective-permute-start(f32[72,128]{1,0:T(8,128)S(1)} %add_add_fusion.3), channel_id=1, source_target_pairs={{168,0},{96,8},{120,16},{176,24},{200,32},{128,40},{152,48},{208,5... | collective-permute-start | bytes 110600 | tf_op jit(solution)/shard_map/ppermute | solution.py:282
  50.4 2.4 %collective-permute-start.14 = (f32[72,128]{1,0:T(8,128)S(1)}, f32[72,128]{1,0:T(8,128)S(1)}, u32[]{:S(2)}, u32[]{:S(2)}) collective-permute-start(f32[72,128]{1,0:T(8,128)S(1)} %add_add_fusion.3), channel_id=1, source_target_pairs={{232,0},{32,8},{56,16},{240,24},{8,32},{64,40},{88,48},{16,56},{40... | collective-permute-start | bytes 110600 | tf_op jit(solution)/shard_map/ppermute | solution.py:282
  52.8 1.4 %collective-permute-done.16 = f32[72,128]{1,0:T(8,128)S(1)} collective-permute-done((f32[72,128]{1,0:T(8,128)S(1)}, f32[72,128]{1,0:T(8,128)S(1)}, u32[]{:S(2)}, u32[]{:S(2)}) %collective-permute-start.16) | collective-permute-done | bytes 36896 | tf_op jit(solution)/shard_map/ppermute | solution.py:282
  54.3 1.1 %collective-permute-done.15 = f32[72,128]{1,0:T(8,128)S(1)} collective-permute-done((f32[72,128]{1,0:T(8,128)S(1)}, f32[72,128]{1,0:T(8,128)S(1)}, u32[]{:S(2)}, u32[]{:S(2)}) %collective-permute-start.15) | collective-permute-done | bytes 36896 | tf_op jit(solution)/shard_map/ppermute | solution.py:282
  55.4 1.5 %collective-permute-start.17 = (f32[72,128]{1,0:T(8,128)S(1)}, f32[72,128]{1,0:T(8,128)S(1)}, u32[]{:S(2)}, u32[]{:S(2)}) collective-permute-start(f32[72,128]{1,0:T(8,128)S(1)} %add_add_fusion.2.mine_ref), channel_id=1, source_target_pairs={{31,0},{24,1},{25,2},{26,3},{27,4},{28,5},{29,6},{30,7},{23,8},{16... | collective-permute-start | bytes 110600 | tf_op jit(solution)/shard_map/ppermute | solution.py:335
  56.9 8.1 %collective-permute-done.17.mine_ref = f32[72,128]{1,0:T(8,128)S(1)} collective-permute-done((f32[72,128]{1,0:T(8,128)S(1)}, f32[72,128]{1,0:T(8,128)S(1)}, u32[]{:S(2)}, u32[]{:S(2)}) %collective-permute-start.17) | collective-permute-done | bytes 36896 | tf_op jit(solution)/shard_map/ppermute | solution.py:335
  65.4 1.8 %shard_map.20 = (f32[128,128]{1,0:T(8,128)S(1)}, f32[128,128]{1,0:T(8,128)S(1)}, f32[128,128]{1,0:T(8,128)S(1)}) custom-call(s32[1]{0:T(128)} %bitcast.core_ref, f32[72,128]{1,0:T(8,128)S(1)} %add_add_fusion.2.mine_ref, f32[72,128]{1,0:T(8,128)S(1)} %collective-permute-done.19.other_ref), custom_call_target="tpu_custom_call" | custom-call | tf_op jit(solution)/shard_map/pallas_call | solution.py:219
  68.3 2.8 %shard_map.23 = (f32[512,128]{1,0:T(8,128)S(1)}, f32[128,128]{1,0:T(8,128)S(1)}, f32[128,128]{1,0:T(8,128)S(1)}, f32[72,128]{1,0:T(8,128)S(1)}, f32[72,128]{1,0:T(8,128)S(1)}) custom-call(s32[1]{0:T(128)} %bitcast.core_ref, f32[72,128]{1,0:T(8,128)S(1)} %collective-permute-done.17.mine_ref, f32[72,128]{1,0:T(8,128)S(1)} %collective-permute-done.18.other_ref, ...), custom_call_target="tpu_custom_call" | custom-call | tf_op jit(solution)/shard_map/pallas_call | solution.py:219
  72.5 1.5 %collective-permute-start.24 = (f32[72,128]{1,0:T(8,128)S(1)}, f32[72,128]{1,0:T(8,128)S(1)}, u32[]{:S(2)}, u32[]{:S(2)}) collective-permute-start(f32[72,128]{1,0:T(8,128)S(1)} %add.73), channel_id=1, source_target_pairs={{48,0},{248,8},{224,16},{40,24},{80,32},{24,40},{0,48},{72,56},{11... | collective-permute-start | bytes 110600 | tf_op jit(solution)/shard_map/ppermute | solution.py:282
  74.0 2.4 %collective-permute-start.23 = (f32[72,128]{1,0:T(8,128)S(1)}, f32[72,128]{1,0:T(8,128)S(1)}, u32[]{:S(2)}, u32[]{:S(2)}) collective-permute-start(f32[72,128]{1,0:T(8,128)S(1)} %add.73), channel_id=1, source_target_pairs={{24,0},{16,8},{8,16},{0,24},{56,32},{48,40},{40,48},{32,56},{88,64... | collective-permute-start | bytes 110600 | tf_op jit(solution)/shard_map/ppermute | solution.py:282
  78.0 3.0 %collective-permute-done.22 = f32[72,128]{1,0:T(8,128)S(1)} collective-permute-done((f32[72,128]{1,0:T(8,128)S(1)}, f32[72,128]{1,0:T(8,128)S(1)}, u32[]{:S(2)}, u32[]{:S(2)}) %collective-permute-start.22) | collective-permute-done | bytes 36896 | tf_op jit(solution)/shard_map/ppermute | solution.py:282
  81.1 3.4 %collective-permute-start.25 = (f32[72,128]{1,0:T(8,128)S(1)}, f32[72,128]{1,0:T(8,128)S(1)}, u32[]{:S(2)}, u32[]{:S(2)}) collective-permute-start(f32[72,128]{1,0:T(8,128)S(1)} %add_add_fusion.1), channel_id=1, source_target_pairs={{232,0},{32,8},{56,16},{240,24},{8,32},{64,40},{88,48},{16,56},{40... | collective-permute-start | bytes 110600 | tf_op jit(solution)/shard_map/ppermute | solution.py:282
  84.5 1.8 %collective-permute-done.27 = f32[72,128]{1,0:T(8,128)S(1)} collective-permute-done((f32[72,128]{1,0:T(8,128)S(1)}, f32[72,128]{1,0:T(8,128)S(1)}, u32[]{:S(2)}, u32[]{:S(2)}) %collective-permute-start.27) | collective-permute-done | bytes 36896 | tf_op jit(solution)/shard_map/ppermute | solution.py:282
  87.5 8.3 %collective-permute-done.28.mine_ref = f32[72,128]{1,0:T(8,128)S(1)} collective-permute-done((f32[72,128]{1,0:T(8,128)S(1)}, f32[72,128]{1,0:T(8,128)S(1)}, u32[]{:S(2)}, u32[]{:S(2)}) %collective-permute-start.28) | collective-permute-done | bytes 36896 | tf_op jit(solution)/shard_map/ppermute | solution.py:335
  96.2 1.8 %shard_map.24 = (f32[128,128]{1,0:T(8,128)S(1)}, f32[128,128]{1,0:T(8,128)S(1)}, f32[128,128]{1,0:T(8,128)S(1)}) custom-call(s32[1]{0:T(128)} %bitcast.core_ref, f32[72,128]{1,0:T(8,128)S(1)} %add_add_fusion.mine_ref, f32[72,128]{1,0:T(8,128)S(1)} %collective-permute-done.30.other_ref), custom_call_target="tpu_custom_call" | custom-call | tf_op jit(solution)/shard_map/pallas_call | solution.py:219
  99.1 3.3 %shard_map.27 = f32[512,256]{1,0:T(8,128)} custom-call(s32[1]{0:T(128)} %bitcast.core_ref, f32[72,128]{1,0:T(8,128)S(1)} %collective-permute-done.28.mine_ref, f32[72,128]{1,0:T(8,128)S(1)} %collective-permute-done.29.other_ref, f32[512,128]{1,0:T(8,128)S(1)} %shard_map.25.own_ref, f32[512,128]{1,0:T(8,128)S(1)} %shard_map.26.refs_0_, ...), custom_call_target="tpu_custom_call" | custom-call | tf_op jit(solution)/shard_map/pallas_call | solution.py:219
  (54 shorter events, 14.4 us)
Async XLA Ops:
  1.4 34.5 %collective-permute-start.9 = (f32[512,256]{1,0:T(8,128)S(1)}, f32[512,256]{1,0:T(8,128)S(1)}, u32[]{:S(2)}, u32[]{:S(2)}) collective-permute-start(f32[512,256]{1,0:T(8,128)S(1)} %get-tuple-element.32.refs_0_), channel_id=1, source_target_pairs={{7,0},{0,1},{1,2},{2,3},{3,4},{4,5},{5,6},{6,7},{15,8},{8,9},{9,10... | collective-permute-start | bytes 1572872 | tf_op jit(solution)/shard_map/ppermute | solution.py:325
  5.2 1.8 %collective-permute-start = (f32[72,128]{1,0:T(8,128)S(1)}, f32[72,128]{1,0:T(8,128)S(1)}, u32[]{:S(2)}, u32[]{:S(2)}) collective-permute-start(f32[72,128]{1,0:T(8,128)S(1)} %get-tuple-element.28), channel_id=1, source_target_pairs={{8,0},{0,8},{24,16},{16,24},{40,32},{32,40},{56,48},{48,56},{72,64... | collective-permute-start | bytes 110600 | tf_op jit(solution)/shard_map/ppermute | solution.py:282
  7.0 7.7 %collective-permute-start.1 = (f32[72,128]{1,0:T(8,128)S(1)}, f32[72,128]{1,0:T(8,128)S(1)}, u32[]{:S(2)}, u32[]{:S(2)}) collective-permute-start(f32[72,128]{1,0:T(8,128)S(1)} %add.60), channel_id=1, source_target_pairs={{40,0},{224,8},{248,16},{48,24},{72,32},{0,40},{24,48},{80,56},{10... | collective-permute-start | bytes 110600 | tf_op jit(solution)/shard_map/ppermute | solution.py:282
  14.7 6.1 %collective-permute-start.4 = (f32[72,128]{1,0:T(8,128)S(1)}, f32[72,128]{1,0:T(8,128)S(1)}, u32[]{:S(2)}, u32[]{:S(2)}) collective-permute-start(f32[72,128]{1,0:T(8,128)S(1)} %add.61), channel_id=1, source_target_pairs={{168,0},{96,8},{120,16},{176,24},{200,32},{128,40},{152,48},{208,5... | collective-permute-start | bytes 110600 | tf_op jit(solution)/shard_map/ppermute | solution.py:282
  16.2 4.9 %collective-permute-start.3 = (f32[72,128]{1,0:T(8,128)S(1)}, f32[72,128]{1,0:T(8,128)S(1)}, u32[]{:S(2)}, u32[]{:S(2)}) collective-permute-start(f32[72,128]{1,0:T(8,128)S(1)} %add.61), channel_id=1, source_target_pairs={{64,0},{200,8},{208,16},{88,24},{96,32},{232,40},{240,48},{120,56}... | collective-permute-start | bytes 110600 | tf_op jit(solution)/shard_map/ppermute | solution.py:282
  18.3 4.6 %collective-permute-start.2 = (f32[72,128]{1,0:T(8,128)S(1)}, f32[72,128]{1,0:T(8,128)S(1)}, u32[]{:S(2)}, u32[]{:S(2)}) collective-permute-start(f32[72,128]{1,0:T(8,128)S(1)} %add.61), channel_id=1, source_target_pairs={{232,0},{32,8},{56,16},{240,24},{8,32},{64,40},{88,48},{16,56},{40... | collective-permute-start | bytes 110600 | tf_op jit(solution)/shard_map/ppermute | solution.py:282
  22.9 3.5 %collective-permute-start.5 = (f32[72,128]{1,0:T(8,128)S(1)}, f32[72,128]{1,0:T(8,128)S(1)}, u32[]{:S(2)}, u32[]{:S(2)}) collective-permute-start(f32[72,128]{1,0:T(8,128)S(1)} %add_add_fusion.4), channel_id=1, source_target_pairs={{24,0},{16,8},{8,16},{0,24},{56,32},{48,40},{40,48},{32,56},{88,64... | collective-permute-start | bytes 110600 | tf_op jit(solution)/shard_map/ppermute | solution.py:282
  26.3 6.7 %collective-permute-start.6 = (f32[72,128]{1,0:T(8,128)S(1)}, f32[72,128]{1,0:T(8,128)S(1)}, u32[]{:S(2)}, u32[]{:S(2)}) collective-permute-start(f32[72,128]{1,0:T(8,128)S(1)} %add.65.mine_ref), channel_id=1, source_target_pairs={{31,0},{24,1},{25,2},{26,3},{27,4},{28,5},{29,6},{30,7},{23,8},{16... | collective-permute-start | bytes 110600 | tf_op jit(solution)/shard_map/ppermute | solution.py:335
  28.5 4.6 %collective-permute-start.8 = (f32[72,128]{1,0:T(8,128)S(1)}, f32[72,128]{1,0:T(8,128)S(1)}, u32[]{:S(2)}, u32[]{:S(2)}) collective-permute-start(f32[72,128]{1,0:T(8,128)S(1)} %add.65.mine_ref), channel_id=1, source_target_pairs={{8,0},{0,8},{24,16},{16,24},{40,32},{32,40},{56,48},{48,56},{72,64... | collective-permute-start | bytes 110600 | tf_op jit(solution)/shard_map/ppermute | solution.py:282
  33.0 2.8 %collective-permute-start.7 = (f32[72,128]{1,0:T(8,128)S(1)}, f32[72,128]{1,0:T(8,128)S(1)}, u32[]{:S(2)}, u32[]{:S(2)}) collective-permute-start(f32[72,128]{1,0:T(8,128)S(1)} %collective-permute-done.6.mine_ref), channel_id=1, source_target_pairs={{8,0},{0,8},{24,16},{16,24},{40,32},{32,40},{56,48},{48,56},{72,64... | collective-permute-start | bytes 110600 | tf_op jit(solution)/shard_map/ppermute | solution.py:282
  38.7 1.5 %collective-permute-start.10 = (f32[72,128]{1,0:T(8,128)S(1)}, f32[72,128]{1,0:T(8,128)S(1)}, u32[]{:S(2)}, u32[]{:S(2)}) collective-permute-start(f32[72,128]{1,0:T(8,128)S(1)} %get-tuple-element.34), channel_id=1, source_target_pairs={{8,0},{0,8},{24,16},{16,24},{40,32},{32,40},{56,48},{48,56},{72,64... | collective-permute-start | bytes 110600 | tf_op jit(solution)/shard_map/ppermute | solution.py:282
  40.1 4.9 %collective-permute-start.13 = (f32[72,128]{1,0:T(8,128)S(1)}, f32[72,128]{1,0:T(8,128)S(1)}, u32[]{:S(2)}, u32[]{:S(2)}) collective-permute-start(f32[72,128]{1,0:T(8,128)S(1)} %add.66), channel_id=1, source_target_pairs={{48,0},{248,8},{224,16},{40,24},{80,32},{24,40},{0,48},{72,56},{11... | collective-permute-start | bytes 110600 | tf_op jit(solution)/shard_map/ppermute | solution.py:282
  42.0 4.0 %collective-permute-start.12 = (f32[72,128]{1,0:T(8,128)S(1)}, f32[72,128]{1,0:T(8,128)S(1)}, u32[]{:S(2)}, u32[]{:S(2)}) collective-permute-start(f32[72,128]{1,0:T(8,128)S(1)} %add.66), channel_id=1, source_target_pairs={{24,0},{16,8},{8,16},{0,24},{56,32},{48,40},{40,48},{32,56},{88,64... | collective-permute-start | bytes 110600 | tf_op jit(solution)/shard_map/ppermute | solution.py:282
  44.4 4.6 %collective-permute-start.11 = (f32[72,128]{1,0:T(8,128)S(1)}, f32[72,128]{1,0:T(8,128)S(1)}, u32[]{:S(2)}, u32[]{:S(2)}) collective-permute-start(f32[72,128]{1,0:T(8,128)S(1)} %add.66), channel_id=1, source_target_pairs={{40,0},{224,8},{248,16},{48,24},{72,32},{0,40},{24,48},{80,56},{10... | collective-permute-start | bytes 110600 | tf_op jit(solution)/shard_map/ppermute | solution.py:282
  49.0 5.3 %collective-permute-start.16 = (f32[72,128]{1,0:T(8,128)S(1)}, f32[72,128]{1,0:T(8,128)S(1)}, u32[]{:S(2)}, u32[]{:S(2)}) collective-permute-start(f32[72,128]{1,0:T(8,128)S(1)} %add_add_fusion.3), channel_id=1, source_target_pairs={{168,0},{96,8},{120,16},{176,24},{200,32},{128,40},{152,48},{208,5... | collective-permute-start | bytes 110600 | tf_op jit(solution)/shard_map/ppermute | solution.py:282
  50.4 5.0 %collective-permute-start.15 = (f32[72,128]{1,0:T(8,128)S(1)}, f32[72,128]{1,0:T(8,128)S(1)}, u32[]{:S(2)}, u32[]{:S(2)}) collective-permute-start(f32[72,128]{1,0:T(8,128)S(1)} %add_add_fusion.3), channel_id=1, source_target_pairs={{64,0},{200,8},{208,16},{88,24},{96,32},{232,40},{240,48},{120,56}... | collective-permute-start | bytes 110600 | tf_op jit(solution)/shard_map/ppermute | solution.py:282
  50.4 5.0 %collective-permute-start.14 = (f32[72,128]{1,0:T(8,128)S(1)}, f32[72,128]{1,0:T(8,128)S(1)}, u32[]{:S(2)}, u32[]{:S(2)}) collective-permute-start(f32[72,128]{1,0:T(8,128)S(1)} %add_add_fusion.3), channel_id=1, source_target_pairs={{232,0},{32,8},{56,16},{240,24},{8,32},{64,40},{88,48},{16,56},{40... | collective-permute-start | bytes 110600 | tf_op jit(solution)/shard_map/ppermute | solution.py:282
  52.8 15.4 %collective-permute-start.20 = (f32[512,128]{1,0:T(8,128)S(1)}, f32[512,128]{1,0:T(8,128)S(1)}, u32[]{:S(2)}, u32[]{:S(2)}) collective-permute-start(f32[512,128]{1,0:T(8,128)S(1)} %get-tuple-element.38.refs_1_), channel_id=1, source_target_pairs={{7,0},{0,1},{1,2},{2,3},{3,4},{4,5},{5,6},{6,7},{15,8},{8,9},{9,10... | collective-permute-start | bytes 786440 | tf_op jit(solution)/shard_map/ppermute | solution.py:325
  55.4 9.6 %collective-permute-start.17 = (f32[72,128]{1,0:T(8,128)S(1)}, f32[72,128]{1,0:T(8,128)S(1)}, u32[]{:S(2)}, u32[]{:S(2)}) collective-permute-start(f32[72,128]{1,0:T(8,128)S(1)} %add_add_fusion.2.mine_ref), channel_id=1, source_target_pairs={{31,0},{24,1},{25,2},{26,3},{27,4},{28,5},{29,6},{30,7},{23,8},{16... | collective-permute-start | bytes 110600 | tf_op jit(solution)/shard_map/ppermute | solution.py:335
  56.9 8.5 %collective-permute-start.19 = (f32[72,128]{1,0:T(8,128)S(1)}, f32[72,128]{1,0:T(8,128)S(1)}, u32[]{:S(2)}, u32[]{:S(2)}) collective-permute-start(f32[72,128]{1,0:T(8,128)S(1)} %add_add_fusion.2.mine_ref), channel_id=1, source_target_pairs={{8,0},{0,8},{24,16},{16,24},{40,32},{32,40},{56,48},{48,56},{72,64... | collective-permute-start | bytes 110600 | tf_op jit(solution)/shard_map/ppermute | solution.py:282
  65.0 3.3 %collective-permute-start.18 = (f32[72,128]{1,0:T(8,128)S(1)}, f32[72,128]{1,0:T(8,128)S(1)}, u32[]{:S(2)}, u32[]{:S(2)}) collective-permute-start(f32[72,128]{1,0:T(8,128)S(1)} %collective-permute-done.17.mine_ref), channel_id=1, source_target_pairs={{8,0},{0,8},{24,16},{16,24},{40,32},{32,40},{56,48},{48,56},{72,64... | collective-permute-start | bytes 110600 | tf_op jit(solution)/shard_map/ppermute | solution.py:282
  71.1 1.4 %collective-permute-start.21 = (f32[72,128]{1,0:T(8,128)S(1)}, f32[72,128]{1,0:T(8,128)S(1)}, u32[]{:S(2)}, u32[]{:S(2)}) collective-permute-start(f32[72,128]{1,0:T(8,128)S(1)} %get-tuple-element.42), channel_id=1, source_target_pairs={{8,0},{0,8},{24,16},{16,24},{40,32},{32,40},{56,48},{48,56},{72,64... | collective-permute-start | bytes 110600 | tf_op jit(solution)/shard_map/ppermute | solution.py:282
  72.5 4.9 %collective-permute-start.24 = (f32[72,128]{1,0:T(8,128)S(1)}, f32[72,128]{1,0:T(8,128)S(1)}, u32[]{:S(2)}, u32[]{:S(2)}) collective-permute-start(f32[72,128]{1,0:T(8,128)S(1)} %add.73), channel_id=1, source_target_pairs={{48,0},{248,8},{224,16},{40,24},{80,32},{24,40},{0,48},{72,56},{11... | collective-permute-start | bytes 110600 | tf_op jit(solution)/shard_map/ppermute | solution.py:282
  74.0 4.0 %collective-permute-start.23 = (f32[72,128]{1,0:T(8,128)S(1)}, f32[72,128]{1,0:T(8,128)S(1)}, u32[]{:S(2)}, u32[]{:S(2)}) collective-permute-start(f32[72,128]{1,0:T(8,128)S(1)} %add.73), channel_id=1, source_target_pairs={{24,0},{16,8},{8,16},{0,24},{56,32},{48,40},{40,48},{32,56},{88,64... | collective-permute-start | bytes 110600 | tf_op jit(solution)/shard_map/ppermute | solution.py:282
  76.3 4.6 %collective-permute-start.22 = (f32[72,128]{1,0:T(8,128)S(1)}, f32[72,128]{1,0:T(8,128)S(1)}, u32[]{:S(2)}, u32[]{:S(2)}) collective-permute-start(f32[72,128]{1,0:T(8,128)S(1)} %add.73), channel_id=1, source_target_pairs={{40,0},{224,8},{248,16},{48,24},{72,32},{0,40},{24,48},{80,56},{10... | collective-permute-start | bytes 110600 | tf_op jit(solution)/shard_map/ppermute | solution.py:282
  80.9 5.4 %collective-permute-start.27 = (f32[72,128]{1,0:T(8,128)S(1)}, f32[72,128]{1,0:T(8,128)S(1)}, u32[]{:S(2)}, u32[]{:S(2)}) collective-permute-start(f32[72,128]{1,0:T(8,128)S(1)} %add_add_fusion.1), channel_id=1, source_target_pairs={{168,0},{96,8},{120,16},{176,24},{200,32},{128,40},{152,48},{208,5... | collective-permute-start | bytes 110600 | tf_op jit(solution)/shard_map/ppermute | solution.py:282
  81.0 5.3 %collective-permute-start.26 = (f32[72,128]{1,0:T(8,128)S(1)}, f32[72,128]{1,0:T(8,128)S(1)}, u32[]{:S(2)}, u32[]{:S(2)}) collective-permute-start(f32[72,128]{1,0:T(8,128)S(1)} %add_add_fusion.1), channel_id=1, source_target_pairs={{64,0},{200,8},{208,16},{88,24},{96,32},{232,40},{240,48},{120,56}... | collective-permute-start | bytes 110600 | tf_op jit(solution)/shard_map/ppermute | solution.py:282
  81.1 5.8 %collective-permute-start.25 = (f32[72,128]{1,0:T(8,128)S(1)}, f32[72,128]{1,0:T(8,128)S(1)}, u32[]{:S(2)}, u32[]{:S(2)}) collective-permute-start(f32[72,128]{1,0:T(8,128)S(1)} %add_add_fusion.1), channel_id=1, source_target_pairs={{232,0},{32,8},{56,16},{240,24},{8,32},{64,40},{88,48},{16,56},{40... | collective-permute-start | bytes 110600 | tf_op jit(solution)/shard_map/ppermute | solution.py:282
  84.5 14.5 %collective-permute-start.31 = (f32[512,128]{1,0:T(8,128)S(1)}, f32[512,128]{1,0:T(8,128)S(1)}, u32[]{:S(2)}, u32[]{:S(2)}) collective-permute-start(f32[512,128]{1,0:T(8,128)S(1)} %get-tuple-element.46.refs_1_), channel_id=1, source_target_pairs={{7,0},{0,1},{1,2},{2,3},{3,4},{4,5},{5,6},{6,7},{15,8},{8,9},{9,10... | collective-permute-start | bytes 786440 | tf_op jit(solution)/shard_map/ppermute | solution.py:325
  87.0 8.9 %collective-permute-start.28 = (f32[72,128]{1,0:T(8,128)S(1)}, f32[72,128]{1,0:T(8,128)S(1)}, u32[]{:S(2)}, u32[]{:S(2)}) collective-permute-start(f32[72,128]{1,0:T(8,128)S(1)} %add_add_fusion.mine_ref), channel_id=1, source_target_pairs={{31,0},{24,1},{25,2},{26,3},{27,4},{28,5},{29,6},{30,7},{23,8},{16... | collective-permute-start | bytes 110600 | tf_op jit(solution)/shard_map/ppermute | solution.py:335
  87.3 8.9 %collective-permute-start.30 = (f32[72,128]{1,0:T(8,128)S(1)}, f32[72,128]{1,0:T(8,128)S(1)}, u32[]{:S(2)}, u32[]{:S(2)}) collective-permute-start(f32[72,128]{1,0:T(8,128)S(1)} %add_add_fusion.mine_ref), channel_id=1, source_target_pairs={{8,0},{0,8},{24,16},{16,24},{40,32},{32,40},{56,48},{48,56},{72,64... | collective-permute-start | bytes 110600 | tf_op jit(solution)/shard_map/ppermute | solution.py:282
  95.8 3.2 %collective-permute-start.29 = (f32[72,128]{1,0:T(8,128)S(1)}, f32[72,128]{1,0:T(8,128)S(1)}, u32[]{:S(2)}, u32[]{:S(2)}) collective-permute-start(f32[72,128]{1,0:T(8,128)S(1)} %collective-permute-done.28.mine_ref), channel_id=1, source_target_pairs={{8,0},{0,8},{24,16},{16,24},{40,32},{32,40},{56,48},{48,56},{72,64... | collective-permute-start | bytes 110600 | tf_op jit(solution)/shard_map/ppermute | solution.py:282

commit v12 on v10

--- a/solution.py
+++ b/solution.py
@@ -14,7 +14,7 @@
 
 QUAD = 4
 PAD = 8
-CHUNKS = 4
+CHUNKS = 2
 
 
 def split(x):
@@ -59,7 +59,7 @@
 def rough_inverse(d, dt):
     n = d.shape[0]
     eye = identity(n)
-    base = eye + times(d, dt)
+    base = eye + times3(left3(d), right3(dt))
     top = 1.0 + 1.001 * (0.25 * n) ** 2
     start = 2.0 / (1.0 + top)
     gap = (top - 1.0) / (top + 1.0)
@@ -69,13 +69,15 @@
         z = 2.0 * eye - y
         stretch = 2.0 / (2.0 - gap * gap)
         right = right3(z)
+        gap = gap * gap / (2.0 - gap * gap)
         if x is None:
             y = stretch * times3(left3(y), right)
             x = (stretch * start) * z
-        else:
+        elif gap > 0.05:
             both = stretch * times3(jnp.concatenate([left3(x), left3(y)], 0), right)
             x, y = both[:n], both[n:]
-        gap = gap * gap / (2.0 - gap * gap)
+        else:
+            x = stretch * times3(left3(x), right)
     left = eye - times3(left3(x), right3(base))
     x = x + times3(left3(left), right3(x))
     return base, x

time: 103 us -> 102 us (level)
  no operation moved by 1% of the time
where the time goes in v12:
time: 102 us
  waiting for transfers between devices  43.1 us (42%)
  starting transfers between devices  39.8 us (39%)
  Pallas kernels  19 us (19%)
    ppermute x26, starting transfers between devices, from_row(): return lax.ppermute(x, 'row', route)  34.4 us
    ppermute x26, waiting for transfers between devices, from_row(): return lax.ppermute(x, 'row', route)  21.6 us
    ppermute x3, waiting for transfers between devices, hopped_over(): return lax.ppermute(half, ('row', 'pair'), route)  21.5 us
    pallas_call x11, Pallas kernels, vmem_call(): pl.pallas_call(kernel, out_shape=shapes, in_specs=specs, scratch_shapes=s...  17.6 us
    ppermute x3, starting transfers between devices, shifted(): return lax.ppermute(block, 'pair', route)  3.81 us
  transfers between devices with their start and end apart: 32, of which 19 were waited for; matrix products, arithmetic and copies ran while one was open for 0% of the time, Pallas kernels for 9%

profile of v12, /device:TPU:1, one launch (start us, length us, event | category | flops | bytes accessed | tf_op | source)
XLA Modules:
  0.0 102.3 jit_solution(1969196082623636192)
XLA Ops:
  0.0 1.3 %load.1 = (f32[512,256]{1,0:T(8,128)S(1)}, f32[72,128]{1,0:T(8,128)S(1)}, f32[72,128]{1,0:T(8,128)S(1)}) custom-call(s32[1]{0:T(128)} %bitcast.core_ref, f32[512,256]{1,0:T(8,128)} %panel_ref.1), custom_call_target="tpu_custom_call" | custom-call | tf_op jit(solution)/shard_map/load/pallas_call | solution.py:233
  1.4 3.8 %collective-permute-start.9 = (f32[512,256]{1,0:T(8,128)S(1)}, f32[512,256]{1,0:T(8,128)S(1)}, u32[]{:S(2)}, u32[]{:S(2)}) collective-permute-start(f32[512,256]{1,0:T(8,128)S(1)} %get-tuple-element.32.refs_0_), channel_id=1, source_target_pairs={{7,0},{0,1},{1,2},{2,3},{3,4},{4,5},{5,6},{6,7},{15,8},{8,9},{9,10... | collective-permute-start | bytes 1572872 | tf_op jit(solution)/shard_map/ppermute | solution.py:329
  7.0 1.9 %collective-permute-start.1 = (f32[72,128]{1,0:T(8,128)S(1)}, f32[72,128]{1,0:T(8,128)S(1)}, u32[]{:S(2)}, u32[]{:S(2)}) collective-permute-start(f32[72,128]{1,0:T(8,128)S(1)} %add.60), channel_id=1, source_target_pairs={{40,0},{32,8},{56,16},{48,24},{8,32},{0,40},{24,48},{16,56},{104,6... | collective-permute-start | bytes 110600 | tf_op jit(solution)/shard_map/ppermute | solution.py:284
  8.9 1.6 %collective-permute-done.1 = f32[72,128]{1,0:T(8,128)S(1)} collective-permute-done((f32[72,128]{1,0:T(8,128)S(1)}, f32[72,128]{1,0:T(8,128)S(1)}, u32[]{:S(2)}, u32[]{:S(2)}) %collective-permute-start.1) | collective-permute-done | bytes 36896 | tf_op jit(solution)/shard_map/ppermute | solution.py:284
  10.5 6.6 %collective-permute-start.4 = (f32[72,128]{1,0:T(8,128)S(1)}, f32[72,128]{1,0:T(8,128)S(1)}, u32[]{:S(2)}, u32[]{:S(2)}) collective-permute-start(f32[72,128]{1,0:T(8,128)S(1)} %add.61), channel_id=1, source_target_pairs={{168,0},{160,8},{184,16},{176,24},{136,32},{128,40},{152,48},{144,... | collective-permute-start | bytes 110600 | tf_op jit(solution)/shard_map/ppermute | solution.py:284
  17.4 3.5 %collective-permute-start.2 = (f32[72,128]{1,0:T(8,128)S(1)}, f32[72,128]{1,0:T(8,128)S(1)}, u32[]{:S(2)}, u32[]{:S(2)}) collective-permute-start(f32[72,128]{1,0:T(8,128)S(1)} %add.61), channel_id=1, source_target_pairs={{232,0},{224,8},{248,16},{240,24},{72,32},{64,40},{88,48},{80,56},... | collective-permute-start | bytes 110600 | tf_op jit(solution)/shard_map/ppermute | solution.py:284
  20.9 2.0 %collective-permute-done.2 = f32[72,128]{1,0:T(8,128)S(1)} collective-permute-done((f32[72,128]{1,0:T(8,128)S(1)}, f32[72,128]{1,0:T(8,128)S(1)}, u32[]{:S(2)}, u32[]{:S(2)}) %collective-permute-start.2) | collective-permute-done | bytes 36896 | tf_op jit(solution)/shard_map/ppermute | solution.py:284
  23.1 3.3 %collective-permute-done.5 = f32[72,128]{1,0:T(8,128)S(1)} collective-permute-done((f32[72,128]{1,0:T(8,128)S(1)}, f32[72,128]{1,0:T(8,128)S(1)}, u32[]{:S(2)}, u32[]{:S(2)}) %collective-permute-start.5) | collective-permute-done | bytes 36896 | tf_op jit(solution)/shard_map/ppermute | solution.py:284
  26.4 1.4 %collective-permute-start.6 = (f32[72,128]{1,0:T(8,128)S(1)}, f32[72,128]{1,0:T(8,128)S(1)}, u32[]{:S(2)}, u32[]{:S(2)}) collective-permute-start(f32[72,128]{1,0:T(8,128)S(1)} %add.65.mine_ref), channel_id=1, source_target_pairs={{31,0},{24,1},{25,2},{26,3},{27,4},{28,5},{29,6},{30,7},{23,8},{16... | collective-permute-start | bytes 110600 | tf_op jit(solution)/shard_map/ppermute | solution.py:339
  28.5 4.6 %collective-permute-done.6.mine_ref = f32[72,128]{1,0:T(8,128)S(1)} collective-permute-done((f32[72,128]{1,0:T(8,128)S(1)}, f32[72,128]{1,0:T(8,128)S(1)}, u32[]{:S(2)}, u32[]{:S(2)}) %collective-permute-start.6) | collective-permute-done | bytes 36896 | tf_op jit(solution)/shard_map/ppermute | solution.py:339
  33.1 1.8 %shard_map.17 = (f32[128,128]{1,0:T(8,128)S(1)}, f32[128,128]{1,0:T(8,128)S(1)}, f32[128,128]{1,0:T(8,128)S(1)}) custom-call(s32[1]{0:T(128)} %bitcast.core_ref, f32[72,128]{1,0:T(8,128)S(1)} %add.65.mine_ref, f32[72,128]{1,0:T(8,128)S(1)} %collective-permute-done.8.other_ref), custom_call_target="tpu_custom_call" | custom-call | tf_op jit(solution)/shard_map/pallas_call | solution.py:221
  35.8 2.7 %shard_map.19 = (f32[512,128]{1,0:T(8,128)S(1)}, f32[128,128]{1,0:T(8,128)S(1)}, f32[128,128]{1,0:T(8,128)S(1)}, f32[72,128]{1,0:T(8,128)S(1)}, f32[72,128]{1,0:T(8,128)S(1)}) custom-call(s32[1]{0:T(128)} %bitcast.core_ref, f32[72,128]{1,0:T(8,128)S(1)} %collective-permute-done.6.mine_ref, f32[72,128]{1,0:T(8,128)S(1)} %collective-permute-done.7.other_ref, ...), custom_call_target="tpu_custom_call" | custom-call | tf_op jit(solution)/shard_map/pallas_call | solution.py:221
  40.8 2.1 %collective-permute-start.12 = (f32[72,128]{1,0:T(8,128)S(1)}, f32[72,128]{1,0:T(8,128)S(1)}, u32[]{:S(2)}, u32[]{:S(2)}) collective-permute-start(f32[72,128]{1,0:T(8,128)S(1)} %add.66), channel_id=1, source_target_pairs={{24,0},{16,8},{8,16},{0,24},{56,32},{48,40},{40,48},{32,56},{88,64... | collective-permute-start | bytes 110600 | tf_op jit(solution)/shard_map/ppermute | solution.py:284
  43.8 1.2 %collective-permute-done.12 = f32[72,128]{1,0:T(8,128)S(1)} collective-permute-done((f32[72,128]{1,0:T(8,128)S(1)}, f32[72,128]{1,0:T(8,128)S(1)}, u32[]{:S(2)}, u32[]{:S(2)}) %collective-permute-start.12) | collective-permute-done | bytes 36896 | tf_op jit(solution)/shard_map/ppermute | solution.py:284
  45.0 1.3 %collective-permute-done.11 = f32[72,128]{1,0:T(8,128)S(1)} collective-permute-done((f32[72,128]{1,0:T(8,128)S(1)}, f32[72,128]{1,0:T(8,128)S(1)}, u32[]{:S(2)}, u32[]{:S(2)}) %collective-permute-start.11) | collective-permute-done | bytes 36896 | tf_op jit(solution)/shard_map/ppermute | solution.py:284
  46.3 3.5 %collective-permute-start.16 = (f32[72,128]{1,0:T(8,128)S(1)}, f32[72,128]{1,0:T(8,128)S(1)}, u32[]{:S(2)}, u32[]{:S(2)}) collective-permute-start(f32[72,128]{1,0:T(8,128)S(1)} %add_add_fusion.3), channel_id=1, source_target_pairs={{168,0},{160,8},{184,16},{176,24},{136,32},{128,40},{152,48},{144,... | collective-permute-start | bytes 110600 | tf_op jit(solution)/shard_map/ppermute | solution.py:284
  50.4 2.5 %collective-permute-start.14 = (f32[72,128]{1,0:T(8,128)S(1)}, f32[72,128]{1,0:T(8,128)S(1)}, u32[]{:S(2)}, u32[]{:S(2)}) collective-permute-start(f32[72,128]{1,0:T(8,128)S(1)} %add_add_fusion.3), channel_id=1, source_target_pairs={{232,0},{224,8},{248,16},{240,24},{72,32},{64,40},{88,48},{80,56},... | collective-permute-start | bytes 110600 | tf_op jit(solution)/shard_map/ppermute | solution.py:284
  53.6 2.1 %collective-permute-done.14 = f32[72,128]{1,0:T(8,128)S(1)} collective-permute-done((f32[72,128]{1,0:T(8,128)S(1)}, f32[72,128]{1,0:T(8,128)S(1)}, u32[]{:S(2)}, u32[]{:S(2)}) %collective-permute-start.14) | collective-permute-done | bytes 36896 | tf_op jit(solution)/shard_map/ppermute | solution.py:284
  56.3 9.1 %collective-permute-done.17.mine_ref = f32[72,128]{1,0:T(8,128)S(1)} collective-permute-done((f32[72,128]{1,0:T(8,128)S(1)}, f32[72,128]{1,0:T(8,128)S(1)}, u32[]{:S(2)}, u32[]{:S(2)}) %collective-permute-start.17) | collective-permute-done | bytes 36896 | tf_op jit(solution)/shard_map/ppermute | solution.py:339
  65.8 1.8 %shard_map.20 = (f32[128,128]{1,0:T(8,128)S(1)}, f32[128,128]{1,0:T(8,128)S(1)}, f32[128,128]{1,0:T(8,128)S(1)}) custom-call(s32[1]{0:T(128)} %bitcast.core_ref, f32[72,128]{1,0:T(8,128)S(1)} %add_add_fusion.2.mine_ref, f32[72,128]{1,0:T(8,128)S(1)} %collective-permute-done.19.other_ref), custom_call_target="tpu_custom_call" | custom-call | tf_op jit(solution)/shard_map/pallas_call | solution.py:221
  68.5 2.7 %shard_map.23 = (f32[512,128]{1,0:T(8,128)S(1)}, f32[128,128]{1,0:T(8,128)S(1)}, f32[128,128]{1,0:T(8,128)S(1)}, f32[72,128]{1,0:T(8,128)S(1)}, f32[72,128]{1,0:T(8,128)S(1)}) custom-call(s32[1]{0:T(128)} %bitcast.core_ref, f32[72,128]{1,0:T(8,128)S(1)} %collective-permute-done.17.mine_ref, f32[72,128]{1,0:T(8,128)S(1)} %collective-permute-done.18.other_ref, ...), custom_call_target="tpu_custom_call" | custom-call | tf_op jit(solution)/shard_map/pallas_call | solution.py:221
  72.7 1.7 %collective-permute-start.23 = (f32[72,128]{1,0:T(8,128)S(1)}, f32[72,128]{1,0:T(8,128)S(1)}, u32[]{:S(2)}, u32[]{:S(2)}) collective-permute-start(f32[72,128]{1,0:T(8,128)S(1)} %add.73), channel_id=1, source_target_pairs={{24,0},{16,8},{8,16},{0,24},{56,32},{48,40},{40,48},{32,56},{88,64... | collective-permute-start | bytes 110600 | tf_op jit(solution)/shard_map/ppermute | solution.py:284
  74.5 1.2 %collective-permute-start.22 = (f32[72,128]{1,0:T(8,128)S(1)}, f32[72,128]{1,0:T(8,128)S(1)}, u32[]{:S(2)}, u32[]{:S(2)}) collective-permute-start(f32[72,128]{1,0:T(8,128)S(1)} %add.73), channel_id=1, source_target_pairs={{40,0},{32,8},{56,16},{48,24},{8,32},{0,40},{24,48},{16,56},{104,6... | collective-permute-start | bytes 110600 | tf_op jit(solution)/shard_map/ppermute | solution.py:284
  76.7 1.2 %collective-permute-done.22 = f32[72,128]{1,0:T(8,128)S(1)} collective-permute-done((f32[72,128]{1,0:T(8,128)S(1)}, f32[72,128]{1,0:T(8,128)S(1)}, u32[]{:S(2)}, u32[]{:S(2)}) %collective-permute-start.22) | collective-permute-done | bytes 36896 | tf_op jit(solution)/shard_map/ppermute | solution.py:284
  77.9 2.1 %collective-permute-start.27 = (f32[72,128]{1,0:T(8,128)S(1)}, f32[72,128]{1,0:T(8,128)S(1)}, u32[]{:S(2)}, u32[]{:S(2)}) collective-permute-start(f32[72,128]{1,0:T(8,128)S(1)} %add_add_fusion.1), channel_id=1, source_target_pairs={{168,0},{160,8},{184,16},{176,24},{136,32},{128,40},{152,48},{144,... | collective-permute-start | bytes 110600 | tf_op jit(solution)/shard_map/ppermute | solution.py:284
  80.0 2.2 %collective-permute-start.26 = (f32[72,128]{1,0:T(8,128)S(1)}, f32[72,128]{1,0:T(8,128)S(1)}, u32[]{:S(2)}, u32[]{:S(2)}) collective-permute-start(f32[72,128]{1,0:T(8,128)S(1)} %add_add_fusion.1), channel_id=1, source_target_pairs={{64,0},{72,8},{80,16},{88,24},{224,32},{232,40},{240,48},{248,56},... | collective-permute-start | bytes 110600 | tf_op jit(solution)/shard_map/ppermute | solution.py:284
  82.2 1.0 collective-permute-start.25
  83.2 1.3 %collective-permute-done.27 = f32[72,128]{1,0:T(8,128)S(1)} collective-permute-done((f32[72,128]{1,0:T(8,128)S(1)}, f32[72,128]{1,0:T(8,128)S(1)}, u32[]{:S(2)}, u32[]{:S(2)}) %collective-permute-start.27) | collective-permute-done | bytes 36896 | tf_op jit(solution)/shard_map/ppermute | solution.py:284
  84.5 2.5 %collective-permute-done.25 = f32[72,128]{1,0:T(8,128)S(1)} collective-permute-done((f32[72,128]{1,0:T(8,128)S(1)}, f32[72,128]{1,0:T(8,128)S(1)}, u32[]{:S(2)}, u32[]{:S(2)}) %collective-permute-start.25) | collective-permute-done | bytes 36896 | tf_op jit(solution)/shard_map/ppermute | solution.py:284
  87.8 7.9 %collective-permute-done.28.mine_ref = f32[72,128]{1,0:T(8,128)S(1)} collective-permute-done((f32[72,128]{1,0:T(8,128)S(1)}, f32[72,128]{1,0:T(8,128)S(1)}, u32[]{:S(2)}, u32[]{:S(2)}) %collective-permute-start.28) | collective-permute-done | bytes 36896 | tf_op jit(solution)/shard_map/ppermute | solution.py:339
  96.2 1.8 %shard_map.24 = (f32[128,128]{1,0:T(8,128)S(1)}, f32[128,128]{1,0:T(8,128)S(1)}, f32[128,128]{1,0:T(8,128)S(1)}) custom-call(s32[1]{0:T(128)} %bitcast.core_ref, f32[72,128]{1,0:T(8,128)S(1)} %add_add_fusion.mine_ref, f32[72,128]{1,0:T(8,128)S(1)} %collective-permute-done.30.other_ref), custom_call_target="tpu_custom_call" | custom-call | tf_op jit(solution)/shard_map/pallas_call | solution.py:221
  98.9 3.2 %shard_map.27 = f32[512,256]{1,0:T(8,128)} custom-call(s32[1]{0:T(128)} %bitcast.core_ref, f32[72,128]{1,0:T(8,128)S(1)} %collective-permute-done.28.mine_ref, f32[72,128]{1,0:T(8,128)S(1)} %collective-permute-done.29.other_ref, f32[512,128]{1,0:T(8,128)S(1)} %shard_map.25.own_ref, f32[512,128]{1,0:T(8,128)S(1)} %shard_map.26.refs_0_, ...), custom_call_target="tpu_custom_call" | custom-call | tf_op jit(solution)/shard_map/pallas_call | solution.py:221
  (54 shorter events, 15.2 us)
Async XLA Ops:
  1.4 34.5 %collective-permute-start.9 = (f32[512,256]{1,0:T(8,128)S(1)}, f32[512,256]{1,0:T(8,128)S(1)}, u32[]{:S(2)}, u32[]{:S(2)}) collective-permute-start(f32[512,256]{1,0:T(8,128)S(1)} %get-tuple-element.32.refs_0_), channel_id=1, source_target_pairs={{7,0},{0,1},{1,2},{2,3},{3,4},{4,5},{5,6},{6,7},{15,8},{8,9},{9,10... | collective-permute-start | bytes 1572872 | tf_op jit(solution)/shard_map/ppermute | solution.py:329
  5.2 1.8 %collective-permute-start = (f32[72,128]{1,0:T(8,128)S(1)}, f32[72,128]{1,0:T(8,128)S(1)}, u32[]{:S(2)}, u32[]{:S(2)}) collective-permute-start(f32[72,128]{1,0:T(8,128)S(1)} %get-tuple-element.28), channel_id=1, source_target_pairs={{8,0},{0,8},{24,16},{16,24},{40,32},{32,40},{56,48},{48,56},{72,64... | collective-permute-start | bytes 110600 | tf_op jit(solution)/shard_map/ppermute | solution.py:284
  7.0 3.5 %collective-permute-start.1 = (f32[72,128]{1,0:T(8,128)S(1)}, f32[72,128]{1,0:T(8,128)S(1)}, u32[]{:S(2)}, u32[]{:S(2)}) collective-permute-start(f32[72,128]{1,0:T(8,128)S(1)} %add.60), channel_id=1, source_target_pairs={{40,0},{32,8},{56,16},{48,24},{8,32},{0,40},{24,48},{16,56},{104,6... | collective-permute-start | bytes 110600 | tf_op jit(solution)/shard_map/ppermute | solution.py:284
  10.5 10.4 %collective-permute-start.4 = (f32[72,128]{1,0:T(8,128)S(1)}, f32[72,128]{1,0:T(8,128)S(1)}, u32[]{:S(2)}, u32[]{:S(2)}) collective-permute-start(f32[72,128]{1,0:T(8,128)S(1)} %add.61), channel_id=1, source_target_pairs={{168,0},{160,8},{184,16},{176,24},{136,32},{128,40},{152,48},{144,... | collective-permute-start | bytes 110600 | tf_op jit(solution)/shard_map/ppermute | solution.py:284
  17.1 3.7 %collective-permute-start.3 = (f32[72,128]{1,0:T(8,128)S(1)}, f32[72,128]{1,0:T(8,128)S(1)}, u32[]{:S(2)}, u32[]{:S(2)}) collective-permute-start(f32[72,128]{1,0:T(8,128)S(1)} %add.61), channel_id=1, source_target_pairs={{64,0},{72,8},{80,16},{88,24},{224,32},{232,40},{240,48},{248,56},... | collective-permute-start | bytes 110600 | tf_op jit(solution)/shard_map/ppermute | solution.py:284
  17.4 5.5 %collective-permute-start.2 = (f32[72,128]{1,0:T(8,128)S(1)}, f32[72,128]{1,0:T(8,128)S(1)}, u32[]{:S(2)}, u32[]{:S(2)}) collective-permute-start(f32[72,128]{1,0:T(8,128)S(1)} %add.61), channel_id=1, source_target_pairs={{232,0},{224,8},{248,16},{240,24},{72,32},{64,40},{88,48},{80,56},... | collective-permute-start | bytes 110600 | tf_op jit(solution)/shard_map/ppermute | solution.py:284
  22.9 3.5 %collective-permute-start.5 = (f32[72,128]{1,0:T(8,128)S(1)}, f32[72,128]{1,0:T(8,128)S(1)}, u32[]{:S(2)}, u32[]{:S(2)}) collective-permute-start(f32[72,128]{1,0:T(8,128)S(1)} %add_add_fusion.4), channel_id=1, source_target_pairs={{24,0},{16,8},{8,16},{0,24},{56,32},{48,40},{40,48},{32,56},{88,64... | collective-permute-start | bytes 110600 | tf_op jit(solution)/shard_map/ppermute | solution.py:284
  26.4 6.7 %collective-permute-start.6 = (f32[72,128]{1,0:T(8,128)S(1)}, f32[72,128]{1,0:T(8,128)S(1)}, u32[]{:S(2)}, u32[]{:S(2)}) collective-permute-start(f32[72,128]{1,0:T(8,128)S(1)} %add.65.mine_ref), channel_id=1, source_target_pairs={{31,0},{24,1},{25,2},{26,3},{27,4},{28,5},{29,6},{30,7},{23,8},{16... | collective-permute-start | bytes 110600 | tf_op jit(solution)/shard_map/ppermute | solution.py:339
  27.8 5.3 %collective-permute-start.8 = (f32[72,128]{1,0:T(8,128)S(1)}, f32[72,128]{1,0:T(8,128)S(1)}, u32[]{:S(2)}, u32[]{:S(2)}) collective-permute-start(f32[72,128]{1,0:T(8,128)S(1)} %add.65.mine_ref), channel_id=1, source_target_pairs={{8,0},{0,8},{24,16},{16,24},{40,32},{32,40},{56,48},{48,56},{72,64... | collective-permute-start | bytes 110600 | tf_op jit(solution)/shard_map/ppermute | solution.py:284
  33.1 2.7 %collective-permute-start.7 = (f32[72,128]{1,0:T(8,128)S(1)}, f32[72,128]{1,0:T(8,128)S(1)}, u32[]{:S(2)}, u32[]{:S(2)}) collective-permute-start(f32[72,128]{1,0:T(8,128)S(1)} %collective-permute-done.6.mine_ref), channel_id=1, source_target_pairs={{8,0},{0,8},{24,16},{16,24},{40,32},{32,40},{56,48},{48,56},{72,64... | collective-permute-start | bytes 110600 | tf_op jit(solution)/shard_map/ppermute | solution.py:284
  38.6 1.5 %collective-permute-start.10 = (f32[72,128]{1,0:T(8,128)S(1)}, f32[72,128]{1,0:T(8,128)S(1)}, u32[]{:S(2)}, u32[]{:S(2)}) collective-permute-start(f32[72,128]{1,0:T(8,128)S(1)} %get-tuple-element.34), channel_id=1, source_target_pairs={{8,0},{0,8},{24,16},{16,24},{40,32},{32,40},{56,48},{48,56},{72,64... | collective-permute-start | bytes 110600 | tf_op jit(solution)/shard_map/ppermute | solution.py:284
  40.1 3.7 %collective-permute-start.13 = (f32[72,128]{1,0:T(8,128)S(1)}, f32[72,128]{1,0:T(8,128)S(1)}, u32[]{:S(2)}, u32[]{:S(2)}) collective-permute-start(f32[72,128]{1,0:T(8,128)S(1)} %add.66), channel_id=1, source_target_pairs={{48,0},{56,8},{32,16},{40,24},{16,32},{24,40},{0,48},{8,56},{112,6... | collective-permute-start | bytes 110600 | tf_op jit(solution)/shard_map/ppermute | solution.py:284
  40.8 4.2 %collective-permute-start.12 = (f32[72,128]{1,0:T(8,128)S(1)}, f32[72,128]{1,0:T(8,128)S(1)}, u32[]{:S(2)}, u32[]{:S(2)}) collective-permute-start(f32[72,128]{1,0:T(8,128)S(1)} %add.66), channel_id=1, source_target_pairs={{24,0},{16,8},{8,16},{0,24},{56,32},{48,40},{40,48},{32,56},{88,64... | collective-permute-start | bytes 110600 | tf_op jit(solution)/shard_map/ppermute | solution.py:284
  42.9 3.4 %collective-permute-start.11 = (f32[72,128]{1,0:T(8,128)S(1)}, f32[72,128]{1,0:T(8,128)S(1)}, u32[]{:S(2)}, u32[]{:S(2)}) collective-permute-start(f32[72,128]{1,0:T(8,128)S(1)} %add.66), channel_id=1, source_target_pairs={{40,0},{32,8},{56,16},{48,24},{8,32},{0,40},{24,48},{16,56},{104,6... | collective-permute-start | bytes 110600 | tf_op jit(solution)/shard_map/ppermute | solution.py:284
  46.3 6.6 %collective-permute-start.16 = (f32[72,128]{1,0:T(8,128)S(1)}, f32[72,128]{1,0:T(8,128)S(1)}, u32[]{:S(2)}, u32[]{:S(2)}) collective-permute-start(f32[72,128]{1,0:T(8,128)S(1)} %add_add_fusion.3), channel_id=1, source_target_pairs={{168,0},{160,8},{184,16},{176,24},{136,32},{128,40},{152,48},{144,... | collective-permute-start | bytes 110600 | tf_op jit(solution)/shard_map/ppermute | solution.py:284
  49.8 3.8 %collective-permute-start.15 = (f32[72,128]{1,0:T(8,128)S(1)}, f32[72,128]{1,0:T(8,128)S(1)}, u32[]{:S(2)}, u32[]{:S(2)}) collective-permute-start(f32[72,128]{1,0:T(8,128)S(1)} %add_add_fusion.3), channel_id=1, source_target_pairs={{64,0},{72,8},{80,16},{88,24},{224,32},{232,40},{240,48},{248,56},... | collective-permute-start | bytes 110600 | tf_op jit(solution)/shard_map/ppermute | solution.py:284
  50.4 5.3 %collective-permute-start.14 = (f32[72,128]{1,0:T(8,128)S(1)}, f32[72,128]{1,0:T(8,128)S(1)}, u32[]{:S(2)}, u32[]{:S(2)}) collective-permute-start(f32[72,128]{1,0:T(8,128)S(1)} %add_add_fusion.3), channel_id=1, source_target_pairs={{232,0},{224,8},{248,16},{240,24},{72,32},{64,40},{88,48},{80,56},... | collective-permute-start | bytes 110600 | tf_op jit(solution)/shard_map/ppermute | solution.py:284
  52.9 15.6 %collective-permute-start.20 = (f32[512,128]{1,0:T(8,128)S(1)}, f32[512,128]{1,0:T(8,128)S(1)}, u32[]{:S(2)}, u32[]{:S(2)}) collective-permute-start(f32[512,128]{1,0:T(8,128)S(1)} %get-tuple-element.38.refs_1_), channel_id=1, source_target_pairs={{7,0},{0,1},{1,2},{2,3},{3,4},{4,5},{5,6},{6,7},{15,8},{8,9},{9,10... | collective-permute-start | bytes 786440 | tf_op jit(solution)/shard_map/ppermute | solution.py:329
  55.6 9.7 %collective-permute-start.17 = (f32[72,128]{1,0:T(8,128)S(1)}, f32[72,128]{1,0:T(8,128)S(1)}, u32[]{:S(2)}, u32[]{:S(2)}) collective-permute-start(f32[72,128]{1,0:T(8,128)S(1)} %add_add_fusion.2.mine_ref), channel_id=1, source_target_pairs={{31,0},{24,1},{25,2},{26,3},{27,4},{28,5},{29,6},{30,7},{23,8},{16... | collective-permute-start | bytes 110600 | tf_op jit(solution)/shard_map/ppermute | solution.py:339
  55.7 10.0 %collective-permute-start.19 = (f32[72,128]{1,0:T(8,128)S(1)}, f32[72,128]{1,0:T(8,128)S(1)}, u32[]{:S(2)}, u32[]{:S(2)}) collective-permute-start(f32[72,128]{1,0:T(8,128)S(1)} %add_add_fusion.2.mine_ref), channel_id=1, source_target_pairs={{8,0},{0,8},{24,16},{16,24},{40,32},{32,40},{56,48},{48,56},{72,64... | collective-permute-start | bytes 110600 | tf_op jit(solution)/shard_map/ppermute | solution.py:284
  65.3 3.2 %collective-permute-start.18 = (f32[72,128]{1,0:T(8,128)S(1)}, f32[72,128]{1,0:T(8,128)S(1)}, u32[]{:S(2)}, u32[]{:S(2)}) collective-permute-start(f32[72,128]{1,0:T(8,128)S(1)} %collective-permute-done.17.mine_ref), channel_id=1, source_target_pairs={{8,0},{0,8},{24,16},{16,24},{40,32},{32,40},{56,48},{48,56},{72,64... | collective-permute-start | bytes 110600 | tf_op jit(solution)/shard_map/ppermute | solution.py:284
  71.3 1.4 %collective-permute-start.21 = (f32[72,128]{1,0:T(8,128)S(1)}, f32[72,128]{1,0:T(8,128)S(1)}, u32[]{:S(2)}, u32[]{:S(2)}) collective-permute-start(f32[72,128]{1,0:T(8,128)S(1)} %get-tuple-element.42), channel_id=1, source_target_pairs={{8,0},{0,8},{24,16},{16,24},{40,32},{32,40},{56,48},{48,56},{72,64... | collective-permute-start | bytes 110600 | tf_op jit(solution)/shard_map/ppermute | solution.py:284
  72.7 3.8 %collective-permute-start.24 = (f32[72,128]{1,0:T(8,128)S(1)}, f32[72,128]{1,0:T(8,128)S(1)}, u32[]{:S(2)}, u32[]{:S(2)}) collective-permute-start(f32[72,128]{1,0:T(8,128)S(1)} %add.73), channel_id=1, source_target_pairs={{48,0},{56,8},{32,16},{40,24},{16,32},{24,40},{0,48},{8,56},{112,6... | collective-permute-start | bytes 110600 | tf_op jit(solution)/shard_map/ppermute | solution.py:284
  72.7 3.9 %collective-permute-start.23 = (f32[72,128]{1,0:T(8,128)S(1)}, f32[72,128]{1,0:T(8,128)S(1)}, u32[]{:S(2)}, u32[]{:S(2)}) collective-permute-start(f32[72,128]{1,0:T(8,128)S(1)} %add.73), channel_id=1, source_target_pairs={{24,0},{16,8},{8,16},{0,24},{56,32},{48,40},{40,48},{32,56},{88,64... | collective-permute-start | bytes 110600 | tf_op jit(solution)/shard_map/ppermute | solution.py:284
  74.5 3.4 %collective-permute-start.22 = (f32[72,128]{1,0:T(8,128)S(1)}, f32[72,128]{1,0:T(8,128)S(1)}, u32[]{:S(2)}, u32[]{:S(2)}) collective-permute-start(f32[72,128]{1,0:T(8,128)S(1)} %add.73), channel_id=1, source_target_pairs={{40,0},{32,8},{56,16},{48,24},{8,32},{0,40},{24,48},{16,56},{104,6... | collective-permute-start | bytes 110600 | tf_op jit(solution)/shard_map/ppermute | solution.py:284
  77.9 6.6 %collective-permute-start.27 = (f32[72,128]{1,0:T(8,128)S(1)}, f32[72,128]{1,0:T(8,128)S(1)}, u32[]{:S(2)}, u32[]{:S(2)}) collective-permute-start(f32[72,128]{1,0:T(8,128)S(1)} %add_add_fusion.1), channel_id=1, source_target_pairs={{168,0},{160,8},{184,16},{176,24},{136,32},{128,40},{152,48},{144,... | collective-permute-start | bytes 110600 | tf_op jit(solution)/shard_map/ppermute | solution.py:284
  80.0 4.5 %collective-permute-start.26 = (f32[72,128]{1,0:T(8,128)S(1)}, f32[72,128]{1,0:T(8,128)S(1)}, u32[]{:S(2)}, u32[]{:S(2)}) collective-permute-start(f32[72,128]{1,0:T(8,128)S(1)} %add_add_fusion.1), channel_id=1, source_target_pairs={{64,0},{72,8},{80,16},{88,24},{224,32},{232,40},{240,48},{248,56},... | collective-permute-start | bytes 110600 | tf_op jit(solution)/shard_map/ppermute | solution.py:284
  82.2 4.8 %collective-permute-start.25 = (f32[72,128]{1,0:T(8,128)S(1)}, f32[72,128]{1,0:T(8,128)S(1)}, u32[]{:S(2)}, u32[]{:S(2)}) collective-permute-start(f32[72,128]{1,0:T(8,128)S(1)} %add_add_fusion.1), channel_id=1, source_target_pairs={{232,0},{224,8},{248,16},{240,24},{72,32},{64,40},{88,48},{80,56},... | collective-permute-start | bytes 110600 | tf_op jit(solution)/shard_map/ppermute | solution.py:284
  83.2 15.7 %collective-permute-start.31 = (f32[512,128]{1,0:T(8,128)S(1)}, f32[512,128]{1,0:T(8,128)S(1)}, u32[]{:S(2)}, u32[]{:S(2)}) collective-permute-start(f32[512,128]{1,0:T(8,128)S(1)} %get-tuple-element.46.refs_1_), channel_id=1, source_target_pairs={{7,0},{0,1},{1,2},{2,3},{3,4},{4,5},{5,6},{6,7},{15,8},{8,9},{9,10... | collective-permute-start | bytes 786440 | tf_op jit(solution)/shard_map/ppermute | solution.py:329
  87.0 8.6 %collective-permute-start.28 = (f32[72,128]{1,0:T(8,128)S(1)}, f32[72,128]{1,0:T(8,128)S(1)}, u32[]{:S(2)}, u32[]{:S(2)}) collective-permute-start(f32[72,128]{1,0:T(8,128)S(1)} %add_add_fusion.mine_ref), channel_id=1, source_target_pairs={{31,0},{24,1},{25,2},{26,3},{27,4},{28,5},{29,6},{30,7},{23,8},{16... | collective-permute-start | bytes 110600 | tf_op jit(solution)/shard_map/ppermute | solution.py:339
  87.1 9.1 %collective-permute-start.30 = (f32[72,128]{1,0:T(8,128)S(1)}, f32[72,128]{1,0:T(8,128)S(1)}, u32[]{:S(2)}, u32[]{:S(2)}) collective-permute-start(f32[72,128]{1,0:T(8,128)S(1)} %add_add_fusion.mine_ref), channel_id=1, source_target_pairs={{8,0},{0,8},{24,16},{16,24},{40,32},{32,40},{56,48},{48,56},{72,64... | collective-permute-start | bytes 110600 | tf_op jit(solution)/shard_map/ppermute | solution.py:284
  95.6 3.3 %collective-permute-start.29 = (f32[72,128]{1,0:T(8,128)S(1)}, f32[72,128]{1,0:T(8,128)S(1)}, u32[]{:S(2)}, u32[]{:S(2)}) collective-permute-start(f32[72,128]{1,0:T(8,128)S(1)} %collective-permute-done.28.mine_ref), channel_id=1, source_target_pairs={{8,0},{0,8},{24,16},{16,24},{40,32},{32,40},{56,48},{48,56},{72,64... | collective-permute-start | bytes 110600 | tf_op jit(solution)/shard_map/ppermute | solution.py:284
